TPU v7x, 256 devices: a whole 4x4x8 slice. The times are simulated.
256 devices in a mesh: px: 8 (over y, core), pz: 16 (over z, x_lo), tr: 2 (over x_hi).
Axes of the slice: x: 4 (x_hi: 2, x_lo: 2; x = x_hi * 2 + x_lo), y: 4, z: 8, core: 2. Of those that a mesh axis runs over, the one named last changes fastest.
Arguments:
- velocity: float32 [1024, 64, 3, 256], P('pz', ('px', 'tr')), may hold values from -6 to 6
- viscosity: float32 [1024, 64, 256], P('pz', ('px', 'tr')), may hold values from 0.5 to 2
- implicit_inverse: float32 [1024, 1024], replicated, may hold values from -0.1875 to 0.1875
- row_index: int32 [8, 16, 2, 32, 24], P('px', 'pz', 'tr'), may hold values from 0 to 255, as said below
- row_counts: int32 [8, 16, 2, 32], P('px', 'pz', 'tr'), may hold values from 0 to 24, as said below
- weight_in: bfloat16 [32, 768, 1024], P(('pz', 'tr')), may hold values from -0.21875 to 0.21875
- weight_out: bfloat16 [32, 1024, 768], P(('pz', 'tr')), may hold values from -0.1875 to 0.1875
Outputs:
- velocity_out: float32 [1024, 64, 3, 256], P('pz', ('px', 'tr'))
- grad_in: float32 [32, 768, 1024], P(('pz', 'tr'), 'px')
- grad_out: float32 [32, 1024, 768], P(('pz', 'tr'), 'px')
Inputs may be any that keep to these rules, and one draw needn't show every extreme that they name: `row_index`: A slot's row number within its source device's block of 64 x 4 rows: wall-normal offset times 4 plus spanwise offset; on the first pz index rows lean toward the lower wall, on the last toward the upper wall; slots at or beyond the count are read but unused. `row_counts`: the first pz index, the last one, and every member whose number is a multiple of 8 have all 24 slots live.
All inputs are finite; a program needn't handle non-finite values.
Results may differ from a plain program's by a relative error of at most 0.02.
Values may be sent and summed in bfloat16 or wider, within the bound.
No kernel may reach another device: no remote copies, remote signals or barrier semaphores. Data moves between devices by JAX's collectives and lax.ppermute only.
A program may use at most 64 MiB of HBM per device.

v0:
```python
import math

import jax
import jax.numpy as jnp
from jax import lax
from jax.sharding import PartitionSpec as P

diffusion_factor = 0.08


def with_halo(array, sides, width):
    for axis, dim in sides:
        size, length = (lax.axis_size(axis), array.shape[dim])
        up = [(i, (i + 1) % size) for i in range(size)]
        down = [(j, i) for i, j in up]
        last = lax.slice_in_dim(array, length - width, length, axis=dim)
        initial = lax.slice_in_dim(array, 0, width, axis=dim)
        before = lax.ppermute(last, axis, up)
        after = lax.ppermute(initial, axis, down)
        array = jnp.concatenate([before, array, after], axis=dim)
    return array


def substep(current, viscosity, implicit_inverse):
    padded = with_halo(current.astype(jnp.bfloat16), (("pz", 0), (("px", "tr"), 1)), 1).astype(
        current.dtype
    )
    rows_here = current.shape[0]
    position = lax.axis_index("pz")
    row_number = jnp.arange(rows_here, dtype=jnp.int32)[:, None, None, None]
    keep_lower = jnp.logical_or(position > 0, row_number > 0)
    keep_upper = jnp.logical_or(position < lax.axis_size("pz") - 1, row_number < rows_here - 1)
    neighbours = jnp.where(keep_lower, padded[:-2, 1:-1], 0.0) + jnp.where(
        keep_upper, padded[2:, 1:-1], 0.0
    )
    neighbours = neighbours + padded[1:-1, :-2] + padded[1:-1, 2:]
    neighbours = neighbours + jnp.roll(current, 1, 3) + jnp.roll(current, -1, 3)
    explicit = current + diffusion_factor * viscosity[:, :, None, :] * (neighbours - 6.0 * current)
    columns = lax.all_to_all(
        explicit.reshape(rows_here, -1).astype(jnp.bfloat16),
        "pz",
        split_axis=1,
        concat_axis=0,
        tiled=True,
    ).astype(jnp.float32)
    mixed_cols = jnp.dot(
        implicit_inverse,
        columns,
        precision=lax.Precision.HIGHEST,
        preferred_element_type=jnp.float32,
    )
    planes = lax.all_to_all(
        mixed_cols.astype(jnp.bfloat16), "pz", split_axis=0, concat_axis=1, tiled=True
    ).astype(mixed_cols.dtype)
    return planes.reshape(current.shape)


def pick_rows(current, row_index, row_counts):
    member_count = row_index.shape[3]
    slot_count = row_index.shape[4]
    row_table = current.reshape(current.shape[0] * current.shape[1], -1)
    chosen = jnp.take(row_table, row_index.reshape(-1), axis=0)
    live_slot = (
        jnp.arange(slot_count, dtype=jnp.int32)[None, :] < row_counts.reshape(member_count, 1)
    ).reshape(-1, 1)
    return (
        jnp.where(live_slot, chosen, 0.0).astype(jnp.bfloat16).reshape(member_count, slot_count, -1)
    )


def per_device(velocity, viscosity, implicit_inverse, row_index, row_counts, weight_in, weight_out):
    after_one = substep(velocity, viscosity, implicit_inverse)
    after_two = substep(after_one, viscosity, implicit_inverse)
    sent_inputs, sent_targets = (
        lax.all_to_all(
            pick_rows(after_one, row_index, row_counts),
            ("pz", "tr"),
            split_axis=0,
            concat_axis=0,
            tiled=True,
        ),
        lax.all_to_all(
            pick_rows(after_two, row_index, row_counts),
            ("pz", "tr"),
            split_axis=0,
            concat_axis=0,
            tiled=True,
        ),
    )
    row_width = sent_inputs.shape[-1]
    batch_in = sent_inputs.reshape(-1, row_width)
    batch_target = sent_targets.reshape(-1, row_width)
    member_in = weight_in[0]
    member_out = weight_out[0]
    loss_scale = 1.0 / math.sqrt(lax.axis_size("px") * batch_in.shape[0])
    preact = jnp.dot(batch_in, member_in, preferred_element_type=jnp.float32)
    logistic = jax.nn.sigmoid(preact)
    hidden = (preact * logistic).astype(jnp.bfloat16)
    predicted = jnp.dot(hidden, member_out, preferred_element_type=jnp.float32)
    delta_out = ((predicted - batch_target.astype(jnp.float32)) * loss_scale).astype(jnp.bfloat16)
    back_hidden = lax.dot_general(
        delta_out, member_out, (((1,), (1,)), ((), ())), preferred_element_type=jnp.float32
    )
    delta_in = (back_hidden * logistic * (1.0 + preact * (1.0 - logistic))).astype(jnp.bfloat16)
    part_in = lax.dot_general(
        batch_in, delta_in, (((0,), (0,)), ((), ())), preferred_element_type=jnp.float32
    ).astype(jnp.bfloat16)
    part_out = lax.dot_general(
        hidden, delta_out, (((0,), (0,)), ((), ())), preferred_element_type=jnp.float32
    ).astype(jnp.bfloat16)
    part_in, part_out = lax.optimization_barrier((part_in, part_out))
    part_in = part_in.astype(jnp.float32)
    part_out = part_out.astype(jnp.float32)
    share_in, share_out = (
        lax.psum_scatter(
            part_in.astype(jnp.bfloat16), "px", scatter_dimension=0, tiled=True
        ).astype(jnp.float32),
        lax.psum_scatter(
            part_out.astype(jnp.bfloat16), "px", scatter_dimension=0, tiled=True
        ).astype(jnp.float32),
    )
    return (after_two, share_in[None], share_out[None])


def solution(mesh):
    in_specs = (
        P("pz", ("px", "tr"), None, None),
        P("pz", ("px", "tr"), None),
        P(),
        P("px", "pz", "tr", None, None),
        P("px", "pz", "tr", None),
        P(("pz", "tr"), None, None),
        P(("pz", "tr"), None, None),
    )
    out_specs = (
        P("pz", ("px", "tr"), None, None),
        P(("pz", "tr"), "px", None),
        P(("pz", "tr"), "px", None),
    )
    return jax.shard_map(
        per_device, mesh=mesh, in_specs=in_specs, out_specs=out_specs, check_vma=False
    )
```

profile of v0, /device:TPU:2, one launch (start us, length us, event | category | flops | bytes accessed | tf_op | source)
XLA Modules:
  0.0 329.3 jit_solution(13165785521015189481)
XLA Ops:
  7.2 1.6 copy.52
  8.8 0.6 fusion.35
  9.4 1.9 collective-permute-start
  11.6 1.0 fusion.30
  12.7 1.6 fusion.31
  14.4 1.2 copy.51
  16.0 0.7 copy-done.2
  17.3 2.1 collective-permute-start.2
  19.4 3.3 %collective-permute-start.3 = (bf16[66,1,3,256]{3,2,1,0:T(4,128)(2,1)S(1)}, bf16[66,1,3,256]{3,2,1,0:T(4,128)(2,1)S(1)}, u32[]{:S(2)}, u32[]{:S(2)}) collective-permute-start(bf16[66,1,3,256]{3,2,1,0:T(4,128)(2,1)S(1)} %get-tuple-element.23), channel_id=1, source_target_pairs={{1,0},{32,1},{33,32},{64,33},{65,64},{96,65},{97,96},{128,97},{129... | collective-permute-start | bytes 304136 | tf_op jit(solution)/shard_map/ppermute | solution.py:19
  22.7 3.8 %collective-permute-done.2 = bf16[66,1,3,256]{3,2,1,0:T(4,128)(2,1)S(1)} collective-permute-done((bf16[66,1,3,256]{3,2,1,0:T(4,128)(2,1)S(1)}, bf16[66,1,3,256]{3,2,1,0:T(4,128)(2,1)S(1)}, u32[]{:S(2)}, u32[]{:S(2)}) %collective-permute-start.2) | collective-permute-done | bytes 101408 | tf_op jit(solution)/shard_map/ppermute | solution.py:18
  27.6 2.3 fusion.27
  30.6 26.6 %all_to_all.74 = bf16[64,16,192]{2,0,1:T(8,128)(2,1)S(1)} all-to-all(bf16[64,16,192]{2,0,1:T(8,128)(2,1)S(1)} %copy.36), channel_id=1, replica_groups=mesh['px'=8,'pz'=16,'tr'=2] {'pz'}, dimensions={1} | all-to-all | bytes 786432 | tf_op jit(solution)/shard_map/all_to_all | solution.py:39
  57.1 4.8 %fusion.13 = bf16[1024,192]{0,1:T(8,128)(2,1)S(1)} fusion(bf16[1024,192]{1,0:T(8,128)(2,1)S(1)} %bitcast.56, f32[1024,1024]{1,0:T(8,128)} %param.11), kind=kOutput, calls=%fused_computation.21 | convolution fusion | flops 2416115712 | bytes 4980736 | tf_op jit(solution)/shard_map/dot_general | solution.py:46
  62.1 19.7 %all_to_all.75 = bf16[16,64,192]{2,1,0:T(8,128)(2,1)S(1)} all-to-all(bf16[16,64,192]{2,1,0:T(8,128)(2,1)S(1)} %bitcast.58), channel_id=1, replica_groups=mesh['px'=8,'pz'=16,'tr'=2] {'pz'}, dimensions={0} | all-to-all | bytes 786432 | tf_op jit(solution)/shard_map/all_to_all | solution.py:52
  81.9 1.1 copy.38
  83.2 1.1 collective-permute-start.4
  84.3 1.1 collective-permute-start.5
  85.4 1.8 all_to_all.60
  88.1 0.8 collective-permute-done.5
  89.0 2.4 collective-permute-start.6
  91.4 3.0 collective-permute-start.7
  94.7 3.0 collective-permute-done.6
  97.7 1.2 collective-permute-done.7
  99.4 2.9 fusion.28
  102.3 1.7 convert_element_type.107
  104.2 23.2 %all_to_all.76 = bf16[64,16,192]{2,0,1:T(8,128)(2,1)S(1)} all-to-all(bf16[64,16,192]{2,0,1:T(8,128)(2,1)S(1)} %copy.39), channel_id=1, replica_groups=mesh['px'=8,'pz'=16,'tr'=2] {'pz'}, dimensions={1} | all-to-all | bytes 786432 | tf_op jit(solution)/shard_map/all_to_all | solution.py:39
  127.3 4.8 %fusion.14 = bf16[1024,192]{0,1:T(8,128)(2,1)S(1)} fusion(bf16[1024,192]{1,0:T(8,128)(2,1)S(1)} %bitcast.57, f32[1024,1024]{1,0:T(8,128)} %param.11), kind=kOutput, calls=%fused_computation.22 | convolution fusion | flops 2416115712 | bytes 4980736 | tf_op jit(solution)/shard_map/dot_general | solution.py:46
  132.1 1.0 copy.40
  133.1 5.1 %all-to-all-start.3 = ((bf16[16,64,192]{2,1,0:T(8,128)(2,1)}), bf16[16,64,192]{2,1,0:T(8,128)(2,1)S(1)}, u32[]{:S(2)}, u32[]{:S(2)}) async-start(bf16[16,64,192]{2,1,0:T(8,128)(2,1)} %bitcast.8), calls=%async_computation.3 | async-start | bytes 1048576 | tf_op jit(solution)/shard_map/all_to_all | solution.py:52
  139.4 3.5 %gather_fusion = bf16[768,768]{1,0:T(8,128)(2,1)} fusion(bf16[256,768]{1,0:T(8,128)(2,1)S(1)} %reshape.99, s32[1024]{0:T(1024)S(1)} %pad_clamp_fusion), kind=kCustom, calls=%fused_computation.clone | custom fusion | bytes 2362368 | tf_op jit(solution)/shard_map/jit(_take)/gather | solution.py:62
  142.9 10.2 %all-to-all-done.3 = bf16[16,64,192]{2,1,0:T(8,128)(2,1)S(1)} async-done(((bf16[16,64,192]{2,1,0:T(8,128)(2,1)}), bf16[16,64,192]{2,1,0:T(8,128)(2,1)S(1)}, u32[]{:S(2)}, u32[]{:S(2)}) %all-to-all-start.3) | async-done | bytes 393248 | tf_op jit(solution)/shard_map/all_to_all | solution.py:52
  153.2 0.6 copy.41
  154.3 3.5 %gather_fusion.1 = bf16[768,768]{1,0:T(8,128)(2,1)} fusion(bf16[256,768]{1,0:T(8,128)(2,1)S(1)} %reshape.100, s32[1024]{0:T(1024)S(1)} %pad_clamp_fusion), kind=kCustom, calls=%fused_computation.1.clone | custom fusion | bytes 2362368 | tf_op jit(solution)/shard_map/jit(_take)/gather | solution.py:62
  157.8 3.3 %fusion.2 = (bf16[768,768]{1,0:T(8,128)(2,1)}, bf16[768,768]{1,0:T(8,128)(2,1)S(1)}) fusion(bf16[768,768]{1,0:T(8,128)(2,1)} %gather_fusion.1, pred[768]{0:T(1024)(128)(4,1)S(1)} %compare_and_fusion, pred[768]{0:T(1024)(128)(4,1)S(1)} %lt.54, bf16[768,768]{1,0:T(8,128)(2,1)} %gather_fusion), kind=kLoop, calls=%fused_computation.9 | loop fusion | flops 2359296 | bytes 4720128 | tf_op jit(solution)/shard_map/convert_element_type | solution.py:67
  161.1 40.0 %all_to_all.77 = bf16[32,24,768]{2,1,0:T(8,128)(2,1)} all-to-all(bf16[32,24,768]{2,1,0:T(8,128)(2,1)S(1)} %bitcast.55), channel_id=1, replica_groups=mesh['px'=8,'pz'=16,'tr'=2] {'pz','tr'}, dimensions={0} | all-to-all | bytes 2359296 | tf_op jit(solution)/shard_map/all_to_all | solution.py:75
  201.1 5.9 %all-to-all-start.5 = ((bf16[32,24,768]{2,1,0:T(8,128)(2,1)}), bf16[32,24,768]{2,1,0:T(8,128)(2,1)}, u32[]{:S(2)}, u32[]{:S(2)}) async-start(bf16[32,24,768]{2,1,0:T(8,128)(2,1)} %bitcast.54), calls=%async_computation.5 | async-start | bytes 2359296 | tf_op jit(solution)/shard_map/all_to_all | solution.py:82
  207.0 4.8 %fusion.7 = f32[768,1024]{1,0:T(8,128)} fusion(bf16[768,768]{1,0:T(8,128)(2,1)} %bitcast.59, bf16[1,768,1024]{2,1,0:T(8,128)(2,1)} %param.14), kind=kOutput, calls=%fused_computation.17 | convolution fusion | flops 1207959552 | bytes 5898240 | tf_op jit(solution)/shard_map/dot_general | solution.py:96
  211.8 24.9 %all-to-all-done.5 = bf16[32,24,768]{2,1,0:T(8,128)(2,1)} async-done(((bf16[32,24,768]{2,1,0:T(8,128)(2,1)}), bf16[32,24,768]{2,1,0:T(8,128)(2,1)}, u32[]{:S(2)}, u32[]{:S(2)}) %all-to-all-start.5) | async-done | bytes 1179680 | tf_op jit(solution)/shard_map/all_to_all | solution.py:82
  236.7 5.0 %fusion.1 = bf16[768,768]{1,0:T(8,128)(2,1)} fusion(bf16[768,768]{1,0:T(8,128)(2,1)} %bitcast.21, bf16[1,1024,768]{2,1,0:T(8,128)(2,1)S(1)} %copy-done, f32[768,1024]{1,0:T(8,128)} %fusion.7), kind=kOutput, calls=%fused_computation.7 | convolution fusion | flops 1214251008 | bytes 7077888 | tf_op jit(solution)/shard_map/dot_general | solution.py:99
  241.7 6.7 %convolution_convert_fusion.1 = bf16[768,1024]{1,0:T(8,128)(2,1)} fusion(bf16[768,768]{1,0:T(8,128)(2,1)} %bitcast.60, f32[768,1024]{1,0:T(8,128)} %fusion.7, bf16[768,768]{1,0:T(8,128)(2,1)} %fusion.1, bf16[1,1024,768]{2,1,0:T(8,128)(2,1)S(1)} %copy-done), kind=kOutput, calls=%fused_computation.13 | convolution fusion | flops 2423783424 | bytes 8650752 | tf_op jit(solution)/shard_map/dot_general | solution.py:105
  248.5 5.1 %convolution_convert_fusion = bf16[1024,768]{1,0:T(8,128)(2,1)} fusion(bf16[768,768]{1,0:T(8,128)(2,1)} %fusion.1, f32[768,1024]{1,0:T(8,128)} %fusion.7), kind=kOutput, calls=%fused_computation.12 | convolution fusion | flops 1212678144 | bytes 5898240 | tf_op jit(solution)/shard_map/dot_general | solution.py:108
  253.6 0.7 reduce-scatter.3.cloned.1.call-update
  254.3 1.7 reshape.98
  256.0 2.3 copy.45
  258.3 25.8 %reduce-scatter.5.cloned.1.call-done = bf16[128,768]{1,0:T(8,128)(2,1)} async-done(((bf16[1024,768]{1,0:T(8,128)(2,1)}), bf16[128,768]{1,0:T(8,128)(2,1)}) %reduce-scatter.5.cloned.1.call-update) | async-done | bytes 196624 | tf_op jit(solution)/shard_map/reduce_scatter | solution.py:118
  284.1 1.7 bitcast_convert_fusion
  285.8 35.0 %reduce-scatter.3.cloned.1.call-done = bf16[96,1024]{1,0:T(8,128)(2,1)} async-done(((bf16[768,1024]{1,0:T(8,128)(2,1)}), bf16[96,1024]{1,0:T(8,128)(2,1)}) %reduce-scatter.3.cloned.1.call-update) | async-done | bytes 196624 | tf_op jit(solution)/shard_map/reduce_scatter | solution.py:115
  320.8 1.7 bitcast_convert_fusion.1
  (53 shorter events, 7.3 us)
Async XLA Ops:
  7.2 229.5 %copy-start = (bf16[1,1024,768]{2,1,0:T(8,128)(2,1)S(1)}, bf16[1,1024,768]{2,1,0:T(8,128)(2,1)}, u32[]{:S(2)}) copy-start(bf16[1,1024,768]{2,1,0:T(8,128)(2,1)} %param.15) | copy-start | bytes 4718596
  7.2 4.5 %copy-start.1 = (f32[64,4,3,256]{3,1,2,0:T(4,128)S(1)}, f32[64,4,3,256]{3,1,2,0:T(4,128)}, u32[]{:S(2)}) copy-start(f32[64,4,3,256]{3,1,2,0:T(4,128)} %param.9) | copy-start | bytes 2359300
  9.4 7.7 %collective-permute-start = (bf16[1,4,3,256]{3,2,1,0:T(4,128)(2,1)}, bf16[1,4,3,256]{3,2,1,0:T(4,128)(2,1)S(1)}, u32[]{:S(2)}, u32[]{:S(2)}) collective-permute-start(bf16[1,4,3,256]{3,2,1,0:T(4,128)(2,1)} %get-tuple-element.28), channel_id=1, source_target_pairs={{0,2},{2,4},{4,6},{6,8},{8,10},{10,12},{12,14},{14,16},{16,18},{18... | collective-permute-start | bytes 18440 | tf_op jit(solution)/shard_map/ppermute | solution.py:18
  11.2 5.8 %collective-permute-start.1 = (bf16[1,4,3,256]{3,2,1,0:T(4,128)(2,1)}, bf16[1,4,3,256]{3,2,1,0:T(4,128)(2,1)S(1)}, u32[]{:S(2)}, u32[]{:S(2)}) collective-permute-start(bf16[1,4,3,256]{3,2,1,0:T(4,128)(2,1)} %get-tuple-element.29), channel_id=1, source_target_pairs={{2,0},{4,2},{6,4},{8,6},{10,8},{12,10},{14,12},{16,14},{18,16},{20... | collective-permute-start | bytes 18440 | tf_op jit(solution)/shard_map/ppermute | solution.py:19
  12.7 1.6 copy-start.4
  14.3 1.4 copy-start.3
  15.6 1.1 copy-start.2
  17.3 9.3 %collective-permute-start.2 = (bf16[66,1,3,256]{3,2,1,0:T(4,128)(2,1)S(1)}, bf16[66,1,3,256]{3,2,1,0:T(4,128)(2,1)S(1)}, u32[]{:S(2)}, u32[]{:S(2)}) collective-permute-start(bf16[66,1,3,256]{3,2,1,0:T(4,128)(2,1)S(1)} %get-tuple-element.22), channel_id=1, source_target_pairs={{0,1},{1,32},{32,33},{33,64},{64,65},{65,96},{96,97},{97,128},{128... | collective-permute-start | bytes 304136 | tf_op jit(solution)/shard_map/ppermute | solution.py:18
  19.4 7.6 %collective-permute-start.3 = (bf16[66,1,3,256]{3,2,1,0:T(4,128)(2,1)S(1)}, bf16[66,1,3,256]{3,2,1,0:T(4,128)(2,1)S(1)}, u32[]{:S(2)}, u32[]{:S(2)}) collective-permute-start(bf16[66,1,3,256]{3,2,1,0:T(4,128)(2,1)S(1)} %get-tuple-element.23), channel_id=1, source_target_pairs={{1,0},{32,1},{33,32},{64,33},{65,64},{96,65},{97,96},{128,97},{129... | collective-permute-start | bytes 304136 | tf_op jit(solution)/shard_map/ppermute | solution.py:19
  83.2 4.6 %collective-permute-start.4 = (bf16[1,4,3,256]{3,2,1,0:T(4,128)(2,1)S(1)}, bf16[1,4,3,256]{3,2,1,0:T(4,128)(2,1)S(1)}, u32[]{:S(2)}, u32[]{:S(2)}) collective-permute-start(bf16[1,4,3,256]{3,2,1,0:T(4,128)(2,1)S(1)} %slice.95), channel_id=1, source_target_pairs={{0,2},{2,4},{4,6},{6,8},{8,10},{10,12},{12,14},{14,16},{16,18},{18... | collective-permute-start | bytes 18440 | tf_op jit(solution)/shard_map/ppermute | solution.py:18
  84.3 4.5 %collective-permute-start.5 = (bf16[1,4,3,256]{3,2,1,0:T(4,128)(2,1)S(1)}, bf16[1,4,3,256]{3,2,1,0:T(4,128)(2,1)S(1)}, u32[]{:S(2)}, u32[]{:S(2)}) collective-permute-start(bf16[1,4,3,256]{3,2,1,0:T(4,128)(2,1)S(1)} %slice.97), channel_id=1, source_target_pairs={{2,0},{4,2},{6,4},{8,6},{10,8},{12,10},{14,12},{16,14},{18,16},{20... | collective-permute-start | bytes 18440 | tf_op jit(solution)/shard_map/ppermute | solution.py:19
  89.0 8.7 %collective-permute-start.6 = (bf16[66,1,3,256]{3,2,1,0:T(4,128)(2,1)S(1)}, bf16[66,1,3,256]{3,2,1,0:T(4,128)(2,1)S(1)}, u32[]{:S(2)}, u32[]{:S(2)}) collective-permute-start(bf16[66,1,3,256]{3,2,1,0:T(4,128)(2,1)S(1)} %get-tuple-element.20), channel_id=1, source_target_pairs={{0,1},{1,32},{32,33},{33,64},{64,65},{65,96},{96,97},{97,128},{128... | collective-permute-start | bytes 304136 | tf_op jit(solution)/shard_map/ppermute | solution.py:18
  91.4 7.5 %collective-permute-start.7 = (bf16[66,1,3,256]{3,2,1,0:T(4,128)(2,1)S(1)}, bf16[66,1,3,256]{3,2,1,0:T(4,128)(2,1)S(1)}, u32[]{:S(2)}, u32[]{:S(2)}) collective-permute-start(bf16[66,1,3,256]{3,2,1,0:T(4,128)(2,1)S(1)} %get-tuple-element.21), channel_id=1, source_target_pairs={{1,0},{32,1},{33,32},{64,33},{65,64},{96,65},{97,96},{128,97},{129... | collective-permute-start | bytes 304136 | tf_op jit(solution)/shard_map/ppermute | solution.py:19
  132.1 6.1 %copy-start.6 = (s32[1,1,1,32]{3,2,1,0:T(1,128)S(1)}, s32[1,1,1,32]{3,2,1,0:T(1,128)}, u32[]{:S(2)}) copy-start(s32[1,1,1,32]{3,2,1,0:T(1,128)} %param.13) | copy-start | bytes 388
  132.1 6.3 %copy-start.5 = (s32[1,1,1,32,24]{3,4,2,1,0:T(8,128)S(1)}, s32[1,1,1,32,24]{3,4,2,1,0:T(8,128)}, u32[]{:S(2)}) copy-start(s32[1,1,1,32,24]{3,4,2,1,0:T(8,128)} %param.12) | copy-start | bytes 9220
  133.1 20.0 %all-to-all-start.3 = ((bf16[16,64,192]{2,1,0:T(8,128)(2,1)}), bf16[16,64,192]{2,1,0:T(8,128)(2,1)S(1)}, u32[]{:S(2)}, u32[]{:S(2)}) async-start(bf16[16,64,192]{2,1,0:T(8,128)(2,1)} %bitcast.8), calls=%async_computation.3 | async-start | bytes 1048576 | tf_op jit(solution)/shard_map/all_to_all | solution.py:52
  201.1 35.6 %all-to-all-start.5 = ((bf16[32,24,768]{2,1,0:T(8,128)(2,1)}), bf16[32,24,768]{2,1,0:T(8,128)(2,1)}, u32[]{:S(2)}, u32[]{:S(2)}) async-start(bf16[32,24,768]{2,1,0:T(8,128)(2,1)} %bitcast.54), calls=%async_computation.5 | async-start | bytes 2359296 | tf_op jit(solution)/shard_map/all_to_all | solution.py:82
  206.9 77.1 %reduce-scatter.5.cloned.1.call-start = ((), (), s32[]{:S(2)}) async-start(), calls=%async_computation.9 | async-start | bytes 1769472 | tf_op jit(solution)/shard_map/reduce_scatter | solution.py:118
  253.6 67.2 %reduce-scatter.3.cloned.1.call-start = ((), (), s32[]{:S(2)}) async-start(), calls=%async_computation.8 | async-start | bytes 1769472 | tf_op jit(solution)/shard_map/reduce_scatter | solution.py:115
Sparse Core Ops, SparseCore 0:
  253.7 30.3 reduce-scatter.4
  286.6 34.1 reduce-scatter.2
where the time goes:
time: 330 us; the launch traced here: 329 us
  blocking collectives  109 us (33%)
  waiting for transfers between devices  106 us (32%)
  matrix products  31.2 us (9%)
  local copies, waits for them, and re-layouts  28.5 us (9%)
  starting transfers between devices  26.4 us (8%)
  between operations  14.4 us (4%)
  other arithmetic  13.5 us (4%)
    all_to_all x2, blocking collectives, substep(): lax.all_to_all(explicit.reshape(rows_here, -1).astype(jnp.bfloat16), 'pz'...  49.7 us
    all_to_all x1, blocking collectives, per_device(): lax.all_to_all(pick_rows(after_one, row_index, row_counts), ('pz', 'tr'),...  40 us
    reduce_scatter x1, waiting for transfers between devices, per_device(): lax.psum_scatter(part_in.astype(jnp.bfloat16), 'px', scatter_dimension=0,...  35 us
    reduce_scatter x1, waiting for transfers between devices, per_device(): lax.psum_scatter(part_out.astype(jnp.bfloat16), 'px', scatter_dimension=0...  25.8 us
    all_to_all x1, waiting for transfers between devices, per_device(): lax.all_to_all(pick_rows(after_two, row_index, row_counts), ('pz', 'tr'),...  24.9 us
    all_to_all x1, blocking collectives, substep(): lax.all_to_all(mixed_cols.astype(jnp.bfloat16), 'pz', split_axis=0, conca...  19.7 us
    all_to_all x1, waiting for transfers between devices, substep(): lax.all_to_all(mixed_cols.astype(jnp.bfloat16), 'pz', split_axis=0, conca...  10.2 us
    dot_general x2, matrix products, substep(): jnp.dot(implicit_inverse, columns, precision=lax.Precision.HIGHEST, prefe...  9.54 us
  transfers between devices with their start and end apart: 12, of which 9 were waited for; matrix products, arithmetic and copies ran while one was open for 6% of the time, Pallas kernels for 0%

commit v1 on v0

v1 whole, which is shorter than its diff:
```python
import math

import jax
import jax.numpy as jnp
from jax import lax
from jax.experimental import pallas as pl
from jax.experimental.pallas import tpu as pltpu
from jax.sharding import PartitionSpec as P

diffusion_factor = 0.08
F32 = jnp.float32
BF16 = jnp.bfloat16
MIB = 1 << 20


def call(kernel, out_shape, args, scratch=(), flops=1e6, vmem=48):
    outs = jax.tree.leaves(out_shape)
    moved = sum(math.prod(x.shape) * x.dtype.itemsize for x in list(args) + outs)
    return pl.pallas_call(
        kernel,
        out_shape=out_shape,
        in_specs=[pl.BlockSpec(memory_space=pltpu.VMEM)] * len(args),
        out_specs=jax.tree.map(lambda _: pl.BlockSpec(memory_space=pltpu.VMEM), out_shape),
        scratch_shapes=list(scratch),
        compiler_params=pltpu.CompilerParams(vmem_limit_bytes=vmem * MIB),
        cost_estimate=pl.CostEstimate(
            flops=int(flops), bytes_accessed=int(moved), transcendentals=0
        ),
    )(*args)


def shaped(shape, dtype):
    return jax.ShapeDtypeStruct(shape, dtype)


def shift(array, axis, wrap=True):
    last, first = array
    size = lax.axis_size(axis)
    up = [(i, (i + 1) % size) for i in range(size if wrap else size - 1)]
    down = [(j, i) for i, j in up]
    return lax.ppermute(last, axis, up), lax.ppermute(first, axis, down)


def explicit_kernel(v, w, zlo, zhi, ylo, yhi, out):
    comps, zn, yn, xn = v.shape
    peers = out.shape[0]
    xl = xn // peers
    row = lax.broadcasted_iota(jnp.int32, (yn, xn), 0)
    y_before = ylo[...].astype(F32)
    y_after = yhi[...].astype(F32)
    half = (comps + 1) * xl
    for zh in range(zn // 2):
        for c in range(comps + 1):
            pair = []
            for z in (2 * zh, 2 * zh + 1):
                if c == comps:
                    pair.append(w[z])
                    continue
                cur = v[c, z]
                r = c * zn + z
                total = v[c, z - 1] if z > 0 else zlo[c].astype(F32)
                total = total + (v[c, z + 1] if z < zn - 1 else zhi[c].astype(F32))
                total = total + jnp.where(row == 0, y_before[r : r + 1], pltpu.roll(cur, 1, 0))
                total = total + jnp.where(
                    row == yn - 1, y_after[r : r + 1], pltpu.roll(cur, yn - 1, 0)
                )
                total = total + pltpu.roll(cur, 1, 1) + pltpu.roll(cur, xn - 1, 1)
                pair.append(cur + diffusion_factor * w[z] * (total - 6.0 * cur))
            turned = jnp.concatenate(pair, axis=0).T.astype(BF16)
            base = zh * half + c * xl
            for q in range(peers):
                out[q, base : base + xl, :] = turned[q * xl : (q + 1) * xl]


def solve(e, a):
    return lax.dot_general(
        e[...], a[...], (((1,), (1,)), ((), ())), preferred_element_type=F32
    )


def pack_columns(u, packed, zn):
    peers, rows, lanes = packed.shape
    f = rows // (zn // 2)
    yn = lanes // 2
    low = lax.broadcasted_iota(jnp.int32, (f, lanes), 1) < yn
    for j in range(peers // 2):
        for zh in range(zn // 2):
            first = u[(2 * zh) * f : (2 * zh + 1) * f, j * lanes : (j + 1) * lanes]
            second = u[(2 * zh + 1) * f : (2 * zh + 2) * f, j * lanes : (j + 1) * lanes]
            even = jnp.where(low, first, pltpu.roll(second, yn, 1))
            odd = jnp.where(low, pltpu.roll(first, yn, 1), second)
            packed[2 * j, zh * f : (zh + 1) * f, :] = even.astype(BF16)
            packed[2 * j + 1, zh * f : (zh + 1) * f, :] = odd.astype(BF16)


def first_solve_kernel(got, a, u, w, packed, zlo, zhi, xlo, xhi, e):
    peers, rows, lanes = got.shape
    yn = lanes // 2
    zn = 4
    half = rows // 2
    xl = w.shape[0] // zn
    f = half - xl
    low = lax.broadcasted_iota(jnp.int32, (rows, lanes), 1) < yn
    for j in range(peers // 2):
        one = got[2 * j].astype(F32)
        two = got[2 * j + 1].astype(F32)
        sides = (
            jnp.where(low, one, pltpu.roll(two, yn, 1)),
            jnp.where(low, pltpu.roll(one, yn, 1), two),
        )
        at = slice(j * lanes, (j + 1) * lanes)
        for zh in range(zn // 2):
            for side in range(2):
                z = 2 * zh + side
                e[z * f : (z + 1) * f, at] = sides[side][zh * half : zh * half + f].astype(BF16)
                w[z * xl : (z + 1) * xl, at] = sides[side][zh * half + f : (zh + 1) * half]
    u[...] = solve(e, a)
    zlo[...] = u[0:f].astype(BF16)
    zhi[...] = u[(zn - 1) * f : zn * f].astype(BF16)
    groups = u.shape[0] // xl
    xlo[...] = jnp.concatenate([u[r * xl : r * xl + 1] for r in range(groups)], axis=0).astype(BF16)
    xhi[...] = jnp.concatenate(
        [u[(r + 1) * xl - 1 : (r + 1) * xl] for r in range(groups)], axis=0
    ).astype(BF16)
    pack_columns(u, packed, zn)


def second_solve_kernel(u, w, zlo, zhi, xlo, xhi, a, packed, e, out):
    cols = u.shape[1]
    f = zlo.shape[0]
    zn = u.shape[0] // f
    xl = w.shape[0] // zn
    comps = f // xl
    row = lax.broadcasted_iota(jnp.int32, (xl, cols), 0)
    lane = lax.broadcasted_iota(jnp.int32, (xl, cols), 1)
    x_before = xlo[...].astype(F32)
    x_after = xhi[...].astype(F32)
    for z in range(zn):
        for c in range(comps):
            r = z * comps + c
            at = slice(r * xl, (r + 1) * xl)
            cur = u[at]
            if z > 0:
                total = u[(r - comps) * xl : (r - comps + 1) * xl]
            else:
                total = zlo[c * xl : (c + 1) * xl].astype(F32)
            if z < zn - 1:
                total = total + u[(r + comps) * xl : (r + comps + 1) * xl]
            else:
                total = total + zhi[c * xl : (c + 1) * xl].astype(F32)
            total = total + jnp.where(row == 0, x_before[r : r + 1], pltpu.roll(cur, 1, 0))
            total = total + jnp.where(row == xl - 1, x_after[r : r + 1], pltpu.roll(cur, xl - 1, 0))
            total = total + jnp.where(lane == 0, 0.0, pltpu.roll(cur, 1, 1))
            total = total + jnp.where(lane == cols - 1, 0.0, pltpu.roll(cur, cols - 1, 1))
            step = diffusion_factor * w[z * xl : (z + 1) * xl] * (total - 6.0 * cur)
            e[at] = (cur + step).astype(BF16)
    out[...] = solve(e, a)
    pack_columns(out, packed, zn)


GROUP = 8


def sample_kernel(packed, ids, out, picked):
    peers, rows, lanes = packed.shape
    f = rows // 2
    yn = lanes // 2
    blocks = picked.shape[2] // lanes
    r = lax.broadcasted_iota(jnp.int32, (2 * lanes, lanes), 0)
    row_id = (r % yn) * 4 + r // yn
    for q in range(peers):
        table = jnp.concatenate([packed[q, 0:f], packed[q, f:rows]], axis=1)
        wanted = pltpu.roll(ids[q], (GROUP * q) % lanes, 1) if q else ids[q]
        for b in range(blocks):
            hot = jnp.where(row_id == wanted[b : b + 1], 1.0, 0.0).astype(BF16)
            picked[q, :, b * lanes : (b + 1) * lanes] = jnp.dot(
                table, hot, preferred_element_type=F32
            )
    group = lax.broadcasted_iota(jnp.int32, (f, lanes), 1) // GROUP
    per = lanes // GROUP
    halves = out.shape[0] // per
    for b in range(blocks):
        kg, mh = b // halves, b % halves
        held = [picked[q, :, b * lanes : (b + 1) * lanes] for q in range(peers)]
        step = 1
        while step < peers:
            take = (group // step) % 2 == 1
            held = [jnp.where(take, held[(i + step) % peers], held[i]) for i in range(peers)]
            step *= 2
        for ml in range(per):
            out[mh * per + ml, :, kg * lanes : (kg + 1) * lanes] = held[(-ml) % peers].astype(BF16)


def slot_table(row_index, row_counts):
    members, slots = row_index.shape[3:]
    index = row_index.reshape(members, slots)
    counts = row_counts.reshape(members, 1)
    live = jnp.arange(slots, dtype=jnp.int32)[None, :] < counts
    index = jnp.where(live, index, -1)
    per = 128 // GROUP
    index = index.reshape(members // per, per, slots // GROUP, GROUP).transpose(2, 0, 1, 3)
    index = index.reshape(-1, 128)
    index = jnp.concatenate([index, jnp.full((8 - index.shape[0], 128), -1, jnp.int32)], axis=0)
    return lax.all_gather(index, "pz")


def gather_rows(got, turned, comps=3):
    sources, f, slots = got.shape
    sides = 2
    peers = sources // sides
    xl = f // comps
    for q in range(peers):
        for side in range(sides):
            for c in range(comps):
                at = (c * peers + q) * xl
                turned[at : at + xl, side * slots : (side + 1) * slots] = got[
                    q * sides + side, c * xl : (c + 1) * xl
                ]


def forward_kernel(got, w_in, w_out, x_out, hidden, slope, predicted, x):
    gather_rows(got, x)
    x_out[...] = x[...]
    wide = 256
    count = hidden.shape[0] // wide

    def chunk(i, carry):
        at = pl.ds(pl.multiple_of(i * wide, wide), wide)
        pre = jnp.dot(w_in[at, :], x[...], preferred_element_type=F32)
        logistic = jax.nn.sigmoid(pre)
        hidden[at, :] = (pre * logistic).astype(BF16)
        slope[at, :] = (logistic * (1.0 + pre * (1.0 - logistic))).astype(slope.dtype)
        return carry

    lax.fori_loop(0, count, chunk, 0)

    def second(i, carry):
        at = pl.ds(pl.multiple_of(i * wide, wide), wide)
        predicted[at, :] = jnp.dot(w_out[at, :], hidden[...], preferred_element_type=F32)
        return carry

    lax.fori_loop(0, predicted.shape[0] // wide, second, 0)


def backward_kernel(scale, got, predicted, hidden, slope, x, w_out, part_out, part_in, d, din):
    wide = 256
    gather_rows(got, d)
    d[...] = ((predicted[...] - d[...].astype(F32)) * scale).astype(BF16)
    contract_rows = (((1,), (1,)), ((), ()))

    def first(i, carry):
        at = pl.ds(pl.multiple_of(i * wide, wide), wide)
        part_out[at, :] = lax.dot_general(
            hidden[at, :], d[...], contract_rows, preferred_element_type=F32
        ).astype(BF16)
        back = jnp.dot(w_out[at, :], d[...], preferred_element_type=F32)
        din[at, :] = (back * slope[at, :].astype(F32)).astype(BF16)
        return carry

    lax.fori_loop(0, hidden.shape[0] // wide, first, 0)

    def second(i, carry):
        at = pl.ds(pl.multiple_of(i * wide, wide), wide)
        part_in[at, :] = lax.dot_general(
            x[at, :], din[...], contract_rows, preferred_element_type=F32
        ).astype(BF16)
        return carry

    lax.fori_loop(0, x.shape[0] // wide, second, 0)


def planes_kernel(got, out):
    comps, zn, yn, xn = out.shape
    peers = got.shape[0]
    xl = xn // peers
    f = comps * xl
    for zh in range(zn // 2):
        for c in range(comps):
            base = zh * f + c * xl
            block = jnp.concatenate(
                [got[q, base : base + xl, :] for q in range(peers)], axis=0
            ).astype(F32)
            turned = block.T
            out[c, 2 * zh] = turned[0:yn]
            out[c, 2 * zh + 1] = turned[yn : 2 * yn]


def exchange(array, axis):
    return lax.all_to_all(array, axis, split_axis=0, concat_axis=0, tiled=True)


def sum_shares(part, axis):
    size = lax.axis_size(axis)
    shares = exchange(part.reshape(size, part.shape[0] // size, part.shape[1]), axis)
    return jnp.sum(shares.astype(F32), axis=0)


def per_device(velocity, viscosity, implicit_inverse, row_index, row_counts, weight_in, weight_out):
    yn, zn, comps, xn = velocity.shape
    peers = lax.axis_size("pz")
    total_y = yn * peers
    xl = xn // peers
    f = comps * xl
    lanes = 2 * yn
    members, slots = row_index.shape[3:]

    v = velocity.transpose(2, 1, 0, 3)
    edges = velocity.astype(BF16)
    z_edge = lambda z: edges[:, z].transpose(1, 0, 2)
    y_edge = lambda y: edges[y].transpose(1, 0, 2).reshape(comps * zn, xn)
    zlo, zhi = shift((z_edge(zn - 1), z_edge(0)), ("px", "tr"))
    ylo, yhi = shift((y_edge(yn - 1), y_edge(0)), "pz", wrap=False)
    sent = call(
        explicit_kernel,
        shaped((peers, 2 * (f + xl), lanes), BF16),
        (v, viscosity.transpose(1, 0, 2), zlo, zhi, ylo, yhi),
        flops=2e7,
    )
    ids = slot_table(row_index, row_counts)
    inverse = implicit_inverse.astype(BF16)
    got = exchange(sent, "pz")
    solve_flops = 2 * zn * f * total_y * total_y
    u, w, packed, zlo, zhi, xlo, xhi = call(
        first_solve_kernel,
        (
            shaped((zn * f, total_y), F32),
            shaped((zn * xl, total_y), F32),
            shaped((peers, 2 * f, lanes), BF16),
            shaped((f, total_y), BF16),
            shaped((f, total_y), BF16),
            shaped((zn * comps, total_y), BF16),
            shaped((zn * comps, total_y), BF16),
        ),
        (got, inverse),
        scratch=[pltpu.VMEM((zn * f, total_y), BF16)],
        flops=solve_flops,
    )
    zlo, zhi = shift((zhi, zlo), ("px", "tr"))
    xlo, xhi = shift((xhi, xlo), "pz")

    def sample(packed):
        sent = call(
            sample_kernel,
            shaped((members, f, peers * slots), BF16),
            (packed, ids),
            scratch=[pltpu.VMEM((peers, f, members * slots), F32)],
            flops=2 * peers * 256 * 256 * members * slots,
        )
        return exchange(sent, ("pz", "tr"))

    rows_in = sample(packed)
    packed = call(
        second_solve_kernel,
        shaped((peers, 2 * f, lanes), BF16),
        (u, w, zlo, zhi, xlo, xhi, inverse),
        scratch=[pltpu.VMEM((zn * f, total_y), BF16), pltpu.VMEM((zn * f, total_y), F32)],
        flops=solve_flops,
    )
    rows_target = sample(packed)
    planes = exchange(packed, "pz")

    member_in = weight_in[0]
    member_out = weight_out[0]
    width, hid = member_in.shape
    batch = 2 * peers * slots
    loss_scale = 1.0 / math.sqrt(lax.axis_size("px") * batch)
    x, hidden, slope, predicted = call(
        forward_kernel,
        (
            shaped((width, batch), BF16),
            shaped((hid, batch), BF16),
            shaped((hid, batch), F32),
            shaped((width, batch), F32),
        ),
        (rows_in, member_in.T, member_out.T),
        scratch=[pltpu.VMEM((width, batch), BF16)],
        flops=4 * hid * width * batch,
    )

    def backward(*refs):
        backward_kernel(loss_scale, *refs)

    part_out, part_in = call(
        backward,
        (shaped((hid, width), BF16), shaped((width, hid), BF16)),
        (rows_target, predicted, hidden, slope, x, member_out),
        scratch=[pltpu.VMEM((width, batch), BF16), pltpu.VMEM((hid, batch), BF16)],
        flops=6 * hid * width * batch,
    )
    share_out = sum_shares(part_out, "px")
    share_in = sum_shares(part_in, "px")
    result = call(planes_kernel, shaped((comps, zn, yn, xn), F32), (planes,), flops=1e6)
    return (result.transpose(2, 1, 0, 3), share_in[None], share_out[None])


def solution(mesh):
    in_specs = (
        P("pz", ("px", "tr"), None, None),
        P("pz", ("px", "tr"), None),
        P(),
        P("px", "pz", "tr", None, None),
        P("px", "pz", "tr", None),
        P(("pz", "tr"), None, None),
        P(("pz", "tr"), None, None),
    )
    out_specs = (
        P("pz", ("px", "tr"), None, None),
        P(("pz", "tr"), "px", None),
        P(("pz", "tr"), "px", None),
    )
    return jax.shard_map(
        per_device, mesh=mesh, in_specs=in_specs, out_specs=out_specs, check_vma=False
    )
```

time: 330 us -> 222 us (0.67)
  waiting for transfers between devices: 106 us -> 34.8 us
  matrix products: 31.2 us -> 0 us
  Pallas kernels: 0 us -> 26.6 us
  starting transfers between devices: 26.4 us -> 47 us
  blocking collectives: 109 us -> 93.1 us
  local copies, waits for them, and re-layouts: 28.5 us -> 13.6 us
  between operations: 14.4 us -> 0.89 us
  other arithmetic: 13.5 us -> 5.24 us
    reduce_scatter x2 -> x0, waiting for transfers between devices: 60.8 us -> none  [the longest x1 35 us: per_device(): lax.psum_scatter(part_in.astype(jnp.bfloat16), 'px', scatter_dimension=0,...]
    all_to_all x4 -> x2, blocking collectives: 109 us -> 61.6 us  [exchange(): return lax.all_to_all(array, axis, split_axis=0, concat_axis=0, tiled=True)]
    all_gather x0 -> x1, blocking collectives: none -> 31.6 us  [slot_table(): return lax.all_gather(index, 'pz')]
    dot_general x6 -> x0, matrix products: 31.2 us -> none  [the longest x2 9.54 us: substep(): jnp.dot(implicit_inverse, columns, precision=lax.Precision.HIGHEST, prefe...]
    pallas_call x0 -> x8, Pallas kernels: none -> 26.6 us  [call(): pl.pallas_call(kernel, out_shape=out_shape, in_specs=[pl.BlockSpec(memory...]
    all_to_all x2 -> x4, starting transfers between devices: 10.9 us -> 28.2 us  [exchange(): return lax.all_to_all(array, axis, split_axis=0, concat_axis=0, tiled=True)]
    all_to_all x2 -> x4, waiting for transfers between devices: 35.2 us -> 18.9 us  [exchange(): return lax.all_to_all(array, axis, split_axis=0, concat_axis=0, tiled=True)]
    convert_element_type x11 -> x0, local copies, waits for them, and re-layouts: 7.27 us -> none  [the longest x5 3.53 us: substep(): planes = lax.all_to_all(mixed_cols.astype(jnp.bfloat16), 'pz', split_axis...]
  transfers between devices with their start and end apart: 12 -> 12, of which waited for: 9 -> 4; matrix products, arithmetic and copies ran while one was open for 6% -> 5% of each run, Pallas kernels for 0% -> 10%
where the time goes in v1:
time: 222 us; the launch traced here: 221 us
  blocking collectives  93.1 us (42%)
  starting transfers between devices  47 us (21%)
  waiting for transfers between devices  34.8 us (16%)
  Pallas kernels  26.6 us (12%)
  local copies, waits for them, and re-layouts  13.6 us (6%)
  other arithmetic  5.24 us (2%)
    all_to_all x2, blocking collectives, exchange(): return lax.all_to_all(array, axis, split_axis=0, concat_axis=0, tiled=True)  61.6 us
    all_gather x1, blocking collectives, slot_table(): return lax.all_gather(index, 'pz')  31.6 us
    all_to_all x4, starting transfers between devices, exchange(): return lax.all_to_all(array, axis, split_axis=0, concat_axis=0, tiled=True)  28.2 us
    pallas_call x8, Pallas kernels, call(): pl.pallas_call(kernel, out_shape=out_shape, in_specs=[pl.BlockSpec(memory...  26.6 us
    all_to_all x4, waiting for transfers between devices, exchange(): return lax.all_to_all(array, axis, split_axis=0, concat_axis=0, tiled=True)  18.9 us
    ppermute x8, starting transfers between devices, shift(): return (lax.ppermute(last, axis, up), lax.ppermute(first, axis, down))  18.8 us
    ppermute x8, waiting for transfers between devices, shift(): return (lax.ppermute(last, axis, up), lax.ppermute(first, axis, down))  15.9 us
    unnamed x36, local copies, waits for them, and re-layouts  10.6 us
  transfers between devices with their start and end apart: 12, of which 4 were waited for; matrix products, arithmetic and copies ran while one was open for 5% of the time, Pallas kernels for 10%

profile of v1, /device:TPU:2, one launch (start us, length us, event | category | flops | bytes accessed | tf_op | source)
XLA Modules:
  0.0 221.3 jit_solution(6432621143298514651)
XLA Ops:
  0.6 1.3 copy.33
  2.0 2.2 collective-permute-start
  4.2 3.2 %collective-permute-start.1 = (bf16[3,64,256]{2,1,0:T(8,128)(2,1)S(1)}, bf16[3,64,256]{2,1,0:T(8,128)(2,1)S(1)}, u32[]{:S(2)}, u32[]{:S(2)}) collective-permute-start(bf16[3,64,256]{2,1,0:T(8,128)(2,1)S(1)} %get-tuple-element.37), channel_id=1, source_target_pairs={{1,0},{32,1},{33,32},{64,33},{65,64},{96,65},{97,96},{128,97},{129... | collective-permute-start | bytes 294920 | tf_op jit(solution)/shard_map/ppermute | solution.py:41
  7.5 3.8 %collective-permute-start.2 = (bf16[12,256]{1,0:T(8,128)(2,1)S(1)}, bf16[12,256]{1,0:T(8,128)(2,1)S(1)}, u32[]{:S(2)}, u32[]{:S(2)}) collective-permute-start(bf16[12,256]{1,0:T(8,128)(2,1)S(1)} %reshape.42), channel_id=1, source_target_pairs={{0,2},{2,4},{4,6},{6,8},{8,10},{10,12},{12,14},{14,16},{16,18},{18... | collective-permute-start | bytes 18440 | tf_op jit(solution)/shard_map/ppermute | solution.py:41
  11.3 2.0 collective-permute-start.3
  13.4 0.1 copy.34
  13.6 4.2 %collective-permute-done.3.yhi = bf16[12,256]{1,0:T(8,128)(2,1)S(1)} collective-permute-done((bf16[12,256]{1,0:T(8,128)(2,1)S(1)}, bf16[12,256]{1,0:T(8,128)(2,1)S(1)}, u32[]{:S(2)}, u32[]{:S(2)}) %collective-permute-start.3) | collective-permute-done | bytes 6176 | tf_op jit(solution)/shard_map/ppermute | solution.py:41
  17.8 1.6 shard_map.94
  19.4 9.8 %all-to-all-start = ((bf16[16,128,128]{2,1,0:T(8,128)(2,1)}), bf16[16,128,128]{2,1,0:T(8,128)(2,1)S(1)}, u32[]{:S(2)}, u32[]{:S(2)}) async-start(bf16[16,128,128]{2,1,0:T(8,128)(2,1)} %shard_map.94), calls=%async_computation | async-start | bytes 1048576 | tf_op jit(solution)/shard_map/all_to_all | solution.py:289
  29.2 2.5 %convert_element_type.13.a = bf16[1024,1024]{1,0:T(8,128)(2,1)S(1)} convert(f32[1024,1024]{1,0:T(8,128)} %param.9) | non-fusion elementwise | flops 1048576 | bytes 6291456 | tf_op jit(solution)/shard_map/convert_element_type | solution.py:320
  31.7 0.1 reshape.44
  31.8 0.1 copy.24
  31.9 0.5 broadcast.18
  32.4 0.7 reduce.3
  33.1 0.1 lt.26
  33.2 0.1 select_bitcast_fusion
  33.2 0.1 reshape.45
  33.3 31.6 %all-gather = s32[128,128]{1,0:T(8,128)S(1)} all-gather(s32[8,128]{1,0:T(8,128)S(1)} %concatenate.3), channel_id=2, replica_groups=mesh['px'=8,'pz'=16,'tr'=2] {'pz'}, dimensions={0}, use_global_device_ids=true | all-gather | bytes 69632 | tf_op jit(solution)/shard_map/all_gather | solution.py:204
  64.9 1.0 shard_map.95
  65.9 0.9 copy-done.2
  66.8 0.6 copy-done.9
  67.4 0.6 copy-done.8
  68.0 1.8 shard_map.99
  69.8 1.0 copy-done
  70.9 9.5 %all-to-all-start.3 = ((bf16[32,48,384]{2,1,0:T(8,128)(2,1)}), bf16[32,48,384]{2,1,0:T(8,128)(2,1)S(1)}, u32[]{:S(2)}, u32[]{:S(2)}) async-start(bf16[32,48,384]{2,1,0:T(8,128)(2,1)} %copy-done), calls=%async_computation.3 | async-start | bytes 2359296 | tf_op jit(solution)/shard_map/all_to_all | solution.py:289
  80.4 2.2 collective-permute-start.4
  82.5 3.3 %collective-permute-start.5 = (bf16[48,1024]{1,0:T(8,128)(2,1)}, bf16[48,1024]{1,0:T(8,128)(2,1)S(1)}, u32[]{:S(2)}, u32[]{:S(2)}) collective-permute-start(bf16[48,1024]{1,0:T(8,128)(2,1)} %copy-done.6), channel_id=1, source_target_pairs={{1,0},{32,1},{33,32},{64,33},{65,64},{96,65},{97,96},{128,97},{129... | collective-permute-start | bytes 294920 | tf_op jit(solution)/shard_map/ppermute | solution.py:41
  85.8 1.5 collective-permute-start.6
  87.3 0.6 collective-permute-start.7
  87.9 8.3 %collective-permute-done.6.xlo = bf16[12,1024]{1,0:T(8,128)(2,1)S(1)} collective-permute-done((bf16[12,1024]{1,0:T(8,128)(2,1)}, bf16[12,1024]{1,0:T(8,128)(2,1)S(1)}, u32[]{:S(2)}, u32[]{:S(2)}) %collective-permute-start.6) | collective-permute-done | bytes 24608 | tf_op jit(solution)/shard_map/ppermute | solution.py:41
  96.1 3.5 %collective-permute-done.7.xhi = bf16[12,1024]{1,0:T(8,128)(2,1)S(1)} collective-permute-done((bf16[12,1024]{1,0:T(8,128)(2,1)}, bf16[12,1024]{1,0:T(8,128)(2,1)S(1)}, u32[]{:S(2)}, u32[]{:S(2)}) %collective-permute-start.7) | collective-permute-done | bytes 24608 | tf_op jit(solution)/shard_map/ppermute | solution.py:41
  99.6 1.1 copy-done.3
  100.7 1.9 shard_map.96.packed
  102.6 2.8 %shard_map.98 = bf16[32,48,384]{2,1,0:T(8,128)(2,1)S(1)} custom-call(bf16[16,96,128]{2,1,0:T(8,128)(2,1)} %shard_map.96.packed, s32[16,8,128]{2,1,0:T(8,128)S(1)} %bitcast.50), custom_call_target="tpu_custom_call" | custom-call | flops 1610612736 | bytes 1638400 | tf_op jit(solution)/shard_map/pallas_call | solution.py:19
  105.4 35.5 %all_to_all.30.refs_0_ = bf16[32,48,384]{2,1,0:T(8,128)(2,1)} all-to-all(bf16[32,48,384]{2,1,0:T(8,128)(2,1)S(1)} %shard_map.98), channel_id=1, replica_groups=mesh['px'=8,'pz'=16,'tr'=2] {'pz','tr'}, dimensions={0} | all-to-all | bytes 2359296 | tf_op jit(solution)/shard_map/all_to_all | solution.py:289
  140.9 5.3 %all-to-all-start.1 = ((bf16[16,96,128]{2,1,0:T(8,128)(2,1)}), bf16[16,96,128]{2,1,0:T(8,128)(2,1)S(1)}, u32[]{:S(2)}, u32[]{:S(2)}) async-start(bf16[16,96,128]{2,1,0:T(8,128)(2,1)} %shard_map.96.packed), calls=%async_computation.1 | async-start | bytes 786432 | tf_op jit(solution)/shard_map/all_to_all | solution.py:289
  146.2 1.7 copy.25
  148.0 2.6 %copy.26.w_out = bf16[768,1024]{1,0:T(8,128)(2,1)} copy(bf16[768,1024]{0,1:T(8,128)(2,1)} %bitcast.51) | data formatting | bytes 3145728 | tf_op jit(solution)/shard_map/transpose | solution.py:375
  150.5 7.5 %shard_map.100 = (bf16[768,768]{1,0:T(8,128)(2,1)S(1)}, bf16[1024,768]{1,0:T(8,128)(2,1)S(1)}, f32[1024,768]{1,0:T(8,128)}, f32[768,768]{1,0:T(8,128)}) custom-call(bf16[32,48,384]{2,1,0:T(8,128)(2,1)S(1)} %all-to-all-done.3.got, bf16[1024,768]{1,0:T(8,128)(2,1)S(1)} %bitcast.47, bf16[768,1024]{1,0:T(8,128)(2,1)} %copy.26.w_out), custom_call_target="tpu_custom_call" | custom-call | flops 2415919104 | bytes 12582912 | tf_op jit(solution)/shard_map/pallas_call | solution.py:19
  158.1 1.2 copy-done.10
  159.2 9.9 %shard_map.101 = (bf16[1024,768]{1,0:T(8,128)(2,1)}, bf16[768,1024]{1,0:T(8,128)(2,1)S(1)}) custom-call(bf16[32,48,384]{2,1,0:T(8,128)(2,1)S(1)} %copy-done.1, f32[768,768]{1,0:T(8,128)} %get-tuple-element.23.refs_1_, bf16[1024,768]{1,0:T(8,128)(2,1)} %copy-done.10, f32[1024,768]{1,0:T(8,128)} %get-tuple-element.25.refs_3_, ...), custom_call_target="tpu_custom_call" | custom-call | flops 3623878656 | bytes 14155776 | tf_op jit(solution)/shard_map/pallas_call | solution.py:19
  169.2 26.1 %all_to_all.31 = bf16[8,96,1024]{2,1,0:T(8,128)(2,1)S(1)} all-to-all(bf16[8,96,1024]{2,1,0:T(8,128)(2,1)S(1)} %bitcast.46), channel_id=1, replica_groups=mesh['px'=8,'pz'=16,'tr'=2] {'px'}, dimensions={0} | all-to-all | bytes 3145728 | tf_op jit(solution)/shard_map/all_to_all | solution.py:289
  195.2 3.6 %all-to-all-start.5 = ((bf16[8,128,768]{2,1,0:T(8,128)(2,1)}), bf16[8,128,768]{2,1,0:T(8,128)(2,1)S(1)}, u32[]{:S(2)}, u32[]{:S(2)}) async-start(bf16[8,128,768]{2,1,0:T(8,128)(2,1)} %bitcast.19), calls=%async_computation.5 | async-start | bytes 3145728 | tf_op jit(solution)/shard_map/all_to_all | solution.py:289
  198.8 0.2 shard_map.97
  199.0 1.4 copy.27
  200.4 1.0 convert_reduce_fusion.1
  201.4 18.9 %all-to-all-done.5 = bf16[8,128,768]{2,1,0:T(8,128)(2,1)S(1)} async-done(((bf16[8,128,768]{2,1,0:T(8,128)(2,1)}), bf16[8,128,768]{2,1,0:T(8,128)(2,1)S(1)}, u32[]{:S(2)}, u32[]{:S(2)}) %all-to-all-start.5) | async-done | bytes 1572896 | tf_op jit(solution)/shard_map/all_to_all | solution.py:289
  220.3 1.0 convert_reduce_fusion
  (41 shorter events, 0.2 us)
Async XLA Ops:
  0.6 12.8 %copy-start.11 = (f32[64,4,3,256]{3,1,2,0:T(4,128)S(1)}, f32[64,4,3,256]{3,1,2,0:T(4,128)}, u32[]{:S(2)}) copy-start(f32[64,4,3,256]{3,1,2,0:T(4,128)} %param.7) | copy-start | bytes 2359300
  0.6 12.9 %copy-start.12 = (f32[64,4,256]{2,1,0:T(4,128)S(1)}, f32[64,4,256]{2,1,0:T(4,128)}, u32[]{:S(2)}) copy-start(f32[64,4,256]{2,1,0:T(4,128)} %param.8) | copy-start | bytes 786436
  2.0 15.8 %collective-permute-start = (bf16[3,64,256]{2,1,0:T(8,128)(2,1)S(1)}, bf16[3,64,256]{2,1,0:T(8,128)(2,1)S(1)}, u32[]{:S(2)}, u32[]{:S(2)}) collective-permute-start(bf16[3,64,256]{2,1,0:T(8,128)(2,1)S(1)} %get-tuple-element.38), channel_id=1, source_target_pairs={{0,1},{1,32},{32,33},{33,64},{64,65},{65,96},{96,97},{97,128},{128... | collective-permute-start | bytes 294920 | tf_op jit(solution)/shard_map/ppermute | solution.py:41
  4.2 13.6 %collective-permute-start.1 = (bf16[3,64,256]{2,1,0:T(8,128)(2,1)S(1)}, bf16[3,64,256]{2,1,0:T(8,128)(2,1)S(1)}, u32[]{:S(2)}, u32[]{:S(2)}) collective-permute-start(bf16[3,64,256]{2,1,0:T(8,128)(2,1)S(1)} %get-tuple-element.37), channel_id=1, source_target_pairs={{1,0},{32,1},{33,32},{64,33},{65,64},{96,65},{97,96},{128,97},{129... | collective-permute-start | bytes 294920 | tf_op jit(solution)/shard_map/ppermute | solution.py:41
  7.5 6.1 %collective-permute-start.2 = (bf16[12,256]{1,0:T(8,128)(2,1)S(1)}, bf16[12,256]{1,0:T(8,128)(2,1)S(1)}, u32[]{:S(2)}, u32[]{:S(2)}) collective-permute-start(bf16[12,256]{1,0:T(8,128)(2,1)S(1)} %reshape.42), channel_id=1, source_target_pairs={{0,2},{2,4},{4,6},{6,8},{8,10},{10,12},{12,14},{14,16},{16,18},{18... | collective-permute-start | bytes 18440 | tf_op jit(solution)/shard_map/ppermute | solution.py:41
  11.3 6.4 %collective-permute-start.3 = (bf16[12,256]{1,0:T(8,128)(2,1)S(1)}, bf16[12,256]{1,0:T(8,128)(2,1)S(1)}, u32[]{:S(2)}, u32[]{:S(2)}) collective-permute-start(bf16[12,256]{1,0:T(8,128)(2,1)S(1)} %reshape.43), channel_id=1, source_target_pairs={{2,0},{4,2},{6,4},{8,6},{10,8},{12,10},{14,12},{16,14},{18,16},{20... | collective-permute-start | bytes 18440 | tf_op jit(solution)/shard_map/ppermute | solution.py:41
  19.4 45.6 %all-to-all-start = ((bf16[16,128,128]{2,1,0:T(8,128)(2,1)}), bf16[16,128,128]{2,1,0:T(8,128)(2,1)S(1)}, u32[]{:S(2)}, u32[]{:S(2)}) async-start(bf16[16,128,128]{2,1,0:T(8,128)(2,1)} %shard_map.94), calls=%async_computation | async-start | bytes 1048576 | tf_op jit(solution)/shard_map/all_to_all | solution.py:289
  29.2 2.6 %copy-start.13 = (s32[1,1,1,32,24]{3,4,2,1,0:T(8,128)S(1)}, s32[1,1,1,32,24]{3,4,2,1,0:T(8,128)}, u32[]{:S(2)}) copy-start(s32[1,1,1,32,24]{3,4,2,1,0:T(8,128)} %param.10) | copy-start | bytes 9220
  29.2 3.2 %copy-start.14 = (s32[1,1,1,32]{3,2,1,0:T(1,128)S(1)}, s32[1,1,1,32]{3,2,1,0:T(1,128)}, u32[]{:S(2)}) copy-start(s32[1,1,1,32]{3,2,1,0:T(1,128)} %param.11) | copy-start | bytes 388
  64.9 4.9 %copy-start.4 = (s32[128,128]{1,0:T(8,128)}, s32[128,128]{1,0:T(8,128)S(1)}, u32[]{:S(2)}) copy-start(s32[128,128]{1,0:T(8,128)S(1)} %all-gather) | copy-start | bytes 196612
  65.9 0.9 copy-start.2
  66.8 0.6 copy-start.9
  67.4 0.6 copy-start.8
  67.4 3.4 %copy-start.6 = (bf16[48,1024]{1,0:T(8,128)(2,1)}, bf16[48,1024]{1,0:T(8,128)(2,1)S(1)}, u32[]{:S(2)}) copy-start(bf16[48,1024]{1,0:T(8,128)(2,1)S(1)} %get-tuple-element.19) | copy-start | bytes 294916
  67.4 3.4 %copy-start.7 = (bf16[48,1024]{1,0:T(8,128)(2,1)}, bf16[48,1024]{1,0:T(8,128)(2,1)S(1)}, u32[]{:S(2)}) copy-start(bf16[48,1024]{1,0:T(8,128)(2,1)S(1)} %get-tuple-element.18) | copy-start | bytes 294916
  69.8 1.0 copy-start
  70.9 34.5 %all-to-all-start.3 = ((bf16[32,48,384]{2,1,0:T(8,128)(2,1)}), bf16[32,48,384]{2,1,0:T(8,128)(2,1)S(1)}, u32[]{:S(2)}, u32[]{:S(2)}) async-start(bf16[32,48,384]{2,1,0:T(8,128)(2,1)} %copy-done), calls=%async_computation.3 | async-start | bytes 2359296 | tf_op jit(solution)/shard_map/all_to_all | solution.py:289
  80.4 19.2 %collective-permute-start.4 = (bf16[48,1024]{1,0:T(8,128)(2,1)}, bf16[48,1024]{1,0:T(8,128)(2,1)S(1)}, u32[]{:S(2)}, u32[]{:S(2)}) collective-permute-start(bf16[48,1024]{1,0:T(8,128)(2,1)} %copy-done.7), channel_id=1, source_target_pairs={{0,1},{1,32},{32,33},{33,64},{64,65},{65,96},{96,97},{97,128},{128... | collective-permute-start | bytes 294920 | tf_op jit(solution)/shard_map/ppermute | solution.py:41
  82.5 17.1 %collective-permute-start.5 = (bf16[48,1024]{1,0:T(8,128)(2,1)}, bf16[48,1024]{1,0:T(8,128)(2,1)S(1)}, u32[]{:S(2)}, u32[]{:S(2)}) collective-permute-start(bf16[48,1024]{1,0:T(8,128)(2,1)} %copy-done.6), channel_id=1, source_target_pairs={{1,0},{32,1},{33,32},{64,33},{65,64},{96,65},{97,96},{128,97},{129... | collective-permute-start | bytes 294920 | tf_op jit(solution)/shard_map/ppermute | solution.py:41
  85.8 10.3 %collective-permute-start.6 = (bf16[12,1024]{1,0:T(8,128)(2,1)}, bf16[12,1024]{1,0:T(8,128)(2,1)S(1)}, u32[]{:S(2)}, u32[]{:S(2)}) collective-permute-start(bf16[12,1024]{1,0:T(8,128)(2,1)} %copy-done.9), channel_id=1, source_target_pairs={{0,2},{2,4},{4,6},{6,8},{8,10},{10,12},{12,14},{14,16},{16,18},{18... | collective-permute-start | bytes 73736 | tf_op jit(solution)/shard_map/ppermute | solution.py:41
  87.3 12.3 %collective-permute-start.7 = (bf16[12,1024]{1,0:T(8,128)(2,1)}, bf16[12,1024]{1,0:T(8,128)(2,1)S(1)}, u32[]{:S(2)}, u32[]{:S(2)}) collective-permute-start(bf16[12,1024]{1,0:T(8,128)(2,1)} %copy-done.8), channel_id=1, source_target_pairs={{2,0},{4,2},{6,4},{8,6},{10,8},{12,10},{14,12},{16,14},{18,16},{20... | collective-permute-start | bytes 73736 | tf_op jit(solution)/shard_map/ppermute | solution.py:41
  99.6 1.1 copy-start.3
  100.7 1.9 copy-start.5
  140.9 28.3 %all-to-all-start.1 = ((bf16[16,96,128]{2,1,0:T(8,128)(2,1)}), bf16[16,96,128]{2,1,0:T(8,128)(2,1)S(1)}, u32[]{:S(2)}, u32[]{:S(2)}) async-start(bf16[16,96,128]{2,1,0:T(8,128)(2,1)} %shard_map.96.packed), calls=%async_computation.1 | async-start | bytes 786432 | tf_op jit(solution)/shard_map/all_to_all | solution.py:289
  150.5 8.7 %copy-start.1 = (bf16[32,48,384]{2,1,0:T(8,128)(2,1)S(1)}, bf16[32,48,384]{2,1,0:T(8,128)(2,1)}, u32[]{:S(2)}) copy-start(bf16[32,48,384]{2,1,0:T(8,128)(2,1)} %all_to_all.30.refs_0_) | copy-start | bytes 3538948
  158.1 1.2 copy-start.10
  195.2 25.1 %all-to-all-start.5 = ((bf16[8,128,768]{2,1,0:T(8,128)(2,1)}), bf16[8,128,768]{2,1,0:T(8,128)(2,1)S(1)}, u32[]{:S(2)}, u32[]{:S(2)}) async-start(bf16[8,128,768]{2,1,0:T(8,128)(2,1)} %bitcast.19), calls=%async_computation.5 | async-start | bytes 3145728 | tf_op jit(solution)/shard_map/all_to_all | solution.py:289

commit v2 on v1

--- a/solution.py
+++ b/solution.py
@@ -13,16 +13,21 @@
 MIB = 1 << 20
 
 
-def call(kernel, out_shape, args, scratch=(), flops=1e6, vmem=48):
+def call(kernel, out_shape, args, scratch=(), flops=1e6):
     outs = jax.tree.leaves(out_shape)
-    moved = sum(math.prod(x.shape) * x.dtype.itemsize for x in list(args) + outs)
+    size = lambda x: math.prod(x.shape) * x.dtype.itemsize
+    moved = sum(size(x) for x in list(args) + outs)
+    held = moved + sum(math.prod(x.shape) * jnp.dtype(x.dtype).itemsize for x in scratch)
+    scalars = lambda x: x.ndim == 1
     return pl.pallas_call(
         kernel,
         out_shape=out_shape,
-        in_specs=[pl.BlockSpec(memory_space=pltpu.VMEM)] * len(args),
+        in_specs=[
+            pl.BlockSpec(memory_space=pltpu.SMEM if scalars(x) else pltpu.VMEM) for x in args
+        ],
         out_specs=jax.tree.map(lambda _: pl.BlockSpec(memory_space=pltpu.VMEM), out_shape),
         scratch_shapes=list(scratch),
-        compiler_params=pltpu.CompilerParams(vmem_limit_bytes=vmem * MIB),
+        compiler_params=pltpu.CompilerParams(vmem_limit_bytes=held + 6 * MIB),
         cost_estimate=pl.CostEstimate(
             flops=int(flops), bytes_accessed=int(moved), transcendentals=0
         ),
@@ -41,7 +46,7 @@
     return lax.ppermute(last, axis, up), lax.ppermute(first, axis, down)
 
 
-def explicit_kernel(v, w, zlo, zhi, ylo, yhi, out):
+def explicit_kernel(v, w, zlo, zhi, ylo, yhi, ids, out):
     comps, zn, yn, xn = v.shape
     peers = out.shape[0]
     xl = xn // peers
@@ -70,6 +75,9 @@
             base = zh * half + c * xl
             for q in range(peers):
                 out[q, base : base + xl, :] = turned[q * xl : (q + 1) * xl]
+    numbers = ids[...].astype(F32).astype(BF16)
+    for q in range(peers):
+        out[q, (zn // 2) * half : (zn // 2) * half + ids.shape[0], :] = numbers
 
 
 def solve(e, a):
@@ -93,8 +101,10 @@
             packed[2 * j + 1, zh * f : (zh + 1) * f, :] = odd.astype(BF16)
 
 
-def first_solve_kernel(got, a, u, w, packed, zlo, zhi, xlo, xhi, e):
+def first_solve_kernel(got, a, u, w, packed, zlo, zhi, xlo, xhi, ids, e):
     peers, rows, lanes = got.shape
+    rows = rows - ids.shape[1]
+    ids[...] = got[:, rows:, :].astype(F32).astype(jnp.int32)
     yn = lanes // 2
     zn = 4
     half = rows // 2
@@ -102,8 +112,8 @@
     f = half - xl
     low = lax.broadcasted_iota(jnp.int32, (rows, lanes), 1) < yn
     for j in range(peers // 2):
-        one = got[2 * j].astype(F32)
-        two = got[2 * j + 1].astype(F32)
+        one = got[2 * j, 0:rows].astype(F32)
+        two = got[2 * j + 1, 0:rows].astype(F32)
         sides = (
             jnp.where(low, one, pltpu.roll(two, yn, 1)),
             jnp.where(low, pltpu.roll(one, yn, 1), two),
@@ -200,8 +210,8 @@
     per = 128 // GROUP
     index = index.reshape(members // per, per, slots // GROUP, GROUP).transpose(2, 0, 1, 3)
     index = index.reshape(-1, 128)
-    index = jnp.concatenate([index, jnp.full((8 - index.shape[0], 128), -1, jnp.int32)], axis=0)
-    return lax.all_gather(index, "pz")
+    fill = jnp.full((8 - index.shape[0], 128), -1, jnp.int32)
+    return jnp.concatenate([index, fill], axis=0)
 
 
 def gather_rows(got, turned, comps=3):
@@ -218,11 +228,16 @@
                 ]
 
 
-def forward_kernel(got, w_in, w_out, x_out, hidden, slope, predicted, x):
+CONTRACT_ROWS = (((1,), (1,)), ((), ()))
+
+
+def over_rows(left, right):
+    return lax.dot_general(left, right, CONTRACT_ROWS, preferred_element_type=F32)
+
+
+def forward_kernel(got, w_in, w_out, x, hidden, slope, predicted):
     gather_rows(got, x)
-    x_out[...] = x[...]
     wide = 256
-    count = hidden.shape[0] // wide
 
     def chunk(i, carry):
         at = pl.ds(pl.multiple_of(i * wide, wide), wide)
@@ -232,7 +247,7 @@
         slope[at, :] = (logistic * (1.0 + pre * (1.0 - logistic))).astype(slope.dtype)
         return carry
 
-    lax.fori_loop(0, count, chunk, 0)
+    lax.fori_loop(0, hidden.shape[0] // wide, chunk, 0)
 
     def second(i, carry):
         at = pl.ds(pl.multiple_of(i * wide, wide), wide)
@@ -242,31 +257,100 @@
     lax.fori_loop(0, predicted.shape[0] // wide, second, 0)
 
 
-def backward_kernel(scale, got, predicted, hidden, slope, x, w_out, part_out, part_in, d, din):
-    wide = 256
+def block_rows(array, y, core, rows):
+    return array[pl.ds(pl.multiple_of((2 * y + core) * rows, rows), rows), :]
+
+
+def away_blocks(array, right, core, away, rows):
+    for pair in range(away.shape[0] // (2 * rows)):
+        left = jnp.concatenate(
+            [block_rows(array, 2 * pair + k, 1 - core, rows) for k in range(2)], axis=0
+        )
+        away[2 * pair * rows : 2 * (pair + 1) * rows] = over_rows(left, right[...]).astype(BF16)
+
+
+def delta_out_kernel(scale, place, got, predicted, hidden, d, away):
     gather_rows(got, d)
     d[...] = ((predicted[...] - d[...].astype(F32)) * scale).astype(BF16)
-    contract_rows = (((1,), (1,)), ((), ()))
-
-    def first(i, carry):
+    away_blocks(hidden, d, place[0], away, away.shape[0] // 4)
+
+
+def delta_in_kernel(place, d, slope, w_out, x, din, away):
+    wide = 256
+
+    def chunk(i, carry):
         at = pl.ds(pl.multiple_of(i * wide, wide), wide)
-        part_out[at, :] = lax.dot_general(
-            hidden[at, :], d[...], contract_rows, preferred_element_type=F32
-        ).astype(BF16)
         back = jnp.dot(w_out[at, :], d[...], preferred_element_type=F32)
         din[at, :] = (back * slope[at, :].astype(F32)).astype(BF16)
         return carry
 
-    lax.fori_loop(0, hidden.shape[0] // wide, first, 0)
-
-    def second(i, carry):
-        at = pl.ds(pl.multiple_of(i * wide, wide), wide)
-        part_in[at, :] = lax.dot_general(
-            x[at, :], din[...], contract_rows, preferred_element_type=F32
+    lax.fori_loop(0, din.shape[0] // wide, chunk, 0)
+    away_blocks(x, din, place[0], away, away.shape[0] // 4)
+
+
+def fold(block, rows, width):
+    extra = rows - block.shape[0]
+    pieces = [
+        block[g * extra : (g + 1) * extra, width:] for g in range(block.shape[0] // extra)
+    ]
+    return jnp.concatenate([block[:, :width], jnp.concatenate(pieces, axis=1)], axis=0)
+
+
+def unfold(block, rows):
+    extra = block.shape[0] - rows
+    count = rows // extra
+    wide = block.shape[1] // count
+    pieces = [block[rows:, g * wide : (g + 1) * wide] for g in range(count)]
+    return jnp.concatenate([block[:rows], jnp.concatenate(pieces, axis=0)], axis=1)
+
+
+def keep_kernel(place, hidden, d, x, din, got_out, got_in, own, plus, minus, top, bottom):
+    core, y = place[0], place[1]
+    rows, width = own.shape[1:]
+    half = rows // 2
+
+    def put(which, k, block):
+        if k == 0:
+            own[which] = block
+        elif k == 1:
+            plus[which] = block.astype(BF16)
+        elif k == 3:
+            minus[which] = block.astype(BF16)
+        else:
+            top[which] = block[:half].astype(BF16)
+            bottom[which] = block[half:].astype(BF16)
+
+    for which, (left, right, got) in enumerate(((hidden, d, got_out), (x, din, got_in))):
+        size = got.shape[0] // 4
+        for ks in ((2, 1), (3, 0)):
+            ys = [lax.rem(y + k, 4) for k in ks]
+            blocks = jnp.concatenate([block_rows(left, at, core, size) for at in ys], axis=0)
+            value = over_rows(blocks, right[...])
+            for n, (k, at) in enumerate(zip(ks, ys)):
+                block = value[n * size : (n + 1) * size]
+                block = block + got[pl.ds(pl.multiple_of(at * size, size), size), :].astype(F32)
+                put(which, k, block if which == 0 else fold(block, rows, width))
+
+
+def relay_kernel(plus, minus, from_before, from_after, plus_out, minus_out):
+    half = from_before.shape[1]
+    for which in range(plus.shape[0]):
+        plus_out[which, :half] = (
+            plus[which, :half].astype(F32) + from_before[which].astype(F32)
         ).astype(BF16)
-        return carry
-
-    lax.fori_loop(0, x.shape[0] // wide, second, 0)
+        plus_out[which, half:] = plus[which, half:]
+        minus_out[which, :half] = minus[which, :half]
+        minus_out[which, half:] = (
+            minus[which, half:].astype(F32) + from_after[which].astype(F32)
+        ).astype(BF16)
+
+
+def finish_kernel(own, from_before, from_after, share_out, share_in):
+    total = [
+        own[k] + from_before[k].astype(F32) + from_after[k].astype(F32) for k in range(2)
+    ]
+    share_out[...] = total[0]
+    share_in[...] = unfold(total[1], share_in.shape[0])
 
 
 def planes_kernel(got, out):
@@ -289,10 +373,16 @@
     return lax.all_to_all(array, axis, split_axis=0, concat_axis=0, tiled=True)
 
 
-def sum_shares(part, axis):
-    size = lax.axis_size(axis)
-    shares = exchange(part.reshape(size, part.shape[0] // size, part.shape[1]), axis)
-    return jnp.sum(shares.astype(F32), axis=0)
+def swap_cores(array):
+    size = lax.axis_size("px")
+    return lax.ppermute(array, "px", [(i, i ^ 1) for i in range(size)])
+
+
+def shift_chips(forward, backward):
+    size = lax.axis_size("px")
+    up = [(i, (i + 2) % size) for i in range(size)]
+    down = [(j, i) for i, j in up]
+    return lax.ppermute(forward, "px", up), lax.ppermute(backward, "px", down)
 
 
 def per_device(velocity, viscosity, implicit_inverse, row_index, row_counts, weight_in, weight_out):
@@ -310,17 +400,17 @@
     y_edge = lambda y: edges[y].transpose(1, 0, 2).reshape(comps * zn, xn)
     zlo, zhi = shift((z_edge(zn - 1), z_edge(0)), ("px", "tr"))
     ylo, yhi = shift((y_edge(yn - 1), y_edge(0)), "pz", wrap=False)
+    ids = slot_table(row_index, row_counts)
     sent = call(
         explicit_kernel,
-        shaped((peers, 2 * (f + xl), lanes), BF16),
-        (v, viscosity.transpose(1, 0, 2), zlo, zhi, ylo, yhi),
+        shaped((peers, 2 * (f + xl) + ids.shape[0], lanes), BF16),
+        (v, viscosity.transpose(1, 0, 2), zlo, zhi, ylo, yhi, ids),
         flops=2e7,
     )
-    ids = slot_table(row_index, row_counts)
     inverse = implicit_inverse.astype(BF16)
     got = exchange(sent, "pz")
     solve_flops = 2 * zn * f * total_y * total_y
-    u, w, packed, zlo, zhi, xlo, xhi = call(
+    u, w, packed, zlo, zhi, xlo, xhi, ids = call(
         first_solve_kernel,
         (
             shaped((zn * f, total_y), F32),
@@ -330,6 +420,7 @@
             shaped((f, total_y), BF16),
             shaped((zn * comps, total_y), BF16),
             shaped((zn * comps, total_y), BF16),
+            shaped((peers,) + ids.shape, jnp.int32),
         ),
         (got, inverse),
         scratch=[pltpu.VMEM((zn * f, total_y), BF16)],
@@ -357,39 +448,72 @@
         flops=solve_flops,
     )
     rows_target = sample(packed)
-    planes = exchange(packed, "pz")
-
     member_in = weight_in[0]
     member_out = weight_out[0]
     width, hid = member_in.shape
     batch = 2 * peers * slots
-    loss_scale = 1.0 / math.sqrt(lax.axis_size("px") * batch)
+    spots = lax.axis_size("px")
+    loss_scale = 1.0 / math.sqrt(spots * batch)
+    matmul_flops = 2 * hid * width * batch
     x, hidden, slope, predicted = call(
         forward_kernel,
         (
             shaped((width, batch), BF16),
             shaped((hid, batch), BF16),
-            shaped((hid, batch), F32),
+            shaped((hid, batch), BF16),
             shaped((width, batch), F32),
         ),
         (rows_in, member_in.T, member_out.T),
-        scratch=[pltpu.VMEM((width, batch), BF16)],
-        flops=4 * hid * width * batch,
-    )
-
-    def backward(*refs):
-        backward_kernel(loss_scale, *refs)
-
-    part_out, part_in = call(
-        backward,
-        (shaped((hid, width), BF16), shaped((width, hid), BF16)),
-        (rows_target, predicted, hidden, slope, x, member_out),
-        scratch=[pltpu.VMEM((width, batch), BF16), pltpu.VMEM((hid, batch), BF16)],
-        flops=6 * hid * width * batch,
-    )
-    share_out = sum_shares(part_out, "px")
-    share_in = sum_shares(part_in, "px")
-    result = call(planes_kernel, shaped((comps, zn, yn, xn), F32), (planes,), flops=1e6)
+        flops=2 * matmul_flops,
+    )
+    position = lax.axis_index("px")
+    place = jnp.stack([position % 2, position // 2]).astype(jnp.int32)
+
+    def delta_out(*refs):
+        delta_out_kernel(loss_scale, *refs)
+
+    d, away_out = call(
+        delta_out,
+        (shaped((width, batch), BF16), shaped((hid // 2, width), BF16)),
+        (place, rows_target, predicted, hidden),
+        flops=matmul_flops // 2,
+    )
+    got_out = swap_cores(away_out)
+    din, away_in = call(
+        delta_in_kernel,
+        (shaped((hid, batch), BF16), shaped((width // 2, hid), BF16)),
+        (place, d, slope, member_out, x),
+        flops=matmul_flops * 3 // 2,
+    )
+    got_in = swap_cores(away_in)
+    packed, away_in = lax.optimization_barrier((packed, away_in))
+    planes = exchange(packed, "pz")
+    rows = hid // spots
+    own, plus, minus, top, bottom = call(
+        keep_kernel,
+        (
+            shaped((2, rows, width), F32),
+            shaped((2, rows, width), BF16),
+            shaped((2, rows, width), BF16),
+            shaped((2, rows // 2, width), BF16),
+            shaped((2, rows // 2, width), BF16),
+        ),
+        (place, hidden, d, x, din, got_out, got_in),
+        flops=matmul_flops,
+    )
+    from_before, from_after = shift_chips(top, bottom)
+    plus, minus = call(
+        relay_kernel,
+        (shaped(plus.shape, BF16), shaped(minus.shape, BF16)),
+        (plus, minus, from_before, from_after),
+    )
+    from_before, from_after = shift_chips(plus, minus)
+    share_out, share_in = call(
+        finish_kernel,
+        (shaped((rows, width), F32), shaped((width // spots, hid), F32)),
+        (own, from_before, from_after),
+    )
+    result = call(planes_kernel, shaped((comps, zn, yn, xn), F32), (planes,))
     return (result.transpose(2, 1, 0, 3), share_in[None], share_out[None])
 
 

time: 222 us -> 175 us (0.79)
  blocking collectives: 93.1 us -> 0 us
  waiting for transfers between devices: 34.8 us -> 54.8 us
  starting transfers between devices: 47 us -> 63.7 us
  local copies, waits for them, and re-layouts: 13.6 us -> 25.5 us
    all_to_all x2 -> x0, blocking collectives: 61.6 us -> none  [exchange(): return lax.all_to_all(array, axis, split_axis=0, concat_axis=0, tiled=True)]
    all_gather x1 -> x0, blocking collectives: 31.6 us -> none  [slot_table(): return lax.all_gather(index, 'pz')]
    ppermute x0 -> x6, starting transfers between devices: none -> 15.5 us  [the longest x4 15 us: shift_chips(): return (lax.ppermute(forward, 'px', up), lax.ppermute(backward, 'px', down))]
    unnamed x36 -> x66, local copies, waits for them, and re-layouts: 10.6 us -> 23.4 us
    ppermute x0 -> x6, waiting for transfers between devices: none -> 10.7 us  [the longest x4 10.7 us: shift_chips(): return (lax.ppermute(forward, 'px', up), lax.ppermute(backward, 'px', down))]
    ppermute x8, waiting for transfers between devices: 15.9 us -> 23 us  [shift(): return (lax.ppermute(last, axis, up), lax.ppermute(first, axis, down))]
    all_to_all x4, starting transfers between devices: 28.2 us -> 30.9 us  [exchange(): return lax.all_to_all(array, axis, split_axis=0, concat_axis=0, tiled=True)]
    pallas_call x8 -> x12, Pallas kernels: 26.6 us -> 25.6 us  [call(): pl.pallas_call(kernel, out_shape=out_shape, in_specs=[pl.BlockSpec(memory...]
  transfers between devices with their start and end apart: 12 -> 18, of which waited for: 4 -> 8; matrix products, arithmetic and copies ran while one was open for 5% -> 6% of each run, Pallas kernels for 10% -> 8%
where the time goes in v2:
time: 175 us; the launch traced here: 174 us
  starting transfers between devices  63.7 us (36%)
  waiting for transfers between devices  54.8 us (31%)
  Pallas kernels  25.6 us (15%)
  local copies, waits for them, and re-layouts  25.5 us (15%)
  other arithmetic  3.33 us (2%)
    all_to_all x4, starting transfers between devices, exchange(): return lax.all_to_all(array, axis, split_axis=0, concat_axis=0, tiled=True)  30.9 us
    pallas_call x12, Pallas kernels, call(): pl.pallas_call(kernel, out_shape=out_shape, in_specs=[pl.BlockSpec(memory...  25.6 us
    unnamed x66, local copies, waits for them, and re-layouts  23.4 us
    ppermute x8, waiting for transfers between devices, shift(): return (lax.ppermute(last, axis, up), lax.ppermute(first, axis, down))  23 us
    all_to_all x4, waiting for transfers between devices, exchange(): return lax.all_to_all(array, axis, split_axis=0, concat_axis=0, tiled=True)  21.1 us
    ppermute x8, starting transfers between devices, shift(): return (lax.ppermute(last, axis, up), lax.ppermute(first, axis, down))  17.3 us
    ppermute x4, starting transfers between devices, shift_chips(): return (lax.ppermute(forward, 'px', up), lax.ppermute(backward, 'px', down))  15 us
    ppermute x4, waiting for transfers between devices, shift_chips(): return (lax.ppermute(forward, 'px', up), lax.ppermute(backward, 'px', down))  10.7 us
  transfers between devices with their start and end apart: 18, of which 8 were waited for; matrix products, arithmetic and copies ran while one was open for 6% of the time, Pallas kernels for 8%

profile of v2, /device:TPU:2, one launch (start us, length us, event | category | flops | bytes accessed | tf_op | source)
XLA Modules:
  0.0 173.8 jit_solution(4734007015835125267)
XLA Ops:
  0.7 1.3 copy.33
  2.1 3.8 %collective-permute-start.2 = (bf16[12,256]{1,0:T(8,128)(2,1)S(1)}, bf16[12,256]{1,0:T(8,128)(2,1)S(1)}, u32[]{:S(2)}, u32[]{:S(2)}) collective-permute-start(bf16[12,256]{1,0:T(8,128)(2,1)S(1)} %reshape.36), channel_id=1, source_target_pairs={{0,2},{2,4},{4,6},{6,8},{8,10},{10,12},{12,14},{14,16},{16,18},{18... | collective-permute-start | bytes 18440 | tf_op jit(solution)/shard_map/ppermute | solution.py:46
  5.9 2.0 %collective-permute-start.3 = (bf16[12,256]{1,0:T(8,128)(2,1)S(1)}, bf16[12,256]{1,0:T(8,128)(2,1)S(1)}, u32[]{:S(2)}, u32[]{:S(2)}) collective-permute-start(bf16[12,256]{1,0:T(8,128)(2,1)S(1)} %reshape.37), channel_id=1, source_target_pairs={{2,0},{4,2},{6,4},{8,6},{10,8},{12,10},{14,12},{16,14},{18,16},{20... | collective-permute-start | bytes 18440 | tf_op jit(solution)/shard_map/ppermute | solution.py:46
  8.0 4.0 %collective-permute-start.1 = (bf16[3,64,256]{2,1,0:T(8,128)(2,1)S(1)}, bf16[3,64,256]{2,1,0:T(8,128)(2,1)S(1)}, u32[]{:S(2)}, u32[]{:S(2)}) collective-permute-start(bf16[3,64,256]{2,1,0:T(8,128)(2,1)S(1)} %get-tuple-element.63), channel_id=1, source_target_pairs={{1,0},{32,1},{33,32},{64,33},{65,64},{96,65},{97,96},{128,97},{129... | collective-permute-start | bytes 294920 | tf_op jit(solution)/shard_map/ppermute | solution.py:46
  14.2 5.5 %collective-permute-done.zlo = bf16[3,64,256]{2,1,0:T(8,128)(2,1)S(1)} collective-permute-done((bf16[3,64,256]{2,1,0:T(8,128)(2,1)S(1)}, bf16[3,64,256]{2,1,0:T(8,128)(2,1)S(1)}, u32[]{:S(2)}, u32[]{:S(2)}) %collective-permute-start) | collective-permute-done | bytes 98336 | tf_op jit(solution)/shard_map/ppermute | solution.py:46
  19.7 1.6 shard_map.94
  21.3 11.8 %all-to-all-start = ((bf16[16,136,128]{2,1,0:T(8,128)(2,1)}), bf16[16,136,128]{2,1,0:T(8,128)(2,1)S(1)}, u32[]{:S(2)}, u32[]{:S(2)}) async-start(bf16[16,136,128]{2,1,0:T(8,128)(2,1)} %shard_map.94), calls=%async_computation | async-start | bytes 1114112 | tf_op jit(solution)/shard_map/all_to_all | solution.py:373
  33.2 2.5 %convert_element_type.7.a = bf16[1024,1024]{1,0:T(8,128)(2,1)S(1)} convert(f32[1024,1024]{1,0:T(8,128)} %param.9) | non-fusion elementwise | flops 1048576 | bytes 6291456 | tf_op jit(solution)/shard_map/convert_element_type | solution.py:410
  35.7 11.0 %all-to-all-done.got = bf16[16,136,128]{2,1,0:T(8,128)(2,1)S(1)} async-done(((bf16[16,136,128]{2,1,0:T(8,128)(2,1)}), bf16[16,136,128]{2,1,0:T(8,128)(2,1)S(1)}, u32[]{:S(2)}, u32[]{:S(2)}) %all-to-all-start) | async-done | bytes 557088 | tf_op jit(solution)/shard_map/all_to_all | solution.py:373
  46.7 1.0 shard_map.95
  49.2 1.8 %shard_map.98 = bf16[32,48,384]{2,1,0:T(8,128)(2,1)S(1)} custom-call(bf16[16,96,128]{2,1,0:T(8,128)(2,1)S(1)} %get-tuple-element.36.packed, s32[16,8,128]{2,1,0:T(8,128)S(1)} %get-tuple-element.35.ids), custom_call_target="tpu_custom_call" | custom-call | flops 1610612736 | bytes 1638400 | tf_op jit(solution)/shard_map/pallas_call | solution.py:22
  51.0 1.1 copy-done.13
  52.7 5.1 %all-to-all-start.2 = ((bf16[32,48,384]{2,1,0:T(8,128)(2,1)}), bf16[32,48,384]{2,1,0:T(8,128)(2,1)S(1)}, u32[]{:S(2)}, u32[]{:S(2)}) async-start(bf16[32,48,384]{2,1,0:T(8,128)(2,1)} %copy-done.13), calls=%async_computation.2 | async-start | bytes 2359296 | tf_op jit(solution)/shard_map/all_to_all | solution.py:373
  57.7 2.2 %collective-permute-start.4 = (bf16[48,1024]{1,0:T(8,128)(2,1)}, bf16[48,1024]{1,0:T(8,128)(2,1)S(1)}, u32[]{:S(2)}, u32[]{:S(2)}) collective-permute-start(bf16[48,1024]{1,0:T(8,128)(2,1)} %copy-done.19), channel_id=1, source_target_pairs={{0,1},{1,32},{32,33},{33,64},{64,65},{65,96},{96,97},{97,128},{128... | collective-permute-start | bytes 294920 | tf_op jit(solution)/shard_map/ppermute | solution.py:46
  59.9 3.3 %collective-permute-start.5 = (bf16[48,1024]{1,0:T(8,128)(2,1)}, bf16[48,1024]{1,0:T(8,128)(2,1)S(1)}, u32[]{:S(2)}, u32[]{:S(2)}) collective-permute-start(bf16[48,1024]{1,0:T(8,128)(2,1)} %copy-done.18), channel_id=1, source_target_pairs={{1,0},{32,1},{33,32},{64,33},{65,64},{96,65},{97,96},{128,97},{129... | collective-permute-start | bytes 294920 | tf_op jit(solution)/shard_map/ppermute | solution.py:46
  63.2 1.6 collective-permute-start.6
  65.2 13.4 %collective-permute-done.6.xlo = bf16[12,1024]{1,0:T(8,128)(2,1)S(1)} collective-permute-done((bf16[12,1024]{1,0:T(8,128)(2,1)}, bf16[12,1024]{1,0:T(8,128)(2,1)S(1)}, u32[]{:S(2)}, u32[]{:S(2)}) %collective-permute-start.6) | collective-permute-done | bytes 24608 | tf_op jit(solution)/shard_map/ppermute | solution.py:46
  78.6 3.6 %collective-permute-done.7.xhi = bf16[12,1024]{1,0:T(8,128)(2,1)S(1)} collective-permute-done((bf16[12,1024]{1,0:T(8,128)(2,1)}, bf16[12,1024]{1,0:T(8,128)(2,1)S(1)}, u32[]{:S(2)}, u32[]{:S(2)}) %collective-permute-start.7) | collective-permute-done | bytes 24608 | tf_op jit(solution)/shard_map/ppermute | solution.py:46
  82.3 1.1 copy-done.17
  83.4 1.9 %shard_map.96.packed = bf16[16,96,128]{2,1,0:T(8,128)(2,1)} custom-call(f32[192,1024]{1,0:T(8,128)S(1)} %copy-done.17, f32[64,1024]{1,0:T(8,128)S(1)} %get-tuple-element.30.w, bf16[48,1024]{1,0:T(8,128)(2,1)S(1)} %collective-permute-done.4.zlo, bf16[48,1024]{1,0:T(8,128)(2,1)S(1)} %collective-permute-done.5.zhi, ...), custom_call_target="tpu_custom_call" | custom-call | flops 402653184 | bytes 3784704 | tf_op jit(solution)/shard_map/pallas_call | solution.py:22
  85.3 3.9 %shard_map.97 = bf16[32,48,384]{2,1,0:T(8,128)(2,1)} custom-call(bf16[16,96,128]{2,1,0:T(8,128)(2,1)} %shard_map.96.packed, s32[16,8,128]{2,1,0:T(8,128)S(1)} %copy-done.21), custom_call_target="tpu_custom_call" | custom-call | flops 1610612736 | bytes 1638400 | tf_op jit(solution)/shard_map/pallas_call | solution.py:22
  89.2 1.0 copy-done.11
  90.3 9.1 %all-to-all-start.1 = ((bf16[32,48,384]{2,1,0:T(8,128)(2,1)}), bf16[32,48,384]{2,1,0:T(8,128)(2,1)S(1)}, u32[]{:S(2)}, u32[]{:S(2)}) async-start(bf16[32,48,384]{2,1,0:T(8,128)(2,1)} %shard_map.97), calls=%async_computation.1 | async-start | bytes 2359296 | tf_op jit(solution)/shard_map/all_to_all | solution.py:373
  99.4 2.7 %copy.25 = bf16[1,768,1024]{1,2,0:T(8,128)(2,1)} copy(bf16[1,768,1024]{2,1,0:T(8,128)(2,1)} %param.12) | data formatting | bytes 3145728 | tf_op args[5]
  102.2 1.6 copy.26.w_out
  103.9 1.4 copy-done.4
  105.3 1.4 copy-done.5
  106.7 1.3 copy-done.12
  107.9 4.1 %shard_map.99 = (bf16[768,768]{1,0:T(8,128)(2,1)S(1)}, bf16[1024,768]{1,0:T(8,128)(2,1)S(1)}, bf16[1024,768]{1,0:T(8,128)(2,1)S(1)}, f32[768,768]{1,0:T(8,128)S(1)}) custom-call(bf16[32,48,384]{2,1,0:T(8,128)(2,1)S(1)} %copy-done.12, bf16[1024,768]{1,0:T(8,128)(2,1)S(1)} %bitcast.47, bf16[768,1024]{1,0:T(8,128)(2,1)S(1)} %copy-done.5), custom_call_target="tpu_custom_call" | custom-call | flops 2415919104 | bytes 11010048 | tf_op jit(solution)/shard_map/pallas_call | solution.py:22
  112.1 1.4 copy-done
  113.5 1.0 copy-done.6
  114.5 1.2 copy-done.24
  115.7 10.1 %all-to-all-done.1.refs_1_ = bf16[32,48,384]{2,1,0:T(8,128)(2,1)S(1)} async-done(((bf16[32,48,384]{2,1,0:T(8,128)(2,1)}), bf16[32,48,384]{2,1,0:T(8,128)(2,1)S(1)}, u32[]{:S(2)}, u32[]{:S(2)}) %all-to-all-start.1) | async-done | bytes 1179680 | tf_op jit(solution)/shard_map/all_to_all | solution.py:373
  125.8 1.7 copy-done.1
  127.5 2.4 %shard_map.100 = (bf16[768,768]{1,0:T(8,128)(2,1)S(1)}, bf16[512,768]{1,0:T(8,128)(2,1)}) custom-call(s32[2]{0:T(128)S(1)} %pad_add_fusion.refs_0_.place, bf16[32,48,384]{2,1,0:T(8,128)(2,1)S(1)} %all-to-all-done.1.refs_1_, f32[768,768]{1,0:T(8,128)S(1)} %copy-done.1, bf16[1024,768]{1,0:T(8,128)(2,1)S(1)} %get-tuple-element.38.refs_3_.hidden), custom_call_target="tpu_custom_call" | custom-call | flops 603979776 | bytes 7077896 | tf_op jit(solution)/shard_map/pallas_call | solution.py:22
  129.9 4.5 %shard_map.101 = (bf16[1024,768]{1,0:T(8,128)(2,1)S(1)}, bf16[384,1024]{1,0:T(8,128)(2,1)}) custom-call(s32[2]{0:T(128)S(1)} %pad_add_fusion.refs_0_.place, bf16[768,768]{1,0:T(8,128)(2,1)S(1)} %get-tuple-element.39.d, bf16[1024,768]{1,0:T(8,128)(2,1)S(1)} %copy-done.25, bf16[1024,768]{1,0:T(8,128)(2,1)S(1)} %bitcast.46, bf16[768,768]{1,0:T(8,128)(2,1)S(1)} %copy-done.7), custom_call_target="tpu_custom_call" | custom-call | flops 1811939328 | bytes 7864328 | tf_op jit(solution)/shard_map/pallas_call | solution.py:22
  134.9 4.8 %all-to-all-start.3 = ((bf16[16,96,128]{2,1,0:T(8,128)(2,1)}), bf16[16,96,128]{2,1,0:T(8,128)(2,1)S(1)}, u32[]{:S(2)}, u32[]{:S(2)}) async-start(bf16[16,96,128]{2,1,0:T(8,128)(2,1)} %shard_map.96.packed), calls=%async_computation.3 | async-start | bytes 786432 | tf_op jit(solution)/shard_map/all_to_all | solution.py:373
  139.7 1.3 copy-done.8
  141.0 1.3 copy-done.10
  142.3 3.2 %shard_map.103 = (f32[2,128,768]{2,1,0:T(8,128)S(1)}, bf16[2,128,768]{2,1,0:T(8,128)(2,1)S(1)}, bf16[2,128,768]{2,1,0:T(8,128)(2,1)S(1)}, bf16[2,64,768]{2,1,0:T(8,128)(2,1)S(1)}, bf16[2,64,768]{2,1,0:T(8,128)(2,1)S(1)}) custom-call(s32[2]{0:T(128)S(1)} %pad_add_fusion.refs_0_.place, bf16[1024,768]{1,0:T(8,128)(2,1)S(1)} %get-tuple-element.38.refs_3_.hidden, ...), custom_call_target="tpu_custom_call" | custom-call | flops 1207959552 | bytes 9043976 | tf_op jit(solution)/shard_map/pallas_call | solution.py:22
  145.5 9.8 %collective-permute-start.10 = (bf16[2,64,768]{2,1,0:T(8,128)(2,1)S(1)}, bf16[2,64,768]{2,1,0:T(8,128)(2,1)S(1)}, u32[]{:S(2)}, u32[]{:S(2)}) collective-permute-start(bf16[2,64,768]{2,1,0:T(8,128)(2,1)S(1)} %get-tuple-element.49), channel_id=1, source_target_pairs={{0,64},{32,96},{64,128},{96,160},{128,192},{160,224},{192,0},{224,... | collective-permute-start | bytes 589832 | tf_op jit(solution)/shard_map/ppermute | solution.py:385
  155.3 1.9 %collective-permute-start.11 = (bf16[2,64,768]{2,1,0:T(8,128)(2,1)S(1)}, bf16[2,64,768]{2,1,0:T(8,128)(2,1)S(1)}, u32[]{:S(2)}, u32[]{:S(2)}) collective-permute-start(bf16[2,64,768]{2,1,0:T(8,128)(2,1)S(1)} %get-tuple-element.50), channel_id=1, source_target_pairs={{64,0},{96,32},{128,64},{160,96},{192,128},{224,160},{0,192},{32,2... | collective-permute-start | bytes 589832 | tf_op jit(solution)/shard_map/ppermute | solution.py:385
  157.2 4.4 %collective-permute-done.10.from_before = bf16[2,64,768]{2,1,0:T(8,128)(2,1)S(1)} collective-permute-done((bf16[2,64,768]{2,1,0:T(8,128)(2,1)S(1)}, bf16[2,64,768]{2,1,0:T(8,128)(2,1)S(1)}, u32[]{:S(2)}, u32[]{:S(2)}) %collective-permute-start.10) | collective-permute-done | bytes 196640 | tf_op jit(solution)/shard_map/ppermute | solution.py:385
  161.7 1.3 collective-permute-start.12
  163.0 2.0 %collective-permute-start.13 = (bf16[2,128,768]{2,1,0:T(8,128)(2,1)S(1)}, bf16[2,128,768]{2,1,0:T(8,128)(2,1)S(1)}, u32[]{:S(2)}, u32[]{:S(2)}) collective-permute-start(bf16[2,128,768]{2,1,0:T(8,128)(2,1)S(1)} %get-tuple-element.52), channel_id=1, source_target_pairs={{64,0},{96,32},{128,64},{160,96},{192,128},{224,160},{0,192},{32,2... | collective-permute-start | bytes 1179656 | tf_op jit(solution)/shard_map/ppermute | solution.py:385
  165.2 1.4 copy.27
  166.6 6.3 %collective-permute-done.12.from_before = bf16[2,128,768]{2,1,0:T(8,128)(2,1)S(1)} collective-permute-done((bf16[2,128,768]{2,1,0:T(8,128)(2,1)S(1)}, bf16[2,128,768]{2,1,0:T(8,128)(2,1)S(1)}, u32[]{:S(2)}, u32[]{:S(2)}) %collective-permute-start.12) | collective-permute-done | bytes 393248 | tf_op jit(solution)/shard_map/ppermute | solution.py:385
  172.8 0.9 shard_map.105
  (83 shorter events, 5.7 us)
Async XLA Ops:
  0.6 12.9 %copy-start.26 = (f32[64,4,3,256]{3,1,2,0:T(4,128)S(1)}, f32[64,4,3,256]{3,1,2,0:T(4,128)}, u32[]{:S(2)}) copy-start(f32[64,4,3,256]{3,1,2,0:T(4,128)} %param.7) | copy-start | bytes 2359300
  0.6 11.8 %copy-start.29 = (s32[1,1,1,32]{3,2,1,0:T(1,128)S(1)}, s32[1,1,1,32]{3,2,1,0:T(1,128)}, u32[]{:S(2)}) copy-start(s32[1,1,1,32]{3,2,1,0:T(1,128)} %param.11) | copy-start | bytes 388
  0.7 12.6 %copy-start.28 = (s32[1,1,1,32,24]{3,4,2,1,0:T(8,128)S(1)}, s32[1,1,1,32,24]{3,4,2,1,0:T(8,128)}, u32[]{:S(2)}) copy-start(s32[1,1,1,32,24]{3,4,2,1,0:T(8,128)} %param.10) | copy-start | bytes 9220
  0.7 13.1 %copy-start.27 = (f32[64,4,256]{2,1,0:T(4,128)S(1)}, f32[64,4,256]{2,1,0:T(4,128)}, u32[]{:S(2)}) copy-start(f32[64,4,256]{2,1,0:T(4,128)} %param.8) | copy-start | bytes 786436
  2.1 11.7 %collective-permute-start.2 = (bf16[12,256]{1,0:T(8,128)(2,1)S(1)}, bf16[12,256]{1,0:T(8,128)(2,1)S(1)}, u32[]{:S(2)}, u32[]{:S(2)}) collective-permute-start(bf16[12,256]{1,0:T(8,128)(2,1)S(1)} %reshape.36), channel_id=1, source_target_pairs={{0,2},{2,4},{4,6},{6,8},{8,10},{10,12},{12,14},{14,16},{16,18},{18... | collective-permute-start | bytes 18440 | tf_op jit(solution)/shard_map/ppermute | solution.py:46
  5.9 7.9 %collective-permute-start.3 = (bf16[12,256]{1,0:T(8,128)(2,1)S(1)}, bf16[12,256]{1,0:T(8,128)(2,1)S(1)}, u32[]{:S(2)}, u32[]{:S(2)}) collective-permute-start(bf16[12,256]{1,0:T(8,128)(2,1)S(1)} %reshape.37), channel_id=1, source_target_pairs={{2,0},{4,2},{6,4},{8,6},{10,8},{12,10},{14,12},{16,14},{18,16},{20... | collective-permute-start | bytes 18440 | tf_op jit(solution)/shard_map/ppermute | solution.py:46
  8.0 6.2 %collective-permute-start.1 = (bf16[3,64,256]{2,1,0:T(8,128)(2,1)S(1)}, bf16[3,64,256]{2,1,0:T(8,128)(2,1)S(1)}, u32[]{:S(2)}, u32[]{:S(2)}) collective-permute-start(bf16[3,64,256]{2,1,0:T(8,128)(2,1)S(1)} %get-tuple-element.63), channel_id=1, source_target_pairs={{1,0},{32,1},{33,32},{64,33},{65,64},{96,65},{97,96},{128,97},{129... | collective-permute-start | bytes 294920 | tf_op jit(solution)/shard_map/ppermute | solution.py:46
  12.0 7.8 %collective-permute-start = (bf16[3,64,256]{2,1,0:T(8,128)(2,1)S(1)}, bf16[3,64,256]{2,1,0:T(8,128)(2,1)S(1)}, u32[]{:S(2)}, u32[]{:S(2)}) collective-permute-start(bf16[3,64,256]{2,1,0:T(8,128)(2,1)S(1)} %get-tuple-element.64), channel_id=1, source_target_pairs={{0,1},{1,32},{32,33},{33,64},{64,65},{65,96},{96,97},{97,128},{128... | collective-permute-start | bytes 294920 | tf_op jit(solution)/shard_map/ppermute | solution.py:46
  21.3 25.4 %all-to-all-start = ((bf16[16,136,128]{2,1,0:T(8,128)(2,1)}), bf16[16,136,128]{2,1,0:T(8,128)(2,1)S(1)}, u32[]{:S(2)}, u32[]{:S(2)}) async-start(bf16[16,136,128]{2,1,0:T(8,128)(2,1)} %shard_map.94), calls=%async_computation | async-start | bytes 1114112 | tf_op jit(solution)/shard_map/all_to_all | solution.py:373
  47.7 0.9 copy-start.16
  48.6 0.6 copy-start.23
  49.2 3.5 %copy-start.18 = (bf16[48,1024]{1,0:T(8,128)(2,1)}, bf16[48,1024]{1,0:T(8,128)(2,1)S(1)}, u32[]{:S(2)}) copy-start(bf16[48,1024]{1,0:T(8,128)(2,1)S(1)} %get-tuple-element.32) | copy-start | bytes 294916
  49.2 3.5 %copy-start.19 = (bf16[48,1024]{1,0:T(8,128)(2,1)}, bf16[48,1024]{1,0:T(8,128)(2,1)S(1)}, u32[]{:S(2)}) copy-start(bf16[48,1024]{1,0:T(8,128)(2,1)S(1)} %get-tuple-element.31) | copy-start | bytes 294916
  49.2 3.5 %copy-start.22 = (bf16[12,1024]{1,0:T(8,128)(2,1)}, bf16[12,1024]{1,0:T(8,128)(2,1)S(1)}, u32[]{:S(2)}) copy-start(bf16[12,1024]{1,0:T(8,128)(2,1)S(1)} %get-tuple-element.34) | copy-start | bytes 73732
  51.0 1.1 copy-start.13
  52.0 0.6 copy-start.20
  52.7 36.6 %all-to-all-start.2 = ((bf16[32,48,384]{2,1,0:T(8,128)(2,1)}), bf16[32,48,384]{2,1,0:T(8,128)(2,1)S(1)}, u32[]{:S(2)}, u32[]{:S(2)}) async-start(bf16[32,48,384]{2,1,0:T(8,128)(2,1)} %copy-done.13), calls=%async_computation.2 | async-start | bytes 2359296 | tf_op jit(solution)/shard_map/all_to_all | solution.py:373
  57.7 24.5 %collective-permute-start.4 = (bf16[48,1024]{1,0:T(8,128)(2,1)}, bf16[48,1024]{1,0:T(8,128)(2,1)S(1)}, u32[]{:S(2)}, u32[]{:S(2)}) collective-permute-start(bf16[48,1024]{1,0:T(8,128)(2,1)} %copy-done.19), channel_id=1, source_target_pairs={{0,1},{1,32},{32,33},{33,64},{64,65},{65,96},{96,97},{97,128},{128... | collective-permute-start | bytes 294920 | tf_op jit(solution)/shard_map/ppermute | solution.py:46
  59.9 22.4 %collective-permute-start.5 = (bf16[48,1024]{1,0:T(8,128)(2,1)}, bf16[48,1024]{1,0:T(8,128)(2,1)S(1)}, u32[]{:S(2)}, u32[]{:S(2)}) collective-permute-start(bf16[48,1024]{1,0:T(8,128)(2,1)} %copy-done.18), channel_id=1, source_target_pairs={{1,0},{32,1},{33,32},{64,33},{65,64},{96,65},{97,96},{128,97},{129... | collective-permute-start | bytes 294920 | tf_op jit(solution)/shard_map/ppermute | solution.py:46
  63.2 15.4 %collective-permute-start.6 = (bf16[12,1024]{1,0:T(8,128)(2,1)}, bf16[12,1024]{1,0:T(8,128)(2,1)S(1)}, u32[]{:S(2)}, u32[]{:S(2)}) collective-permute-start(bf16[12,1024]{1,0:T(8,128)(2,1)} %copy-done.23), channel_id=1, source_target_pairs={{0,2},{2,4},{4,6},{6,8},{8,10},{10,12},{12,14},{14,16},{16,18},{18... | collective-permute-start | bytes 73736 | tf_op jit(solution)/shard_map/ppermute | solution.py:46
  64.8 17.5 %collective-permute-start.7 = (bf16[12,1024]{1,0:T(8,128)(2,1)}, bf16[12,1024]{1,0:T(8,128)(2,1)S(1)}, u32[]{:S(2)}, u32[]{:S(2)}) collective-permute-start(bf16[12,1024]{1,0:T(8,128)(2,1)} %copy-done.22), channel_id=1, source_target_pairs={{2,0},{4,2},{6,4},{8,6},{10,8},{12,10},{14,12},{16,14},{18,16},{20... | collective-permute-start | bytes 73736 | tf_op jit(solution)/shard_map/ppermute | solution.py:46
  82.3 1.1 copy-start.17
  83.4 1.9 %copy-start.21 = (s32[16,8,128]{2,1,0:T(8,128)S(1)}, s32[16,8,128]{2,1,0:T(8,128)}, u32[]{:S(2)}) copy-start(s32[16,8,128]{2,1,0:T(8,128)} %copy-done.20) | copy-start | bytes 196612
  89.2 1.0 copy-start.11
  90.3 35.5 %all-to-all-start.1 = ((bf16[32,48,384]{2,1,0:T(8,128)(2,1)}), bf16[32,48,384]{2,1,0:T(8,128)(2,1)S(1)}, u32[]{:S(2)}, u32[]{:S(2)}) async-start(bf16[32,48,384]{2,1,0:T(8,128)(2,1)} %shard_map.97), calls=%async_computation.1 | async-start | bytes 2359296 | tf_op jit(solution)/shard_map/all_to_all | solution.py:373
  99.4 2.7 %copy-start.2 = (bf16[1,1024,768]{2,1,0:T(8,128)(2,1)S(1)}, bf16[1,1024,768]{2,1,0:T(8,128)(2,1)}, u32[]{:S(2)}) copy-start(bf16[1,1024,768]{2,1,0:T(8,128)(2,1)} %param.13) | copy-start | bytes 4718596
  103.9 1.4 copy-start.4
  105.3 1.4 copy-start.5
  106.7 1.3 copy-start.12
  112.1 1.4 copy-start
  113.5 1.0 copy-start.6
  114.5 1.2 copy-start.24
  125.8 1.7 copy-start.1
  127.5 2.4 %copy-start.3 = (bf16[1,1024,768]{2,1,0:T(8,128)(2,1)S(1)}, bf16[1,1024,768]{2,1,0:T(8,128)(2,1)}, u32[]{:S(2)}) copy-start(bf16[1,1024,768]{2,1,0:T(8,128)(2,1)} %param.13) | copy-start | bytes 4718596
  127.5 2.4 %copy-start.7 = (bf16[768,768]{1,0:T(8,128)(2,1)S(1)}, bf16[768,768]{1,0:T(8,128)(2,1)}, u32[]{:S(2)}) copy-start(bf16[768,768]{1,0:T(8,128)(2,1)} %copy-done.6) | copy-start | bytes 3538948
  127.5 2.4 %copy-start.25 = (bf16[1024,768]{1,0:T(8,128)(2,1)S(1)}, bf16[1024,768]{1,0:T(8,128)(2,1)}, u32[]{:S(2)}) copy-start(bf16[1024,768]{1,0:T(8,128)(2,1)} %copy-done.24) | copy-start | bytes 4718596
  129.9 4.5 %copy-start.9 = (bf16[768,768]{1,0:T(8,128)(2,1)}, bf16[768,768]{1,0:T(8,128)(2,1)S(1)}, u32[]{:S(2)}) copy-start(bf16[768,768]{1,0:T(8,128)(2,1)S(1)} %get-tuple-element.39.d) | copy-start | bytes 3538948
  134.4 5.3 %collective-permute-start.9 = (bf16[384,1024]{1,0:T(8,128)(2,1)}, bf16[384,1024]{1,0:T(8,128)(2,1)}, u32[]{:S(2)}, u32[]{:S(2)}) collective-permute-start(bf16[384,1024]{1,0:T(8,128)(2,1)} %get-tuple-element.42), channel_id=1, source_target_pairs={{0,32},{32,0},{64,96},{96,64},{128,160},{160,128},{192,224},{224,1... | collective-permute-start | bytes 2359304 | tf_op jit(solution)/shard_map/ppermute | solution.py:378
  134.4 5.3 %collective-permute-start.8 = (bf16[512,768]{1,0:T(8,128)(2,1)}, bf16[512,768]{1,0:T(8,128)(2,1)}, u32[]{:S(2)}, u32[]{:S(2)}) collective-permute-start(bf16[512,768]{1,0:T(8,128)(2,1)} %get-tuple-element.45), channel_id=1, source_target_pairs={{0,32},{32,0},{64,96},{96,64},{128,160},{160,128},{192,224},{224,1... | collective-permute-start | bytes 2359304 | tf_op jit(solution)/shard_map/ppermute | solution.py:378
  134.9 30.1 %all-to-all-start.3 = ((bf16[16,96,128]{2,1,0:T(8,128)(2,1)}), bf16[16,96,128]{2,1,0:T(8,128)(2,1)S(1)}, u32[]{:S(2)}, u32[]{:S(2)}) async-start(bf16[16,96,128]{2,1,0:T(8,128)(2,1)} %shard_map.96.packed), calls=%async_computation.3 | async-start | bytes 786432 | tf_op jit(solution)/shard_map/all_to_all | solution.py:373
  139.7 1.3 copy-start.8
  141.0 1.3 copy-start.10
  145.5 17.5 %copy-start.14 = (f32[2,128,768]{2,1,0:T(8,128)}, f32[2,128,768]{2,1,0:T(8,128)S(1)}, u32[]{:S(2)}) copy-start(f32[2,128,768]{2,1,0:T(8,128)S(1)} %get-tuple-element.46.own) | copy-start | bytes 2359300
  145.5 16.1 %collective-permute-start.10 = (bf16[2,64,768]{2,1,0:T(8,128)(2,1)S(1)}, bf16[2,64,768]{2,1,0:T(8,128)(2,1)S(1)}, u32[]{:S(2)}, u32[]{:S(2)}) collective-permute-start(bf16[2,64,768]{2,1,0:T(8,128)(2,1)S(1)} %get-tuple-element.49), channel_id=1, source_target_pairs={{0,64},{32,96},{64,128},{96,160},{128,192},{160,224},{192,0},{224,... | collective-permute-start | bytes 589832 | tf_op jit(solution)/shard_map/ppermute | solution.py:385
  155.3 6.3 %collective-permute-start.11 = (bf16[2,64,768]{2,1,0:T(8,128)(2,1)S(1)}, bf16[2,64,768]{2,1,0:T(8,128)(2,1)S(1)}, u32[]{:S(2)}, u32[]{:S(2)}) collective-permute-start(bf16[2,64,768]{2,1,0:T(8,128)(2,1)S(1)} %get-tuple-element.50), channel_id=1, source_target_pairs={{64,0},{96,32},{128,64},{160,96},{192,128},{224,160},{0,192},{32,2... | collective-permute-start | bytes 589832 | tf_op jit(solution)/shard_map/ppermute | solution.py:385
  161.7 11.1 %collective-permute-start.12 = (bf16[2,128,768]{2,1,0:T(8,128)(2,1)S(1)}, bf16[2,128,768]{2,1,0:T(8,128)(2,1)S(1)}, u32[]{:S(2)}, u32[]{:S(2)}) collective-permute-start(bf16[2,128,768]{2,1,0:T(8,128)(2,1)S(1)} %get-tuple-element.51), channel_id=1, source_target_pairs={{0,64},{32,96},{64,128},{96,160},{128,192},{160,224},{192,0},{224,... | collective-permute-start | bytes 1179656 | tf_op jit(solution)/shard_map/ppermute | solution.py:385
  163.0 9.8 %collective-permute-start.13 = (bf16[2,128,768]{2,1,0:T(8,128)(2,1)S(1)}, bf16[2,128,768]{2,1,0:T(8,128)(2,1)S(1)}, u32[]{:S(2)}, u32[]{:S(2)}) collective-permute-start(bf16[2,128,768]{2,1,0:T(8,128)(2,1)S(1)} %get-tuple-element.52), channel_id=1, source_target_pairs={{64,0},{96,32},{128,64},{160,96},{192,128},{224,160},{0,192},{32,2... | collective-permute-start | bytes 1179656 | tf_op jit(solution)/shard_map/ppermute | solution.py:385
  165.0 7.8 %copy-start.15 = (f32[2,128,768]{2,1,0:T(8,128)S(1)}, f32[2,128,768]{2,1,0:T(8,128)}, u32[]{:S(2)}) copy-start(f32[2,128,768]{2,1,0:T(8,128)} %copy-done.14) | copy-start | bytes 2359300

commit v3 on v2

--- a/solution.py
+++ b/solution.py
@@ -13,25 +13,52 @@
 MIB = 1 << 20
 
 
-def call(kernel, out_shape, args, scratch=(), flops=1e6):
+def call(kernel, out_shape, args, scratch=(), flops=1e6, far_in=(), far_out=()):
     outs = jax.tree.leaves(out_shape)
-    size = lambda x: math.prod(x.shape) * x.dtype.itemsize
-    moved = sum(size(x) for x in list(args) + outs)
-    held = moved + sum(math.prod(x.shape) * jnp.dtype(x.dtype).itemsize for x in scratch)
-    scalars = lambda x: x.ndim == 1
+    size = lambda x: math.prod(x.shape) * jnp.dtype(x.dtype).itemsize
+    near = [x for k, x in enumerate(args) if k not in far_in]
+    near += [x for k, x in enumerate(outs) if k not in far_out]
+    held = sum(size(x) for x in near) + sum(size(x) for x in scratch if x.dtype in (F32, BF16, jnp.int32))
+
+    def spec(k, far, scalar=False):
+        space = pltpu.HBM if k in far else pltpu.SMEM if scalar else pltpu.VMEM
+        return pl.BlockSpec(memory_space=space)
+
+    out_specs = tuple(spec(k, far_out) for k in range(len(outs)))
     return pl.pallas_call(
         kernel,
         out_shape=out_shape,
-        in_specs=[
-            pl.BlockSpec(memory_space=pltpu.SMEM if scalars(x) else pltpu.VMEM) for x in args
-        ],
-        out_specs=jax.tree.map(lambda _: pl.BlockSpec(memory_space=pltpu.VMEM), out_shape),
+        in_specs=[spec(k, far_in, x.ndim == 1) for k, x in enumerate(args)],
+        out_specs=out_specs if isinstance(out_shape, tuple) else out_specs[0],
         scratch_shapes=list(scratch),
         compiler_params=pltpu.CompilerParams(vmem_limit_bytes=held + 6 * MIB),
         cost_estimate=pl.CostEstimate(
-            flops=int(flops), bytes_accessed=int(moved), transcendentals=0
+            flops=int(flops),
+            bytes_accessed=int(sum(size(x) for x in list(args) + outs)),
+            transcendentals=0,
         ),
     )(*args)
+
+
+class Copies:
+    def __init__(self, sems):
+        self.sems, self.used, self.open = sems, 0, []
+
+    def start(self, source, target):
+        copy = pltpu.make_async_copy(source, target, self.sems.at[self.used])
+        copy.start()
+        self.used += 1
+        self.open.append(copy)
+        return copy
+
+    def finish(self):
+        for copy in self.open:
+            copy.wait()
+        self.open = []
+
+    def wait(self, copy):
+        copy.wait()
+        self.open.remove(copy)
 
 
 def shaped(shape, dtype):
@@ -46,38 +73,37 @@
     return lax.ppermute(last, axis, up), lax.ppermute(first, axis, down)
 
 
-def explicit_kernel(v, w, zlo, zhi, ylo, yhi, ids, out):
+HALO_ROWS = 24
+
+
+def columns_kernel(v, w, ids, out, edge):
     comps, zn, yn, xn = v.shape
     peers = out.shape[0]
     xl = xn // peers
-    row = lax.broadcasted_iota(jnp.int32, (yn, xn), 0)
-    y_before = ylo[...].astype(F32)
-    y_after = yhi[...].astype(F32)
     half = (comps + 1) * xl
     for zh in range(zn // 2):
         for c in range(comps + 1):
-            pair = []
-            for z in (2 * zh, 2 * zh + 1):
-                if c == comps:
-                    pair.append(w[z])
-                    continue
-                cur = v[c, z]
-                r = c * zn + z
-                total = v[c, z - 1] if z > 0 else zlo[c].astype(F32)
-                total = total + (v[c, z + 1] if z < zn - 1 else zhi[c].astype(F32))
-                total = total + jnp.where(row == 0, y_before[r : r + 1], pltpu.roll(cur, 1, 0))
-                total = total + jnp.where(
-                    row == yn - 1, y_after[r : r + 1], pltpu.roll(cur, yn - 1, 0)
-                )
-                total = total + pltpu.roll(cur, 1, 1) + pltpu.roll(cur, xn - 1, 1)
-                pair.append(cur + diffusion_factor * w[z] * (total - 6.0 * cur))
-            turned = jnp.concatenate(pair, axis=0).T.astype(BF16)
+            source = w if c == comps else v.at[c]
+            pair = [source[z].astype(F32) for z in (2 * zh, 2 * zh + 1)]
+            turned = jnp.concatenate(pair, axis=0).T
             base = zh * half + c * xl
             for q in range(peers):
-                out[q, base : base + xl, :] = turned[q * xl : (q + 1) * xl]
-    numbers = ids[...].astype(F32).astype(BF16)
+                out[q, base : base + xl, :] = turned[q * xl : (q + 1) * xl].astype(BF16)
+            if c == comps:
+                continue
+            for q in range(peers):
+                before = (q * xl - 1) % xn
+                after = (q + 1) * xl % xn
+                r = q * HALO_ROWS + zh * comps + c
+                edge[r : r + 1] = turned[before : before + 1]
+                edge[r + zn // 2 * comps : r + zn // 2 * comps + 1] = turned[after : after + 1]
+    start = zn // 2 * half
+    numbers = ids[...].astype(F32)
     for q in range(peers):
-        out[q, (zn // 2) * half : (zn // 2) * half + ids.shape[0], :] = numbers
+        edge[(q + 1) * HALO_ROWS - 8 : (q + 1) * HALO_ROWS] = numbers
+        out[q, start : start + HALO_ROWS, :] = edge[
+            q * HALO_ROWS : (q + 1) * HALO_ROWS
+        ].astype(BF16)
 
 
 def solve(e, a):
@@ -101,19 +127,19 @@
             packed[2 * j + 1, zh * f : (zh + 1) * f, :] = odd.astype(BF16)
 
 
-def first_solve_kernel(got, a, u, w, packed, zlo, zhi, xlo, xhi, ids, e):
+def spread_kernel(got, v, w, xlo, xhi, zlo, zhi, ids):
     peers, rows, lanes = got.shape
-    rows = rows - ids.shape[1]
-    ids[...] = got[:, rows:, :].astype(F32).astype(jnp.int32)
+    ids[...] = got[:, rows - 8 :, :].astype(F32).astype(jnp.int32)
     yn = lanes // 2
     zn = 4
-    half = rows // 2
+    half = (rows - HALO_ROWS) // 2
     xl = w.shape[0] // zn
     f = half - xl
+    comps = f // xl
     low = lax.broadcasted_iota(jnp.int32, (rows, lanes), 1) < yn
     for j in range(peers // 2):
-        one = got[2 * j, 0:rows].astype(F32)
-        two = got[2 * j + 1, 0:rows].astype(F32)
+        one = got[2 * j].astype(F32)
+        two = got[2 * j + 1].astype(F32)
         sides = (
             jnp.where(low, one, pltpu.roll(two, yn, 1)),
             jnp.where(low, pltpu.roll(one, yn, 1), two),
@@ -122,56 +148,105 @@
         for zh in range(zn // 2):
             for side in range(2):
                 z = 2 * zh + side
-                e[z * f : (z + 1) * f, at] = sides[side][zh * half : zh * half + f].astype(BF16)
-                w[z * xl : (z + 1) * xl, at] = sides[side][zh * half + f : (zh + 1) * half]
-    u[...] = solve(e, a)
-    zlo[...] = u[0:f].astype(BF16)
-    zhi[...] = u[(zn - 1) * f : zn * f].astype(BF16)
-    groups = u.shape[0] // xl
-    xlo[...] = jnp.concatenate([u[r * xl : r * xl + 1] for r in range(groups)], axis=0).astype(BF16)
-    xhi[...] = jnp.concatenate(
-        [u[(r + 1) * xl - 1 : (r + 1) * xl] for r in range(groups)], axis=0
-    ).astype(BF16)
-    pack_columns(u, packed, zn)
-
-
-def second_solve_kernel(u, w, zlo, zhi, xlo, xhi, a, packed, e, out):
-    cols = u.shape[1]
-    f = zlo.shape[0]
+                whole = sides[side]
+                v[z * f : (z + 1) * f, at] = whole[zh * half : zh * half + f].astype(BF16)
+                w[z * xl : (z + 1) * xl, at] = whole[zh * half + f : (zh + 1) * half].astype(BF16)
+                r = zn // 2 * half + zh * comps
+                xlo[z * comps : (z + 1) * comps, at] = whole[r : r + comps]
+                r = r + zn // 2 * comps
+                xhi[z * comps : (z + 1) * comps, at] = whole[r : r + comps]
+    zlo[...] = v[0:f]
+    zhi[...] = v[(zn - 1) * f : zn * f]
+
+
+def explicit_plane(z, u, w, zlo, zhi, x_before, x_after, e):
+    f, cols = zlo.shape
     zn = u.shape[0] // f
     xl = w.shape[0] // zn
     comps = f // xl
     row = lax.broadcasted_iota(jnp.int32, (xl, cols), 0)
     lane = lax.broadcasted_iota(jnp.int32, (xl, cols), 1)
-    x_before = xlo[...].astype(F32)
-    x_after = xhi[...].astype(F32)
+    factor = diffusion_factor * w[z * xl : (z + 1) * xl].astype(F32)
+    for c in range(comps):
+        r = z * comps + c
+        at = slice(r * xl, (r + 1) * xl)
+        cur = u[at].astype(F32)
+        if z > 0:
+            total = u[(r - comps) * xl : (r - comps + 1) * xl].astype(F32)
+        else:
+            total = zlo[c * xl : (c + 1) * xl].astype(F32)
+        if z < zn - 1:
+            total = total + u[(r + comps) * xl : (r + comps + 1) * xl].astype(F32)
+        else:
+            total = total + zhi[c * xl : (c + 1) * xl].astype(F32)
+        total = total + jnp.where(row == 0, x_before[r : r + 1], pltpu.roll(cur, 1, 0))
+        total = total + jnp.where(row == xl - 1, x_after[r : r + 1], pltpu.roll(cur, xl - 1, 0))
+        total = total + jnp.where(lane == 0, 0.0, pltpu.roll(cur, 1, 1))
+        total = total + jnp.where(lane == cols - 1, 0.0, pltpu.roll(cur, cols - 1, 1))
+        e[at] = (cur + factor * (total - 6.0 * cur)).astype(BF16)
+
+
+def first_kernel(
+    v, w, xlo, xhi, zlo, zhi, ids, a,
+    u_far, w_far, ids_far, zlo_far, zhi_far, xlo_far, xhi_far, sent_far,
+    e, u, packed, picked, sent, z_edge, x_edge, sems,
+):
+    copies = Copies(sems)
+    copies.start(w, w_far)
+    copies.start(ids, ids_far)
+    x_before, x_after = xlo[...], xhi[...]
+    zn = 4
     for z in range(zn):
-        for c in range(comps):
-            r = z * comps + c
-            at = slice(r * xl, (r + 1) * xl)
-            cur = u[at]
-            if z > 0:
-                total = u[(r - comps) * xl : (r - comps + 1) * xl]
-            else:
-                total = zlo[c * xl : (c + 1) * xl].astype(F32)
-            if z < zn - 1:
-                total = total + u[(r + comps) * xl : (r + comps + 1) * xl]
-            else:
-                total = total + zhi[c * xl : (c + 1) * xl].astype(F32)
-            total = total + jnp.where(row == 0, x_before[r : r + 1], pltpu.roll(cur, 1, 0))
-            total = total + jnp.where(row == xl - 1, x_after[r : r + 1], pltpu.roll(cur, xl - 1, 0))
-            total = total + jnp.where(lane == 0, 0.0, pltpu.roll(cur, 1, 1))
-            total = total + jnp.where(lane == cols - 1, 0.0, pltpu.roll(cur, cols - 1, 1))
-            step = diffusion_factor * w[z * xl : (z + 1) * xl] * (total - 6.0 * cur)
-            e[at] = (cur + step).astype(BF16)
-    out[...] = solve(e, a)
-    pack_columns(out, packed, zn)
+        explicit_plane(z, v, w, zlo, zhi, x_before, x_after, e)
+    u[...] = solve(e, a)
+    copies.start(u, u_far)
+    f = zlo.shape[0]
+    z_edge[0] = u[0:f].astype(BF16)
+    z_edge[1] = u[(zn - 1) * f : zn * f].astype(BF16)
+    xl = w.shape[0] // zn
+    groups = u.shape[0] // xl
+    for r in range(groups):
+        x_edge[0, r : r + 1] = u[r * xl : r * xl + 1]
+        x_edge[1, r : r + 1] = u[(r + 1) * xl - 1 : (r + 1) * xl]
+    for k, (edge, far) in enumerate(
+        ((z_edge, zlo_far), (z_edge, zhi_far), (x_edge, xlo_far), (x_edge, xhi_far))
+    ):
+        copies.start(edge.at[k % 2], far)
+    pack_columns(u, packed, zn)
+    sample(packed, ids, picked, sent, lambda part: copies.start(sent.at[part], sent_far.at[part]))
+    copies.finish()
+
+
+def second_kernel(
+    u_far, w_far, ids_far, zlo, zhi, xlo, xhi, a, packed_far, sent_far,
+    e, u, w, ids, packed, picked, sent, sems,
+):
+    copies = Copies(sems)
+    f = zlo.shape[0]
+    zn = u.shape[0] // f
+    w_copy = copies.start(w_far, w)
+    parts = [pl.ds(z * f, f) for z in range(zn)]
+    arriving = [copies.start(u_far.at[part], u.at[part]) for part in parts]
+    ids_copy = copies.start(ids_far, ids)
+    copies.wait(w_copy)
+    copies.wait(arriving[0])
+    x_before, x_after = xlo[...], xhi[...]
+    for z in range(zn):
+        if z < zn - 1:
+            copies.wait(arriving[z + 1])
+        explicit_plane(z, u, w, zlo, zhi, x_before, x_after, e)
+    u[...] = solve(e, a)
+    pack_columns(u, packed, zn)
+    copies.start(packed, packed_far)
+    copies.wait(ids_copy)
+    sample(packed, ids, picked, sent, lambda part: copies.start(sent.at[part], sent_far.at[part]))
+    copies.finish()
 
 
 GROUP = 8
 
 
-def sample_kernel(packed, ids, out, picked):
+def sample(packed, ids, picked, out, ready):
     peers, rows, lanes = packed.shape
     f = rows // 2
     yn = lanes // 2
@@ -199,6 +274,7 @@
             step *= 2
         for ml in range(per):
             out[mh * per + ml, :, kg * lanes : (kg + 1) * lanes] = held[(-ml) % peers].astype(BF16)
+        ready((pl.ds(mh * per, per), slice(None), pl.ds(kg * lanes, lanes)))
 
 
 def slot_table(row_index, row_counts):
@@ -235,8 +311,13 @@
     return lax.dot_general(left, right, CONTRACT_ROWS, preferred_element_type=F32)
 
 
-def forward_kernel(got, w_in, w_out, x, hidden, slope, predicted):
+def forward_kernel(
+    got, w_in, w_out, x_far, hidden_far, slope_far, predicted_far,
+    x, hidden, slope, predicted, sems,
+):
+    copies = Copies(sems)
     gather_rows(got, x)
+    copies.start(x, x_far)
     wide = 256
 
     def chunk(i, carry):
@@ -248,6 +329,8 @@
         return carry
 
     lax.fori_loop(0, hidden.shape[0] // wide, chunk, 0)
+    copies.start(hidden, hidden_far)
+    copies.start(slope, slope_far)
 
     def second(i, carry):
         at = pl.ds(pl.multiple_of(i * wide, wide), wide)
@@ -255,6 +338,8 @@
         return carry
 
     lax.fori_loop(0, predicted.shape[0] // wide, second, 0)
+    copies.start(predicted, predicted_far)
+    copies.finish()
 
 
 def block_rows(array, y, core, rows):
@@ -269,9 +354,19 @@
         away[2 * pair * rows : 2 * (pair + 1) * rows] = over_rows(left, right[...]).astype(BF16)
 
 
-def delta_out_kernel(scale, place, got, predicted, hidden, d, away):
+def delta_out_kernel(scale, place, got, predicted_far, hidden_far, d, away, predicted, hidden, sems):
+    copies = Copies(sems)
+    count = 3
+    rows = d.shape[0] // count
+    parts = [pl.ds(k * rows, rows) for k in range(count)]
+    arriving = [copies.start(predicted_far.at[part], predicted.at[part]) for part in parts]
+    copies.start(hidden_far, hidden)
     gather_rows(got, d)
-    d[...] = ((predicted[...] - d[...].astype(F32)) * scale).astype(BF16)
+    for k in range(count):
+        copies.wait(arriving[k])
+        at = slice(k * rows, (k + 1) * rows)
+        d[at] = ((predicted[at] - d[at].astype(F32)) * scale).astype(BF16)
+    copies.finish()
     away_blocks(hidden, d, place[0], away, away.shape[0] // 4)
 
 
@@ -394,60 +489,70 @@
     lanes = 2 * yn
     members, slots = row_index.shape[3:]
 
-    v = velocity.transpose(2, 1, 0, 3)
-    edges = velocity.astype(BF16)
-    z_edge = lambda z: edges[:, z].transpose(1, 0, 2)
-    y_edge = lambda y: edges[y].transpose(1, 0, 2).reshape(comps * zn, xn)
-    zlo, zhi = shift((z_edge(zn - 1), z_edge(0)), ("px", "tr"))
-    ylo, yhi = shift((y_edge(yn - 1), y_edge(0)), "pz", wrap=False)
+    v = velocity.astype(BF16).transpose(2, 1, 0, 3)
     ids = slot_table(row_index, row_counts)
     sent = call(
-        explicit_kernel,
-        shaped((peers, 2 * (f + xl) + ids.shape[0], lanes), BF16),
-        (v, viscosity.transpose(1, 0, 2), zlo, zhi, ylo, yhi, ids),
-        flops=2e7,
+        columns_kernel,
+        shaped((peers, 2 * (f + xl) + HALO_ROWS, lanes), BF16),
+        (v, viscosity.astype(BF16).transpose(1, 0, 2), ids),
+        scratch=[pltpu.VMEM((peers * HALO_ROWS, lanes), F32)],
     )
     inverse = implicit_inverse.astype(BF16)
     got = exchange(sent, "pz")
     solve_flops = 2 * zn * f * total_y * total_y
-    u, w, packed, zlo, zhi, xlo, xhi, ids = call(
-        first_solve_kernel,
-        (
-            shaped((zn * f, total_y), F32),
-            shaped((zn * xl, total_y), F32),
-            shaped((peers, 2 * f, lanes), BF16),
-            shaped((f, total_y), BF16),
-            shaped((f, total_y), BF16),
-            shaped((zn * comps, total_y), BF16),
-            shaped((zn * comps, total_y), BF16),
-            shaped((peers,) + ids.shape, jnp.int32),
-        ),
-        (got, inverse),
-        scratch=[pltpu.VMEM((zn * f, total_y), BF16)],
-        flops=solve_flops,
-    )
+    edge = shaped((f, total_y), BF16)
+    x_edge = shaped((zn * comps, total_y), F32)
+    ids_all = shaped((peers,) + ids.shape, jnp.int32)
+    v, w, xlo, xhi, zlo, zhi, ids = call(
+        spread_kernel,
+        (shaped((zn * f, total_y), BF16), shaped((zn * xl, total_y), BF16))
+        + (x_edge, x_edge, edge, edge, ids_all),
+        (got,),
+    )
+    zlo, zhi = shift((zhi, zlo), ("px", "tr"))
+    message = shaped((members, f, peers * slots), BF16)
+    sample_flops = 2 * peers * f * 256 * members * slots
+    sampling = [
+        pltpu.VMEM((peers, 2 * f, lanes), BF16),
+        pltpu.VMEM((peers, f, members * slots), F32),
+        pltpu.VMEM(message.shape, BF16),
+    ]
+    u, w, ids, zlo, zhi, xlo, xhi, sent = call(
+        first_kernel,
+        (shaped((zn * f, total_y), F32), shaped(w.shape, BF16), ids_all)
+        + (edge, edge, x_edge, x_edge, message),
+        (v, w, xlo, xhi, zlo, zhi, ids, inverse),
+        scratch=[pltpu.VMEM((zn * f, total_y), BF16), pltpu.VMEM((zn * f, total_y), F32)]
+        + sampling
+        + [
+            pltpu.VMEM((2, f, total_y), BF16),
+            pltpu.VMEM((2, zn * comps, total_y), F32),
+            pltpu.SemaphoreType.DMA((16,)),
+        ],
+        flops=solve_flops + sample_flops,
+        far_out=range(8),
+    )
+    rows_in = exchange(sent, ("pz", "tr"))
     zlo, zhi = shift((zhi, zlo), ("px", "tr"))
     xlo, xhi = shift((xhi, xlo), "pz")
-
-    def sample(packed):
-        sent = call(
-            sample_kernel,
-            shaped((members, f, peers * slots), BF16),
-            (packed, ids),
-            scratch=[pltpu.VMEM((peers, f, members * slots), F32)],
-            flops=2 * peers * 256 * 256 * members * slots,
-        )
-        return exchange(sent, ("pz", "tr"))
-
-    rows_in = sample(packed)
-    packed = call(
-        second_solve_kernel,
-        shaped((peers, 2 * f, lanes), BF16),
-        (u, w, zlo, zhi, xlo, xhi, inverse),
-        scratch=[pltpu.VMEM((zn * f, total_y), BF16), pltpu.VMEM((zn * f, total_y), F32)],
-        flops=solve_flops,
-    )
-    rows_target = sample(packed)
+    packed, sent = call(
+        second_kernel,
+        (shaped((peers, 2 * f, lanes), BF16), message),
+        (u, w, ids, zlo, zhi, xlo, xhi, inverse),
+        scratch=[
+            pltpu.VMEM((zn * f, total_y), BF16),
+            pltpu.VMEM((zn * f, total_y), F32),
+            pltpu.VMEM(w.shape, BF16),
+            pltpu.VMEM(ids.shape, jnp.int32),
+        ]
+        + sampling
+        + [pltpu.SemaphoreType.DMA((16,))],
+        flops=solve_flops + sample_flops,
+        far_in=(0, 1, 2),
+        far_out=(0, 1),
+    )
+    rows_target = exchange(sent, ("pz", "tr"))
+
     member_in = weight_in[0]
     member_out = weight_out[0]
     width, hid = member_in.shape
@@ -464,7 +569,15 @@
             shaped((width, batch), F32),
         ),
         (rows_in, member_in.T, member_out.T),
+        scratch=[
+            pltpu.VMEM((width, batch), BF16),
+            pltpu.VMEM((hid, batch), BF16),
+            pltpu.VMEM((hid, batch), BF16),
+            pltpu.VMEM((width, batch), F32),
+            pltpu.SemaphoreType.DMA((4,)),
+        ],
         flops=2 * matmul_flops,
+        far_out=range(4),
     )
     position = lax.axis_index("px")
     place = jnp.stack([position % 2, position // 2]).astype(jnp.int32)
@@ -476,7 +589,13 @@
         delta_out,
         (shaped((width, batch), BF16), shaped((hid // 2, width), BF16)),
         (place, rows_target, predicted, hidden),
+        scratch=[
+            pltpu.VMEM((width, batch), F32),
+            pltpu.VMEM((hid, batch), BF16),
+            pltpu.SemaphoreType.DMA((4,)),
+        ],
         flops=matmul_flops // 2,
+        far_in=(2, 3),
     )
     got_out = swap_cores(away_out)
     din, away_in = call(
@@ -486,8 +605,6 @@
         flops=matmul_flops * 3 // 2,
     )
     got_in = swap_cores(away_in)
-    packed, away_in = lax.optimization_barrier((packed, away_in))
-    planes = exchange(packed, "pz")
     rows = hid // spots
     own, plus, minus, top, bottom = call(
         keep_kernel,
@@ -501,7 +618,9 @@
         (place, hidden, d, x, din, got_out, got_in),
         flops=matmul_flops,
     )
+    packed, top = lax.optimization_barrier((packed, top))
     from_before, from_after = shift_chips(top, bottom)
+    planes = exchange(packed, "pz")
     plus, minus = call(
         relay_kernel,
         (shaped(plus.shape, BF16), shaped(minus.shape, BF16)),

time: 175 us -> 177 us (1.011)
  blocking collectives: 0 us -> 28.6 us
  starting transfers between devices: 63.7 us -> 39.6 us
  local copies, waits for them, and re-layouts: 25.5 us -> 27.6 us
  Pallas kernels: 25.6 us -> 23.8 us
    all_to_all x0 -> x1, blocking collectives: none -> 28.6 us  [exchange(): return lax.all_to_all(array, axis, split_axis=0, concat_axis=0, tiled=True)]
    all_to_all x4 -> x3, starting transfers between devices: 30.9 us -> 19.6 us  [exchange(): return lax.all_to_all(array, axis, split_axis=0, concat_axis=0, tiled=True)]
    ppermute x4, starting transfers between devices: 15 us -> 6.55 us  [shift_chips(): return (lax.ppermute(forward, 'px', up), lax.ppermute(backward, 'px', down))]
    all_to_all x4 -> x3, waiting for transfers between devices: 21.1 us -> 14.1 us  [exchange(): return lax.all_to_all(array, axis, split_axis=0, concat_axis=0, tiled=True)]
    ppermute x8 -> x6, starting transfers between devices: 17.3 us -> 12.9 us  [shift(): return (lax.ppermute(last, axis, up), lax.ppermute(first, axis, down))]
    ppermute x2, waiting for transfers between devices: 0.01 us -> 2.9 us  [swap_cores(): return lax.ppermute(array, 'px', [(i, i ^ 1) for i in range(size)])]
    convert_element_type x1, other arithmetic: 2.51 us -> 0.32 us  [per_device(): inverse = implicit_inverse.astype(BF16)]
    ppermute x8 -> x6, waiting for transfers between devices: 23 us -> 25 us  [shift(): return (lax.ppermute(last, axis, up), lax.ppermute(first, axis, down))]
  transfers between devices with their start and end apart: 18 -> 15, of which waited for: 8 -> 10; matrix products, arithmetic and copies ran while one was open for 6% -> 3% of each run, Pallas kernels for 8% -> 6%
where the time goes in v3:
time: 177 us; the launch traced here: 176 us
  waiting for transfers between devices  54.2 us (31%)
  starting transfers between devices  39.6 us (22%)
  blocking collectives  28.6 us (16%)
  local copies, waits for them, and re-layouts  27.6 us (16%)
  Pallas kernels  23.8 us (13%)
  other arithmetic  1.79 us (1%)
    all_to_all x1, blocking collectives, exchange(): return lax.all_to_all(array, axis, split_axis=0, concat_axis=0, tiled=True)  28.6 us
    ppermute x6, waiting for transfers between devices, shift(): return (lax.ppermute(last, axis, up), lax.ppermute(first, axis, down))  25 us
    unnamed x49, local copies, waits for them, and re-layouts  24.9 us
    pallas_call x11, Pallas kernels, call(): pl.pallas_call(kernel, out_shape=out_shape, in_specs=[spec(k, far_in, x.n...  23.8 us
    all_to_all x3, starting transfers between devices, exchange(): return lax.all_to_all(array, axis, split_axis=0, concat_axis=0, tiled=True)  19.6 us
    all_to_all x3, waiting for transfers between devices, exchange(): return lax.all_to_all(array, axis, split_axis=0, concat_axis=0, tiled=True)  14.1 us
    ppermute x6, starting transfers between devices, shift(): return (lax.ppermute(last, axis, up), lax.ppermute(first, axis, down))  12.9 us
    ppermute x4, waiting for transfers between devices, shift_chips(): return (lax.ppermute(forward, 'px', up), lax.ppermute(backward, 'px', down))  12.2 us
  transfers between devices with their start and end apart: 15, of which 10 were waited for; matrix products, arithmetic and copies ran while one was open for 3% of the time, Pallas kernels for 6%

profile of v3, /device:TPU:2, one launch (start us, length us, event | category | flops | bytes accessed | tf_op | source)
XLA Modules:
  0.0 176.4 jit_solution(5720416151936311696)
XLA Ops:
  1.2 1.3 reduce.3
  2.6 0.8 reshape.30
  3.6 1.0 copy.29
  4.6 1.4 copy.28
  6.3 28.6 %all_to_all.20.got = bf16[16,152,128]{2,1,0:T(8,128)(2,1)S(1)} all-to-all(bf16[16,152,128]{2,1,0:T(8,128)(2,1)S(1)} %shard_map.94), channel_id=1, replica_groups=mesh['px'=8,'pz'=16,'tr'=2] {'pz'}, dimensions={0} | all-to-all | bytes 1245184 | tf_op jit(solution)/shard_map/all_to_all | solution.py:468
  35.1 2.2 %collective-permute-start = (bf16[48,1024]{1,0:T(8,128)(2,1)S(1)}, bf16[48,1024]{1,0:T(8,128)(2,1)S(1)}, u32[]{:S(2)}, u32[]{:S(2)}) collective-permute-start(bf16[48,1024]{1,0:T(8,128)(2,1)S(1)} %get-tuple-element.43), channel_id=1, source_target_pairs={{0,1},{1,32},{32,33},{33,64},{64,65},{65,96},{96,97},{97,128},{128... | collective-permute-start | bytes 294920 | tf_op jit(solution)/shard_map/ppermute | solution.py:73
  37.4 3.2 %collective-permute-start.1 = (bf16[48,1024]{1,0:T(8,128)(2,1)S(1)}, bf16[48,1024]{1,0:T(8,128)(2,1)S(1)}, u32[]{:S(2)}, u32[]{:S(2)}) collective-permute-start(bf16[48,1024]{1,0:T(8,128)(2,1)S(1)} %get-tuple-element.44), channel_id=1, source_target_pairs={{1,0},{32,1},{33,32},{64,33},{65,64},{96,65},{97,96},{128,97},{129... | collective-permute-start | bytes 294920 | tf_op jit(solution)/shard_map/ppermute | solution.py:73
  40.9 2.5 %collective-permute-done.zlo = bf16[48,1024]{1,0:T(8,128)(2,1)S(1)} collective-permute-done((bf16[48,1024]{1,0:T(8,128)(2,1)S(1)}, bf16[48,1024]{1,0:T(8,128)(2,1)S(1)}, u32[]{:S(2)}, u32[]{:S(2)}) %collective-permute-start) | collective-permute-done | bytes 98336 | tf_op jit(solution)/shard_map/ppermute | solution.py:73
  43.9 4.4 %shard_map.96 = (f32[192,1024]{1,0:T(8,128)S(1)}, bf16[64,1024]{1,0:T(8,128)(2,1)S(1)}, s32[16,8,128]{2,1,0:T(8,128)S(1)}, bf16[48,1024]{1,0:T(8,128)(2,1)S(1)},...) custom-call(bf16[192,1024]{1,0:T(8,128)(2,1)S(1)} %get-tuple-element, ...), custom_call_target="tpu_custom_call" | custom-call | flops 704643072 | bytes 5439488 | tf_op jit(solution)/shard_map/pallas_call | solution.py:28
  48.3 1.0 copy-done.11
  49.3 0.9 copy-done.12
  52.1 5.2 %all-to-all-start.1 = ((bf16[32,48,384]{2,1,0:T(8,128)(2,1)}), bf16[32,48,384]{2,1,0:T(8,128)(2,1)S(1)}, u32[]{:S(2)}, u32[]{:S(2)}) async-start(bf16[32,48,384]{2,1,0:T(8,128)(2,1)} %copy-done.11), calls=%async_computation.1 | async-start | bytes 2359296 | tf_op jit(solution)/shard_map/all_to_all | solution.py:468
  57.4 2.2 %collective-permute-start.2 = (bf16[48,1024]{1,0:T(8,128)(2,1)}, bf16[48,1024]{1,0:T(8,128)(2,1)S(1)}, u32[]{:S(2)}, u32[]{:S(2)}) collective-permute-start(bf16[48,1024]{1,0:T(8,128)(2,1)} %copy-done.17), channel_id=1, source_target_pairs={{0,1},{1,32},{32,33},{33,64},{64,65},{65,96},{96,97},{97,128},{128... | collective-permute-start | bytes 294920 | tf_op jit(solution)/shard_map/ppermute | solution.py:73
  59.6 3.3 %collective-permute-start.3 = (bf16[48,1024]{1,0:T(8,128)(2,1)}, bf16[48,1024]{1,0:T(8,128)(2,1)S(1)}, u32[]{:S(2)}, u32[]{:S(2)}) collective-permute-start(bf16[48,1024]{1,0:T(8,128)(2,1)} %copy-done.16), channel_id=1, source_target_pairs={{1,0},{32,1},{33,32},{64,33},{65,64},{96,65},{97,96},{128,97},{129... | collective-permute-start | bytes 294920 | tf_op jit(solution)/shard_map/ppermute | solution.py:73
  62.8 1.5 collective-permute-start.4
  64.9 19.5 %collective-permute-done.4.xlo = f32[12,1024]{1,0:T(8,128)S(1)} collective-permute-done((f32[12,1024]{1,0:T(8,128)}, f32[12,1024]{1,0:T(8,128)S(1)}, u32[]{:S(2)}, u32[]{:S(2)}) %collective-permute-start.4) | collective-permute-done | bytes 49184 | tf_op jit(solution)/shard_map/ppermute | solution.py:73
  84.3 2.5 %collective-permute-done.5.xhi = f32[12,1024]{1,0:T(8,128)S(1)} collective-permute-done((f32[12,1024]{1,0:T(8,128)S(1)}, f32[12,1024]{1,0:T(8,128)S(1)}, u32[]{:S(2)}, u32[]{:S(2)}) %collective-permute-start.5) | collective-permute-done | bytes 49184 | tf_op jit(solution)/shard_map/ppermute | solution.py:73
  86.9 1.1 copy-done.13
  88.0 4.8 %shard_map.97 = (bf16[16,96,128]{2,1,0:T(8,128)(2,1)}, bf16[32,48,384]{2,1,0:T(8,128)(2,1)S(1)}) custom-call(f32[192,1024]{1,0:T(8,128)S(1)} %copy-done.13, bf16[64,1024]{1,0:T(8,128)(2,1)S(1)} %get-tuple-element.47.w_far, s32[16,8,128]{2,1,0:T(8,128)S(1)} %get-tuple-element.48.ids_far, bf16[48,1024]{1,0:T(8,128)(2,1)S(1)} %collective-permute-done.2.zlo, ...), custom_call_target="tpu_custom_call" | custom-call | flops 704643072 | bytes 4947968 | tf_op jit(solution)/shard_map/pallas_call | solution.py:28
  92.8 1.1 copy-done.10
  93.9 1.0 copy-done.8
  94.9 9.5 %all-to-all-start.2 = ((bf16[32,48,384]{2,1,0:T(8,128)(2,1)}), bf16[32,48,384]{2,1,0:T(8,128)(2,1)S(1)}, u32[]{:S(2)}, u32[]{:S(2)}) async-start(bf16[32,48,384]{2,1,0:T(8,128)(2,1)} %copy-done.10), calls=%async_computation.2 | async-start | bytes 2359296 | tf_op jit(solution)/shard_map/all_to_all | solution.py:468
  104.4 2.7 %copy.19 = bf16[1,768,1024]{1,2,0:T(8,128)(2,1)} copy(bf16[1,768,1024]{2,1,0:T(8,128)(2,1)} %param.12) | data formatting | bytes 3145728 | tf_op args[5]
  107.2 1.6 copy.20.w_out
  108.8 1.4 copy-done.4
  110.3 1.4 copy-done.5
  111.7 1.3 copy-done.9
  112.9 4.8 %shard_map.98 = (bf16[768,768]{1,0:T(8,128)(2,1)S(1)}, bf16[1024,768]{1,0:T(8,128)(2,1)S(1)}, bf16[1024,768]{1,0:T(8,128)(2,1)S(1)}, f32[768,768]{1,0:T(8,128)S(1)}) custom-call(bf16[32,48,384]{2,1,0:T(8,128)(2,1)S(1)} %copy-done.9, bf16[1024,768]{1,0:T(8,128)(2,1)S(1)} %bitcast.28, bf16[768,1024]{1,0:T(8,128)(2,1)S(1)} %copy-done.5), custom_call_target="tpu_custom_call" | custom-call | flops 2415919104 | bytes 11010048 | tf_op jit(solution)/shard_map/pallas_call | solution.py:28
  117.8 1.4 copy-done
  119.2 1.0 copy-done.6
  120.2 1.1 copy-done.19
  121.4 14.1 %all-to-all-done.2.refs_1_ = bf16[32,48,384]{2,1,0:T(8,128)(2,1)S(1)} async-done(((bf16[32,48,384]{2,1,0:T(8,128)(2,1)}), bf16[32,48,384]{2,1,0:T(8,128)(2,1)S(1)}, u32[]{:S(2)}, u32[]{:S(2)}) %all-to-all-start.2) | async-done | bytes 1179680 | tf_op jit(solution)/shard_map/all_to_all | solution.py:468
  135.5 1.7 copy-done.1
  137.2 2.1 %shard_map.99 = (bf16[768,768]{1,0:T(8,128)(2,1)S(1)}, bf16[512,768]{1,0:T(8,128)(2,1)S(1)}) custom-call(s32[2]{0:T(128)S(1)} %pad_add_fusion.refs_0_.place, bf16[32,48,384]{2,1,0:T(8,128)(2,1)S(1)} %all-to-all-done.2.refs_1_, f32[768,768]{1,0:T(8,128)S(1)} %copy-done.1, bf16[1024,768]{1,0:T(8,128)(2,1)S(1)} %get-tuple-element.55.refs_3_.hidden), custom_call_target="tpu_custom_call" | custom-call | flops 603979776 | bytes 7077896 | tf_op jit(solution)/shard_map/pallas_call | solution.py:28
  139.4 3.6 %shard_map.100 = (bf16[1024,768]{1,0:T(8,128)(2,1)S(1)}, bf16[384,1024]{1,0:T(8,128)(2,1)S(1)}) custom-call(s32[2]{0:T(128)S(1)} %pad_add_fusion.refs_0_.place, bf16[768,768]{1,0:T(8,128)(2,1)S(1)} %get-tuple-element.58.d, bf16[1024,768]{1,0:T(8,128)(2,1)S(1)} %copy-done.20, bf16[1024,768]{1,0:T(8,128)(2,1)S(1)} %bitcast.27, bf16[768,768]{1,0:T(8,128)(2,1)S(1)} %copy-done.7), custom_call_target="tpu_custom_call" | custom-call | flops 1811939328 | bytes 7864328 | tf_op jit(solution)/shard_map/pallas_call | solution.py:28
  143.7 1.8 %collective-permute-done.7.got_in = bf16[384,1024]{1,0:T(8,128)(2,1)S(1)} collective-permute-done((bf16[384,1024]{1,0:T(8,128)(2,1)S(1)}, bf16[384,1024]{1,0:T(8,128)(2,1)S(1)}, u32[]{:S(2)}, u32[]{:S(2)}) %collective-permute-start.7) | collective-permute-done | bytes 786464 | tf_op jit(solution)/shard_map/ppermute | solution.py:473
  145.4 1.1 collective-permute-done.6.got_out
  146.6 2.3 %shard_map.101 = (f32[2,128,768]{2,1,0:T(8,128)S(1)}, bf16[2,128,768]{2,1,0:T(8,128)(2,1)S(1)}, bf16[2,128,768]{2,1,0:T(8,128)(2,1)S(1)}, bf16[2,64,768]{2,1,0:T(8,128)(2,1)S(1)}, bf16[2,64,768]{2,1,0:T(8,128)(2,1)S(1)}) custom-call(s32[2]{0:T(128)S(1)} %pad_add_fusion.refs_0_.place, bf16[1024,768]{1,0:T(8,128)(2,1)S(1)} %get-tuple-element.55.refs_3_.hidden, ...), custom_call_target="tpu_custom_call" | custom-call | flops 1207959552 | bytes 9043976 | tf_op jit(solution)/shard_map/pallas_call | solution.py:28
  149.6 0.7 copy-done.15
  150.2 4.8 %all-to-all-start.3 = ((bf16[16,96,128]{2,1,0:T(8,128)(2,1)}), bf16[16,96,128]{2,1,0:T(8,128)(2,1)S(1)}, u32[]{:S(2)}, u32[]{:S(2)}) async-start(bf16[16,96,128]{2,1,0:T(8,128)(2,1)} %get-tuple-element.65), calls=%async_computation.3 | async-start | bytes 786432 | tf_op jit(solution)/shard_map/all_to_all | solution.py:468
  155.1 1.6 collective-permute-start.8
  156.6 1.7 collective-permute-start.9
  158.3 4.6 %collective-permute-done.8.from_before = bf16[2,64,768]{2,1,0:T(8,128)(2,1)S(1)} collective-permute-done((bf16[2,64,768]{2,1,0:T(8,128)(2,1)}, bf16[2,64,768]{2,1,0:T(8,128)(2,1)S(1)}, u32[]{:S(2)}, u32[]{:S(2)}) %collective-permute-start.8) | collective-permute-done | bytes 196640 | tf_op jit(solution)/shard_map/ppermute | solution.py:480
  163.0 1.3 collective-permute-start.10
  164.4 2.0 %collective-permute-start.11 = (bf16[2,128,768]{2,1,0:T(8,128)(2,1)S(1)}, bf16[2,128,768]{2,1,0:T(8,128)(2,1)S(1)}, u32[]{:S(2)}, u32[]{:S(2)}) collective-permute-start(bf16[2,128,768]{2,1,0:T(8,128)(2,1)S(1)} %get-tuple-element.72), channel_id=1, source_target_pairs={{64,0},{96,32},{128,64},{160,96},{192,128},{224,160},{0,192},{32,2... | collective-permute-start | bytes 1179656 | tf_op jit(solution)/shard_map/ppermute | solution.py:480
  166.4 7.6 %collective-permute-done.10.from_before = bf16[2,128,768]{2,1,0:T(8,128)(2,1)S(1)} collective-permute-done((bf16[2,128,768]{2,1,0:T(8,128)(2,1)S(1)}, bf16[2,128,768]{2,1,0:T(8,128)(2,1)S(1)}, u32[]{:S(2)}, u32[]{:S(2)}) %collective-permute-start.10) | collective-permute-done | bytes 393248 | tf_op jit(solution)/shard_map/ppermute | solution.py:480
  173.9 0.9 shard_map.104
  175.1 1.4 copy.21
  (54 shorter events, 6.5 us)
Async XLA Ops:
  4.6 36.0 %copy-start.21 = (f32[1024,1024]{1,0:T(8,128)S(1)}, f32[1024,1024]{1,0:T(8,128)}, u32[]{:S(2)}) copy-start(f32[1024,1024]{1,0:T(8,128)} %param.9) | copy-start | bytes 12582916
  35.1 8.3 %collective-permute-start = (bf16[48,1024]{1,0:T(8,128)(2,1)S(1)}, bf16[48,1024]{1,0:T(8,128)(2,1)S(1)}, u32[]{:S(2)}, u32[]{:S(2)}) collective-permute-start(bf16[48,1024]{1,0:T(8,128)(2,1)S(1)} %get-tuple-element.43), channel_id=1, source_target_pairs={{0,1},{1,32},{32,33},{33,64},{64,65},{65,96},{96,97},{97,128},{128... | collective-permute-start | bytes 294920 | tf_op jit(solution)/shard_map/ppermute | solution.py:73
  37.4 6.5 %collective-permute-start.1 = (bf16[48,1024]{1,0:T(8,128)(2,1)S(1)}, bf16[48,1024]{1,0:T(8,128)(2,1)S(1)}, u32[]{:S(2)}, u32[]{:S(2)}) collective-permute-start(bf16[48,1024]{1,0:T(8,128)(2,1)S(1)} %get-tuple-element.44), channel_id=1, source_target_pairs={{1,0},{32,1},{33,32},{64,33},{65,64},{96,65},{97,96},{128,97},{129... | collective-permute-start | bytes 294920 | tf_op jit(solution)/shard_map/ppermute | solution.py:73
  48.3 1.0 copy-start.11
  49.3 0.9 copy-start.12
  50.2 0.6 copy-start.16
  50.9 0.6 copy-start.17
  51.5 0.6 copy-start.18
  52.1 41.7 %all-to-all-start.1 = ((bf16[32,48,384]{2,1,0:T(8,128)(2,1)}), bf16[32,48,384]{2,1,0:T(8,128)(2,1)S(1)}, u32[]{:S(2)}, u32[]{:S(2)}) async-start(bf16[32,48,384]{2,1,0:T(8,128)(2,1)} %copy-done.11), calls=%async_computation.1 | async-start | bytes 2359296 | tf_op jit(solution)/shard_map/all_to_all | solution.py:468
  57.4 29.5 %collective-permute-start.2 = (bf16[48,1024]{1,0:T(8,128)(2,1)}, bf16[48,1024]{1,0:T(8,128)(2,1)S(1)}, u32[]{:S(2)}, u32[]{:S(2)}) collective-permute-start(bf16[48,1024]{1,0:T(8,128)(2,1)} %copy-done.17), channel_id=1, source_target_pairs={{0,1},{1,32},{32,33},{33,64},{64,65},{65,96},{96,97},{97,128},{128... | collective-permute-start | bytes 294920 | tf_op jit(solution)/shard_map/ppermute | solution.py:73
  59.6 27.3 %collective-permute-start.3 = (bf16[48,1024]{1,0:T(8,128)(2,1)}, bf16[48,1024]{1,0:T(8,128)(2,1)S(1)}, u32[]{:S(2)}, u32[]{:S(2)}) collective-permute-start(bf16[48,1024]{1,0:T(8,128)(2,1)} %copy-done.16), channel_id=1, source_target_pairs={{1,0},{32,1},{33,32},{64,33},{65,64},{96,65},{97,96},{128,97},{129... | collective-permute-start | bytes 294920 | tf_op jit(solution)/shard_map/ppermute | solution.py:73
  62.8 21.5 %collective-permute-start.4 = (f32[12,1024]{1,0:T(8,128)}, f32[12,1024]{1,0:T(8,128)S(1)}, u32[]{:S(2)}, u32[]{:S(2)}) collective-permute-start(f32[12,1024]{1,0:T(8,128)} %copy-done.18), channel_id=1, source_target_pairs={{0,2},{2,4},{4,6},{6,8},{8,10},{10,12},{12,14},{14,16},{16,18},{18... | collective-permute-start | bytes 147464 | tf_op jit(solution)/shard_map/ppermute | solution.py:73
  64.3 22.5 %collective-permute-start.5 = (f32[12,1024]{1,0:T(8,128)S(1)}, f32[12,1024]{1,0:T(8,128)S(1)}, u32[]{:S(2)}, u32[]{:S(2)}) collective-permute-start(f32[12,1024]{1,0:T(8,128)S(1)} %get-tuple-element.52), channel_id=1, source_target_pairs={{2,0},{4,2},{6,4},{8,6},{10,8},{12,10},{14,12},{16,14},{18,16},{20... | collective-permute-start | bytes 147464 | tf_op jit(solution)/shard_map/ppermute | solution.py:73
  86.9 1.1 copy-start.13
  92.8 1.1 copy-start.10
  93.9 1.0 copy-start.8
  94.9 40.6 %all-to-all-start.2 = ((bf16[32,48,384]{2,1,0:T(8,128)(2,1)}), bf16[32,48,384]{2,1,0:T(8,128)(2,1)S(1)}, u32[]{:S(2)}, u32[]{:S(2)}) async-start(bf16[32,48,384]{2,1,0:T(8,128)(2,1)} %copy-done.10), calls=%async_computation.2 | async-start | bytes 2359296 | tf_op jit(solution)/shard_map/all_to_all | solution.py:468
  104.4 2.7 %copy-start.2 = (bf16[1,1024,768]{2,1,0:T(8,128)(2,1)S(1)}, bf16[1,1024,768]{2,1,0:T(8,128)(2,1)}, u32[]{:S(2)}) copy-start(bf16[1,1024,768]{2,1,0:T(8,128)(2,1)} %param.13) | copy-start | bytes 4718596
  108.8 1.4 copy-start.4
  110.3 1.4 copy-start.5
  111.7 1.3 copy-start.9
  117.8 1.4 copy-start
  119.2 1.0 copy-start.6
  120.2 1.1 copy-start.19
  135.5 1.7 copy-start.1
  137.2 2.1 %copy-start.3 = (bf16[1,1024,768]{2,1,0:T(8,128)(2,1)S(1)}, bf16[1,1024,768]{2,1,0:T(8,128)(2,1)}, u32[]{:S(2)}) copy-start(bf16[1,1024,768]{2,1,0:T(8,128)(2,1)} %param.13) | copy-start | bytes 4718596
  137.2 2.1 %copy-start.7 = (bf16[768,768]{1,0:T(8,128)(2,1)S(1)}, bf16[768,768]{1,0:T(8,128)(2,1)}, u32[]{:S(2)}) copy-start(bf16[768,768]{1,0:T(8,128)(2,1)} %copy-done.6) | copy-start | bytes 3538948
  137.2 2.2 %copy-start.20 = (bf16[1024,768]{1,0:T(8,128)(2,1)S(1)}, bf16[1024,768]{1,0:T(8,128)(2,1)}, u32[]{:S(2)}) copy-start(bf16[1024,768]{1,0:T(8,128)(2,1)} %copy-done.19) | copy-start | bytes 4718596
  143.1 2.4 %collective-permute-start.7 = (bf16[384,1024]{1,0:T(8,128)(2,1)S(1)}, bf16[384,1024]{1,0:T(8,128)(2,1)S(1)}, u32[]{:S(2)}, u32[]{:S(2)}) collective-permute-start(bf16[384,1024]{1,0:T(8,128)(2,1)S(1)} %get-tuple-element.63), channel_id=1, source_target_pairs={{0,32},{32,0},{64,96},{96,64},{128,160},{160,128},{192,224},{224,1... | collective-permute-start | bytes 2359304 | tf_op jit(solution)/shard_map/ppermute | solution.py:473
  143.2 3.4 %collective-permute-start.6 = (bf16[512,768]{1,0:T(8,128)(2,1)S(1)}, bf16[512,768]{1,0:T(8,128)(2,1)S(1)}, u32[]{:S(2)}, u32[]{:S(2)}) collective-permute-start(bf16[512,768]{1,0:T(8,128)(2,1)S(1)} %get-tuple-element.62), channel_id=1, source_target_pairs={{0,32},{32,0},{64,96},{96,64},{128,160},{160,128},{192,224},{224,1... | collective-permute-start | bytes 2359304 | tf_op jit(solution)/shard_map/ppermute | solution.py:473
  148.9 0.7 copy-start.14
  149.6 0.7 copy-start.15
  150.2 24.6 %all-to-all-start.3 = ((bf16[16,96,128]{2,1,0:T(8,128)(2,1)}), bf16[16,96,128]{2,1,0:T(8,128)(2,1)S(1)}, u32[]{:S(2)}, u32[]{:S(2)}) async-start(bf16[16,96,128]{2,1,0:T(8,128)(2,1)} %get-tuple-element.65), calls=%async_computation.3 | async-start | bytes 786432 | tf_op jit(solution)/shard_map/all_to_all | solution.py:468
  155.1 7.8 %collective-permute-start.8 = (bf16[2,64,768]{2,1,0:T(8,128)(2,1)}, bf16[2,64,768]{2,1,0:T(8,128)(2,1)S(1)}, u32[]{:S(2)}, u32[]{:S(2)}) collective-permute-start(bf16[2,64,768]{2,1,0:T(8,128)(2,1)} %copy-done.15), channel_id=1, source_target_pairs={{0,64},{32,96},{64,128},{96,160},{128,192},{160,224},{192,0},{224,... | collective-permute-start | bytes 589832 | tf_op jit(solution)/shard_map/ppermute | solution.py:480
  156.6 6.3 %collective-permute-start.9 = (bf16[2,64,768]{2,1,0:T(8,128)(2,1)}, bf16[2,64,768]{2,1,0:T(8,128)(2,1)S(1)}, u32[]{:S(2)}, u32[]{:S(2)}) collective-permute-start(bf16[2,64,768]{2,1,0:T(8,128)(2,1)} %copy-done.14), channel_id=1, source_target_pairs={{64,0},{96,32},{128,64},{160,96},{192,128},{224,160},{0,192},{32,2... | collective-permute-start | bytes 589832 | tf_op jit(solution)/shard_map/ppermute | solution.py:480
  163.0 10.9 %collective-permute-start.10 = (bf16[2,128,768]{2,1,0:T(8,128)(2,1)S(1)}, bf16[2,128,768]{2,1,0:T(8,128)(2,1)S(1)}, u32[]{:S(2)}, u32[]{:S(2)}) collective-permute-start(bf16[2,128,768]{2,1,0:T(8,128)(2,1)S(1)} %get-tuple-element.71), channel_id=1, source_target_pairs={{0,64},{32,96},{64,128},{96,160},{128,192},{160,224},{192,0},{224,... | collective-permute-start | bytes 1179656 | tf_op jit(solution)/shard_map/ppermute | solution.py:480
  164.4 9.6 %collective-permute-start.11 = (bf16[2,128,768]{2,1,0:T(8,128)(2,1)S(1)}, bf16[2,128,768]{2,1,0:T(8,128)(2,1)S(1)}, u32[]{:S(2)}, u32[]{:S(2)}) collective-permute-start(bf16[2,128,768]{2,1,0:T(8,128)(2,1)S(1)} %get-tuple-element.72), channel_id=1, source_target_pairs={{64,0},{96,32},{128,64},{160,96},{192,128},{224,160},{0,192},{32,2... | collective-permute-start | bytes 1179656 | tf_op jit(solution)/shard_map/ppermute | solution.py:480

commit v4 on v3

--- a/solution.py
+++ b/solution.py
@@ -25,9 +25,16 @@
         return pl.BlockSpec(memory_space=space)
 
     out_specs = tuple(spec(k, far_out) for k in range(len(outs)))
+    args = [
+        pltpu.with_memory_space_constraint(x, pltpu.HBM) if k in far_in else x
+        for k, x in enumerate(args)
+    ]
+    pinned = tuple(
+        pltpu.HBM(x.shape, x.dtype) if k in far_out else x for k, x in enumerate(outs)
+    )
     return pl.pallas_call(
         kernel,
-        out_shape=out_shape,
+        out_shape=pinned if isinstance(out_shape, tuple) else pinned[0],
         in_specs=[spec(k, far_in, x.ndim == 1) for k, x in enumerate(args)],
         out_specs=out_specs if isinstance(out_shape, tuple) else out_specs[0],
         scratch_shapes=list(scratch),
@@ -74,12 +81,14 @@
 
 
 HALO_ROWS = 24
-
-
-def columns_kernel(v, w, ids, out, edge):
+GROUP = 8
+
+
+def columns_kernel(v, w, index, counts, out, edge):
     comps, zn, yn, xn = v.shape
     peers = out.shape[0]
     xl = xn // peers
+    lanes_of = out.shape[2]
     half = (comps + 1) * xl
     for zh in range(zn // 2):
         for c in range(comps + 1):
@@ -98,7 +107,13 @@
                 edge[r : r + 1] = turned[before : before + 1]
                 edge[r + zn // 2 * comps : r + zn // 2 * comps + 1] = turned[after : after + 1]
     start = zn // 2 * half
-    numbers = ids[...].astype(F32)
+    slots, members = index.shape
+    slot = lax.broadcasted_iota(jnp.int32, (slots, members), 0)
+    live = jnp.where(slot < counts[...], index[...], -1).astype(F32)
+    sides = lanes_of // members
+    rows = slots // sides
+    numbers = jnp.concatenate([live[k * rows : (k + 1) * rows] for k in range(sides)], axis=1)
+    numbers = jnp.concatenate([numbers, jnp.zeros((8 - rows, lanes_of), F32)], axis=0)
     for q in range(peers):
         edge[(q + 1) * HALO_ROWS - 8 : (q + 1) * HALO_ROWS] = numbers
         out[q, start : start + HALO_ROWS, :] = edge[
@@ -129,7 +144,24 @@
 
 def spread_kernel(got, v, w, xlo, xhi, zlo, zhi, ids):
     peers, rows, lanes = got.shape
-    ids[...] = got[:, rows - 8 :, :].astype(F32).astype(jnp.int32)
+    table = got[:, rows - 8 :, :].astype(F32).reshape(peers * 8, lanes).astype(BF16)
+    members = 32
+    per = lanes // GROUP
+    source = lax.broadcasted_iota(jnp.int32, (lanes, lanes), 0)
+    lane = lax.broadcasted_iota(jnp.int32, (lanes, lanes), 1)
+    late = lax.broadcasted_iota(jnp.int32, (1, lanes), 1) % GROUP >= GROUP // 2
+    halves = members // per
+    for mh in range(halves):
+        wanted = (lane % (GROUP // 2)) * members + mh * per + lane // GROUP
+        moved = jnp.dot(
+            table, jnp.where(source == wanted, 1.0, 0.0).astype(BF16), preferred_element_type=F32
+        )
+        for q in range(peers):
+            for kg in range(3):
+                r = q * 8 + 2 * kg
+                line = jnp.where(late, moved[r + 1 : r + 2], moved[r : r + 1])
+                at = kg * halves + mh
+                ids[q, at : at + 1, :] = line.astype(jnp.int32)
     yn = lanes // 2
     zn = 4
     half = (rows - HALO_ROWS) // 2
@@ -187,63 +219,70 @@
 
 
 def first_kernel(
-    v, w, xlo, xhi, zlo, zhi, ids, a,
-    u_far, w_far, ids_far, zlo_far, zhi_far, xlo_far, xhi_far, sent_far,
-    e, u, packed, picked, sent, z_edge, x_edge, sems,
+    v, w, xlo, xhi, zlo, zhi, ids, a_far,
+    u_far, w_far, ids_far, packed, z_first, z_last, x_first, x_last,
+    e, u, a, sems,
 ):
     copies = Copies(sems)
+    a_copy = copies.start(a_far, a)
     copies.start(w, w_far)
     copies.start(ids, ids_far)
     x_before, x_after = xlo[...], xhi[...]
     zn = 4
     for z in range(zn):
         explicit_plane(z, v, w, zlo, zhi, x_before, x_after, e)
+    copies.wait(a_copy)
     u[...] = solve(e, a)
     copies.start(u, u_far)
     f = zlo.shape[0]
-    z_edge[0] = u[0:f].astype(BF16)
-    z_edge[1] = u[(zn - 1) * f : zn * f].astype(BF16)
+    z_first[...] = u[0:f].astype(BF16)
+    z_last[...] = u[(zn - 1) * f : zn * f].astype(BF16)
     xl = w.shape[0] // zn
     groups = u.shape[0] // xl
     for r in range(groups):
-        x_edge[0, r : r + 1] = u[r * xl : r * xl + 1]
-        x_edge[1, r : r + 1] = u[(r + 1) * xl - 1 : (r + 1) * xl]
-    for k, (edge, far) in enumerate(
-        ((z_edge, zlo_far), (z_edge, zhi_far), (x_edge, xlo_far), (x_edge, xhi_far))
-    ):
-        copies.start(edge.at[k % 2], far)
+        x_first[r : r + 1] = u[r * xl : r * xl + 1]
+        x_last[r : r + 1] = u[(r + 1) * xl - 1 : (r + 1) * xl]
     pack_columns(u, packed, zn)
+    copies.finish()
+
+
+def sample_kernel(packed, ids, sent_far, picked, sent, sems):
+    copies = Copies(sems)
     sample(packed, ids, picked, sent, lambda part: copies.start(sent.at[part], sent_far.at[part]))
     copies.finish()
 
 
 def second_kernel(
-    u_far, w_far, ids_far, zlo, zhi, xlo, xhi, a, packed_far, sent_far,
-    e, u, w, ids, packed, picked, sent, sems,
+    u_far, w_far, ids_far, zlo_far, zhi_far, xlo_far, xhi_far, a_far, packed_far, sent_far,
+    e, u, w, ids, zlo, zhi, xlo, xhi, a, packed, picked, sent, sems,
 ):
     copies = Copies(sems)
     f = zlo.shape[0]
     zn = u.shape[0] // f
-    w_copy = copies.start(w_far, w)
+    first = [
+        copies.start(far, near)
+        for far, near in (
+            (w_far, w), (zlo_far, zlo), (xlo_far, xlo), (xhi_far, xhi),
+        )
+    ]
     parts = [pl.ds(z * f, f) for z in range(zn)]
     arriving = [copies.start(u_far.at[part], u.at[part]) for part in parts]
+    zhi_copy = copies.start(zhi_far, zhi)
+    a_copy = copies.start(a_far, a)
     ids_copy = copies.start(ids_far, ids)
-    copies.wait(w_copy)
-    copies.wait(arriving[0])
+    for copy in first + arriving[:1]:
+        copies.wait(copy)
     x_before, x_after = xlo[...], xhi[...]
     for z in range(zn):
-        if z < zn - 1:
-            copies.wait(arriving[z + 1])
+        copies.wait(arriving[z + 1] if z < zn - 1 else zhi_copy)
         explicit_plane(z, u, w, zlo, zhi, x_before, x_after, e)
+    copies.wait(a_copy)
     u[...] = solve(e, a)
     pack_columns(u, packed, zn)
     copies.start(packed, packed_far)
     copies.wait(ids_copy)
     sample(packed, ids, picked, sent, lambda part: copies.start(sent.at[part], sent_far.at[part]))
     copies.finish()
-
-
-GROUP = 8
 
 
 def sample(packed, ids, picked, out, ready):
@@ -277,19 +316,6 @@
         ready((pl.ds(mh * per, per), slice(None), pl.ds(kg * lanes, lanes)))
 
 
-def slot_table(row_index, row_counts):
-    members, slots = row_index.shape[3:]
-    index = row_index.reshape(members, slots)
-    counts = row_counts.reshape(members, 1)
-    live = jnp.arange(slots, dtype=jnp.int32)[None, :] < counts
-    index = jnp.where(live, index, -1)
-    per = 128 // GROUP
-    index = index.reshape(members // per, per, slots // GROUP, GROUP).transpose(2, 0, 1, 3)
-    index = index.reshape(-1, 128)
-    fill = jnp.full((8 - index.shape[0], 128), -1, jnp.int32)
-    return jnp.concatenate([index, fill], axis=0)
-
-
 def gather_rows(got, turned, comps=3):
     sources, f, slots = got.shape
     sides = 2
@@ -312,10 +338,11 @@
 
 
 def forward_kernel(
-    got, w_in, w_out, x_far, hidden_far, slope_far, predicted_far,
-    x, hidden, slope, predicted, sems,
+    got_far, w_in, w_out, x_far, hidden_far, slope_far, predicted_far,
+    got, x, hidden, slope, predicted, sems,
 ):
     copies = Copies(sems)
+    copies.wait(copies.start(got_far, got))
     gather_rows(got, x)
     copies.start(x, x_far)
     wide = 256
@@ -354,13 +381,18 @@
         away[2 * pair * rows : 2 * (pair + 1) * rows] = over_rows(left, right[...]).astype(BF16)
 
 
-def delta_out_kernel(scale, place, got, predicted_far, hidden_far, d, away, predicted, hidden, sems):
+def delta_out_kernel(
+    scale, place, got_far, predicted_far, hidden_far, d, away,
+    got, predicted, hidden, sems,
+):
     copies = Copies(sems)
+    got_copy = copies.start(got_far, got)
     count = 3
     rows = d.shape[0] // count
     parts = [pl.ds(k * rows, rows) for k in range(count)]
     arriving = [copies.start(predicted_far.at[part], predicted.at[part]) for part in parts]
     copies.start(hidden_far, hidden)
+    copies.wait(got_copy)
     gather_rows(got, d)
     for k in range(count):
         copies.wait(arriving[k])
@@ -383,69 +415,38 @@
     away_blocks(x, din, place[0], away, away.shape[0] // 4)
 
 
-def fold(block, rows, width):
-    extra = rows - block.shape[0]
-    pieces = [
-        block[g * extra : (g + 1) * extra, width:] for g in range(block.shape[0] // extra)
-    ]
-    return jnp.concatenate([block[:, :width], jnp.concatenate(pieces, axis=1)], axis=0)
-
-
-def unfold(block, rows):
-    extra = block.shape[0] - rows
-    count = rows // extra
-    wide = block.shape[1] // count
-    pieces = [block[rows:, g * wide : (g + 1) * wide] for g in range(count)]
-    return jnp.concatenate([block[:rows], jnp.concatenate(pieces, axis=0)], axis=1)
-
-
-def keep_kernel(place, hidden, d, x, din, got_out, got_in, own, plus, minus, top, bottom):
+def keep_kernel(place, array, right, got, own, plus, minus, top, bottom):
     core, y = place[0], place[1]
-    rows, width = own.shape[1:]
+    rows = own.shape[0]
     half = rows // 2
-
-    def put(which, k, block):
-        if k == 0:
-            own[which] = block
-        elif k == 1:
-            plus[which] = block.astype(BF16)
-        elif k == 3:
-            minus[which] = block.astype(BF16)
-        else:
-            top[which] = block[:half].astype(BF16)
-            bottom[which] = block[half:].astype(BF16)
-
-    for which, (left, right, got) in enumerate(((hidden, d, got_out), (x, din, got_in))):
-        size = got.shape[0] // 4
-        for ks in ((2, 1), (3, 0)):
-            ys = [lax.rem(y + k, 4) for k in ks]
-            blocks = jnp.concatenate([block_rows(left, at, core, size) for at in ys], axis=0)
-            value = over_rows(blocks, right[...])
-            for n, (k, at) in enumerate(zip(ks, ys)):
-                block = value[n * size : (n + 1) * size]
-                block = block + got[pl.ds(pl.multiple_of(at * size, size), size), :].astype(F32)
-                put(which, k, block if which == 0 else fold(block, rows, width))
+    for ks in ((2, 1), (3, 0)):
+        ys = [lax.rem(y + k, 4) for k in ks]
+        blocks = jnp.concatenate([block_rows(array, at, core, rows) for at in ys], axis=0)
+        value = over_rows(blocks, right[...])
+        for n, (k, at) in enumerate(zip(ks, ys)):
+            block = value[n * rows : (n + 1) * rows]
+            block = block + got[pl.ds(pl.multiple_of(at * rows, rows), rows), :].astype(F32)
+            if k == 0:
+                own[...] = block
+            elif k == 1:
+                plus[...] = block.astype(BF16)
+            elif k == 3:
+                minus[...] = block.astype(BF16)
+            else:
+                top[...] = block[:half].astype(BF16)
+                bottom[...] = block[half:].astype(BF16)
 
 
 def relay_kernel(plus, minus, from_before, from_after, plus_out, minus_out):
-    half = from_before.shape[1]
-    for which in range(plus.shape[0]):
-        plus_out[which, :half] = (
-            plus[which, :half].astype(F32) + from_before[which].astype(F32)
-        ).astype(BF16)
-        plus_out[which, half:] = plus[which, half:]
-        minus_out[which, :half] = minus[which, :half]
-        minus_out[which, half:] = (
-            minus[which, half:].astype(F32) + from_after[which].astype(F32)
-        ).astype(BF16)
-
-
-def finish_kernel(own, from_before, from_after, share_out, share_in):
-    total = [
-        own[k] + from_before[k].astype(F32) + from_after[k].astype(F32) for k in range(2)
-    ]
-    share_out[...] = total[0]
-    share_in[...] = unfold(total[1], share_in.shape[0])
+    half = from_before.shape[0]
+    plus_out[:half] = (plus[:half].astype(F32) + from_before[...].astype(F32)).astype(BF16)
+    plus_out[half:] = plus[half:]
+    minus_out[:half] = minus[:half]
+    minus_out[half:] = (minus[half:].astype(F32) + from_after[...].astype(F32)).astype(BF16)
+
+
+def finish_kernel(own, from_before, from_after, share):
+    share[...] = own[...] + from_before[...].astype(F32) + from_after[...].astype(F32)
 
 
 def planes_kernel(got, out):
@@ -490,11 +491,15 @@
     members, slots = row_index.shape[3:]
 
     v = velocity.astype(BF16).transpose(2, 1, 0, 3)
-    ids = slot_table(row_index, row_counts)
     sent = call(
         columns_kernel,
         shaped((peers, 2 * (f + xl) + HALO_ROWS, lanes), BF16),
-        (v, viscosity.astype(BF16).transpose(1, 0, 2), ids),
+        (
+            v,
+            viscosity.astype(BF16).transpose(1, 0, 2),
+            row_index.reshape(members, slots).T,
+            row_counts.reshape(1, members),
+        ),
         scratch=[pltpu.VMEM((peers * HALO_ROWS, lanes), F32)],
     )
     inverse = implicit_inverse.astype(BF16)
@@ -502,7 +507,7 @@
     solve_flops = 2 * zn * f * total_y * total_y
     edge = shaped((f, total_y), BF16)
     x_edge = shaped((zn * comps, total_y), F32)
-    ids_all = shaped((peers,) + ids.shape, jnp.int32)
+    ids_all = shaped((peers, 8, lanes), jnp.int32)
     v, w, xlo, xhi, zlo, zhi, ids = call(
         spread_kernel,
         (shaped((zn * f, total_y), BF16), shaped((zn * xl, total_y), BF16))
@@ -517,41 +522,58 @@
         pltpu.VMEM((peers, f, members * slots), F32),
         pltpu.VMEM(message.shape, BF16),
     ]
-    u, w, ids, zlo, zhi, xlo, xhi, sent = call(
+    u, w_far, ids_far, packed, z_first, z_last, x_first, x_last = call(
         first_kernel,
         (shaped((zn * f, total_y), F32), shaped(w.shape, BF16), ids_all)
-        + (edge, edge, x_edge, x_edge, message),
+        + (shaped((peers, 2 * f, lanes), BF16), edge, edge, x_edge, x_edge),
         (v, w, xlo, xhi, zlo, zhi, ids, inverse),
-        scratch=[pltpu.VMEM((zn * f, total_y), BF16), pltpu.VMEM((zn * f, total_y), F32)]
-        + sampling
-        + [
-            pltpu.VMEM((2, f, total_y), BF16),
-            pltpu.VMEM((2, zn * comps, total_y), F32),
-            pltpu.SemaphoreType.DMA((16,)),
+        scratch=[
+            pltpu.VMEM((zn * f, total_y), BF16),
+            pltpu.VMEM((zn * f, total_y), F32),
+            pltpu.VMEM(inverse.shape, BF16),
+            pltpu.SemaphoreType.DMA((4,)),
         ],
-        flops=solve_flops + sample_flops,
-        far_out=range(8),
-    )
+        flops=solve_flops,
+        far_in=(7,),
+        far_out=(0, 1, 2),
+    )
+    zlo, zhi = shift((z_last, z_first), ("px", "tr"))
+    xlo, xhi = shift((x_last, x_first), "pz")
+    sent = call(
+        sample_kernel,
+        message,
+        (packed, ids),
+        scratch=sampling[1:] + [pltpu.SemaphoreType.DMA((6,))],
+        flops=sample_flops,
+        far_out=(0,),
+    )
+    sent, zlo, zhi, xlo, xhi = lax.optimization_barrier((sent, zlo, zhi, xlo, xhi))
     rows_in = exchange(sent, ("pz", "tr"))
-    zlo, zhi = shift((zhi, zlo), ("px", "tr"))
-    xlo, xhi = shift((xhi, xlo), "pz")
     packed, sent = call(
         second_kernel,
         (shaped((peers, 2 * f, lanes), BF16), message),
-        (u, w, ids, zlo, zhi, xlo, xhi, inverse),
+        (u, w_far, ids_far, zlo, zhi, xlo, xhi, inverse),
         scratch=[
             pltpu.VMEM((zn * f, total_y), BF16),
             pltpu.VMEM((zn * f, total_y), F32),
             pltpu.VMEM(w.shape, BF16),
-            pltpu.VMEM(ids.shape, jnp.int32),
+            pltpu.VMEM(ids_all.shape, jnp.int32),
+            pltpu.VMEM(edge.shape, BF16),
+            pltpu.VMEM(edge.shape, BF16),
+            pltpu.VMEM(x_edge.shape, F32),
+            pltpu.VMEM(x_edge.shape, F32),
+            pltpu.VMEM(inverse.shape, BF16),
         ]
         + sampling
-        + [pltpu.SemaphoreType.DMA((16,))],
+        + [pltpu.SemaphoreType.DMA((20,))],
         flops=solve_flops + sample_flops,
-        far_in=(0, 1, 2),
+        far_in=range(8),
         far_out=(0, 1),
     )
+    sent, rows_in = lax.optimization_barrier((sent, rows_in))
     rows_target = exchange(sent, ("pz", "tr"))
+    packed, rows_target = lax.optimization_barrier((packed, rows_target))
+    planes = exchange(packed, "pz")
 
     member_in = weight_in[0]
     member_out = weight_out[0]
@@ -570,13 +592,15 @@
         ),
         (rows_in, member_in.T, member_out.T),
         scratch=[
+            pltpu.VMEM(message.shape, BF16),
             pltpu.VMEM((width, batch), BF16),
             pltpu.VMEM((hid, batch), BF16),
             pltpu.VMEM((hid, batch), BF16),
             pltpu.VMEM((width, batch), F32),
-            pltpu.SemaphoreType.DMA((4,)),
+            pltpu.SemaphoreType.DMA((5,)),
         ],
         flops=2 * matmul_flops,
+        far_in=(0,),
         far_out=range(4),
     )
     position = lax.axis_index("px")
@@ -590,12 +614,13 @@
         (shaped((width, batch), BF16), shaped((hid // 2, width), BF16)),
         (place, rows_target, predicted, hidden),
         scratch=[
+            pltpu.VMEM(message.shape, BF16),
             pltpu.VMEM((width, batch), F32),
             pltpu.VMEM((hid, batch), BF16),
-            pltpu.SemaphoreType.DMA((4,)),
+            pltpu.SemaphoreType.DMA((5,)),
         ],
         flops=matmul_flops // 2,
-        far_in=(2, 3),
+        far_in=(1, 2, 3),
     )
     got_out = swap_cores(away_out)
     din, away_in = call(
@@ -605,33 +630,36 @@
         flops=matmul_flops * 3 // 2,
     )
     got_in = swap_cores(away_in)
-    rows = hid // spots
-    own, plus, minus, top, bottom = call(
-        keep_kernel,
-        (
-            shaped((2, rows, width), F32),
-            shaped((2, rows, width), BF16),
-            shaped((2, rows, width), BF16),
-            shaped((2, rows // 2, width), BF16),
-            shaped((2, rows // 2, width), BF16),
-        ),
-        (place, hidden, d, x, din, got_out, got_in),
-        flops=matmul_flops,
-    )
-    packed, top = lax.optimization_barrier((packed, top))
-    from_before, from_after = shift_chips(top, bottom)
-    planes = exchange(packed, "pz")
-    plus, minus = call(
-        relay_kernel,
-        (shaped(plus.shape, BF16), shaped(minus.shape, BF16)),
-        (plus, minus, from_before, from_after),
-    )
-    from_before, from_after = shift_chips(plus, minus)
-    share_out, share_in = call(
-        finish_kernel,
-        (shaped((rows, width), F32), shaped((width // spots, hid), F32)),
-        (own, from_before, from_after),
-    )
+
+    def keep(array, right, got):
+        rows, wide = got.shape[0] // 4, got.shape[1]
+        block = shaped((rows, wide), BF16)
+        part = shaped((rows // 2, wide), BF16)
+        return call(
+            keep_kernel,
+            (shaped((rows, wide), F32), block, block, part, part),
+            (place, array, right, got),
+            flops=matmul_flops // 2,
+        )
+
+    def relay(plus, minus, arrived):
+        block = shaped(plus.shape, BF16)
+        return call(relay_kernel, (block, block), (plus, minus, *arrived))
+
+    def finish(own, arrived):
+        return call(finish_kernel, shaped(own.shape, F32), (own, *arrived))
+
+    own_out, *sides_out, top, bottom = keep(hidden, d, got_out)
+    top, got_in = lax.optimization_barrier((top, got_in))
+    arrived_out = shift_chips(top, bottom)
+    own_in, *sides_in, top, bottom = keep(x, din, got_in)
+    arrived_in = shift_chips(top, bottom)
+    sides_out = relay(*sides_out, arrived_out)
+    sides_out, arrived_in = lax.optimization_barrier((sides_out, arrived_in))
+    arrived_out = shift_chips(*sides_out)
+    arrived_in = shift_chips(*relay(*sides_in, arrived_in))
+    share_out = finish(own_out, arrived_out)
+    share_in = finish(own_in, arrived_in)
     result = call(planes_kernel, shaped((comps, zn, yn, xn), F32), (planes,))
     return (result.transpose(2, 1, 0, 3), share_in[None], share_out[None])
 

time: 177 us -> 171 us (0.966)
  local copies, waits for them, and re-layouts: 27.6 us -> 11.4 us
  Pallas kernels: 23.8 us -> 34.8 us
  waiting for transfers between devices: 54.2 us -> 49 us
  starting transfers between devices: 39.6 us -> 43.9 us
    all_to_all x3, waiting for transfers between devices: 14.1 us -> 40.8 us  [exchange(): return lax.all_to_all(array, axis, split_axis=0, concat_axis=0, tiled=True)]
    ppermute x6, waiting for transfers between devices: 25 us -> 3.59 us  [shift(): return (lax.ppermute(last, axis, up), lax.ppermute(first, axis, down))]
    unnamed x49 -> x40, local copies, waits for them, and re-layouts: 24.9 us -> 9.81 us
    pallas_call x11 -> x15, Pallas kernels: 23.8 us -> 34.8 us  [call(): pl.pallas_call(kernel, out_shape=pinned if isinstance(out_shape, tuple) e...]
    ppermute x4 -> x8, waiting for transfers between devices: 12.2 us -> 4.66 us  [shift_chips(): return (lax.ppermute(forward, 'px', up), lax.ppermute(backward, 'px', down))]
    ppermute x4 -> x8, starting transfers between devices: 6.55 us -> 13.4 us  [shift_chips(): return (lax.ppermute(forward, 'px', up), lax.ppermute(backward, 'px', down))]
    ppermute x2, waiting for transfers between devices: 2.9 us -> 0.01 us  [swap_cores(): return lax.ppermute(array, 'px', [(i, i ^ 1) for i in range(size)])]
    all_to_all x3, starting transfers between devices: 19.6 us -> 17 us  [exchange(): return lax.all_to_all(array, axis, split_axis=0, concat_axis=0, tiled=True)]
  transfers between devices with their start and end apart: 15 -> 19, of which waited for: 10 -> 9; matrix products, arithmetic and copies ran while one was open for 3% -> 4% of each run, Pallas kernels for 6% -> 14%
where the time goes in v4:
time: 171 us; the launch traced here: 170 us
  waiting for transfers between devices  49 us (29%)
  starting transfers between devices  43.9 us (26%)
  Pallas kernels  34.8 us (20%)
  blocking collectives  28.6 us (17%)
  local copies, waits for them, and re-layouts  11.4 us (7%)
  other arithmetic  1.74 us (1%)
    all_to_all x3, waiting for transfers between devices, exchange(): return lax.all_to_all(array, axis, split_axis=0, concat_axis=0, tiled=True)  40.8 us
    pallas_call x15, Pallas kernels, call(): pl.pallas_call(kernel, out_shape=pinned if isinstance(out_shape, tuple) e...  34.8 us
    all_to_all x1, blocking collectives, exchange(): return lax.all_to_all(array, axis, split_axis=0, concat_axis=0, tiled=True)  28.6 us
    all_to_all x3, starting transfers between devices, exchange(): return lax.all_to_all(array, axis, split_axis=0, concat_axis=0, tiled=True)  17 us
    ppermute x8, starting transfers between devices, shift_chips(): return (lax.ppermute(forward, 'px', up), lax.ppermute(backward, 'px', down))  13.4 us
    ppermute x6, starting transfers between devices, shift(): return (lax.ppermute(last, axis, up), lax.ppermute(first, axis, down))  12.9 us
    unnamed x40, local copies, waits for them, and re-layouts  9.81 us
    ppermute x8, waiting for transfers between devices, shift_chips(): return (lax.ppermute(forward, 'px', up), lax.ppermute(backward, 'px', down))  4.66 us
  transfers between devices with their start and end apart: 19, of which 9 were waited for; matrix products, arithmetic and copies ran while one was open for 4% of the time, Pallas kernels for 14%

profile of v4, /device:TPU:2, one launch (start us, length us, event | category | flops | bytes accessed | tf_op | source)
XLA Modules:
  0.0 170.4 jit_solution(2158295515162403391)
XLA Ops:
  0.7 1.4 copy.21
  2.1 1.1 copy.22
  3.2 0.2 shard_map.94
  3.4 28.6 %all_to_all.20.got = bf16[16,152,128]{2,1,0:T(8,128)(2,1)S(1)} all-to-all(bf16[16,152,128]{2,1,0:T(8,128)(2,1)S(1)} %shard_map.94), channel_id=1, replica_groups=mesh['px'=8,'pz'=16,'tr'=2] {'pz'}, dimensions={0} | all-to-all | bytes 1245184 | tf_op jit(solution)/shard_map/all_to_all | solution.py:469
  32.0 0.3 shard_map.95
  32.3 2.2 %collective-permute-start = (bf16[48,1024]{1,0:T(8,128)(2,1)S(1)}, bf16[48,1024]{1,0:T(8,128)(2,1)S(1)}, u32[]{:S(2)}, u32[]{:S(2)}) collective-permute-start(bf16[48,1024]{1,0:T(8,128)(2,1)S(1)} %get-tuple-element.61), channel_id=1, source_target_pairs={{0,1},{1,32},{32,33},{33,64},{64,65},{65,96},{96,97},{97,128},{128... | collective-permute-start | bytes 294920 | tf_op jit(solution)/shard_map/ppermute | solution.py:80
  34.5 3.2 %collective-permute-start.1 = (bf16[48,1024]{1,0:T(8,128)(2,1)S(1)}, bf16[48,1024]{1,0:T(8,128)(2,1)S(1)}, u32[]{:S(2)}, u32[]{:S(2)}) collective-permute-start(bf16[48,1024]{1,0:T(8,128)(2,1)S(1)} %get-tuple-element.62), channel_id=1, source_target_pairs={{1,0},{32,1},{33,32},{64,33},{65,64},{96,65},{97,96},{128,97},{129... | collective-permute-start | bytes 294920 | tf_op jit(solution)/shard_map/ppermute | solution.py:80
  37.8 1.7 convert_element_type.11.a_far
  39.4 1.2 collective-permute-done.zlo
  40.6 0.4 collective-permute-done.1.zhi
  41.1 3.8 %shard_map.96 = (f32[192,1024]{1,0:T(8,128)}, bf16[64,1024]{1,0:T(8,128)(2,1)}, s32[16,8,128]{2,1,0:T(8,128)}, bf16[16,96,128]{2,1,0:T(8,128)(2,1)S(1)}, bf16[48...) custom-call(bf16[192,1024]{1,0:T(8,128)(2,1)S(1)} %get-tuple-element.57.v, ...), custom_call_target="tpu_custom_call" | custom-call | flops 402653184 | bytes 4653056 | tf_op jit(solution)/shard_map/pallas_call | solution.py:35
  44.9 0.2 collective-permute-start.2
  45.2 5.2 %collective-permute-start.3 = (bf16[48,1024]{1,0:T(8,128)(2,1)S(1)}, bf16[48,1024]{1,0:T(8,128)(2,1)S(1)}, u32[]{:S(2)}, u32[]{:S(2)}) collective-permute-start(bf16[48,1024]{1,0:T(8,128)(2,1)S(1)} %get-tuple-element.69), channel_id=1, source_target_pairs={{1,0},{32,1},{33,32},{64,33},{65,64},{96,65},{97,96},{128,97},{129... | collective-permute-start | bytes 294920 | tf_op jit(solution)/shard_map/ppermute | solution.py:80
  50.4 1.5 collective-permute-start.4
  51.9 0.5 collective-permute-start.5
  52.4 2.7 %shard_map.97 = bf16[32,48,384]{2,1,0:T(8,128)(2,1)} custom-call(bf16[16,96,128]{2,1,0:T(8,128)(2,1)S(1)} %get-tuple-element.67.packed, s32[16,8,128]{2,1,0:T(8,128)S(1)} %get-tuple-element.63.ids), custom_call_target="tpu_custom_call" | custom-call | flops 301989888 | bytes 1638400 | tf_op jit(solution)/shard_map/pallas_call | solution.py:35
  55.1 0.2 collective-permute-done.4.xlo_far
  55.3 1.7 %collective-permute-done.5.xhi_far = f32[12,1024]{1,0:T(8,128)S(1)} collective-permute-done((f32[12,1024]{1,0:T(8,128)S(1)}, f32[12,1024]{1,0:T(8,128)S(1)}, u32[]{:S(2)}, u32[]{:S(2)}) %collective-permute-start.5) | collective-permute-done | bytes 49184 | tf_op jit(solution)/shard_map/ppermute | solution.py:80
  57.1 6.9 %all-to-all-start.1 = ((bf16[32,48,384]{2,1,0:T(8,128)(2,1)}), bf16[32,48,384]{2,1,0:T(8,128)(2,1)S(1)}, u32[]{:S(2)}, u32[]{:S(2)}) async-start(bf16[32,48,384]{2,1,0:T(8,128)(2,1)} %shard_map.97), calls=%async_computation.1 | async-start | bytes 2359296 | tf_op jit(solution)/shard_map/all_to_all | solution.py:469
  64.1 5.7 %shard_map.98 = (bf16[16,96,128]{2,1,0:T(8,128)(2,1)}, bf16[32,48,384]{2,1,0:T(8,128)(2,1)}) custom-call(f32[192,1024]{1,0:T(8,128)} %get-tuple-element.64.u_far, bf16[64,1024]{1,0:T(8,128)(2,1)} %get-tuple-element.65.w_far, s32[16,8,128]{2,1,0:T(8,128)} %get-tuple-element.66.ids_far, bf16[48,1024]{1,0:T(8,128)(2,1)} %copy-done.14, ...), custom_call_target="tpu_custom_call" | custom-call | flops 704643072 | bytes 4947968 | tf_op jit(solution)/shard_map/pallas_call | solution.py:35
  69.7 23.4 %all-to-all-done.1.got_far = bf16[32,48,384]{2,1,0:T(8,128)(2,1)S(1)} async-done(((bf16[32,48,384]{2,1,0:T(8,128)(2,1)}), bf16[32,48,384]{2,1,0:T(8,128)(2,1)S(1)}, u32[]{:S(2)}, u32[]{:S(2)}) %all-to-all-start.1) | async-done | bytes 1179680 | tf_op jit(solution)/shard_map/all_to_all | solution.py:469
  93.1 5.3 %all-to-all-start.2 = ((bf16[32,48,384]{2,1,0:T(8,128)(2,1)}), bf16[32,48,384]{2,1,0:T(8,128)(2,1)}, u32[]{:S(2)}, u32[]{:S(2)}) async-start(bf16[32,48,384]{2,1,0:T(8,128)(2,1)} %get-tuple-element.79), calls=%async_computation.2 | async-start | bytes 2359296 | tf_op jit(solution)/shard_map/all_to_all | solution.py:469
  98.4 1.8 %copy.12 = bf16[1,768,1024]{1,2,0:T(8,128)(2,1)S(1)} copy(bf16[1,768,1024]{2,1,0:T(8,128)(2,1)} %param.12) | data formatting | bytes 3145728 | tf_op args[5]
  100.3 1.6 copy.13.w_out
  102.0 1.4 copy-done.2
  103.4 6.9 %shard_map.100 = (bf16[768,768]{1,0:T(8,128)(2,1)}, bf16[1024,768]{1,0:T(8,128)(2,1)}, bf16[1024,768]{1,0:T(8,128)(2,1)}, f32[768,768]{1,0:T(8,128)}) custom-call(bf16[32,48,384]{2,1,0:T(8,128)(2,1)} %copy-done.13, bf16[1024,768]{1,0:T(8,128)(2,1)S(1)} %bitcast.24, bf16[768,1024]{1,0:T(8,128)(2,1)S(1)} %copy-done.2), custom_call_target="tpu_custom_call" | custom-call | flops 2415919104 | bytes 11010048 | tf_op jit(solution)/shard_map/pallas_call | solution.py:35
  110.3 17.4 %all-to-all-done.2.refs_1_ = bf16[32,48,384]{2,1,0:T(8,128)(2,1)} async-done(((bf16[32,48,384]{2,1,0:T(8,128)(2,1)}), bf16[32,48,384]{2,1,0:T(8,128)(2,1)}, u32[]{:S(2)}, u32[]{:S(2)}) %all-to-all-start.2) | async-done | bytes 1179680 | tf_op jit(solution)/shard_map/all_to_all | solution.py:469
  127.7 5.0 %shard_map.101 = (bf16[768,768]{1,0:T(8,128)(2,1)S(1)}, bf16[512,768]{1,0:T(8,128)(2,1)}) custom-call(s32[2]{0:T(128)S(1)} %pad_add_fusion.refs_0_.place, bf16[32,48,384]{2,1,0:T(8,128)(2,1)} %all-to-all-done.2.refs_1_, f32[768,768]{1,0:T(8,128)} %get-tuple-element.84.refs_2_, bf16[1024,768]{1,0:T(8,128)(2,1)} %get-tuple-element.85.refs_3_.array), custom_call_target="tpu_custom_call" | custom-call | flops 603979776 | bytes 7077896 | tf_op jit(solution)/shard_map/pallas_call | solution.py:35
  132.9 4.6 %shard_map.102 = (bf16[1024,768]{1,0:T(8,128)(2,1)S(1)}, bf16[384,1024]{1,0:T(8,128)(2,1)}) custom-call(s32[2]{0:T(128)S(1)} %pad_add_fusion.refs_0_.place, bf16[768,768]{1,0:T(8,128)(2,1)S(1)} %get-tuple-element.86.d.right, bf16[1024,768]{1,0:T(8,128)(2,1)S(1)} %copy-done.11, bf16[1024,768]{1,0:T(8,128)(2,1)S(1)} %bitcast.23, bf16[768,768]{1,0:T(8,128)(2,1)S(1)} %copy-done.5), custom_call_target="tpu_custom_call" | custom-call | flops 1811939328 | bytes 7864328 | tf_op jit(solution)/shard_map/pallas_call | solution.py:35
  137.4 1.2 copy-done.3
  138.6 0.5 collective-permute-start.7
  139.1 4.8 %all-to-all-start.3 = ((bf16[16,96,128]{2,1,0:T(8,128)(2,1)}), bf16[16,96,128]{2,1,0:T(8,128)(2,1)S(1)}, u32[]{:S(2)}, u32[]{:S(2)}) async-start(bf16[16,96,128]{2,1,0:T(8,128)(2,1)} %get-tuple-element.80), calls=%async_computation.3 | async-start | bytes 786432 | tf_op jit(solution)/shard_map/all_to_all | solution.py:469
  143.9 1.4 copy-done.8
  145.4 2.0 %shard_map.103 = (f32[128,768]{1,0:T(8,128)S(1)}, bf16[128,768]{1,0:T(8,128)(2,1)S(1)}, bf16[128,768]{1,0:T(8,128)(2,1)S(1)}, bf16[64,768]{1,0:T(8,128)(2,1)S(1)}, bf16[64,768]{1,0:T(8,128)(2,1)S(1)}) custom-call(s32[2]{0:T(128)S(1)} %pad_add_fusion.refs_0_.place, bf16[1024,768]{1,0:T(8,128)(2,1)S(1)} %copy-done, bf16[768,768]{1,0:T(8,128)(2,1)S(1)} %copy-done.8, ...), custom_call_target="tpu_custom_call" | custom-call | flops 603979776 | bytes 4521992 | tf_op jit(solution)/shard_map/pallas_call | solution.py:35
  147.3 2.5 %collective-permute-start.8 = (bf16[64,768]{1,0:T(8,128)(2,1)S(1)}, bf16[64,768]{1,0:T(8,128)(2,1)S(1)}, u32[]{:S(2)}, u32[]{:S(2)}) collective-permute-start(bf16[64,768]{1,0:T(8,128)(2,1)S(1)} %get-tuple-element.98), channel_id=1, source_target_pairs={{0,64},{32,96},{64,128},{96,160},{128,192},{160,224},{192,0},{224,... | collective-permute-start | bytes 294920 | tf_op jit(solution)/shard_map/ppermute | solution.py:481
  149.8 0.8 collective-permute-start.9
  150.7 1.7 %shard_map.104 = (f32[96,1024]{1,0:T(8,128)S(1)}, bf16[96,1024]{1,0:T(8,128)(2,1)S(1)}, bf16[96,1024]{1,0:T(8,128)(2,1)S(1)}, bf16[48,1024]{1,0:T(8,128)(2,1)S(1)}, bf16[48,1024]{1,0:T(8,128)(2,1)S(1)}) custom-call(s32[2]{0:T(128)S(1)} %pad_add_fusion.refs_0_.place, bf16[768,768]{1,0:T(8,128)(2,1)S(1)} %copy-done.6, bf16[1024,768]{1,0:T(8,128)(2,1)S(1)} %copy-done.4, ...), custom_call_target="tpu_custom_call" | custom-call | flops 603979776 | bytes 4521992 | tf_op jit(solution)/shard_map/pallas_call | solution.py:35
  152.4 1.5 collective-permute-start.10
  153.9 2.0 %collective-permute-start.11 = (bf16[48,1024]{1,0:T(8,128)(2,1)S(1)}, bf16[48,1024]{1,0:T(8,128)(2,1)S(1)}, u32[]{:S(2)}, u32[]{:S(2)}) collective-permute-start(bf16[48,1024]{1,0:T(8,128)(2,1)S(1)} %get-tuple-element.103), channel_id=1, source_target_pairs={{64,0},{96,32},{128,64},{160,96},{192,128},{224,160},{0,192},{32,2... | collective-permute-start | bytes 294920 | tf_op jit(solution)/shard_map/ppermute | solution.py:481
  156.0 2.5 %collective-permute-done.10.from_before = bf16[48,1024]{1,0:T(8,128)(2,1)S(1)} collective-permute-done((bf16[48,1024]{1,0:T(8,128)(2,1)S(1)}, bf16[48,1024]{1,0:T(8,128)(2,1)S(1)}, u32[]{:S(2)}, u32[]{:S(2)}) %collective-permute-start.10) | collective-permute-done | bytes 98336 | tf_op jit(solution)/shard_map/ppermute | solution.py:481
  158.5 1.1 collective-permute-start.14
  159.7 2.1 %collective-permute-start.15 = (bf16[128,768]{1,0:T(8,128)(2,1)S(1)}, bf16[128,768]{1,0:T(8,128)(2,1)S(1)}, u32[]{:S(2)}, u32[]{:S(2)}) collective-permute-start(bf16[128,768]{1,0:T(8,128)(2,1)S(1)} %get-tuple-element.110), channel_id=1, source_target_pairs={{64,0},{96,32},{128,64},{160,96},{192,128},{224,160},{0,192},{32,2... | collective-permute-start | bytes 589832 | tf_op jit(solution)/shard_map/ppermute | solution.py:481
  161.9 3.2 %collective-permute-start.13 = (bf16[96,1024]{1,0:T(8,128)(2,1)S(1)}, bf16[96,1024]{1,0:T(8,128)(2,1)S(1)}, u32[]{:S(2)}, u32[]{:S(2)}) collective-permute-start(bf16[96,1024]{1,0:T(8,128)(2,1)S(1)} %get-tuple-element.107), channel_id=1, source_target_pairs={{64,0},{96,32},{128,64},{160,96},{192,128},{224,160},{0,192},{32,2... | collective-permute-start | bytes 589832 | tf_op jit(solution)/shard_map/ppermute | solution.py:481
  165.3 1.4 copy.14
  166.7 0.6 collective-permute-done.14.from_before
  167.4 0.8 shard_map.108
  168.2 1.5 collective-permute-done.12.from_before
  169.6 0.8 shard_map.107
  (49 shorter events, 0.6 us)
Async XLA Ops:
  0.6 2.5 %copy-start.9 = (s32[1,1,1,32,24]{3,4,2,1,0:T(8,128)S(1)}, s32[1,1,1,32,24]{3,4,2,1,0:T(8,128)}, u32[]{:S(2)}) copy-start(s32[1,1,1,32,24]{3,4,2,1,0:T(8,128)} %param.10) | copy-start | bytes 9220
  0.6 2.5 %copy-start.10 = (s32[1,1,1,32]{3,2,1,0:T(1,128)S(1)}, s32[1,1,1,32]{3,2,1,0:T(1,128)}, u32[]{:S(2)}) copy-start(s32[1,1,1,32]{3,2,1,0:T(1,128)} %param.11) | copy-start | bytes 388
  0.7 37.1 %copy-start.12 = (f32[1024,1024]{1,0:T(8,128)S(1)}, f32[1024,1024]{1,0:T(8,128)}, u32[]{:S(2)}) copy-start(f32[1024,1024]{1,0:T(8,128)} %param.9) | copy-start | bytes 12582916
  32.3 8.3 %collective-permute-start = (bf16[48,1024]{1,0:T(8,128)(2,1)S(1)}, bf16[48,1024]{1,0:T(8,128)(2,1)S(1)}, u32[]{:S(2)}, u32[]{:S(2)}) collective-permute-start(bf16[48,1024]{1,0:T(8,128)(2,1)S(1)} %get-tuple-element.61), channel_id=1, source_target_pairs={{0,1},{1,32},{32,33},{33,64},{64,65},{65,96},{96,97},{97,128},{128... | collective-permute-start | bytes 294920 | tf_op jit(solution)/shard_map/ppermute | solution.py:80
  34.5 6.5 %collective-permute-start.1 = (bf16[48,1024]{1,0:T(8,128)(2,1)S(1)}, bf16[48,1024]{1,0:T(8,128)(2,1)S(1)}, u32[]{:S(2)}, u32[]{:S(2)}) collective-permute-start(bf16[48,1024]{1,0:T(8,128)(2,1)S(1)} %get-tuple-element.62), channel_id=1, source_target_pairs={{1,0},{32,1},{33,32},{64,33},{65,64},{96,65},{97,96},{128,97},{129... | collective-permute-start | bytes 294920 | tf_op jit(solution)/shard_map/ppermute | solution.py:80
  44.9 12.1 %collective-permute-start.2 = (bf16[48,1024]{1,0:T(8,128)(2,1)S(1)}, bf16[48,1024]{1,0:T(8,128)(2,1)S(1)}, u32[]{:S(2)}, u32[]{:S(2)}) collective-permute-start(bf16[48,1024]{1,0:T(8,128)(2,1)S(1)} %get-tuple-element.68), channel_id=1, source_target_pairs={{0,1},{1,32},{32,33},{33,64},{64,65},{65,96},{96,97},{97,128},{128... | collective-permute-start | bytes 294920 | tf_op jit(solution)/shard_map/ppermute | solution.py:80
  45.2 11.9 %collective-permute-start.3 = (bf16[48,1024]{1,0:T(8,128)(2,1)S(1)}, bf16[48,1024]{1,0:T(8,128)(2,1)S(1)}, u32[]{:S(2)}, u32[]{:S(2)}) collective-permute-start(bf16[48,1024]{1,0:T(8,128)(2,1)S(1)} %get-tuple-element.69), channel_id=1, source_target_pairs={{1,0},{32,1},{33,32},{64,33},{65,64},{96,65},{97,96},{128,97},{129... | collective-permute-start | bytes 294920 | tf_op jit(solution)/shard_map/ppermute | solution.py:80
  50.4 4.9 %collective-permute-start.4 = (f32[12,1024]{1,0:T(8,128)S(1)}, f32[12,1024]{1,0:T(8,128)S(1)}, u32[]{:S(2)}, u32[]{:S(2)}) collective-permute-start(f32[12,1024]{1,0:T(8,128)S(1)} %get-tuple-element.70), channel_id=1, source_target_pairs={{0,2},{2,4},{4,6},{6,8},{8,10},{10,12},{12,14},{14,16},{16,18},{18... | collective-permute-start | bytes 147464 | tf_op jit(solution)/shard_map/ppermute | solution.py:80
  51.9 5.2 %collective-permute-start.5 = (f32[12,1024]{1,0:T(8,128)S(1)}, f32[12,1024]{1,0:T(8,128)S(1)}, u32[]{:S(2)}, u32[]{:S(2)}) collective-permute-start(f32[12,1024]{1,0:T(8,128)S(1)} %get-tuple-element.71), channel_id=1, source_target_pairs={{2,0},{4,2},{6,4},{8,6},{10,8},{12,10},{14,12},{16,14},{18,16},{20... | collective-permute-start | bytes 147464 | tf_op jit(solution)/shard_map/ppermute | solution.py:80
  55.3 8.7 %copy-start.16 = (f32[12,1024]{1,0:T(8,128)}, f32[12,1024]{1,0:T(8,128)S(1)}, u32[]{:S(2)}) copy-start(f32[12,1024]{1,0:T(8,128)S(1)} %collective-permute-done.4.xlo_far) | copy-start | bytes 147460
  57.1 7.0 %copy-start.17 = (f32[12,1024]{1,0:T(8,128)}, f32[12,1024]{1,0:T(8,128)S(1)}, u32[]{:S(2)}) copy-start(f32[12,1024]{1,0:T(8,128)S(1)} %collective-permute-done.5.xhi_far) | copy-start | bytes 147460
  57.1 7.0 %copy-start.14 = (bf16[48,1024]{1,0:T(8,128)(2,1)}, bf16[48,1024]{1,0:T(8,128)(2,1)S(1)}, u32[]{:S(2)}) copy-start(bf16[48,1024]{1,0:T(8,128)(2,1)S(1)} %collective-permute-done.2.zlo_far) | copy-start | bytes 294916
  57.1 7.0 %copy-start.15 = (bf16[48,1024]{1,0:T(8,128)(2,1)}, bf16[48,1024]{1,0:T(8,128)(2,1)S(1)}, u32[]{:S(2)}) copy-start(bf16[48,1024]{1,0:T(8,128)(2,1)S(1)} %collective-permute-done.3.zhi_far) | copy-start | bytes 294916
  57.1 36.0 %all-to-all-start.1 = ((bf16[32,48,384]{2,1,0:T(8,128)(2,1)}), bf16[32,48,384]{2,1,0:T(8,128)(2,1)S(1)}, u32[]{:S(2)}, u32[]{:S(2)}) async-start(bf16[32,48,384]{2,1,0:T(8,128)(2,1)} %shard_map.97), calls=%async_computation.1 | async-start | bytes 2359296 | tf_op jit(solution)/shard_map/all_to_all | solution.py:469
  93.1 5.3 %copy-start.13 = (bf16[32,48,384]{2,1,0:T(8,128)(2,1)}, bf16[32,48,384]{2,1,0:T(8,128)(2,1)S(1)}, u32[]{:S(2)}) copy-start(bf16[32,48,384]{2,1,0:T(8,128)(2,1)S(1)} %all-to-all-done.1.got_far) | copy-start | bytes 3538948
  93.1 34.6 %all-to-all-start.2 = ((bf16[32,48,384]{2,1,0:T(8,128)(2,1)}), bf16[32,48,384]{2,1,0:T(8,128)(2,1)}, u32[]{:S(2)}, u32[]{:S(2)}) async-start(bf16[32,48,384]{2,1,0:T(8,128)(2,1)} %get-tuple-element.79), calls=%async_computation.2 | async-start | bytes 2359296 | tf_op jit(solution)/shard_map/all_to_all | solution.py:469
  98.4 1.9 %copy-start.1 = (bf16[1,1024,768]{2,1,0:T(8,128)(2,1)S(1)}, bf16[1,1024,768]{2,1,0:T(8,128)(2,1)}, u32[]{:S(2)}) copy-start(bf16[1,1024,768]{2,1,0:T(8,128)(2,1)} %param.13) | copy-start | bytes 4718596
  102.0 1.4 copy-start.2
  127.7 5.1 %copy-start.5 = (bf16[768,768]{1,0:T(8,128)(2,1)S(1)}, bf16[768,768]{1,0:T(8,128)(2,1)}, u32[]{:S(2)}) copy-start(bf16[768,768]{1,0:T(8,128)(2,1)} %get-tuple-element.82.x.array) | copy-start | bytes 3538948
  127.7 5.2 %copy-start.11 = (bf16[1024,768]{1,0:T(8,128)(2,1)S(1)}, bf16[1024,768]{1,0:T(8,128)(2,1)}, u32[]{:S(2)}) copy-start(bf16[1024,768]{1,0:T(8,128)(2,1)} %get-tuple-element.87.slope) | copy-start | bytes 4718596
  132.7 4.7 %copy-start.7 = (bf16[768,768]{1,0:T(8,128)(2,1)}, bf16[768,768]{1,0:T(8,128)(2,1)S(1)}, u32[]{:S(2)}) copy-start(bf16[768,768]{1,0:T(8,128)(2,1)S(1)} %get-tuple-element.86.d.right) | copy-start | bytes 3538948
  132.7 11.2 %collective-permute-start.6 = (bf16[512,768]{1,0:T(8,128)(2,1)}, bf16[512,768]{1,0:T(8,128)(2,1)}, u32[]{:S(2)}, u32[]{:S(2)}) collective-permute-start(bf16[512,768]{1,0:T(8,128)(2,1)} %get-tuple-element.89), channel_id=1, source_target_pairs={{0,32},{32,0},{64,96},{96,64},{128,160},{160,128},{192,224},{224,1... | collective-permute-start | bytes 2359304 | tf_op jit(solution)/shard_map/ppermute | solution.py:474
  132.9 11.1 %copy-start = (bf16[1024,768]{1,0:T(8,128)(2,1)S(1)}, bf16[1024,768]{1,0:T(8,128)(2,1)}, u32[]{:S(2)}) copy-start(bf16[1024,768]{1,0:T(8,128)(2,1)} %get-tuple-element.85.refs_3_.array) | copy-start | bytes 4718596
  137.4 1.2 copy-start.3
  138.6 8.7 %collective-permute-start.7 = (bf16[384,1024]{1,0:T(8,128)(2,1)}, bf16[384,1024]{1,0:T(8,128)(2,1)S(1)}, u32[]{:S(2)}, u32[]{:S(2)}) collective-permute-start(bf16[384,1024]{1,0:T(8,128)(2,1)} %get-tuple-element.91), channel_id=1, source_target_pairs={{0,32},{32,0},{64,96},{96,64},{128,160},{160,128},{192,224},{224,1... | collective-permute-start | bytes 2359304 | tf_op jit(solution)/shard_map/ppermute | solution.py:474
  139.1 26.1 %all-to-all-start.3 = ((bf16[16,96,128]{2,1,0:T(8,128)(2,1)}), bf16[16,96,128]{2,1,0:T(8,128)(2,1)S(1)}, u32[]{:S(2)}, u32[]{:S(2)}) async-start(bf16[16,96,128]{2,1,0:T(8,128)(2,1)} %get-tuple-element.80), calls=%async_computation.3 | async-start | bytes 786432 | tf_op jit(solution)/shard_map/all_to_all | solution.py:469
  143.9 6.8 %copy-start.4 = (bf16[1024,768]{1,0:T(8,128)(2,1)S(1)}, bf16[1024,768]{1,0:T(8,128)(2,1)}, u32[]{:S(2)}) copy-start(bf16[1024,768]{1,0:T(8,128)(2,1)} %copy-done.3) | copy-start | bytes 4718596
  143.9 6.8 %copy-start.6 = (bf16[768,768]{1,0:T(8,128)(2,1)S(1)}, bf16[768,768]{1,0:T(8,128)(2,1)}, u32[]{:S(2)}) copy-start(bf16[768,768]{1,0:T(8,128)(2,1)} %get-tuple-element.82.x.array) | copy-start | bytes 3538948
  143.9 1.4 copy-start.8
  147.3 8.6 %collective-permute-start.8 = (bf16[64,768]{1,0:T(8,128)(2,1)S(1)}, bf16[64,768]{1,0:T(8,128)(2,1)S(1)}, u32[]{:S(2)}, u32[]{:S(2)}) collective-permute-start(bf16[64,768]{1,0:T(8,128)(2,1)S(1)} %get-tuple-element.98), channel_id=1, source_target_pairs={{0,64},{32,96},{64,128},{96,160},{128,192},{160,224},{192,0},{224,... | collective-permute-start | bytes 294920 | tf_op jit(solution)/shard_map/ppermute | solution.py:481
  149.8 6.1 %collective-permute-start.9 = (bf16[64,768]{1,0:T(8,128)(2,1)S(1)}, bf16[64,768]{1,0:T(8,128)(2,1)S(1)}, u32[]{:S(2)}, u32[]{:S(2)}) collective-permute-start(bf16[64,768]{1,0:T(8,128)(2,1)S(1)} %get-tuple-element.99), channel_id=1, source_target_pairs={{64,0},{96,32},{128,64},{160,96},{192,128},{224,160},{0,192},{32,2... | collective-permute-start | bytes 294920 | tf_op jit(solution)/shard_map/ppermute | solution.py:481
  152.4 6.1 %collective-permute-start.10 = (bf16[48,1024]{1,0:T(8,128)(2,1)S(1)}, bf16[48,1024]{1,0:T(8,128)(2,1)S(1)}, u32[]{:S(2)}, u32[]{:S(2)}) collective-permute-start(bf16[48,1024]{1,0:T(8,128)(2,1)S(1)} %get-tuple-element.102), channel_id=1, source_target_pairs={{0,64},{32,96},{64,128},{96,160},{128,192},{160,224},{192,0},{224,... | collective-permute-start | bytes 294920 | tf_op jit(solution)/shard_map/ppermute | solution.py:481
  153.9 4.6 %collective-permute-start.11 = (bf16[48,1024]{1,0:T(8,128)(2,1)S(1)}, bf16[48,1024]{1,0:T(8,128)(2,1)S(1)}, u32[]{:S(2)}, u32[]{:S(2)}) collective-permute-start(bf16[48,1024]{1,0:T(8,128)(2,1)S(1)} %get-tuple-element.103), channel_id=1, source_target_pairs={{64,0},{96,32},{128,64},{160,96},{192,128},{224,160},{0,192},{32,2... | collective-permute-start | bytes 294920 | tf_op jit(solution)/shard_map/ppermute | solution.py:481
  158.5 8.8 %collective-permute-start.14 = (bf16[128,768]{1,0:T(8,128)(2,1)S(1)}, bf16[128,768]{1,0:T(8,128)(2,1)S(1)}, u32[]{:S(2)}, u32[]{:S(2)}) collective-permute-start(bf16[128,768]{1,0:T(8,128)(2,1)S(1)} %get-tuple-element.109), channel_id=1, source_target_pairs={{0,64},{32,96},{64,128},{96,160},{128,192},{160,224},{192,0},{224,... | collective-permute-start | bytes 589832 | tf_op jit(solution)/shard_map/ppermute | solution.py:481
  159.7 7.7 %collective-permute-start.15 = (bf16[128,768]{1,0:T(8,128)(2,1)S(1)}, bf16[128,768]{1,0:T(8,128)(2,1)S(1)}, u32[]{:S(2)}, u32[]{:S(2)}) collective-permute-start(bf16[128,768]{1,0:T(8,128)(2,1)S(1)} %get-tuple-element.110), channel_id=1, source_target_pairs={{64,0},{96,32},{128,64},{160,96},{192,128},{224,160},{0,192},{32,2... | collective-permute-start | bytes 589832 | tf_op jit(solution)/shard_map/ppermute | solution.py:481
  161.8 7.8 %collective-permute-start.12 = (bf16[96,1024]{1,0:T(8,128)(2,1)S(1)}, bf16[96,1024]{1,0:T(8,128)(2,1)S(1)}, u32[]{:S(2)}, u32[]{:S(2)}) collective-permute-start(bf16[96,1024]{1,0:T(8,128)(2,1)S(1)} %get-tuple-element.106), channel_id=1, source_target_pairs={{0,64},{32,96},{64,128},{96,160},{128,192},{160,224},{192,0},{224,... | collective-permute-start | bytes 589832 | tf_op jit(solution)/shard_map/ppermute | solution.py:481
  161.9 7.7 %collective-permute-start.13 = (bf16[96,1024]{1,0:T(8,128)(2,1)S(1)}, bf16[96,1024]{1,0:T(8,128)(2,1)S(1)}, u32[]{:S(2)}, u32[]{:S(2)}) collective-permute-start(bf16[96,1024]{1,0:T(8,128)(2,1)S(1)} %get-tuple-element.107), channel_id=1, source_target_pairs={{64,0},{96,32},{128,64},{160,96},{192,128},{224,160},{0,192},{32,2... | collective-permute-start | bytes 589832 | tf_op jit(solution)/shard_map/ppermute | solution.py:481

commit v5 on v4

--- a/solution.py
+++ b/solution.py
@@ -13,7 +13,7 @@
 MIB = 1 << 20
 
 
-def call(kernel, out_shape, args, scratch=(), flops=1e6, far_in=(), far_out=()):
+def call(kernel, out_shape, args, scratch=(), flops=1e6, far_in=(), far_out=(), aliases=None):
     outs = jax.tree.leaves(out_shape)
     size = lambda x: math.prod(x.shape) * jnp.dtype(x.dtype).itemsize
     near = [x for k, x in enumerate(args) if k not in far_in]
@@ -38,6 +38,7 @@
         in_specs=[spec(k, far_in, x.ndim == 1) for k, x in enumerate(args)],
         out_specs=out_specs if isinstance(out_shape, tuple) else out_specs[0],
         scratch_shapes=list(scratch),
+        input_output_aliases=aliases or {},
         compiler_params=pltpu.CompilerParams(vmem_limit_bytes=held + 6 * MIB),
         cost_estimate=pl.CostEstimate(
             flops=int(flops),
@@ -128,18 +129,18 @@
 
 
 def pack_columns(u, packed, zn):
-    peers, rows, lanes = packed.shape
+    pairs, _, rows, lanes = packed.shape
     f = rows // (zn // 2)
     yn = lanes // 2
     low = lax.broadcasted_iota(jnp.int32, (f, lanes), 1) < yn
-    for j in range(peers // 2):
+    for j in range(pairs):
         for zh in range(zn // 2):
             first = u[(2 * zh) * f : (2 * zh + 1) * f, j * lanes : (j + 1) * lanes]
             second = u[(2 * zh + 1) * f : (2 * zh + 2) * f, j * lanes : (j + 1) * lanes]
             even = jnp.where(low, first, pltpu.roll(second, yn, 1))
             odd = jnp.where(low, pltpu.roll(first, yn, 1), second)
-            packed[2 * j, zh * f : (zh + 1) * f, :] = even.astype(BF16)
-            packed[2 * j + 1, zh * f : (zh + 1) * f, :] = odd.astype(BF16)
+            packed[j, 0, zh * f : (zh + 1) * f, :] = even.astype(BF16)
+            packed[j, 1, zh * f : (zh + 1) * f, :] = odd.astype(BF16)
 
 
 def spread_kernel(got, v, w, xlo, xhi, zlo, zhi, ids):
@@ -219,21 +220,13 @@
 
 
 def first_kernel(
-    v, w, xlo, xhi, zlo, zhi, ids, a_far,
-    u_far, w_far, ids_far, packed, z_first, z_last, x_first, x_last,
-    e, u, a, sems,
+    v, w, xlo, xhi, zlo, zhi, a, u, packed, z_first, z_last, x_first, x_last, e
 ):
-    copies = Copies(sems)
-    a_copy = copies.start(a_far, a)
-    copies.start(w, w_far)
-    copies.start(ids, ids_far)
     x_before, x_after = xlo[...], xhi[...]
     zn = 4
     for z in range(zn):
         explicit_plane(z, v, w, zlo, zhi, x_before, x_after, e)
-    copies.wait(a_copy)
     u[...] = solve(e, a)
-    copies.start(u, u_far)
     f = zlo.shape[0]
     z_first[...] = u[0:f].astype(BF16)
     z_last[...] = u[(zn - 1) * f : zn * f].astype(BF16)
@@ -243,57 +236,52 @@
         x_first[r : r + 1] = u[r * xl : r * xl + 1]
         x_last[r : r + 1] = u[(r + 1) * xl - 1 : (r + 1) * xl]
     pack_columns(u, packed, zn)
-    copies.finish()
 
 
 def sample_kernel(packed, ids, sent_far, picked, sent, sems):
     copies = Copies(sems)
-    sample(packed, ids, picked, sent, lambda part: copies.start(sent.at[part], sent_far.at[part]))
+    sample(packed, ids, picked, sent, message_part(copies, sent, sent_far, 0))
     copies.finish()
 
 
+def message_part(copies, sent, far, which):
+    f = sent.shape[1]
+
+    def ready(part):
+        members, _, lanes = part
+        copies.start(sent.at[part], far.at[members, pl.ds(which * f, f), lanes])
+
+    return ready
+
+
 def second_kernel(
-    u_far, w_far, ids_far, zlo_far, zhi_far, xlo_far, xhi_far, a_far, packed_far, sent_far,
-    e, u, w, ids, zlo, zhi, xlo, xhi, a, packed, picked, sent, sems,
+    u, w, ids, zlo, zhi, xlo, xhi, a, sent_in, packed_far, sent_far,
+    e, after, packed, picked, sent, sems,
 ):
+    del sent_in
     copies = Copies(sems)
-    f = zlo.shape[0]
-    zn = u.shape[0] // f
-    first = [
-        copies.start(far, near)
-        for far, near in (
-            (w_far, w), (zlo_far, zlo), (xlo_far, xlo), (xhi_far, xhi),
-        )
-    ]
-    parts = [pl.ds(z * f, f) for z in range(zn)]
-    arriving = [copies.start(u_far.at[part], u.at[part]) for part in parts]
-    zhi_copy = copies.start(zhi_far, zhi)
-    a_copy = copies.start(a_far, a)
-    ids_copy = copies.start(ids_far, ids)
-    for copy in first + arriving[:1]:
-        copies.wait(copy)
+    zn = u.shape[0] // zlo.shape[0]
     x_before, x_after = xlo[...], xhi[...]
     for z in range(zn):
-        copies.wait(arriving[z + 1] if z < zn - 1 else zhi_copy)
         explicit_plane(z, u, w, zlo, zhi, x_before, x_after, e)
-    copies.wait(a_copy)
-    u[...] = solve(e, a)
-    pack_columns(u, packed, zn)
+    after[...] = solve(e, a)
+    pack_columns(after, packed, zn)
     copies.start(packed, packed_far)
-    copies.wait(ids_copy)
-    sample(packed, ids, picked, sent, lambda part: copies.start(sent.at[part], sent_far.at[part]))
+    sample(packed, ids, picked, sent, message_part(copies, sent, sent_far, 1))
     copies.finish()
 
 
 def sample(packed, ids, picked, out, ready):
-    peers, rows, lanes = packed.shape
+    pairs, _, rows, lanes = packed.shape
+    peers = 2 * pairs
     f = rows // 2
     yn = lanes // 2
     blocks = picked.shape[2] // lanes
     r = lax.broadcasted_iota(jnp.int32, (2 * lanes, lanes), 0)
     row_id = (r % yn) * 4 + r // yn
     for q in range(peers):
-        table = jnp.concatenate([packed[q, 0:f], packed[q, f:rows]], axis=1)
+        at = (q // 2, q % 2)
+        table = jnp.concatenate([packed[(*at, slice(0, f))], packed[(*at, slice(f, rows))]], axis=1)
         wanted = pltpu.roll(ids[q], (GROUP * q) % lanes, 1) if q else ids[q]
         for b in range(blocks):
             hot = jnp.where(row_id == wanted[b : b + 1], 1.0, 0.0).astype(BF16)
@@ -316,17 +304,17 @@
         ready((pl.ds(mh * per, per), slice(None), pl.ds(kg * lanes, lanes)))
 
 
-def gather_rows(got, turned, comps=3):
-    sources, f, slots = got.shape
+def gather_rows(got, start, turned, comps=3):
+    sources, both, slots = got.shape
     sides = 2
     peers = sources // sides
-    xl = f // comps
+    xl = both // 2 // comps
     for q in range(peers):
         for side in range(sides):
             for c in range(comps):
                 at = (c * peers + q) * xl
                 turned[at : at + xl, side * slots : (side + 1) * slots] = got[
-                    q * sides + side, c * xl : (c + 1) * xl
+                    q * sides + side, start + c * xl : start + (c + 1) * xl
                 ]
 
 
@@ -338,35 +326,38 @@
 
 
 def forward_kernel(
-    got_far, w_in, w_out, x_far, hidden_far, slope_far, predicted_far,
-    got, x, hidden, slope, predicted, sems,
+    scale, place, got_far, w_in_far, w_out_far, x, hidden, slope, d, away,
+    got, w_in, w_out, sems,
 ):
     copies = Copies(sems)
-    copies.wait(copies.start(got_far, got))
-    gather_rows(got, x)
-    copies.start(x, x_far)
+    f = got.shape[1] // 2
+    input_part = (slice(None), pl.ds(0, f), slice(None))
+    target_part = (slice(None), pl.ds(f, f), slice(None))
+    first = [copies.start(got_far.at[input_part], got.at[input_part])]
     wide = 256
-
-    def chunk(i, carry):
-        at = pl.ds(pl.multiple_of(i * wide, wide), wide)
+    count = hidden.shape[0] // wide
+    for i in range(count):
+        at = pl.ds(i * wide, wide)
+        first.append(copies.start(w_in_far.at[at], w_in.at[at]))
+    w_out_copy = copies.start(w_out_far, w_out)
+    target_copy = copies.start(got_far.at[target_part], got.at[target_part])
+    copies.wait(first[0])
+    gather_rows(got, 0, x)
+    for i in range(count):
+        copies.wait(first[1 + i])
+        at = slice(i * wide, (i + 1) * wide)
         pre = jnp.dot(w_in[at, :], x[...], preferred_element_type=F32)
         logistic = jax.nn.sigmoid(pre)
         hidden[at, :] = (pre * logistic).astype(BF16)
         slope[at, :] = (logistic * (1.0 + pre * (1.0 - logistic))).astype(slope.dtype)
-        return carry
-
-    lax.fori_loop(0, hidden.shape[0] // wide, chunk, 0)
-    copies.start(hidden, hidden_far)
-    copies.start(slope, slope_far)
-
-    def second(i, carry):
-        at = pl.ds(pl.multiple_of(i * wide, wide), wide)
-        predicted[at, :] = jnp.dot(w_out[at, :], hidden[...], preferred_element_type=F32)
-        return carry
-
-    lax.fori_loop(0, predicted.shape[0] // wide, second, 0)
-    copies.start(predicted, predicted_far)
-    copies.finish()
+    copies.wait(w_out_copy)
+    copies.wait(target_copy)
+    gather_rows(got, f, d)
+    for i in range(d.shape[0] // wide):
+        at = slice(i * wide, (i + 1) * wide)
+        predicted = jnp.dot(w_out[at, :], hidden[...], preferred_element_type=F32)
+        d[at] = ((predicted - d[at].astype(F32)) * scale).astype(BF16)
+    away_blocks(hidden, d, place[0], away, away.shape[0] // 4)
 
 
 def block_rows(array, y, core, rows):
@@ -374,32 +365,8 @@
 
 
 def away_blocks(array, right, core, away, rows):
-    for pair in range(away.shape[0] // (2 * rows)):
-        left = jnp.concatenate(
-            [block_rows(array, 2 * pair + k, 1 - core, rows) for k in range(2)], axis=0
-        )
-        away[2 * pair * rows : 2 * (pair + 1) * rows] = over_rows(left, right[...]).astype(BF16)
-
-
-def delta_out_kernel(
-    scale, place, got_far, predicted_far, hidden_far, d, away,
-    got, predicted, hidden, sems,
-):
-    copies = Copies(sems)
-    got_copy = copies.start(got_far, got)
-    count = 3
-    rows = d.shape[0] // count
-    parts = [pl.ds(k * rows, rows) for k in range(count)]
-    arriving = [copies.start(predicted_far.at[part], predicted.at[part]) for part in parts]
-    copies.start(hidden_far, hidden)
-    copies.wait(got_copy)
-    gather_rows(got, d)
-    for k in range(count):
-        copies.wait(arriving[k])
-        at = slice(k * rows, (k + 1) * rows)
-        d[at] = ((predicted[at] - d[at].astype(F32)) * scale).astype(BF16)
-    copies.finish()
-    away_blocks(hidden, d, place[0], away, away.shape[0] // 4)
+    left = jnp.concatenate([block_rows(array, y, 1 - core, rows) for y in range(4)], axis=0)
+    away[...] = over_rows(left, right[...]).astype(BF16)
 
 
 def delta_in_kernel(place, d, slope, w_out, x, din, away):
@@ -419,7 +386,7 @@
     core, y = place[0], place[1]
     rows = own.shape[0]
     half = rows // 2
-    for ks in ((2, 1), (3, 0)):
+    for ks in ((2, 1, 3, 0),):
         ys = [lax.rem(y + k, 4) for k in ks]
         blocks = jnp.concatenate([block_rows(array, at, core, rows) for at in ys], axis=0)
         value = over_rows(blocks, right[...])
@@ -516,64 +483,48 @@
     )
     zlo, zhi = shift((zhi, zlo), ("px", "tr"))
     message = shaped((members, f, peers * slots), BF16)
+    both = shaped((members, 2 * f, peers * slots), BF16)
     sample_flops = 2 * peers * f * 256 * members * slots
     sampling = [
         pltpu.VMEM((peers, 2 * f, lanes), BF16),
         pltpu.VMEM((peers, f, members * slots), F32),
         pltpu.VMEM(message.shape, BF16),
     ]
-    u, w_far, ids_far, packed, z_first, z_last, x_first, x_last = call(
+    blocks = shaped((peers // 2, 2, 2 * f, lanes), BF16)
+    half_blocks = shaped((peers // 2, 2 * f, lanes), BF16)
+    sampling[0] = pltpu.VMEM(blocks.shape, BF16)
+    u, packed, z_first, z_last, x_first, x_last = call(
         first_kernel,
-        (shaped((zn * f, total_y), F32), shaped(w.shape, BF16), ids_all)
-        + (shaped((peers, 2 * f, lanes), BF16), edge, edge, x_edge, x_edge),
-        (v, w, xlo, xhi, zlo, zhi, ids, inverse),
-        scratch=[
-            pltpu.VMEM((zn * f, total_y), BF16),
-            pltpu.VMEM((zn * f, total_y), F32),
-            pltpu.VMEM(inverse.shape, BF16),
-            pltpu.SemaphoreType.DMA((4,)),
-        ],
+        (shaped((zn * f, total_y), F32), blocks, edge, edge, x_edge, x_edge),
+        (v, w, xlo, xhi, zlo, zhi, inverse),
+        scratch=[pltpu.VMEM((zn * f, total_y), BF16)],
         flops=solve_flops,
-        far_in=(7,),
-        far_out=(0, 1, 2),
     )
     zlo, zhi = shift((z_last, z_first), ("px", "tr"))
     xlo, xhi = shift((x_last, x_first), "pz")
     sent = call(
         sample_kernel,
-        message,
+        both,
         (packed, ids),
         scratch=sampling[1:] + [pltpu.SemaphoreType.DMA((6,))],
         flops=sample_flops,
         far_out=(0,),
     )
-    sent, zlo, zhi, xlo, xhi = lax.optimization_barrier((sent, zlo, zhi, xlo, xhi))
-    rows_in = exchange(sent, ("pz", "tr"))
     packed, sent = call(
         second_kernel,
-        (shaped((peers, 2 * f, lanes), BF16), message),
-        (u, w_far, ids_far, zlo, zhi, xlo, xhi, inverse),
-        scratch=[
-            pltpu.VMEM((zn * f, total_y), BF16),
-            pltpu.VMEM((zn * f, total_y), F32),
-            pltpu.VMEM(w.shape, BF16),
-            pltpu.VMEM(ids_all.shape, jnp.int32),
-            pltpu.VMEM(edge.shape, BF16),
-            pltpu.VMEM(edge.shape, BF16),
-            pltpu.VMEM(x_edge.shape, F32),
-            pltpu.VMEM(x_edge.shape, F32),
-            pltpu.VMEM(inverse.shape, BF16),
-        ]
+        (blocks, both),
+        (u, w, ids, zlo, zhi, xlo, xhi, inverse, sent),
+        scratch=[pltpu.VMEM((zn * f, total_y), BF16), pltpu.VMEM((zn * f, total_y), F32)]
         + sampling
-        + [pltpu.SemaphoreType.DMA((20,))],
+        + [pltpu.SemaphoreType.DMA((7,))],
         flops=solve_flops + sample_flops,
-        far_in=range(8),
+        far_in=(8,),
         far_out=(0, 1),
-    )
-    sent, rows_in = lax.optimization_barrier((sent, rows_in))
-    rows_target = exchange(sent, ("pz", "tr"))
-    packed, rows_target = lax.optimization_barrier((packed, rows_target))
-    planes = exchange(packed, "pz")
+        aliases={8: 1},
+    )
+    rows_all = exchange(sent, ("pz", "tr"))
+    packed, rows_all = lax.optimization_barrier((packed, rows_all))
+    planes = exchange(packed.reshape(peers, 2 * f, lanes), "pz")
 
     member_in = weight_in[0]
     member_out = weight_out[0]
@@ -582,44 +533,29 @@
     spots = lax.axis_size("px")
     loss_scale = 1.0 / math.sqrt(spots * batch)
     matmul_flops = 2 * hid * width * batch
-    x, hidden, slope, predicted = call(
-        forward_kernel,
+    position = lax.axis_index("px")
+    place = jnp.stack([position & 1, position >> 1]).astype(jnp.int32)
+
+    def forward(*refs):
+        forward_kernel(loss_scale, *refs)
+
+    x, hidden, slope, d, away_out = call(
+        forward,
         (
             shaped((width, batch), BF16),
             shaped((hid, batch), BF16),
             shaped((hid, batch), BF16),
-            shaped((width, batch), F32),
+            shaped((width, batch), BF16),
+            shaped((hid // 2, width), BF16),
         ),
-        (rows_in, member_in.T, member_out.T),
+        (place, rows_all, member_in.T, member_out.T),
         scratch=[
-            pltpu.VMEM(message.shape, BF16),
-            pltpu.VMEM((width, batch), BF16),
-            pltpu.VMEM((hid, batch), BF16),
-            pltpu.VMEM((hid, batch), BF16),
-            pltpu.VMEM((width, batch), F32),
-            pltpu.SemaphoreType.DMA((5,)),
+            pltpu.VMEM(both.shape, BF16),
+            pltpu.VMEM((hid, width), BF16),
+            pltpu.VMEM((width, hid), BF16),
+            pltpu.SemaphoreType.DMA((8,)),
         ],
-        flops=2 * matmul_flops,
-        far_in=(0,),
-        far_out=range(4),
-    )
-    position = lax.axis_index("px")
-    place = jnp.stack([position % 2, position // 2]).astype(jnp.int32)
-
-    def delta_out(*refs):
-        delta_out_kernel(loss_scale, *refs)
-
-    d, away_out = call(
-        delta_out,
-        (shaped((width, batch), BF16), shaped((hid // 2, width), BF16)),
-        (place, rows_target, predicted, hidden),
-        scratch=[
-            pltpu.VMEM(message.shape, BF16),
-            pltpu.VMEM((width, batch), F32),
-            pltpu.VMEM((hid, batch), BF16),
-            pltpu.SemaphoreType.DMA((5,)),
-        ],
-        flops=matmul_flops // 2,
+        flops=matmul_flops * 5 // 2,
         far_in=(1, 2, 3),
     )
     got_out = swap_cores(away_out)
@@ -630,6 +566,7 @@
         flops=matmul_flops * 3 // 2,
     )
     got_in = swap_cores(away_in)
+    planes, got_out = lax.optimization_barrier((planes, got_out))
 
     def keep(array, right, got):
         rows, wide = got.shape[0] // 4, got.shape[1]
@@ -660,7 +597,7 @@
     arrived_in = shift_chips(*relay(*sides_in, arrived_in))
     share_out = finish(own_out, arrived_out)
     share_in = finish(own_in, arrived_in)
-    result = call(planes_kernel, shaped((comps, zn, yn, xn), F32), (planes,))
+    result = call(planes_kernel, shaped((comps, zn, yn, xn), F32), (planes,), flops=3e10)
     return (result.transpose(2, 1, 0, 3), share_in[None], share_out[None])
 
 

time: 171 us -> 165 us (0.965)
  waiting for transfers between devices: 49 us -> 61 us
  Pallas kernels: 34.8 us -> 25.2 us
  starting transfers between devices: 43.9 us -> 39.2 us
    pallas_call x15 -> x14, Pallas kernels: 34.8 us -> 25.2 us  [call(): pl.pallas_call(kernel, out_shape=pinned if isinstance(out_shape, tuple) e...]
    all_to_all x3 -> x2, waiting for transfers between devices: 40.8 us -> 50.3 us  [exchange(): return lax.all_to_all(array, axis, split_axis=0, concat_axis=0, tiled=True)]
    all_to_all x3 -> x2, starting transfers between devices: 17 us -> 12.8 us  [exchange(): return lax.all_to_all(array, axis, split_axis=0, concat_axis=0, tiled=True)]
    unnamed x40 -> x26, local copies, waits for them, and re-layouts: 9.81 us -> 8.13 us
  transfers between devices with their start and end apart: 19 -> 18, of which waited for: 9 -> 9; matrix products, arithmetic and copies ran while one was open for 4% -> 3% of each run, Pallas kernels for 14% -> 11%
where the time goes in v5:
time: 165 us
  waiting for transfers between devices  61 us (37%)
  starting transfers between devices  39.2 us (24%)
  blocking collectives  28.6 us (17%)
  Pallas kernels  25.2 us (15%)
  local copies, waits for them, and re-layouts  9.79 us (6%)
    all_to_all x2, waiting for transfers between devices, exchange(): return lax.all_to_all(array, axis, split_axis=0, concat_axis=0, tiled=True)  50.3 us
    all_to_all x1, blocking collectives, exchange(): return lax.all_to_all(array, axis, split_axis=0, concat_axis=0, tiled=True)  28.6 us
    pallas_call x14, Pallas kernels, call(): pl.pallas_call(kernel, out_shape=pinned if isinstance(out_shape, tuple) e...  25.2 us
    ppermute x6, starting transfers between devices, shift(): return (lax.ppermute(last, axis, up), lax.ppermute(first, axis, down))  12.9 us
    all_to_all x2, starting transfers between devices, exchange(): return lax.all_to_all(array, axis, split_axis=0, concat_axis=0, tiled=True)  12.8 us
    ppermute x8, starting transfers between devices, shift_chips(): return (lax.ppermute(forward, 'px', up), lax.ppermute(backward, 'px', down))  12.8 us
    unnamed x26, local copies, waits for them, and re-layouts  8.13 us
    ppermute x8, waiting for transfers between devices, shift_chips(): return (lax.ppermute(forward, 'px', up), lax.ppermute(backward, 'px', down))  5.79 us
  transfers between devices with their start and end apart: 18, of which 9 were waited for; matrix products, arithmetic and copies ran while one was open for 3% of the time, Pallas kernels for 11%

profile of v5, /device:TPU:2, one launch (start us, length us, event | category | flops | bytes accessed | tf_op | source)
XLA Modules:
  0.0 165.0 jit_solution(15063408755836438679)
XLA Ops:
  0.7 1.0 copy.23
  1.7 0.0 copy-start.9
  1.7 1.4 copy.22
  3.1 0.2 shard_map.94
  3.3 28.6 %all_to_all.15.got = bf16[16,152,128]{2,1,0:T(8,128)(2,1)S(1)} all-to-all(bf16[16,152,128]{2,1,0:T(8,128)(2,1)S(1)} %shard_map.94), channel_id=1, replica_groups=mesh['px'=8,'pz'=16,'tr'=2] {'pz'}, dimensions={0} | all-to-all | bytes 1245184 | tf_op jit(solution)/shard_map/all_to_all | solution.py:436
  31.9 0.3 shard_map.95
  32.2 2.2 %collective-permute-start = (bf16[48,1024]{1,0:T(8,128)(2,1)S(1)}, bf16[48,1024]{1,0:T(8,128)(2,1)S(1)}, u32[]{:S(2)}, u32[]{:S(2)}) collective-permute-start(bf16[48,1024]{1,0:T(8,128)(2,1)S(1)} %get-tuple-element.53), channel_id=1, source_target_pairs={{0,1},{1,32},{32,33},{33,64},{64,65},{65,96},{96,97},{97,128},{128... | collective-permute-start | bytes 294920 | tf_op jit(solution)/shard_map/ppermute | solution.py:81
  34.5 3.2 %collective-permute-start.1 = (bf16[48,1024]{1,0:T(8,128)(2,1)S(1)}, bf16[48,1024]{1,0:T(8,128)(2,1)S(1)}, u32[]{:S(2)}, u32[]{:S(2)}) collective-permute-start(bf16[48,1024]{1,0:T(8,128)(2,1)S(1)} %get-tuple-element.54), channel_id=1, source_target_pairs={{1,0},{32,1},{33,32},{64,33},{65,64},{96,65},{97,96},{128,97},{129... | collective-permute-start | bytes 294920 | tf_op jit(solution)/shard_map/ppermute | solution.py:81
  37.7 0.3 convert_element_type.11.a
  38.0 2.5 %collective-permute-done.zlo = bf16[48,1024]{1,0:T(8,128)(2,1)S(1)} collective-permute-done((bf16[48,1024]{1,0:T(8,128)(2,1)S(1)}, bf16[48,1024]{1,0:T(8,128)(2,1)S(1)}, u32[]{:S(2)}, u32[]{:S(2)}) %collective-permute-start) | collective-permute-done | bytes 98336 | tf_op jit(solution)/shard_map/ppermute | solution.py:81
  40.6 0.4 collective-permute-done.1.zhi
  41.0 1.3 shard_map.96
  42.3 0.3 collective-permute-start.2
  42.5 5.2 %collective-permute-start.3 = (bf16[48,1024]{1,0:T(8,128)(2,1)S(1)}, bf16[48,1024]{1,0:T(8,128)(2,1)S(1)}, u32[]{:S(2)}, u32[]{:S(2)}) collective-permute-start(bf16[48,1024]{1,0:T(8,128)(2,1)S(1)} %get-tuple-element.58), channel_id=1, source_target_pairs={{1,0},{32,1},{33,32},{64,33},{65,64},{96,65},{97,96},{128,97},{129... | collective-permute-start | bytes 294920 | tf_op jit(solution)/shard_map/ppermute | solution.py:81
  47.7 1.5 collective-permute-start.4
  49.2 0.5 collective-permute-start.5
  49.7 2.8 %shard_map.97.sent_in = bf16[32,96,384]{2,1,0:T(8,128)(2,1)} custom-call(bf16[8,2,96,128]{3,2,1,0:T(8,128)(2,1)S(1)} %get-tuple-element.61.packed, s32[16,8,128]{2,1,0:T(8,128)S(1)} %get-tuple-element.56.ids), custom_call_target="tpu_custom_call" | custom-call | flops 301989888 | bytes 2818048 | tf_op jit(solution)/shard_map/pallas_call | solution.py:35
  52.5 0.1 collective-permute-done.4.xlo
  52.6 1.7 %collective-permute-done.5.xhi = f32[12,1024]{1,0:T(8,128)S(1)} collective-permute-done((f32[12,1024]{1,0:T(8,128)S(1)}, f32[12,1024]{1,0:T(8,128)S(1)}, u32[]{:S(2)}, u32[]{:S(2)}) %collective-permute-start.5) | collective-permute-done | bytes 49184 | tf_op jit(solution)/shard_map/ppermute | solution.py:81
  54.4 3.8 %shard_map.98 = (bf16[8,2,96,128]{3,2,1,0:T(8,128)(2,1)}, bf16[32,96,384]{2,1,0:T(8,128)(2,1)}) custom-call(f32[192,1024]{1,0:T(8,128)S(1)} %get-tuple-element.55.u, bf16[64,1024]{1,0:T(8,128)(2,1)S(1)} %get-tuple-element.50.w, s32[16,8,128]{2,1,0:T(8,128)S(1)} %get-tuple-element.56.ids, ...), custom_call_target="tpu_custom_call", output_to_operand_aliasing={{1}: (8, {})} | custom-call | flops 704643072 | bytes 8486912 | tf_op jit(solution)/shard_map/pallas_call | solution.py:35
  58.2 7.3 %all-to-all-start.1 = ((bf16[32,96,384]{2,1,0:T(8,128)(2,1)}), bf16[32,96,384]{2,1,0:T(8,128)(2,1)}, u32[]{:S(2)}, u32[]{:S(2)}) async-start(bf16[32,96,384]{2,1,0:T(8,128)(2,1)} %get-tuple-element.63), calls=%async_computation.1 | async-start | bytes 4718592 | tf_op jit(solution)/shard_map/all_to_all | solution.py:436
  65.5 1.6 copy.13
  67.1 1.7 %copy.14.refs_3_ = bf16[768,1024]{1,0:T(8,128)(2,1)} copy(bf16[768,1024]{0,1:T(8,128)(2,1)S(1)} %bitcast.22) | data formatting | bytes 3145728 | tf_op jit(solution)/shard_map/transpose | solution.py:551
  68.8 0.1 pad_add_fusion.refs_0_.place
  68.8 50.3 %all-to-all-done.1.refs_1_ = bf16[32,96,384]{2,1,0:T(8,128)(2,1)} async-done(((bf16[32,96,384]{2,1,0:T(8,128)(2,1)}), bf16[32,96,384]{2,1,0:T(8,128)(2,1)}, u32[]{:S(2)}, u32[]{:S(2)}) %all-to-all-start.1) | async-done | bytes 2359328 | tf_op jit(solution)/shard_map/all_to_all | solution.py:436
  119.1 5.6 %all-to-all-start.2 = ((bf16[16,96,128]{2,1,0:T(8,128)(2,1)}), bf16[16,96,128]{2,1,0:T(8,128)(2,1)S(1)}, u32[]{:S(2)}, u32[]{:S(2)}) async-start(bf16[16,96,128]{2,1,0:T(8,128)(2,1)} %bitcast.5), calls=%async_computation.2 | async-start | bytes 786432 | tf_op jit(solution)/shard_map/all_to_all | solution.py:436
  124.7 7.5 %shard_map.99 = (bf16[768,768]{1,0:T(8,128)(2,1)S(1)}, bf16[1024,768]{1,0:T(8,128)(2,1)S(1)}, bf16[1024,768]{1,0:T(8,128)(2,1)S(1)}, bf16[768,768]{1,0:T(8,128)(2,1)S(1)}, bf16[512,768]{1,0:T(8,128)(2,1)}) custom-call(s32[2]{0:T(128)S(1)} %pad_add_fusion.refs_0_.place, bf16[32,96,384]{2,1,0:T(8,128)(2,1)} %all-to-all-done.1.refs_1_, ...), custom_call_target="tpu_custom_call" | custom-call | flops 3019898880 | bytes 11796488 | tf_op jit(solution)/shard_map/pallas_call | solution.py:35
  132.2 0.1 collective-permute-start.6
  132.3 4.2 %shard_map.101 = (bf16[1024,768]{1,0:T(8,128)(2,1)S(1)}, bf16[384,1024]{1,0:T(8,128)(2,1)}) custom-call(s32[2]{0:T(128)S(1)} %pad_add_fusion.refs_0_.place, bf16[768,768]{1,0:T(8,128)(2,1)S(1)} %get-tuple-element.69.d.right, bf16[1024,768]{1,0:T(8,128)(2,1)S(1)} %get-tuple-element.70.slope, bf16[1024,768]{1,0:T(8,128)(2,1)S(1)} %bitcast.23, ...), custom_call_target="tpu_custom_call" | custom-call | flops 1811939328 | bytes 7864328 | tf_op jit(solution)/shard_map/pallas_call | solution.py:35
  136.4 0.6 collective-permute-start.7
  137.0 1.4 copy-done.2
  138.4 1.3 copy-done.6
  139.7 2.0 %shard_map.102 = (f32[128,768]{1,0:T(8,128)S(1)}, bf16[128,768]{1,0:T(8,128)(2,1)S(1)}, bf16[128,768]{1,0:T(8,128)(2,1)S(1)}, bf16[64,768]{1,0:T(8,128)(2,1)S(1)}, bf16[64,768]{1,0:T(8,128)(2,1)S(1)}) custom-call(s32[2]{0:T(128)S(1)} %pad_add_fusion.refs_0_.place, bf16[1024,768]{1,0:T(8,128)(2,1)S(1)} %copy-done.2, bf16[768,768]{1,0:T(8,128)(2,1)S(1)} %copy-done.6, ...), custom_call_target="tpu_custom_call" | custom-call | flops 603979776 | bytes 4521992 | tf_op jit(solution)/shard_map/pallas_call | solution.py:35
  141.8 2.6 %collective-permute-start.9 = (bf16[64,768]{1,0:T(8,128)(2,1)S(1)}, bf16[64,768]{1,0:T(8,128)(2,1)S(1)}, u32[]{:S(2)}, u32[]{:S(2)}) collective-permute-start(bf16[64,768]{1,0:T(8,128)(2,1)S(1)} %get-tuple-element.83), channel_id=1, source_target_pairs={{64,0},{96,32},{128,64},{160,96},{192,128},{224,160},{0,192},{32,2... | collective-permute-start | bytes 294920 | tf_op jit(solution)/shard_map/ppermute | solution.py:448
  144.4 1.3 shard_map.103
  145.7 1.2 collective-permute-start.10
  146.9 2.2 %collective-permute-start.11 = (bf16[48,1024]{1,0:T(8,128)(2,1)S(1)}, bf16[48,1024]{1,0:T(8,128)(2,1)S(1)}, u32[]{:S(2)}, u32[]{:S(2)}) collective-permute-start(bf16[48,1024]{1,0:T(8,128)(2,1)S(1)} %get-tuple-element.87), channel_id=1, source_target_pairs={{64,0},{96,32},{128,64},{160,96},{192,128},{224,160},{0,192},{32,2... | collective-permute-start | bytes 294920 | tf_op jit(solution)/shard_map/ppermute | solution.py:448
  149.1 1.9 %collective-permute-done.8.from_before = bf16[64,768]{1,0:T(8,128)(2,1)S(1)} collective-permute-done((bf16[64,768]{1,0:T(8,128)(2,1)S(1)}, bf16[64,768]{1,0:T(8,128)(2,1)S(1)}, u32[]{:S(2)}, u32[]{:S(2)}) %collective-permute-start.8) | collective-permute-done | bytes 98336 | tf_op jit(solution)/shard_map/ppermute | solution.py:448
  151.1 1.2 collective-permute-done.10.from_before
  152.4 1.1 collective-permute-start.12
  153.4 2.5 %collective-permute-start.13 = (bf16[96,1024]{1,0:T(8,128)(2,1)S(1)}, bf16[96,1024]{1,0:T(8,128)(2,1)S(1)}, u32[]{:S(2)}, u32[]{:S(2)}) collective-permute-start(bf16[96,1024]{1,0:T(8,128)(2,1)S(1)} %get-tuple-element.91), channel_id=1, source_target_pairs={{64,0},{96,32},{128,64},{160,96},{192,128},{224,160},{0,192},{32,2... | collective-permute-start | bytes 589832 | tf_op jit(solution)/shard_map/ppermute | solution.py:448
  155.9 3.2 %collective-permute-start.15 = (bf16[128,768]{1,0:T(8,128)(2,1)S(1)}, bf16[128,768]{1,0:T(8,128)(2,1)S(1)}, u32[]{:S(2)}, u32[]{:S(2)}) collective-permute-start(bf16[128,768]{1,0:T(8,128)(2,1)S(1)} %get-tuple-element.94), channel_id=1, source_target_pairs={{64,0},{96,32},{128,64},{160,96},{192,128},{224,160},{0,192},{32,2... | collective-permute-start | bytes 589832 | tf_op jit(solution)/shard_map/ppermute | solution.py:448
  159.1 0.2 shard_map.100
  159.3 1.4 copy.15
  160.7 0.8 collective-permute-done.12.from_before
  161.5 0.8 shard_map.106
  162.3 1.9 %collective-permute-done.14.from_before = bf16[128,768]{1,0:T(8,128)(2,1)S(1)} collective-permute-done((bf16[128,768]{1,0:T(8,128)(2,1)S(1)}, bf16[128,768]{1,0:T(8,128)(2,1)S(1)}, u32[]{:S(2)}, u32[]{:S(2)}) %collective-permute-start.14) | collective-permute-done | bytes 196640 | tf_op jit(solution)/shard_map/ppermute | solution.py:448
  164.2 0.8 shard_map.107
  (32 shorter events, 0.2 us)
Async XLA Ops:
  0.6 2.4 %copy-start.8 = (s32[1,1,1,32]{3,2,1,0:T(1,128)S(1)}, s32[1,1,1,32]{3,2,1,0:T(1,128)}, u32[]{:S(2)}) copy-start(s32[1,1,1,32]{3,2,1,0:T(1,128)} %param.11) | copy-start | bytes 388
  0.6 2.4 %copy-start.7 = (s32[1,1,1,32,24]{3,4,2,1,0:T(8,128)S(1)}, s32[1,1,1,32,24]{3,4,2,1,0:T(8,128)}, u32[]{:S(2)}) copy-start(s32[1,1,1,32,24]{3,4,2,1,0:T(8,128)} %param.10) | copy-start | bytes 9220
  1.7 36.0 %copy-start.9 = (f32[1024,1024]{1,0:T(8,128)S(1)}, f32[1024,1024]{1,0:T(8,128)}, u32[]{:S(2)}) copy-start(f32[1024,1024]{1,0:T(8,128)} %param.9) | copy-start | bytes 12582916
  32.2 8.3 %collective-permute-start = (bf16[48,1024]{1,0:T(8,128)(2,1)S(1)}, bf16[48,1024]{1,0:T(8,128)(2,1)S(1)}, u32[]{:S(2)}, u32[]{:S(2)}) collective-permute-start(bf16[48,1024]{1,0:T(8,128)(2,1)S(1)} %get-tuple-element.53), channel_id=1, source_target_pairs={{0,1},{1,32},{32,33},{33,64},{64,65},{65,96},{96,97},{97,128},{128... | collective-permute-start | bytes 294920 | tf_op jit(solution)/shard_map/ppermute | solution.py:81
  34.5 6.5 %collective-permute-start.1 = (bf16[48,1024]{1,0:T(8,128)(2,1)S(1)}, bf16[48,1024]{1,0:T(8,128)(2,1)S(1)}, u32[]{:S(2)}, u32[]{:S(2)}) collective-permute-start(bf16[48,1024]{1,0:T(8,128)(2,1)S(1)} %get-tuple-element.54), channel_id=1, source_target_pairs={{1,0},{32,1},{33,32},{64,33},{65,64},{96,65},{97,96},{128,97},{129... | collective-permute-start | bytes 294920 | tf_op jit(solution)/shard_map/ppermute | solution.py:81
  42.3 12.1 %collective-permute-start.2 = (bf16[48,1024]{1,0:T(8,128)(2,1)S(1)}, bf16[48,1024]{1,0:T(8,128)(2,1)S(1)}, u32[]{:S(2)}, u32[]{:S(2)}) collective-permute-start(bf16[48,1024]{1,0:T(8,128)(2,1)S(1)} %get-tuple-element.57), channel_id=1, source_target_pairs={{0,1},{1,32},{32,33},{33,64},{64,65},{65,96},{96,97},{97,128},{128... | collective-permute-start | bytes 294920 | tf_op jit(solution)/shard_map/ppermute | solution.py:81
  42.5 11.9 %collective-permute-start.3 = (bf16[48,1024]{1,0:T(8,128)(2,1)S(1)}, bf16[48,1024]{1,0:T(8,128)(2,1)S(1)}, u32[]{:S(2)}, u32[]{:S(2)}) collective-permute-start(bf16[48,1024]{1,0:T(8,128)(2,1)S(1)} %get-tuple-element.58), channel_id=1, source_target_pairs={{1,0},{32,1},{33,32},{64,33},{65,64},{96,65},{97,96},{128,97},{129... | collective-permute-start | bytes 294920 | tf_op jit(solution)/shard_map/ppermute | solution.py:81
  47.7 4.9 %collective-permute-start.4 = (f32[12,1024]{1,0:T(8,128)S(1)}, f32[12,1024]{1,0:T(8,128)S(1)}, u32[]{:S(2)}, u32[]{:S(2)}) collective-permute-start(f32[12,1024]{1,0:T(8,128)S(1)} %get-tuple-element.59), channel_id=1, source_target_pairs={{0,2},{2,4},{4,6},{6,8},{8,10},{10,12},{12,14},{14,16},{16,18},{18... | collective-permute-start | bytes 147464 | tf_op jit(solution)/shard_map/ppermute | solution.py:81
  49.2 5.2 %collective-permute-start.5 = (f32[12,1024]{1,0:T(8,128)S(1)}, f32[12,1024]{1,0:T(8,128)S(1)}, u32[]{:S(2)}, u32[]{:S(2)}) collective-permute-start(f32[12,1024]{1,0:T(8,128)S(1)} %get-tuple-element.60), channel_id=1, source_target_pairs={{2,0},{4,2},{6,4},{8,6},{10,8},{12,10},{14,12},{16,14},{18,16},{20... | collective-permute-start | bytes 147464 | tf_op jit(solution)/shard_map/ppermute | solution.py:81
  58.2 7.3 %copy-start.10 = (bf16[1,768,1024]{2,1,0:T(8,128)(2,1)S(1)}, bf16[1,768,1024]{2,1,0:T(8,128)(2,1)}, u32[]{:S(2)}) copy-start(bf16[1,768,1024]{2,1,0:T(8,128)(2,1)} %param.12) | copy-start | bytes 4718596
  58.2 61.0 %all-to-all-start.1 = ((bf16[32,96,384]{2,1,0:T(8,128)(2,1)}), bf16[32,96,384]{2,1,0:T(8,128)(2,1)}, u32[]{:S(2)}, u32[]{:S(2)}) async-start(bf16[32,96,384]{2,1,0:T(8,128)(2,1)} %get-tuple-element.63), calls=%async_computation.1 | async-start | bytes 4718592 | tf_op jit(solution)/shard_map/all_to_all | solution.py:436
  65.5 1.6 copy-start
  119.1 17.9 %all-to-all-start.2 = ((bf16[16,96,128]{2,1,0:T(8,128)(2,1)}), bf16[16,96,128]{2,1,0:T(8,128)(2,1)S(1)}, u32[]{:S(2)}, u32[]{:S(2)}) async-start(bf16[16,96,128]{2,1,0:T(8,128)(2,1)} %bitcast.5), calls=%async_computation.2 | async-start | bytes 786432 | tf_op jit(solution)/shard_map/all_to_all | solution.py:436
  132.1 4.3 %copy-start.1 = (bf16[1024,768]{1,0:T(8,128)(2,1)}, bf16[1024,768]{1,0:T(8,128)(2,1)S(1)}, u32[]{:S(2)}) copy-start(bf16[1024,768]{1,0:T(8,128)(2,1)S(1)} %get-tuple-element.72.array) | copy-start | bytes 4718596
  132.2 4.3 %copy-start.3 = (bf16[768,768]{1,0:T(8,128)(2,1)}, bf16[768,768]{1,0:T(8,128)(2,1)S(1)}, u32[]{:S(2)}) copy-start(bf16[768,768]{1,0:T(8,128)(2,1)S(1)} %get-tuple-element.68.x.array) | copy-start | bytes 3538948
  132.2 4.3 %copy-start.5 = (bf16[768,768]{1,0:T(8,128)(2,1)}, bf16[768,768]{1,0:T(8,128)(2,1)S(1)}, u32[]{:S(2)}) copy-start(bf16[768,768]{1,0:T(8,128)(2,1)S(1)} %get-tuple-element.69.d.right) | copy-start | bytes 3538948
  132.2 4.8 %collective-permute-start.6 = (bf16[512,768]{1,0:T(8,128)(2,1)}, bf16[512,768]{1,0:T(8,128)(2,1)}, u32[]{:S(2)}, u32[]{:S(2)}) collective-permute-start(bf16[512,768]{1,0:T(8,128)(2,1)} %get-tuple-element.66), channel_id=1, source_target_pairs={{0,32},{32,0},{64,96},{96,64},{128,160},{160,128},{192,224},{224,1... | collective-permute-start | bytes 2359304 | tf_op jit(solution)/shard_map/ppermute | solution.py:441
  136.4 7.9 %collective-permute-start.7 = (bf16[384,1024]{1,0:T(8,128)(2,1)}, bf16[384,1024]{1,0:T(8,128)(2,1)S(1)}, u32[]{:S(2)}, u32[]{:S(2)}) collective-permute-start(bf16[384,1024]{1,0:T(8,128)(2,1)} %get-tuple-element.75), channel_id=1, source_target_pairs={{0,32},{32,0},{64,96},{96,64},{128,160},{160,128},{192,224},{224,1... | collective-permute-start | bytes 2359304 | tf_op jit(solution)/shard_map/ppermute | solution.py:441
  137.0 1.4 copy-start.2
  138.4 1.3 copy-start.6
  139.7 4.7 %copy-start.4 = (bf16[768,768]{1,0:T(8,128)(2,1)S(1)}, bf16[768,768]{1,0:T(8,128)(2,1)}, u32[]{:S(2)}) copy-start(bf16[768,768]{1,0:T(8,128)(2,1)} %copy-done.3) | copy-start | bytes 3538948
  141.8 7.4 %collective-permute-start.9 = (bf16[64,768]{1,0:T(8,128)(2,1)S(1)}, bf16[64,768]{1,0:T(8,128)(2,1)S(1)}, u32[]{:S(2)}, u32[]{:S(2)}) collective-permute-start(bf16[64,768]{1,0:T(8,128)(2,1)S(1)} %get-tuple-element.83), channel_id=1, source_target_pairs={{64,0},{96,32},{128,64},{160,96},{192,128},{224,160},{0,192},{32,2... | collective-permute-start | bytes 294920 | tf_op jit(solution)/shard_map/ppermute | solution.py:448
  144.4 6.7 %collective-permute-start.8 = (bf16[64,768]{1,0:T(8,128)(2,1)S(1)}, bf16[64,768]{1,0:T(8,128)(2,1)S(1)}, u32[]{:S(2)}, u32[]{:S(2)}) collective-permute-start(bf16[64,768]{1,0:T(8,128)(2,1)S(1)} %get-tuple-element.82), channel_id=1, source_target_pairs={{0,64},{32,96},{64,128},{96,160},{128,192},{160,224},{192,0},{224,... | collective-permute-start | bytes 294920 | tf_op jit(solution)/shard_map/ppermute | solution.py:448
  145.7 6.6 %collective-permute-start.10 = (bf16[48,1024]{1,0:T(8,128)(2,1)S(1)}, bf16[48,1024]{1,0:T(8,128)(2,1)S(1)}, u32[]{:S(2)}, u32[]{:S(2)}) collective-permute-start(bf16[48,1024]{1,0:T(8,128)(2,1)S(1)} %get-tuple-element.86), channel_id=1, source_target_pairs={{0,64},{32,96},{64,128},{96,160},{128,192},{160,224},{192,0},{224,... | collective-permute-start | bytes 294920 | tf_op jit(solution)/shard_map/ppermute | solution.py:448
  146.9 5.4 %collective-permute-start.11 = (bf16[48,1024]{1,0:T(8,128)(2,1)S(1)}, bf16[48,1024]{1,0:T(8,128)(2,1)S(1)}, u32[]{:S(2)}, u32[]{:S(2)}) collective-permute-start(bf16[48,1024]{1,0:T(8,128)(2,1)S(1)} %get-tuple-element.87), channel_id=1, source_target_pairs={{64,0},{96,32},{128,64},{160,96},{192,128},{224,160},{0,192},{32,2... | collective-permute-start | bytes 294920 | tf_op jit(solution)/shard_map/ppermute | solution.py:448
  152.4 9.1 %collective-permute-start.12 = (bf16[96,1024]{1,0:T(8,128)(2,1)S(1)}, bf16[96,1024]{1,0:T(8,128)(2,1)S(1)}, u32[]{:S(2)}, u32[]{:S(2)}) collective-permute-start(bf16[96,1024]{1,0:T(8,128)(2,1)S(1)} %get-tuple-element.90), channel_id=1, source_target_pairs={{0,64},{32,96},{64,128},{96,160},{128,192},{160,224},{192,0},{224,... | collective-permute-start | bytes 589832 | tf_op jit(solution)/shard_map/ppermute | solution.py:448
  153.4 8.1 %collective-permute-start.13 = (bf16[96,1024]{1,0:T(8,128)(2,1)S(1)}, bf16[96,1024]{1,0:T(8,128)(2,1)S(1)}, u32[]{:S(2)}, u32[]{:S(2)}) collective-permute-start(bf16[96,1024]{1,0:T(8,128)(2,1)S(1)} %get-tuple-element.91), channel_id=1, source_target_pairs={{64,0},{96,32},{128,64},{160,96},{192,128},{224,160},{0,192},{32,2... | collective-permute-start | bytes 589832 | tf_op jit(solution)/shard_map/ppermute | solution.py:448
  155.9 8.3 %collective-permute-start.14 = (bf16[128,768]{1,0:T(8,128)(2,1)S(1)}, bf16[128,768]{1,0:T(8,128)(2,1)S(1)}, u32[]{:S(2)}, u32[]{:S(2)}) collective-permute-start(bf16[128,768]{1,0:T(8,128)(2,1)S(1)} %get-tuple-element.93), channel_id=1, source_target_pairs={{0,64},{32,96},{64,128},{96,160},{128,192},{160,224},{192,0},{224,... | collective-permute-start | bytes 589832 | tf_op jit(solution)/shard_map/ppermute | solution.py:448
  155.9 8.3 %collective-permute-start.15 = (bf16[128,768]{1,0:T(8,128)(2,1)S(1)}, bf16[128,768]{1,0:T(8,128)(2,1)S(1)}, u32[]{:S(2)}, u32[]{:S(2)}) collective-permute-start(bf16[128,768]{1,0:T(8,128)(2,1)S(1)} %get-tuple-element.94), channel_id=1, source_target_pairs={{64,0},{96,32},{128,64},{160,96},{192,128},{224,160},{0,192},{32,2... | collective-permute-start | bytes 589832 | tf_op jit(solution)/shard_map/ppermute | solution.py:448

commit v6 on v5

--- a/solution.py
+++ b/solution.py
@@ -85,16 +85,19 @@
 GROUP = 8
 
 
-def columns_kernel(v, w, index, counts, out, edge):
-    comps, zn, yn, xn = v.shape
+def columns_kernel(v_far, w_far, index_far, counts_far, out, v, w, index, counts, edge, sems):
+    copies = Copies(sems)
+    for far, near in ((index_far, index), (counts_far, counts), (w_far, w), (v_far, v)):
+        copies.start(far, near)
+    copies.finish()
+    yn, comps, zn, xn = v.shape
     peers = out.shape[0]
     xl = xn // peers
     lanes_of = out.shape[2]
     half = (comps + 1) * xl
     for zh in range(zn // 2):
         for c in range(comps + 1):
-            source = w if c == comps else v.at[c]
-            pair = [source[z].astype(F32) for z in (2 * zh, 2 * zh + 1)]
+            pair = [w[:, z, :] if c == comps else v[:, c, z, :] for z in (2 * zh, 2 * zh + 1)]
             turned = jnp.concatenate(pair, axis=0).T
             base = zh * half + c * xl
             for q in range(peers):
@@ -382,42 +385,91 @@
     away_blocks(x, din, place[0], away, away.shape[0] // 4)
 
 
-def keep_kernel(place, array, right, got, own, plus, minus, top, bottom):
+def fold(block, rows, width):
+    extra = rows - block.shape[0]
+    pieces = [block[g * extra : (g + 1) * extra, width:] for g in range(block.shape[0] // extra)]
+    return jnp.concatenate([block[:, :width], jnp.concatenate(pieces, axis=1)], axis=0)
+
+
+def unfold(block, rows):
+    extra = block.shape[0] - rows
+    count = rows // extra
+    wide = block.shape[1] // count
+    pieces = [block[rows:, g * wide : (g + 1) * wide] for g in range(count)]
+    return jnp.concatenate([block[:rows], jnp.concatenate(pieces, axis=0)], axis=1)
+
+
+def own_blocks(place, copies, array_far, left):
     core, y = place[0], place[1]
-    rows = own.shape[0]
+    rows = left.shape[0] // 4
+    started = []
+    for n, k in enumerate((2, 1, 3, 0)):
+        at = (2 * lax.rem(y + k, 4) + core) * rows
+        source = array_far.at[pl.ds(pl.multiple_of(at, rows), rows)]
+        started.append(copies.start(source, left.at[pl.ds(n * rows, rows)]))
+    return started
+
+
+def add_other_core(place, value, got, n, k):
+    rows = value.shape[0] // 4
+    at = pl.multiple_of(lax.rem(place[1] + k, 4) * rows, rows)
+    return value[n * rows : (n + 1) * rows] + got[pl.ds(at, rows), :].astype(F32)
+
+
+def keep_out_kernel(place, hidden_far, d_far, got, own, plus, minus, far, left, d, sems):
+    copies = Copies(sems)
+    copies.start(d_far, d)
+    own_blocks(place, copies, hidden_far, left)
+    copies.finish()
+    value = over_rows(left[...], d[...])
+    far[...] = add_other_core(place, value, got, 0, 2).astype(BF16)
+    plus[...] = add_other_core(place, value, got, 1, 1).astype(BF16)
+    minus[...] = add_other_core(place, value, got, 2, 3).astype(BF16)
+    own[...] = add_other_core(place, value, got, 3, 0)
+
+
+def keep_in_kernel(
+    place, x_far, din, got, plus_out, minus_out, far_out, own, plus, minus, top, bottom, left, sems
+):
+    copies = Copies(sems)
+    own_blocks(place, copies, x_far, left)
+    rows, width = plus_out.shape
     half = rows // 2
-    for ks in ((2, 1, 3, 0),):
-        ys = [lax.rem(y + k, 4) for k in ks]
-        blocks = jnp.concatenate([block_rows(array, at, core, rows) for at in ys], axis=0)
-        value = over_rows(blocks, right[...])
-        for n, (k, at) in enumerate(zip(ks, ys)):
-            block = value[n * rows : (n + 1) * rows]
-            block = block + got[pl.ds(pl.multiple_of(at * rows, rows), rows), :].astype(F32)
-            if k == 0:
-                own[...] = block
-            elif k == 1:
-                plus[...] = block.astype(BF16)
-            elif k == 3:
-                minus[...] = block.astype(BF16)
-            else:
-                top[...] = block[:half].astype(BF16)
-                bottom[...] = block[half:].astype(BF16)
+    plus[0] = plus_out[...]
+    minus[0] = minus_out[...]
+    top[0] = far_out[:half]
+    bottom[0] = far_out[half:]
+    copies.finish()
+    value = over_rows(left[...], din[...])
+    far = fold(add_other_core(place, value, got, 0, 2), rows, width).astype(BF16)
+    top[1] = far[:half]
+    bottom[1] = far[half:]
+    plus[1] = fold(add_other_core(place, value, got, 1, 1), rows, width).astype(BF16)
+    minus[1] = fold(add_other_core(place, value, got, 2, 3), rows, width).astype(BF16)
+    own[...] = add_other_core(place, value, got, 3, 0)
 
 
 def relay_kernel(plus, minus, from_before, from_after, plus_out, minus_out):
-    half = from_before.shape[0]
-    plus_out[:half] = (plus[:half].astype(F32) + from_before[...].astype(F32)).astype(BF16)
-    plus_out[half:] = plus[half:]
-    minus_out[:half] = minus[:half]
-    minus_out[half:] = (minus[half:].astype(F32) + from_after[...].astype(F32)).astype(BF16)
-
-
-def finish_kernel(own, from_before, from_after, share):
-    share[...] = own[...] + from_before[...].astype(F32) + from_after[...].astype(F32)
+    half = from_before.shape[1]
+    for which in range(plus.shape[0]):
+        plus_out[which, :half] = (
+            plus[which, :half].astype(F32) + from_before[which].astype(F32)
+        ).astype(BF16)
+        plus_out[which, half:] = plus[which, half:]
+        minus_out[which, :half] = minus[which, :half]
+        minus_out[which, half:] = (
+            minus[which, half:].astype(F32) + from_after[which].astype(F32)
+        ).astype(BF16)
+
+
+def finish_kernel(own_out, own_in, from_before, from_after, share_out, share_in):
+    total = [from_before[k].astype(F32) + from_after[k].astype(F32) for k in range(2)]
+    share_out[...] = own_out[...] + total[0]
+    share_in[...] = own_in[...] + unfold(total[1], share_in.shape[0])
 
 
 def planes_kernel(got, out):
-    comps, zn, yn, xn = out.shape
+    yn, comps, zn, xn = out.shape
     peers = got.shape[0]
     xl = xn // peers
     f = comps * xl
@@ -428,8 +480,8 @@
                 [got[q, base : base + xl, :] for q in range(peers)], axis=0
             ).astype(F32)
             turned = block.T
-            out[c, 2 * zh] = turned[0:yn]
-            out[c, 2 * zh + 1] = turned[yn : 2 * yn]
+            out[:, c, 2 * zh, :] = turned[0:yn]
+            out[:, c, 2 * zh + 1, :] = turned[yn : 2 * yn]
 
 
 def exchange(array, axis):
@@ -457,17 +509,24 @@
     lanes = 2 * yn
     members, slots = row_index.shape[3:]
 
-    v = velocity.astype(BF16).transpose(2, 1, 0, 3)
     sent = call(
         columns_kernel,
         shaped((peers, 2 * (f + xl) + HALO_ROWS, lanes), BF16),
         (
-            v,
-            viscosity.astype(BF16).transpose(1, 0, 2),
+            velocity.transpose(0, 2, 1, 3),
+            viscosity,
             row_index.reshape(members, slots).T,
             row_counts.reshape(1, members),
         ),
-        scratch=[pltpu.VMEM((peers * HALO_ROWS, lanes), F32)],
+        scratch=[
+            pltpu.VMEM((yn, comps, zn, xn), F32),
+            pltpu.VMEM((yn, zn, xn), F32),
+            pltpu.VMEM((slots, members), jnp.int32),
+            pltpu.VMEM((1, members), jnp.int32),
+            pltpu.VMEM((peers * HALO_ROWS, lanes), F32),
+            pltpu.SemaphoreType.DMA((4,)),
+        ],
+        far_in=range(4),
     )
     inverse = implicit_inverse.astype(BF16)
     got = exchange(sent, "pz")
@@ -568,37 +627,40 @@
     got_in = swap_cores(away_in)
     planes, got_out = lax.optimization_barrier((planes, got_out))
 
-    def keep(array, right, got):
-        rows, wide = got.shape[0] // 4, got.shape[1]
-        block = shaped((rows, wide), BF16)
-        part = shaped((rows // 2, wide), BF16)
-        return call(
-            keep_kernel,
-            (shaped((rows, wide), F32), block, block, part, part),
-            (place, array, right, got),
-            flops=matmul_flops // 2,
-        )
-
-    def relay(plus, minus, arrived):
-        block = shaped(plus.shape, BF16)
-        return call(relay_kernel, (block, block), (plus, minus, *arrived))
-
-    def finish(own, arrived):
-        return call(finish_kernel, shaped(own.shape, F32), (own, *arrived))
-
-    own_out, *sides_out, top, bottom = keep(hidden, d, got_out)
-    top, got_in = lax.optimization_barrier((top, got_in))
-    arrived_out = shift_chips(top, bottom)
-    own_in, *sides_in, top, bottom = keep(x, din, got_in)
-    arrived_in = shift_chips(top, bottom)
-    sides_out = relay(*sides_out, arrived_out)
-    sides_out, arrived_in = lax.optimization_barrier((sides_out, arrived_in))
-    arrived_out = shift_chips(*sides_out)
-    arrived_in = shift_chips(*relay(*sides_in, arrived_in))
-    share_out = finish(own_out, arrived_out)
-    share_in = finish(own_in, arrived_in)
-    result = call(planes_kernel, shaped((comps, zn, yn, xn), F32), (planes,), flops=3e10)
-    return (result.transpose(2, 1, 0, 3), share_in[None], share_out[None])
+    rows_out, rows_in = hid // spots, width // spots
+    block = shaped((rows_out, width), BF16)
+    own_out, plus, minus, far = call(
+        keep_out_kernel,
+        (shaped((rows_out, width), F32), block, block, block),
+        (place, hidden, d, got_out),
+        scratch=[
+            pltpu.VMEM((hid // 2, batch), BF16),
+            pltpu.VMEM((width, batch), BF16),
+            pltpu.SemaphoreType.DMA((5,)),
+        ],
+        flops=matmul_flops // 2,
+        far_in=(1, 2),
+    )
+    block = shaped((2, rows_out, width), BF16)
+    part = shaped((2, rows_out // 2, width), BF16)
+    own_in, plus, minus, top, bottom = call(
+        keep_in_kernel,
+        (shaped((rows_in, hid), F32), block, block, part, part),
+        (place, x, din, got_in, plus, minus, far),
+        scratch=[pltpu.VMEM((width // 2, batch), BF16), pltpu.SemaphoreType.DMA((4,))],
+        flops=matmul_flops // 2,
+        far_in=(1,),
+    )
+    arrived = shift_chips(top, bottom)
+    plus, minus = call(relay_kernel, (block, block), (plus, minus, *arrived))
+    arrived = shift_chips(plus, minus)
+    share_out, share_in = call(
+        finish_kernel,
+        (shaped((rows_out, width), F32), shaped((rows_in, hid), F32)),
+        (own_out, own_in, *arrived),
+    )
+    result = call(planes_kernel, shaped((yn, comps, zn, xn), F32), (planes,))
+    return (result.transpose(0, 2, 1, 3), share_in[None], share_out[None])
 
 
 def solution(mesh):

time: 165 us -> 163 us (0.988)
  local copies, waits for them, and re-layouts: 9.79 us -> 3.26 us
  starting transfers between devices: 39.2 us -> 33.1 us
  Pallas kernels: 25.2 us -> 29.7 us
  waiting for transfers between devices: 61 us -> 64.9 us
  other arithmetic: 0.4 us -> 2.58 us
    unnamed x26 -> x11, local copies, waits for them, and re-layouts: 8.13 us -> 1.63 us
    ppermute x8 -> x4, starting transfers between devices: 12.8 us -> 6.63 us  [shift_chips(): return (lax.ppermute(forward, 'px', up), lax.ppermute(backward, 'px', down))]
    ppermute x8 -> x4, waiting for transfers between devices: 5.79 us -> 11.8 us  [shift_chips(): return (lax.ppermute(forward, 'px', up), lax.ppermute(backward, 'px', down))]
    pallas_call x14 -> x12, Pallas kernels: 25.2 us -> 29.7 us  [call(): pl.pallas_call(kernel, out_shape=pinned if isinstance(out_shape, tuple) e...]
    convert_element_type x1, other arithmetic: 0.32 us -> 2.51 us  [per_device(): inverse = implicit_inverse.astype(BF16)]
    ppermute x6, waiting for transfers between devices: 4.87 us -> 2.73 us  [shift(): return (lax.ppermute(last, axis, up), lax.ppermute(first, axis, down))]
  transfers between devices with their start and end apart: 18 -> 14, of which waited for: 9 -> 8; matrix products, arithmetic and copies ran while one was open for 3% -> 4% of each run, Pallas kernels for 11% -> 12%
where the time goes in v6:
time: 163 us
  waiting for transfers between devices  64.9 us (40%)
  starting transfers between devices  33.1 us (20%)
  Pallas kernels  29.7 us (18%)
  blocking collectives  28.6 us (18%)
  local copies, waits for them, and re-layouts  3.26 us (2%)
  other arithmetic  2.58 us (2%)
    all_to_all x2, waiting for transfers between devices, exchange(): return lax.all_to_all(array, axis, split_axis=0, concat_axis=0, tiled=True)  50.3 us
    pallas_call x12, Pallas kernels, call(): pl.pallas_call(kernel, out_shape=pinned if isinstance(out_shape, tuple) e...  29.7 us
    all_to_all x1, blocking collectives, exchange(): return lax.all_to_all(array, axis, split_axis=0, concat_axis=0, tiled=True)  28.6 us
    ppermute x6, starting transfers between devices, shift(): return (lax.ppermute(last, axis, up), lax.ppermute(first, axis, down))  12.9 us
    all_to_all x2, starting transfers between devices, exchange(): return lax.all_to_all(array, axis, split_axis=0, concat_axis=0, tiled=True)  12.6 us
    ppermute x4, waiting for transfers between devices, shift_chips(): return (lax.ppermute(forward, 'px', up), lax.ppermute(backward, 'px', down))  11.8 us
    ppermute x4, starting transfers between devices, shift_chips(): return (lax.ppermute(forward, 'px', up), lax.ppermute(backward, 'px', down))  6.63 us
  transfers between devices with their start and end apart: 14, of which 8 were waited for; matrix products, arithmetic and copies ran while one was open for 4% of the time, Pallas kernels for 12%

profile of v6, /device:TPU:2, one launch (start us, length us, event | category | flops | bytes accessed | tf_op | source)
XLA Modules:
  0.0 162.8 jit_solution(4766641739740906230)
XLA Ops:
  0.6 1.8 %shard_map.94 = bf16[16,152,128]{2,1,0:T(8,128)(2,1)S(1)} custom-call(f32[64,3,4,256]{3,2,1,0:T(4,128)} %bitcast.20, f32[64,4,256]{2,1,0:T(4,128)} %w_far.1, s32[24,32]{1,0:T(8,128)} %bitcast.22, s32[1,32]{1,0:T(1,128)} %bitcast.23), custom_call_target="tpu_custom_call" | custom-call | flops 1000000 | bytes 1674368 | tf_op jit(solution)/shard_map/pallas_call | solution.py:35
  2.4 28.6 %all_to_all.15.got = bf16[16,152,128]{2,1,0:T(8,128)(2,1)S(1)} all-to-all(bf16[16,152,128]{2,1,0:T(8,128)(2,1)S(1)} %shard_map.94), channel_id=1, replica_groups=mesh['px'=8,'pz'=16,'tr'=2] {'pz'}, dimensions={0} | all-to-all | bytes 1245184 | tf_op jit(solution)/shard_map/all_to_all | solution.py:488
  31.0 0.3 shard_map.95
  31.3 2.2 %collective-permute-start = (bf16[48,1024]{1,0:T(8,128)(2,1)S(1)}, bf16[48,1024]{1,0:T(8,128)(2,1)S(1)}, u32[]{:S(2)}, u32[]{:S(2)}) collective-permute-start(bf16[48,1024]{1,0:T(8,128)(2,1)S(1)} %get-tuple-element.46), channel_id=1, source_target_pairs={{0,1},{1,32},{32,33},{33,64},{64,65},{65,96},{96,97},{97,128},{128... | collective-permute-start | bytes 294920 | tf_op jit(solution)/shard_map/ppermute | solution.py:81
  33.5 3.2 %collective-permute-start.1 = (bf16[48,1024]{1,0:T(8,128)(2,1)S(1)}, bf16[48,1024]{1,0:T(8,128)(2,1)S(1)}, u32[]{:S(2)}, u32[]{:S(2)}) collective-permute-start(bf16[48,1024]{1,0:T(8,128)(2,1)S(1)} %get-tuple-element.47), channel_id=1, source_target_pairs={{1,0},{32,1},{33,32},{64,33},{65,64},{96,65},{97,96},{128,97},{129... | collective-permute-start | bytes 294920 | tf_op jit(solution)/shard_map/ppermute | solution.py:81
  36.8 2.5 %convert_element_type.3.a = bf16[1024,1024]{1,0:T(8,128)(2,1)S(1)} convert(f32[1024,1024]{1,0:T(8,128)} %param.9) | non-fusion elementwise | flops 1048576 | bytes 6291456 | tf_op jit(solution)/shard_map/convert_element_type | solution.py:531
  39.3 0.3 collective-permute-done.zlo
  39.6 0.4 collective-permute-done.1.zhi
  40.1 1.3 shard_map.96
  41.3 0.2 collective-permute-start.2
  41.6 5.2 %collective-permute-start.3 = (bf16[48,1024]{1,0:T(8,128)(2,1)S(1)}, bf16[48,1024]{1,0:T(8,128)(2,1)S(1)}, u32[]{:S(2)}, u32[]{:S(2)}) collective-permute-start(bf16[48,1024]{1,0:T(8,128)(2,1)S(1)} %get-tuple-element.51), channel_id=1, source_target_pairs={{1,0},{32,1},{33,32},{64,33},{65,64},{96,65},{97,96},{128,97},{129... | collective-permute-start | bytes 294920 | tf_op jit(solution)/shard_map/ppermute | solution.py:81
  46.8 1.5 collective-permute-start.4
  48.3 0.5 collective-permute-start.5
  48.8 2.7 %shard_map.97.sent_in = bf16[32,96,384]{2,1,0:T(8,128)(2,1)} custom-call(bf16[8,2,96,128]{3,2,1,0:T(8,128)(2,1)S(1)} %get-tuple-element.54.packed, s32[16,8,128]{2,1,0:T(8,128)S(1)} %get-tuple-element.49.ids), custom_call_target="tpu_custom_call" | custom-call | flops 301989888 | bytes 2818048 | tf_op jit(solution)/shard_map/pallas_call | solution.py:35
  51.5 0.2 collective-permute-done.4.xlo
  51.7 1.7 %collective-permute-done.5.xhi = f32[12,1024]{1,0:T(8,128)S(1)} collective-permute-done((f32[12,1024]{1,0:T(8,128)S(1)}, f32[12,1024]{1,0:T(8,128)S(1)}, u32[]{:S(2)}, u32[]{:S(2)}) %collective-permute-start.5) | collective-permute-done | bytes 49184 | tf_op jit(solution)/shard_map/ppermute | solution.py:81
  53.5 0.0 collective-permute-done.2.zlo
  53.5 0.0 collective-permute-done.3.zhi
  53.5 3.7 %shard_map.98 = (bf16[8,2,96,128]{3,2,1,0:T(8,128)(2,1)}, bf16[32,96,384]{2,1,0:T(8,128)(2,1)}) custom-call(f32[192,1024]{1,0:T(8,128)S(1)} %get-tuple-element.48.u, bf16[64,1024]{1,0:T(8,128)(2,1)S(1)} %get-tuple-element.43.w, s32[16,8,128]{2,1,0:T(8,128)S(1)} %get-tuple-element.49.ids, ...), custom_call_target="tpu_custom_call", output_to_operand_aliasing={{1}: (8, {})} | custom-call | flops 704643072 | bytes 8486912 | tf_op jit(solution)/shard_map/pallas_call | solution.py:35
  57.2 0.0 copy-start.4
  57.2 7.1 %all-to-all-start.1 = ((bf16[32,96,384]{2,1,0:T(8,128)(2,1)}), bf16[32,96,384]{2,1,0:T(8,128)(2,1)}, u32[]{:S(2)}, u32[]{:S(2)}) async-start(bf16[32,96,384]{2,1,0:T(8,128)(2,1)} %get-tuple-element.56), calls=%async_computation.1 | async-start | bytes 4718592 | tf_op jit(solution)/shard_map/all_to_all | solution.py:488
  64.3 0.0 copy-start
  64.3 1.6 copy.11
  65.9 1.6 %copy.12.refs_3_ = bf16[768,1024]{1,0:T(8,128)(2,1)} copy(bf16[768,1024]{0,1:T(8,128)(2,1)S(1)} %bitcast.17) | data formatting | bytes 3145728 | tf_op jit(solution)/shard_map/transpose | solution.py:610
  67.6 0.1 pad_add_fusion.refs_0_.place
  67.7 50.3 %all-to-all-done.1.refs_1_ = bf16[32,96,384]{2,1,0:T(8,128)(2,1)} async-done(((bf16[32,96,384]{2,1,0:T(8,128)(2,1)}), bf16[32,96,384]{2,1,0:T(8,128)(2,1)}, u32[]{:S(2)}, u32[]{:S(2)}) %all-to-all-start.1) | async-done | bytes 2359328 | tf_op jit(solution)/shard_map/all_to_all | solution.py:488
  118.0 5.6 %all-to-all-start.2 = ((bf16[16,96,128]{2,1,0:T(8,128)(2,1)}), bf16[16,96,128]{2,1,0:T(8,128)(2,1)S(1)}, u32[]{:S(2)}, u32[]{:S(2)}) async-start(bf16[16,96,128]{2,1,0:T(8,128)(2,1)} %bitcast.4), calls=%async_computation.2 | async-start | bytes 786432 | tf_op jit(solution)/shard_map/all_to_all | solution.py:488
  123.5 7.5 %shard_map.99 = (bf16[768,768]{1,0:T(8,128)(2,1)S(1)}, bf16[1024,768]{1,0:T(8,128)(2,1)S(1)}, bf16[1024,768]{1,0:T(8,128)(2,1)S(1)}, bf16[768,768]{1,0:T(8,128)(2,1)S(1)}, bf16[512,768]{1,0:T(8,128)(2,1)}) custom-call(s32[2]{0:T(128)S(1)} %pad_add_fusion.refs_0_.place, bf16[32,96,384]{2,1,0:T(8,128)(2,1)} %all-to-all-done.1.refs_1_, ...), custom_call_target="tpu_custom_call" | custom-call | flops 3019898880 | bytes 11796488 | tf_op jit(solution)/shard_map/pallas_call | solution.py:35
  131.0 0.1 collective-permute-start.6
  131.1 4.2 %shard_map.102 = (bf16[1024,768]{1,0:T(8,128)(2,1)S(1)}, bf16[384,1024]{1,0:T(8,128)(2,1)}) custom-call(s32[2]{0:T(128)S(1)} %pad_add_fusion.refs_0_.place, bf16[768,768]{1,0:T(8,128)(2,1)S(1)} %get-tuple-element.62.d_far.d, bf16[1024,768]{1,0:T(8,128)(2,1)S(1)} %get-tuple-element.66.slope, bf16[1024,768]{1,0:T(8,128)(2,1)S(1)} %bitcast.18, ...), custom_call_target="tpu_custom_call" | custom-call | flops 1811939328 | bytes 7864328 | tf_op jit(solution)/shard_map/pallas_call | solution.py:35
  135.3 0.0 copy-done.1
  135.4 0.8 collective-permute-start.7
  136.1 0.0 all-to-all-done.2.got
  136.1 0.0 collective-permute-done.6.got
  136.2 3.5 %shard_map.101 = (f32[128,768]{1,0:T(8,128)S(1)}, bf16[128,768]{1,0:T(8,128)(2,1)S(1)}, bf16[128,768]{1,0:T(8,128)(2,1)S(1)}, bf16[128,768]{1,0:T(8,128)(2,1)S(1)}) custom-call(s32[2]{0:T(128)S(1)} %pad_add_fusion.refs_0_.place, bf16[1024,768]{1,0:T(8,128)(2,1)} %copy-done.1, bf16[768,768]{1,0:T(8,128)(2,1)} %copy-done.3, ...), custom_call_target="tpu_custom_call" | custom-call | flops 603979776 | bytes 4521992 | tf_op jit(solution)/shard_map/pallas_call | solution.py:35
  139.6 0.0 collective-permute-done.7.got
  139.6 2.5 %shard_map.103 = (f32[96,1024]{1,0:T(8,128)S(1)}, bf16[2,128,768]{2,1,0:T(8,128)(2,1)S(1)}, bf16[2,128,768]{2,1,0:T(8,128)(2,1)S(1)}, bf16[2,64,768]{2,1,0:T(8,128)(2,1)S(1)}, bf16[2,64,768]{2,1,0:T(8,128)(2,1)S(1)}) custom-call(s32[2]{0:T(128)S(1)} %pad_add_fusion.refs_0_.place, bf16[768,768]{1,0:T(8,128)(2,1)} %copy-done.2, ...), custom_call_target="tpu_custom_call" | custom-call | flops 603979776 | bytes 5701640 | tf_op jit(solution)/shard_map/pallas_call | solution.py:35
  142.2 1.7 %collective-permute-start.8 = (bf16[2,64,768]{2,1,0:T(8,128)(2,1)S(1)}, bf16[2,64,768]{2,1,0:T(8,128)(2,1)S(1)}, u32[]{:S(2)}, u32[]{:S(2)}) collective-permute-start(bf16[2,64,768]{2,1,0:T(8,128)(2,1)S(1)} %get-tuple-element.75), channel_id=1, source_target_pairs={{0,64},{32,96},{64,128},{96,160},{128,192},{160,224},{192,0},{224,... | collective-permute-start | bytes 589832 | tf_op jit(solution)/shard_map/ppermute | solution.py:500
  143.8 1.7 %collective-permute-start.9 = (bf16[2,64,768]{2,1,0:T(8,128)(2,1)S(1)}, bf16[2,64,768]{2,1,0:T(8,128)(2,1)S(1)}, u32[]{:S(2)}, u32[]{:S(2)}) collective-permute-start(bf16[2,64,768]{2,1,0:T(8,128)(2,1)S(1)} %get-tuple-element.76), channel_id=1, source_target_pairs={{64,0},{96,32},{128,64},{160,96},{192,128},{224,160},{0,192},{32,2... | collective-permute-start | bytes 589832 | tf_op jit(solution)/shard_map/ppermute | solution.py:500
  145.5 4.8 %collective-permute-done.8.from_before = bf16[2,64,768]{2,1,0:T(8,128)(2,1)S(1)} collective-permute-done((bf16[2,64,768]{2,1,0:T(8,128)(2,1)S(1)}, bf16[2,64,768]{2,1,0:T(8,128)(2,1)S(1)}, u32[]{:S(2)}, u32[]{:S(2)}) %collective-permute-start.8) | collective-permute-done | bytes 196640 | tf_op jit(solution)/shard_map/ppermute | solution.py:500
  150.3 0.1 collective-permute-done.9.from_after
  150.4 0.1 shard_map.104
  150.5 1.6 collective-permute-start.10
  152.1 1.7 %collective-permute-start.11 = (bf16[2,128,768]{2,1,0:T(8,128)(2,1)S(1)}, bf16[2,128,768]{2,1,0:T(8,128)(2,1)S(1)}, u32[]{:S(2)}, u32[]{:S(2)}) collective-permute-start(bf16[2,128,768]{2,1,0:T(8,128)(2,1)S(1)} %get-tuple-element.78), channel_id=1, source_target_pairs={{64,0},{96,32},{128,64},{160,96},{192,128},{224,160},{0,192},{32,2... | collective-permute-start | bytes 1179656 | tf_op jit(solution)/shard_map/ppermute | solution.py:500
  153.8 1.2 shard_map.100
  155.0 6.9 %collective-permute-done.10.from_before = bf16[2,128,768]{2,1,0:T(8,128)(2,1)S(1)} collective-permute-done((bf16[2,128,768]{2,1,0:T(8,128)(2,1)S(1)}, bf16[2,128,768]{2,1,0:T(8,128)(2,1)S(1)}, u32[]{:S(2)}, u32[]{:S(2)}) %collective-permute-start.10) | collective-permute-done | bytes 393248 | tf_op jit(solution)/shard_map/ppermute | solution.py:500
  161.9 0.0 collective-permute-done.11.from_after
  161.9 1.0 shard_map.105
  (7 shorter events, 0.0 us)
Async XLA Ops:
  31.3 8.3 %collective-permute-start = (bf16[48,1024]{1,0:T(8,128)(2,1)S(1)}, bf16[48,1024]{1,0:T(8,128)(2,1)S(1)}, u32[]{:S(2)}, u32[]{:S(2)}) collective-permute-start(bf16[48,1024]{1,0:T(8,128)(2,1)S(1)} %get-tuple-element.46), channel_id=1, source_target_pairs={{0,1},{1,32},{32,33},{33,64},{64,65},{65,96},{96,97},{97,128},{128... | collective-permute-start | bytes 294920 | tf_op jit(solution)/shard_map/ppermute | solution.py:81
  33.5 6.5 %collective-permute-start.1 = (bf16[48,1024]{1,0:T(8,128)(2,1)S(1)}, bf16[48,1024]{1,0:T(8,128)(2,1)S(1)}, u32[]{:S(2)}, u32[]{:S(2)}) collective-permute-start(bf16[48,1024]{1,0:T(8,128)(2,1)S(1)} %get-tuple-element.47), channel_id=1, source_target_pairs={{1,0},{32,1},{33,32},{64,33},{65,64},{96,65},{97,96},{128,97},{129... | collective-permute-start | bytes 294920 | tf_op jit(solution)/shard_map/ppermute | solution.py:81
  41.3 12.1 %collective-permute-start.2 = (bf16[48,1024]{1,0:T(8,128)(2,1)S(1)}, bf16[48,1024]{1,0:T(8,128)(2,1)S(1)}, u32[]{:S(2)}, u32[]{:S(2)}) collective-permute-start(bf16[48,1024]{1,0:T(8,128)(2,1)S(1)} %get-tuple-element.50), channel_id=1, source_target_pairs={{0,1},{1,32},{32,33},{33,64},{64,65},{65,96},{96,97},{97,128},{128... | collective-permute-start | bytes 294920 | tf_op jit(solution)/shard_map/ppermute | solution.py:81
  41.6 11.9 %collective-permute-start.3 = (bf16[48,1024]{1,0:T(8,128)(2,1)S(1)}, bf16[48,1024]{1,0:T(8,128)(2,1)S(1)}, u32[]{:S(2)}, u32[]{:S(2)}) collective-permute-start(bf16[48,1024]{1,0:T(8,128)(2,1)S(1)} %get-tuple-element.51), channel_id=1, source_target_pairs={{1,0},{32,1},{33,32},{64,33},{65,64},{96,65},{97,96},{128,97},{129... | collective-permute-start | bytes 294920 | tf_op jit(solution)/shard_map/ppermute | solution.py:81
  46.8 4.9 %collective-permute-start.4 = (f32[12,1024]{1,0:T(8,128)S(1)}, f32[12,1024]{1,0:T(8,128)S(1)}, u32[]{:S(2)}, u32[]{:S(2)}) collective-permute-start(f32[12,1024]{1,0:T(8,128)S(1)} %get-tuple-element.52), channel_id=1, source_target_pairs={{0,2},{2,4},{4,6},{6,8},{8,10},{10,12},{12,14},{14,16},{16,18},{18... | collective-permute-start | bytes 147464 | tf_op jit(solution)/shard_map/ppermute | solution.py:81
  48.3 5.2 %collective-permute-start.5 = (f32[12,1024]{1,0:T(8,128)S(1)}, f32[12,1024]{1,0:T(8,128)S(1)}, u32[]{:S(2)}, u32[]{:S(2)}) collective-permute-start(f32[12,1024]{1,0:T(8,128)S(1)} %get-tuple-element.53), channel_id=1, source_target_pairs={{2,0},{4,2},{6,4},{8,6},{10,8},{12,10},{14,12},{16,14},{18,16},{20... | collective-permute-start | bytes 147464 | tf_op jit(solution)/shard_map/ppermute | solution.py:81
  57.2 7.1 %copy-start.4 = (bf16[1,768,1024]{2,1,0:T(8,128)(2,1)S(1)}, bf16[1,768,1024]{2,1,0:T(8,128)(2,1)}, u32[]{:S(2)}) copy-start(bf16[1,768,1024]{2,1,0:T(8,128)(2,1)} %param.12) | copy-start | bytes 4718596
  57.2 60.8 %all-to-all-start.1 = ((bf16[32,96,384]{2,1,0:T(8,128)(2,1)}), bf16[32,96,384]{2,1,0:T(8,128)(2,1)}, u32[]{:S(2)}, u32[]{:S(2)}) async-start(bf16[32,96,384]{2,1,0:T(8,128)(2,1)} %get-tuple-element.56), calls=%async_computation.1 | async-start | bytes 4718592 | tf_op jit(solution)/shard_map/all_to_all | solution.py:488
  64.3 1.6 copy-start
  118.0 18.2 %all-to-all-start.2 = ((bf16[16,96,128]{2,1,0:T(8,128)(2,1)}), bf16[16,96,128]{2,1,0:T(8,128)(2,1)S(1)}, u32[]{:S(2)}, u32[]{:S(2)}) async-start(bf16[16,96,128]{2,1,0:T(8,128)(2,1)} %bitcast.4), calls=%async_computation.2 | async-start | bytes 786432 | tf_op jit(solution)/shard_map/all_to_all | solution.py:488
  131.0 4.3 %copy-start.1 = (bf16[1024,768]{1,0:T(8,128)(2,1)}, bf16[1024,768]{1,0:T(8,128)(2,1)S(1)}, u32[]{:S(2)}) copy-start(bf16[1024,768]{1,0:T(8,128)(2,1)S(1)} %get-tuple-element.61.hidden_far) | copy-start | bytes 4718596
  131.0 4.3 %copy-start.2 = (bf16[768,768]{1,0:T(8,128)(2,1)}, bf16[768,768]{1,0:T(8,128)(2,1)S(1)}, u32[]{:S(2)}) copy-start(bf16[768,768]{1,0:T(8,128)(2,1)S(1)} %get-tuple-element.65.x.x_far) | copy-start | bytes 3538948
  131.0 4.3 %copy-start.3 = (bf16[768,768]{1,0:T(8,128)(2,1)}, bf16[768,768]{1,0:T(8,128)(2,1)S(1)}, u32[]{:S(2)}) copy-start(bf16[768,768]{1,0:T(8,128)(2,1)S(1)} %get-tuple-element.62.d_far.d) | copy-start | bytes 3538948
  131.0 5.1 %collective-permute-start.6 = (bf16[512,768]{1,0:T(8,128)(2,1)}, bf16[512,768]{1,0:T(8,128)(2,1)}, u32[]{:S(2)}, u32[]{:S(2)}) collective-permute-start(bf16[512,768]{1,0:T(8,128)(2,1)} %get-tuple-element.59), channel_id=1, source_target_pairs={{0,32},{32,0},{64,96},{96,64},{128,160},{160,128},{192,224},{224,1... | collective-permute-start | bytes 2359304 | tf_op jit(solution)/shard_map/ppermute | solution.py:493
  135.4 4.3 %collective-permute-start.7 = (bf16[384,1024]{1,0:T(8,128)(2,1)}, bf16[384,1024]{1,0:T(8,128)(2,1)S(1)}, u32[]{:S(2)}, u32[]{:S(2)}) collective-permute-start(bf16[384,1024]{1,0:T(8,128)(2,1)} %get-tuple-element.68), channel_id=1, source_target_pairs={{0,32},{32,0},{64,96},{96,64},{128,160},{160,128},{192,224},{224,1... | collective-permute-start | bytes 2359304 | tf_op jit(solution)/shard_map/ppermute | solution.py:493
  142.2 8.1 %collective-permute-start.8 = (bf16[2,64,768]{2,1,0:T(8,128)(2,1)S(1)}, bf16[2,64,768]{2,1,0:T(8,128)(2,1)S(1)}, u32[]{:S(2)}, u32[]{:S(2)}) collective-permute-start(bf16[2,64,768]{2,1,0:T(8,128)(2,1)S(1)} %get-tuple-element.75), channel_id=1, source_target_pairs={{0,64},{32,96},{64,128},{96,160},{128,192},{160,224},{192,0},{224,... | collective-permute-start | bytes 589832 | tf_op jit(solution)/shard_map/ppermute | solution.py:500
  143.8 6.6 %collective-permute-start.9 = (bf16[2,64,768]{2,1,0:T(8,128)(2,1)S(1)}, bf16[2,64,768]{2,1,0:T(8,128)(2,1)S(1)}, u32[]{:S(2)}, u32[]{:S(2)}) collective-permute-start(bf16[2,64,768]{2,1,0:T(8,128)(2,1)S(1)} %get-tuple-element.76), channel_id=1, source_target_pairs={{64,0},{96,32},{128,64},{160,96},{192,128},{224,160},{0,192},{32,2... | collective-permute-start | bytes 589832 | tf_op jit(solution)/shard_map/ppermute | solution.py:500
  150.5 11.4 %collective-permute-start.10 = (bf16[2,128,768]{2,1,0:T(8,128)(2,1)S(1)}, bf16[2,128,768]{2,1,0:T(8,128)(2,1)S(1)}, u32[]{:S(2)}, u32[]{:S(2)}) collective-permute-start(bf16[2,128,768]{2,1,0:T(8,128)(2,1)S(1)} %get-tuple-element.77), channel_id=1, source_target_pairs={{0,64},{32,96},{64,128},{96,160},{128,192},{160,224},{192,0},{224,... | collective-permute-start | bytes 1179656 | tf_op jit(solution)/shard_map/ppermute | solution.py:500
  152.1 9.8 %collective-permute-start.11 = (bf16[2,128,768]{2,1,0:T(8,128)(2,1)S(1)}, bf16[2,128,768]{2,1,0:T(8,128)(2,1)S(1)}, u32[]{:S(2)}, u32[]{:S(2)}) collective-permute-start(bf16[2,128,768]{2,1,0:T(8,128)(2,1)S(1)} %get-tuple-element.78), channel_id=1, source_target_pairs={{64,0},{96,32},{128,64},{160,96},{192,128},{224,160},{0,192},{32,2... | collective-permute-start | bytes 1179656 | tf_op jit(solution)/shard_map/ppermute | solution.py:500

commit v7 on v6

--- a/solution.py
+++ b/solution.py
@@ -328,38 +328,23 @@
     return lax.dot_general(left, right, CONTRACT_ROWS, preferred_element_type=F32)
 
 
-def forward_kernel(
-    scale, place, got_far, w_in_far, w_out_far, x, hidden, slope, d, away,
-    got, w_in, w_out, sems,
-):
-    copies = Copies(sems)
+def over_first(left, right):
+    return lax.dot_general(left, right, (((0,), (0,)), ((), ())), preferred_element_type=F32)
+
+
+def forward_kernel(scale, place, got, w_in, w_out, x, hidden, slope, d, away):
     f = got.shape[1] // 2
-    input_part = (slice(None), pl.ds(0, f), slice(None))
-    target_part = (slice(None), pl.ds(f, f), slice(None))
-    first = [copies.start(got_far.at[input_part], got.at[input_part])]
-    wide = 256
-    count = hidden.shape[0] // wide
-    for i in range(count):
-        at = pl.ds(i * wide, wide)
-        first.append(copies.start(w_in_far.at[at], w_in.at[at]))
-    w_out_copy = copies.start(w_out_far, w_out)
-    target_copy = copies.start(got_far.at[target_part], got.at[target_part])
-    copies.wait(first[0])
     gather_rows(got, 0, x)
-    for i in range(count):
-        copies.wait(first[1 + i])
+    wide = 512
+    for i in range(hidden.shape[0] // wide):
         at = slice(i * wide, (i + 1) * wide)
-        pre = jnp.dot(w_in[at, :], x[...], preferred_element_type=F32)
+        pre = over_first(w_in[:, at], x[...])
         logistic = jax.nn.sigmoid(pre)
         hidden[at, :] = (pre * logistic).astype(BF16)
         slope[at, :] = (logistic * (1.0 + pre * (1.0 - logistic))).astype(slope.dtype)
-    copies.wait(w_out_copy)
-    copies.wait(target_copy)
     gather_rows(got, f, d)
-    for i in range(d.shape[0] // wide):
-        at = slice(i * wide, (i + 1) * wide)
-        predicted = jnp.dot(w_out[at, :], hidden[...], preferred_element_type=F32)
-        d[at] = ((predicted - d[at].astype(F32)) * scale).astype(BF16)
+    predicted = over_first(w_out[...], hidden[...])
+    d[...] = ((predicted - d[...].astype(F32)) * scale).astype(BF16)
     away_blocks(hidden, d, place[0], away, away.shape[0] // 4)
 
 
@@ -373,15 +358,11 @@
 
 
 def delta_in_kernel(place, d, slope, w_out, x, din, away):
-    wide = 256
-
-    def chunk(i, carry):
-        at = pl.ds(pl.multiple_of(i * wide, wide), wide)
+    wide = 512
+    for i in range(din.shape[0] // wide):
+        at = slice(i * wide, (i + 1) * wide)
         back = jnp.dot(w_out[at, :], d[...], preferred_element_type=F32)
         din[at, :] = (back * slope[at, :].astype(F32)).astype(BF16)
-        return carry
-
-    lax.fori_loop(0, din.shape[0] // wide, chunk, 0)
     away_blocks(x, din, place[0], away, away.shape[0] // 4)
 
 
@@ -399,15 +380,11 @@
     return jnp.concatenate([block[:rows], jnp.concatenate(pieces, axis=0)], axis=1)
 
 
-def own_blocks(place, copies, array_far, left):
+def own_blocks(place, array, rows):
     core, y = place[0], place[1]
-    rows = left.shape[0] // 4
-    started = []
-    for n, k in enumerate((2, 1, 3, 0)):
-        at = (2 * lax.rem(y + k, 4) + core) * rows
-        source = array_far.at[pl.ds(pl.multiple_of(at, rows), rows)]
-        started.append(copies.start(source, left.at[pl.ds(n * rows, rows)]))
-    return started
+    return jnp.concatenate(
+        [block_rows(array, lax.rem(y + k, 4), core, rows) for k in (2, 1, 3, 0)], axis=0
+    )
 
 
 def add_other_core(place, value, got, n, k):
@@ -416,12 +393,8 @@
     return value[n * rows : (n + 1) * rows] + got[pl.ds(at, rows), :].astype(F32)
 
 
-def keep_out_kernel(place, hidden_far, d_far, got, own, plus, minus, far, left, d, sems):
-    copies = Copies(sems)
-    copies.start(d_far, d)
-    own_blocks(place, copies, hidden_far, left)
-    copies.finish()
-    value = over_rows(left[...], d[...])
+def keep_out_kernel(place, hidden, d, got, own, plus, minus, far):
+    value = over_rows(own_blocks(place, hidden, own.shape[0]), d[...])
     far[...] = add_other_core(place, value, got, 0, 2).astype(BF16)
     plus[...] = add_other_core(place, value, got, 1, 1).astype(BF16)
     minus[...] = add_other_core(place, value, got, 2, 3).astype(BF16)
@@ -429,18 +402,15 @@
 
 
 def keep_in_kernel(
-    place, x_far, din, got, plus_out, minus_out, far_out, own, plus, minus, top, bottom, left, sems
+    place, x, din, got, plus_out, minus_out, far_out, own, plus, minus, top, bottom
 ):
-    copies = Copies(sems)
-    own_blocks(place, copies, x_far, left)
     rows, width = plus_out.shape
     half = rows // 2
     plus[0] = plus_out[...]
     minus[0] = minus_out[...]
     top[0] = far_out[:half]
     bottom[0] = far_out[half:]
-    copies.finish()
-    value = over_rows(left[...], din[...])
+    value = over_rows(own_blocks(place, x, own.shape[0]), din[...])
     far = fold(add_other_core(place, value, got, 0, 2), rows, width).astype(BF16)
     top[1] = far[:half]
     bottom[1] = far[half:]
@@ -503,6 +473,8 @@
 def per_device(velocity, viscosity, implicit_inverse, row_index, row_counts, weight_in, weight_out):
     yn, zn, comps, xn = velocity.shape
     peers = lax.axis_size("pz")
+    position = lax.axis_index("px")
+    place = jnp.stack([position & 1, position >> 1]).astype(jnp.int32)
     total_y = yn * peers
     xl = xn // peers
     f = comps * xl
@@ -581,9 +553,8 @@
         far_out=(0, 1),
         aliases={8: 1},
     )
+    sent, place = lax.optimization_barrier((sent, place))
     rows_all = exchange(sent, ("pz", "tr"))
-    packed, rows_all = lax.optimization_barrier((packed, rows_all))
-    planes = exchange(packed.reshape(peers, 2 * f, lanes), "pz")
 
     member_in = weight_in[0]
     member_out = weight_out[0]
@@ -592,8 +563,6 @@
     spots = lax.axis_size("px")
     loss_scale = 1.0 / math.sqrt(spots * batch)
     matmul_flops = 2 * hid * width * batch
-    position = lax.axis_index("px")
-    place = jnp.stack([position & 1, position >> 1]).astype(jnp.int32)
 
     def forward(*refs):
         forward_kernel(loss_scale, *refs)
@@ -607,15 +576,8 @@
             shaped((width, batch), BF16),
             shaped((hid // 2, width), BF16),
         ),
-        (place, rows_all, member_in.T, member_out.T),
-        scratch=[
-            pltpu.VMEM(both.shape, BF16),
-            pltpu.VMEM((hid, width), BF16),
-            pltpu.VMEM((width, hid), BF16),
-            pltpu.SemaphoreType.DMA((8,)),
-        ],
+        (place, rows_all, member_in, member_out),
         flops=matmul_flops * 5 // 2,
-        far_in=(1, 2, 3),
     )
     got_out = swap_cores(away_out)
     din, away_in = call(
@@ -625,7 +587,6 @@
         flops=matmul_flops * 3 // 2,
     )
     got_in = swap_cores(away_in)
-    planes, got_out = lax.optimization_barrier((planes, got_out))
 
     rows_out, rows_in = hid // spots, width // spots
     block = shaped((rows_out, width), BF16)
@@ -633,13 +594,7 @@
         keep_out_kernel,
         (shaped((rows_out, width), F32), block, block, block),
         (place, hidden, d, got_out),
-        scratch=[
-            pltpu.VMEM((hid // 2, batch), BF16),
-            pltpu.VMEM((width, batch), BF16),
-            pltpu.SemaphoreType.DMA((5,)),
-        ],
         flops=matmul_flops // 2,
-        far_in=(1, 2),
     )
     block = shaped((2, rows_out, width), BF16)
     part = shaped((2, rows_out // 2, width), BF16)
@@ -647,11 +602,11 @@
         keep_in_kernel,
         (shaped((rows_in, hid), F32), block, block, part, part),
         (place, x, din, got_in, plus, minus, far),
-        scratch=[pltpu.VMEM((width // 2, batch), BF16), pltpu.SemaphoreType.DMA((4,))],
         flops=matmul_flops // 2,
-        far_in=(1,),
-    )
+    )
+    packed, top = lax.optimization_barrier((packed, top))
     arrived = shift_chips(top, bottom)
+    planes = exchange(packed.reshape(peers, 2 * f, lanes), "pz")
     plus, minus = call(relay_kernel, (block, block), (plus, minus, *arrived))
     arrived = shift_chips(plus, minus)
     share_out, share_in = call(

time: 163 us -> 159 us (0.975)
  blocking collectives: 28.6 us -> 91.7 us
  waiting for transfers between devices: 64.9 us -> 16.4 us
  starting transfers between devices: 33.1 us -> 25.2 us
  Pallas kernels: 29.7 us -> 21.8 us
  local copies, waits for them, and re-layouts: 3.26 us -> 0.01 us
    all_to_all x1 -> x2, blocking collectives: 28.6 us -> 91.7 us  [exchange(): return lax.all_to_all(array, axis, split_axis=0, concat_axis=0, tiled=True)]
    all_to_all x2 -> x1, waiting for transfers between devices: 50.3 us -> 0.01 us  [exchange(): return lax.all_to_all(array, axis, split_axis=0, concat_axis=0, tiled=True)]
    pallas_call x12, Pallas kernels: 29.7 us -> 21.8 us  [call(): pl.pallas_call(kernel, out_shape=pinned if isinstance(out_shape, tuple) e...]
    all_to_all x2 -> x1, starting transfers between devices: 12.6 us -> 5.1 us  [exchange(): return lax.all_to_all(array, axis, split_axis=0, concat_axis=0, tiled=True)]
    transpose x1 -> x0, local copies, waits for them, and re-layouts: 1.63 us -> none  [per_device(): x, hidden, slope, d, away_out = call(forward, (shaped((width, batch), BF1...]
  transfers between devices with their start and end apart: 14 -> 13, of which waited for: 8 -> 7; matrix products, arithmetic and copies ran while one was open for 4% -> 2% of each run, Pallas kernels for 12% -> 5%
where the time goes in v7:
time: 159 us; the launch traced here: 158 us
  blocking collectives  91.7 us (58%)
  starting transfers between devices  25.2 us (16%)
  Pallas kernels  21.8 us (14%)
  waiting for transfers between devices  16.4 us (10%)
  other arithmetic  2.58 us (2%)
    all_to_all x2, blocking collectives, exchange(): return lax.all_to_all(array, axis, split_axis=0, concat_axis=0, tiled=True)  91.7 us
    pallas_call x12, Pallas kernels, call(): pl.pallas_call(kernel, out_shape=pinned if isinstance(out_shape, tuple) e...  21.8 us
    ppermute x4, waiting for transfers between devices, shift_chips(): return (lax.ppermute(forward, 'px', up), lax.ppermute(backward, 'px', down))  13.3 us
    ppermute x6, starting transfers between devices, shift(): return (lax.ppermute(last, axis, up), lax.ppermute(first, axis, down))  12.9 us
    ppermute x4, starting transfers between devices, shift_chips(): return (lax.ppermute(forward, 'px', up), lax.ppermute(backward, 'px', down))  6.55 us
    all_to_all x1, starting transfers between devices, exchange(): return lax.all_to_all(array, axis, split_axis=0, concat_axis=0, tiled=True)  5.1 us
  transfers between devices with their start and end apart: 13, of which 7 were waited for; matrix products, arithmetic and copies ran while one was open for 2% of the time, Pallas kernels for 5%

profile of v7, /device:TPU:2, one launch (start us, length us, event | category | flops | bytes accessed | tf_op | source)
XLA Modules:
  0.0 158.4 jit_solution(13673350637547407266)
XLA Ops:
  0.6 1.8 %shard_map.94 = bf16[16,152,128]{2,1,0:T(8,128)(2,1)S(1)} custom-call(f32[64,3,4,256]{3,2,1,0:T(4,128)} %bitcast.16, f32[64,4,256]{2,1,0:T(4,128)} %w_far.1, s32[24,32]{1,0:T(8,128)} %bitcast.18, s32[1,32]{1,0:T(1,128)} %bitcast.19), custom_call_target="tpu_custom_call" | custom-call | flops 1000000 | bytes 1674368 | tf_op jit(solution)/shard_map/pallas_call | solution.py:35
  2.4 28.6 %all_to_all.15.got = bf16[16,152,128]{2,1,0:T(8,128)(2,1)S(1)} all-to-all(bf16[16,152,128]{2,1,0:T(8,128)(2,1)S(1)} %shard_map.94), channel_id=1, replica_groups=mesh['px'=8,'pz'=16,'tr'=2] {'pz'}, dimensions={0} | all-to-all | bytes 1245184 | tf_op jit(solution)/shard_map/all_to_all | solution.py:458
  31.0 0.3 shard_map.95
  31.3 2.2 %collective-permute-start = (bf16[48,1024]{1,0:T(8,128)(2,1)S(1)}, bf16[48,1024]{1,0:T(8,128)(2,1)S(1)}, u32[]{:S(2)}, u32[]{:S(2)}) collective-permute-start(bf16[48,1024]{1,0:T(8,128)(2,1)S(1)} %get-tuple-element.46), channel_id=1, source_target_pairs={{0,1},{1,32},{32,33},{33,64},{64,65},{65,96},{96,97},{97,128},{128... | collective-permute-start | bytes 294920 | tf_op jit(solution)/shard_map/ppermute | solution.py:81
  33.5 3.2 %collective-permute-start.1 = (bf16[48,1024]{1,0:T(8,128)(2,1)S(1)}, bf16[48,1024]{1,0:T(8,128)(2,1)S(1)}, u32[]{:S(2)}, u32[]{:S(2)}) collective-permute-start(bf16[48,1024]{1,0:T(8,128)(2,1)S(1)} %get-tuple-element.47), channel_id=1, source_target_pairs={{1,0},{32,1},{33,32},{64,33},{65,64},{96,65},{97,96},{128,97},{129... | collective-permute-start | bytes 294920 | tf_op jit(solution)/shard_map/ppermute | solution.py:81
  36.8 2.5 %convert_element_type.3.a = bf16[1024,1024]{1,0:T(8,128)(2,1)S(1)} convert(f32[1024,1024]{1,0:T(8,128)} %param.9) | non-fusion elementwise | flops 1048576 | bytes 6291456 | tf_op jit(solution)/shard_map/convert_element_type | solution.py:503
  39.3 0.3 collective-permute-done.zlo
  39.6 0.4 collective-permute-done.1.zhi
  40.1 1.3 shard_map.96
  41.3 1.6 %collective-permute-start.4 = (f32[12,1024]{1,0:T(8,128)S(1)}, f32[12,1024]{1,0:T(8,128)S(1)}, u32[]{:S(2)}, u32[]{:S(2)}) collective-permute-start(f32[12,1024]{1,0:T(8,128)S(1)} %get-tuple-element.52), channel_id=1, source_target_pairs={{0,2},{2,4},{4,6},{6,8},{8,10},{10,12},{12,14},{14,16},{16,18},{18... | collective-permute-start | bytes 147464 | tf_op jit(solution)/shard_map/ppermute | solution.py:81
  42.9 0.5 collective-permute-start.5
  43.4 0.2 collective-permute-start.2
  43.6 5.2 %collective-permute-start.3 = (bf16[48,1024]{1,0:T(8,128)(2,1)S(1)}, bf16[48,1024]{1,0:T(8,128)(2,1)S(1)}, u32[]{:S(2)}, u32[]{:S(2)}) collective-permute-start(bf16[48,1024]{1,0:T(8,128)(2,1)S(1)} %get-tuple-element.51), channel_id=1, source_target_pairs={{1,0},{32,1},{33,32},{64,33},{65,64},{96,65},{97,96},{128,97},{129... | collective-permute-start | bytes 294920 | tf_op jit(solution)/shard_map/ppermute | solution.py:81
  48.8 0.1 pad_add_fusion.refs_0_.place
  48.9 2.7 %shard_map.97.sent_in = bf16[32,96,384]{2,1,0:T(8,128)(2,1)} custom-call(bf16[8,2,96,128]{3,2,1,0:T(8,128)(2,1)S(1)} %get-tuple-element.54.packed, s32[16,8,128]{2,1,0:T(8,128)S(1)} %get-tuple-element.49.ids), custom_call_target="tpu_custom_call" | custom-call | flops 301989888 | bytes 2818048 | tf_op jit(solution)/shard_map/pallas_call | solution.py:35
  51.6 0.0 collective-permute-done.4.xlo
  51.6 0.0 collective-permute-done.5.xhi
  51.6 1.7 %collective-permute-done.2.zlo = bf16[48,1024]{1,0:T(8,128)(2,1)S(1)} collective-permute-done((bf16[48,1024]{1,0:T(8,128)(2,1)S(1)}, bf16[48,1024]{1,0:T(8,128)(2,1)S(1)}, u32[]{:S(2)}, u32[]{:S(2)}) %collective-permute-start.2) | collective-permute-done | bytes 98336 | tf_op jit(solution)/shard_map/ppermute | solution.py:81
  53.4 0.0 collective-permute-done.3.zhi
  53.4 3.7 %shard_map.98 = (bf16[8,2,96,128]{3,2,1,0:T(8,128)(2,1)}, bf16[32,96,384]{2,1,0:T(8,128)(2,1)}) custom-call(f32[192,1024]{1,0:T(8,128)S(1)} %get-tuple-element.48.u, bf16[64,1024]{1,0:T(8,128)(2,1)S(1)} %get-tuple-element.43.w, s32[16,8,128]{2,1,0:T(8,128)S(1)} %get-tuple-element.49.ids, ...), custom_call_target="tpu_custom_call", output_to_operand_aliasing={{1}: (8, {})} | custom-call | flops 704643072 | bytes 8486912 | tf_op jit(solution)/shard_map/pallas_call | solution.py:35
  57.1 0.0 copy-start
  57.1 0.0 copy-start.1
  57.1 63.1 %all_to_all.16.refs_1_ = bf16[32,96,384]{2,1,0:T(8,128)(2,1)S(1)} all-to-all(bf16[32,96,384]{2,1,0:T(8,128)(2,1)} %get-tuple-element.58), channel_id=1, replica_groups=mesh['px'=8,'pz'=16,'tr'=2] {'pz','tr'}, dimensions={0} | all-to-all | bytes 4718592 | tf_op jit(solution)/shard_map/all_to_all | solution.py:458
  120.3 0.0 copy-done
  120.3 0.0 copy-done.1
  120.3 4.5 %shard_map.99 = (bf16[768,768]{1,0:T(8,128)(2,1)S(1)}, bf16[1024,768]{1,0:T(8,128)(2,1)S(1)}, bf16[1024,768]{1,0:T(8,128)(2,1)S(1)}, bf16[768,768]{1,0:T(8,128)(2,1)S(1)}, bf16[512,768]{1,0:T(8,128)(2,1)S(1)}) custom-call(s32[2]{0:T(128)S(1)} %pad_add_fusion.refs_0_.place, bf16[32,96,384]{2,1,0:T(8,128)(2,1)S(1)} %all_to_all.16.refs_1_, ...), custom_call_target="tpu_custom_call" | custom-call | flops 3019898880 | bytes 11796488 | tf_op jit(solution)/shard_map/pallas_call | solution.py:35
  124.8 0.1 collective-permute-start.7
  124.9 2.5 %shard_map.100 = (bf16[1024,768]{1,0:T(8,128)(2,1)S(1)}, bf16[384,1024]{1,0:T(8,128)(2,1)S(1)}) custom-call(s32[2]{0:T(128)S(1)} %pad_add_fusion.refs_0_.place, bf16[768,768]{1,0:T(8,128)(2,1)S(1)} %get-tuple-element.60.d, bf16[1024,768]{1,0:T(8,128)(2,1)S(1)} %get-tuple-element.61.slope, bf16[1024,768]{1,0:T(8,128)(2,1)S(1)} %bitcast.15, ...), custom_call_target="tpu_custom_call" | custom-call | flops 1811939328 | bytes 7864328 | tf_op jit(solution)/shard_map/pallas_call | solution.py:35
  127.4 0.6 collective-permute-start.6
  128.0 0.0 collective-permute-done.7.got
  128.0 1.4 shard_map.101
  129.3 0.5 collective-permute-done.6.got
  129.9 1.4 shard_map.102
  131.3 5.1 %all-to-all-start.2 = ((bf16[16,96,128]{2,1,0:T(8,128)(2,1)}), bf16[16,96,128]{2,1,0:T(8,128)(2,1)S(1)}, u32[]{:S(2)}, u32[]{:S(2)}) async-start(bf16[16,96,128]{2,1,0:T(8,128)(2,1)} %bitcast.8), calls=%async_computation.2 | async-start | bytes 786432 | tf_op jit(solution)/shard_map/all_to_all | solution.py:458
  136.4 1.9 %collective-permute-start.8 = (bf16[2,64,768]{2,1,0:T(8,128)(2,1)S(1)}, bf16[2,64,768]{2,1,0:T(8,128)(2,1)S(1)}, u32[]{:S(2)}, u32[]{:S(2)}) collective-permute-start(bf16[2,64,768]{2,1,0:T(8,128)(2,1)S(1)} %get-tuple-element.75), channel_id=1, source_target_pairs={{0,64},{32,96},{64,128},{96,160},{128,192},{160,224},{192,0},{224,... | collective-permute-start | bytes 589832 | tf_op jit(solution)/shard_map/ppermute | solution.py:470
  138.2 1.4 collective-permute-start.9
  139.6 4.9 %collective-permute-done.8.from_before = bf16[2,64,768]{2,1,0:T(8,128)(2,1)S(1)} collective-permute-done((bf16[2,64,768]{2,1,0:T(8,128)(2,1)S(1)}, bf16[2,64,768]{2,1,0:T(8,128)(2,1)S(1)}, u32[]{:S(2)}, u32[]{:S(2)}) %collective-permute-start.8) | collective-permute-done | bytes 196640 | tf_op jit(solution)/shard_map/ppermute | solution.py:470
  144.6 0.3 collective-permute-done.9.from_after
  144.9 0.1 shard_map.104
  145.0 1.3 collective-permute-start.10
  146.2 2.0 %collective-permute-start.11 = (bf16[2,128,768]{2,1,0:T(8,128)(2,1)S(1)}, bf16[2,128,768]{2,1,0:T(8,128)(2,1)S(1)}, u32[]{:S(2)}, u32[]{:S(2)}) collective-permute-start(bf16[2,128,768]{2,1,0:T(8,128)(2,1)S(1)} %get-tuple-element.78), channel_id=1, source_target_pairs={{64,0},{96,32},{128,64},{160,96},{192,128},{224,160},{0,192},{32,2... | collective-permute-start | bytes 1179656 | tf_op jit(solution)/shard_map/ppermute | solution.py:470
  148.3 8.0 %collective-permute-done.10.from_before = bf16[2,128,768]{2,1,0:T(8,128)(2,1)S(1)} collective-permute-done((bf16[2,128,768]{2,1,0:T(8,128)(2,1)S(1)}, bf16[2,128,768]{2,1,0:T(8,128)(2,1)S(1)}, u32[]{:S(2)}, u32[]{:S(2)}) %collective-permute-start.10) | collective-permute-done | bytes 393248 | tf_op jit(solution)/shard_map/ppermute | solution.py:470
  156.3 0.0 collective-permute-done.11.from_after
  156.3 0.9 shard_map.105
  157.2 0.0 all-to-all-done.2.got
  157.2 1.2 shard_map.103
Async XLA Ops:
  31.3 8.3 %collective-permute-start = (bf16[48,1024]{1,0:T(8,128)(2,1)S(1)}, bf16[48,1024]{1,0:T(8,128)(2,1)S(1)}, u32[]{:S(2)}, u32[]{:S(2)}) collective-permute-start(bf16[48,1024]{1,0:T(8,128)(2,1)S(1)} %get-tuple-element.46), channel_id=1, source_target_pairs={{0,1},{1,32},{32,33},{33,64},{64,65},{65,96},{96,97},{97,128},{128... | collective-permute-start | bytes 294920 | tf_op jit(solution)/shard_map/ppermute | solution.py:81
  33.5 6.5 %collective-permute-start.1 = (bf16[48,1024]{1,0:T(8,128)(2,1)S(1)}, bf16[48,1024]{1,0:T(8,128)(2,1)S(1)}, u32[]{:S(2)}, u32[]{:S(2)}) collective-permute-start(bf16[48,1024]{1,0:T(8,128)(2,1)S(1)} %get-tuple-element.47), channel_id=1, source_target_pairs={{1,0},{32,1},{33,32},{64,33},{65,64},{96,65},{97,96},{128,97},{129... | collective-permute-start | bytes 294920 | tf_op jit(solution)/shard_map/ppermute | solution.py:81
  41.3 10.3 %collective-permute-start.4 = (f32[12,1024]{1,0:T(8,128)S(1)}, f32[12,1024]{1,0:T(8,128)S(1)}, u32[]{:S(2)}, u32[]{:S(2)}) collective-permute-start(f32[12,1024]{1,0:T(8,128)S(1)} %get-tuple-element.52), channel_id=1, source_target_pairs={{0,2},{2,4},{4,6},{6,8},{8,10},{10,12},{12,14},{14,16},{16,18},{18... | collective-permute-start | bytes 147464 | tf_op jit(solution)/shard_map/ppermute | solution.py:81
  42.9 8.7 %collective-permute-start.5 = (f32[12,1024]{1,0:T(8,128)S(1)}, f32[12,1024]{1,0:T(8,128)S(1)}, u32[]{:S(2)}, u32[]{:S(2)}) collective-permute-start(f32[12,1024]{1,0:T(8,128)S(1)} %get-tuple-element.53), channel_id=1, source_target_pairs={{2,0},{4,2},{6,4},{8,6},{10,8},{12,10},{14,12},{16,14},{18,16},{20... | collective-permute-start | bytes 147464 | tf_op jit(solution)/shard_map/ppermute | solution.py:81
  43.4 9.9 %collective-permute-start.2 = (bf16[48,1024]{1,0:T(8,128)(2,1)S(1)}, bf16[48,1024]{1,0:T(8,128)(2,1)S(1)}, u32[]{:S(2)}, u32[]{:S(2)}) collective-permute-start(bf16[48,1024]{1,0:T(8,128)(2,1)S(1)} %get-tuple-element.50), channel_id=1, source_target_pairs={{0,1},{1,32},{32,33},{33,64},{64,65},{65,96},{96,97},{97,128},{128... | collective-permute-start | bytes 294920 | tf_op jit(solution)/shard_map/ppermute | solution.py:81
  43.6 9.8 %collective-permute-start.3 = (bf16[48,1024]{1,0:T(8,128)(2,1)S(1)}, bf16[48,1024]{1,0:T(8,128)(2,1)S(1)}, u32[]{:S(2)}, u32[]{:S(2)}) collective-permute-start(bf16[48,1024]{1,0:T(8,128)(2,1)S(1)} %get-tuple-element.51), channel_id=1, source_target_pairs={{1,0},{32,1},{33,32},{64,33},{65,64},{96,65},{97,96},{128,97},{129... | collective-permute-start | bytes 294920 | tf_op jit(solution)/shard_map/ppermute | solution.py:81
  57.1 63.2 %copy-start = (bf16[1,768,1024]{2,1,0:T(8,128)(2,1)S(1)}, bf16[1,768,1024]{2,1,0:T(8,128)(2,1)}, u32[]{:S(2)}) copy-start(bf16[1,768,1024]{2,1,0:T(8,128)(2,1)} %param.12) | copy-start | bytes 4718596
  57.1 63.2 %copy-start.1 = (bf16[1,1024,768]{2,1,0:T(8,128)(2,1)S(1)}, bf16[1,1024,768]{2,1,0:T(8,128)(2,1)}, u32[]{:S(2)}) copy-start(bf16[1,1024,768]{2,1,0:T(8,128)(2,1)} %param.13) | copy-start | bytes 4718596
  124.8 3.2 %collective-permute-start.7 = (bf16[512,768]{1,0:T(8,128)(2,1)S(1)}, bf16[512,768]{1,0:T(8,128)(2,1)S(1)}, u32[]{:S(2)}, u32[]{:S(2)}) collective-permute-start(bf16[512,768]{1,0:T(8,128)(2,1)S(1)} %get-tuple-element.65), channel_id=1, source_target_pairs={{0,32},{32,0},{64,96},{96,64},{128,160},{160,128},{192,224},{224,1... | collective-permute-start | bytes 2359304 | tf_op jit(solution)/shard_map/ppermute | solution.py:463
  127.4 2.5 %collective-permute-start.6 = (bf16[384,1024]{1,0:T(8,128)(2,1)S(1)}, bf16[384,1024]{1,0:T(8,128)(2,1)S(1)}, u32[]{:S(2)}, u32[]{:S(2)}) collective-permute-start(bf16[384,1024]{1,0:T(8,128)(2,1)S(1)} %get-tuple-element.63), channel_id=1, source_target_pairs={{0,32},{32,0},{64,96},{96,64},{128,160},{160,128},{192,224},{224,1... | collective-permute-start | bytes 2359304 | tf_op jit(solution)/shard_map/ppermute | solution.py:463
  131.3 26.0 %all-to-all-start.2 = ((bf16[16,96,128]{2,1,0:T(8,128)(2,1)}), bf16[16,96,128]{2,1,0:T(8,128)(2,1)S(1)}, u32[]{:S(2)}, u32[]{:S(2)}) async-start(bf16[16,96,128]{2,1,0:T(8,128)(2,1)} %bitcast.8), calls=%async_computation.2 | async-start | bytes 786432 | tf_op jit(solution)/shard_map/all_to_all | solution.py:458
  136.4 8.2 %collective-permute-start.8 = (bf16[2,64,768]{2,1,0:T(8,128)(2,1)S(1)}, bf16[2,64,768]{2,1,0:T(8,128)(2,1)S(1)}, u32[]{:S(2)}, u32[]{:S(2)}) collective-permute-start(bf16[2,64,768]{2,1,0:T(8,128)(2,1)S(1)} %get-tuple-element.75), channel_id=1, source_target_pairs={{0,64},{32,96},{64,128},{96,160},{128,192},{160,224},{192,0},{224,... | collective-permute-start | bytes 589832 | tf_op jit(solution)/shard_map/ppermute | solution.py:470
  138.2 6.6 %collective-permute-start.9 = (bf16[2,64,768]{2,1,0:T(8,128)(2,1)S(1)}, bf16[2,64,768]{2,1,0:T(8,128)(2,1)S(1)}, u32[]{:S(2)}, u32[]{:S(2)}) collective-permute-start(bf16[2,64,768]{2,1,0:T(8,128)(2,1)S(1)} %get-tuple-element.76), channel_id=1, source_target_pairs={{64,0},{96,32},{128,64},{160,96},{192,128},{224,160},{0,192},{32,2... | collective-permute-start | bytes 589832 | tf_op jit(solution)/shard_map/ppermute | solution.py:470
  145.0 11.3 %collective-permute-start.10 = (bf16[2,128,768]{2,1,0:T(8,128)(2,1)S(1)}, bf16[2,128,768]{2,1,0:T(8,128)(2,1)S(1)}, u32[]{:S(2)}, u32[]{:S(2)}) collective-permute-start(bf16[2,128,768]{2,1,0:T(8,128)(2,1)S(1)} %get-tuple-element.77), channel_id=1, source_target_pairs={{0,64},{32,96},{64,128},{96,160},{128,192},{160,224},{192,0},{224,... | collective-permute-start | bytes 1179656 | tf_op jit(solution)/shard_map/ppermute | solution.py:470
  146.2 10.1 %collective-permute-start.11 = (bf16[2,128,768]{2,1,0:T(8,128)(2,1)S(1)}, bf16[2,128,768]{2,1,0:T(8,128)(2,1)S(1)}, u32[]{:S(2)}, u32[]{:S(2)}) collective-permute-start(bf16[2,128,768]{2,1,0:T(8,128)(2,1)S(1)} %get-tuple-element.78), channel_id=1, source_target_pairs={{64,0},{96,32},{128,64},{160,96},{192,128},{224,160},{0,192},{32,2... | collective-permute-start | bytes 1179656 | tf_op jit(solution)/shard_map/ppermute | solution.py:470

commit v8 on v7

--- a/solution.py
+++ b/solution.py
@@ -73,12 +73,17 @@
     return jax.ShapeDtypeStruct(shape, dtype)
 
 
-def shift(array, axis, wrap=True):
-    last, first = array
-    size = lax.axis_size(axis)
-    up = [(i, (i + 1) % size) for i in range(size if wrap else size - 1)]
-    down = [(j, i) for i, j in up]
-    return lax.ppermute(last, axis, up), lax.ppermute(first, axis, down)
+def swap_pairs(first, second, axis, stride=1):
+    size = math.prod(lax.axis_size(a) for a in ((axis,) if isinstance(axis, str) else axis))
+    place = lambda i: (i // stride) % 2
+    above = [(i, (i + stride) % size) for i in range(size) if place(i) == 0]
+    below = [(i, (i + stride) % size) for i in range(size) if place(i) == 1]
+    both = lambda pairs: pairs + [(j, i) for i, j in pairs]
+    return lax.ppermute(first, axis, both(above)), lax.ppermute(second, axis, both(below))
+
+
+def even_odd(odd, even_value, odd_value):
+    return jnp.where(odd == 1, odd_value, even_value)
 
 
 HALO_ROWS = 24
@@ -146,7 +151,7 @@
             packed[j, 1, zh * f : (zh + 1) * f, :] = odd.astype(BF16)
 
 
-def spread_kernel(got, v, w, xlo, xhi, zlo, zhi, ids):
+def spread_kernel(place, got, v, w, xlo, xhi, z_first, z_second, ids):
     peers, rows, lanes = got.shape
     table = got[:, rows - 8 :, :].astype(F32).reshape(peers * 8, lanes).astype(BF16)
     members = 32
@@ -191,8 +196,9 @@
                 xlo[z * comps : (z + 1) * comps, at] = whole[r : r + comps]
                 r = r + zn // 2 * comps
                 xhi[z * comps : (z + 1) * comps, at] = whole[r : r + comps]
-    zlo[...] = v[0:f]
-    zhi[...] = v[(zn - 1) * f : zn * f]
+    low_edge, high_edge = v[0:f].astype(F32), v[(zn - 1) * f : zn * f].astype(F32)
+    z_first[...] = even_odd(place[2], high_edge, low_edge).astype(BF16)
+    z_second[...] = even_odd(place[2], low_edge, high_edge).astype(BF16)
 
 
 def explicit_plane(z, u, w, zlo, zhi, x_before, x_after, e):
@@ -210,11 +216,11 @@
         if z > 0:
             total = u[(r - comps) * xl : (r - comps + 1) * xl].astype(F32)
         else:
-            total = zlo[c * xl : (c + 1) * xl].astype(F32)
+            total = zlo[c * xl : (c + 1) * xl]
         if z < zn - 1:
             total = total + u[(r + comps) * xl : (r + comps + 1) * xl].astype(F32)
         else:
-            total = total + zhi[c * xl : (c + 1) * xl].astype(F32)
+            total = total + zhi[c * xl : (c + 1) * xl]
         total = total + jnp.where(row == 0, x_before[r : r + 1], pltpu.roll(cur, 1, 0))
         total = total + jnp.where(row == xl - 1, x_after[r : r + 1], pltpu.roll(cur, xl - 1, 0))
         total = total + jnp.where(lane == 0, 0.0, pltpu.roll(cur, 1, 1))
@@ -222,22 +228,30 @@
         e[at] = (cur + factor * (total - 6.0 * cur)).astype(BF16)
 
 
+def sides(odd, first, second):
+    first, second = (x[...].astype(F32) for x in (first, second))
+    return even_odd(odd, second, first), even_odd(odd, first, second)
+
+
 def first_kernel(
-    v, w, xlo, xhi, zlo, zhi, a, u, packed, z_first, z_last, x_first, x_last, e
+    place, v, w, xlo, xhi, z_in, z_in_other, a,
+    u, packed, z_first, z_second, x_first, x_second, e,
 ):
     x_before, x_after = xlo[...], xhi[...]
+    z_before, z_after = sides(place[2], z_in, z_in_other)
     zn = 4
     for z in range(zn):
-        explicit_plane(z, v, w, zlo, zhi, x_before, x_after, e)
+        explicit_plane(z, v, w, z_before, z_after, x_before, x_after, e)
     u[...] = solve(e, a)
-    f = zlo.shape[0]
-    z_first[...] = u[0:f].astype(BF16)
-    z_last[...] = u[(zn - 1) * f : zn * f].astype(BF16)
+    f = z_in.shape[0]
+    low_edge, high_edge = u[0:f], u[(zn - 1) * f : zn * f]
+    z_first[...] = even_odd(place[2], high_edge, low_edge).astype(BF16)
+    z_second[...] = even_odd(place[2], low_edge, high_edge).astype(BF16)
     xl = w.shape[0] // zn
-    groups = u.shape[0] // xl
-    for r in range(groups):
-        x_first[r : r + 1] = u[r * xl : r * xl + 1]
-        x_last[r : r + 1] = u[(r + 1) * xl - 1 : (r + 1) * xl]
+    for r in range(u.shape[0] // xl):
+        low_row, high_row = u[r * xl : r * xl + 1], u[(r + 1) * xl - 1 : (r + 1) * xl]
+        x_first[r : r + 1] = even_odd(place[3], high_row, low_row)
+        x_second[r : r + 1] = even_odd(place[3], low_row, high_row)
     pack_columns(u, packed, zn)
 
 
@@ -258,15 +272,16 @@
 
 
 def second_kernel(
-    u, w, ids, zlo, zhi, xlo, xhi, a, sent_in, packed_far, sent_far,
+    place, u, w, ids, z_in, z_in_other, x_in, x_in_other, a, sent_in, packed_far, sent_far,
     e, after, packed, picked, sent, sems,
 ):
     del sent_in
     copies = Copies(sems)
-    zn = u.shape[0] // zlo.shape[0]
-    x_before, x_after = xlo[...], xhi[...]
+    zn = u.shape[0] // z_in.shape[0]
+    z_before, z_after = sides(place[2], z_in, z_in_other)
+    x_before, x_after = sides(place[3], x_in, x_in_other)
     for z in range(zn):
-        explicit_plane(z, u, w, zlo, zhi, x_before, x_after, e)
+        explicit_plane(z, u, w, z_before, z_after, x_before, x_after, e)
     after[...] = solve(e, a)
     pack_columns(after, packed, zn)
     copies.start(packed, packed_far)
@@ -332,17 +347,27 @@
     return lax.dot_general(left, right, (((0,), (0,)), ((), ())), preferred_element_type=F32)
 
 
-def forward_kernel(scale, place, got, w_in, w_out, x, hidden, slope, d, away):
+def forward_kernel(
+    scale, place, got, w_in_far, w_out_far, x, hidden, slope, d, away, w_in, w_out, sems
+):
+    copies = Copies(sems)
     f = got.shape[1] // 2
+    wide = 512
+    arriving = []
+    for i in range(hidden.shape[0] // wide):
+        part = (slice(None), pl.ds(i * wide, wide))
+        arriving.append(copies.start(w_in_far.at[part], w_in.at[part]))
+    copies.start(w_out_far, w_out)
     gather_rows(got, 0, x)
-    wide = 512
+    gather_rows(got, f, d)
     for i in range(hidden.shape[0] // wide):
         at = slice(i * wide, (i + 1) * wide)
+        copies.wait(arriving[i])
         pre = over_first(w_in[:, at], x[...])
         logistic = jax.nn.sigmoid(pre)
         hidden[at, :] = (pre * logistic).astype(BF16)
         slope[at, :] = (logistic * (1.0 + pre * (1.0 - logistic))).astype(slope.dtype)
-    gather_rows(got, f, d)
+    copies.finish()
     predicted = over_first(w_out[...], hidden[...])
     d[...] = ((predicted - d[...].astype(F32)) * scale).astype(BF16)
     away_blocks(hidden, d, place[0], away, away.shape[0] // 4)
@@ -402,34 +427,36 @@
 
 
 def keep_in_kernel(
-    place, x, din, got, plus_out, minus_out, far_out, own, plus, minus, top, bottom
+    place, x, din, got, plus_out, minus_out, far_out, own, plus, minus, first, second
 ):
     rows, width = plus_out.shape
     half = rows // 2
     plus[0] = plus_out[...]
     minus[0] = minus_out[...]
-    top[0] = far_out[:half]
-    bottom[0] = far_out[half:]
+    odd = place[1] % 2
+    halves = [far_out[:half].astype(F32), far_out[half:].astype(F32)]
+    first[0] = even_odd(odd, *halves).astype(BF16)
+    second[0] = even_odd(odd, *halves[::-1]).astype(BF16)
     value = over_rows(own_blocks(place, x, own.shape[0]), din[...])
-    far = fold(add_other_core(place, value, got, 0, 2), rows, width).astype(BF16)
-    top[1] = far[:half]
-    bottom[1] = far[half:]
+    far = fold(add_other_core(place, value, got, 0, 2), rows, width)
+    halves = [far[:half], far[half:]]
+    first[1] = even_odd(odd, *halves).astype(BF16)
+    second[1] = even_odd(odd, *halves[::-1]).astype(BF16)
     plus[1] = fold(add_other_core(place, value, got, 1, 1), rows, width).astype(BF16)
     minus[1] = fold(add_other_core(place, value, got, 2, 3), rows, width).astype(BF16)
     own[...] = add_other_core(place, value, got, 3, 0)
 
 
-def relay_kernel(plus, minus, from_before, from_after, plus_out, minus_out):
-    half = from_before.shape[1]
+def relay_kernel(place, plus, minus, got_first, got_second, first, second):
+    half = got_first.shape[1]
+    odd = place[1] % 2
     for which in range(plus.shape[0]):
-        plus_out[which, :half] = (
-            plus[which, :half].astype(F32) + from_before[which].astype(F32)
-        ).astype(BF16)
-        plus_out[which, half:] = plus[which, half:]
-        minus_out[which, :half] = minus[which, :half]
-        minus_out[which, half:] = (
-            minus[which, half:].astype(F32) + from_after[which].astype(F32)
-        ).astype(BF16)
+        before, after = sides(odd, got_first[which], got_second[which])
+        up = [plus[which, :half].astype(F32) + before, plus[which, half:].astype(F32)]
+        down = [minus[which, :half].astype(F32), minus[which, half:].astype(F32) + after]
+        for part, at in enumerate((slice(0, half), slice(half, 2 * half))):
+            first[which, at] = even_odd(odd, up[part], down[part]).astype(BF16)
+            second[which, at] = even_odd(odd, down[part], up[part]).astype(BF16)
 
 
 def finish_kernel(own_out, own_in, from_before, from_after, share_out, share_in):
@@ -454,6 +481,12 @@
             out[:, c, 2 * zh + 1, :] = turned[yn : 2 * yn]
 
 
+def copy_kernel(source_far, target_far, sems):
+    copies = Copies(sems)
+    copies.start(source_far, target_far)
+    copies.finish()
+
+
 def exchange(array, axis):
     return lax.all_to_all(array, axis, split_axis=0, concat_axis=0, tiled=True)
 
@@ -463,18 +496,11 @@
     return lax.ppermute(array, "px", [(i, i ^ 1) for i in range(size)])
 
 
-def shift_chips(forward, backward):
-    size = lax.axis_size("px")
-    up = [(i, (i + 2) % size) for i in range(size)]
-    down = [(j, i) for i, j in up]
-    return lax.ppermute(forward, "px", up), lax.ppermute(backward, "px", down)
-
-
 def per_device(velocity, viscosity, implicit_inverse, row_index, row_counts, weight_in, weight_out):
     yn, zn, comps, xn = velocity.shape
     peers = lax.axis_size("pz")
-    position = lax.axis_index("px")
-    place = jnp.stack([position & 1, position >> 1]).astype(jnp.int32)
+    at_px, at_pz = lax.axis_index("px"), lax.axis_index("pz")
+    place = jnp.stack([at_px & 1, at_px >> 1, lax.axis_index("tr"), at_pz & 1]).astype(jnp.int32)
     total_y = yn * peers
     xl = xn // peers
     f = comps * xl
@@ -510,9 +536,9 @@
         spread_kernel,
         (shaped((zn * f, total_y), BF16), shaped((zn * xl, total_y), BF16))
         + (x_edge, x_edge, edge, edge, ids_all),
-        (got,),
-    )
-    zlo, zhi = shift((zhi, zlo), ("px", "tr"))
+        (place, got),
+    )
+    zlo, zhi = swap_pairs(zlo, zhi, ("px", "tr"))
     message = shaped((members, f, peers * slots), BF16)
     both = shaped((members, 2 * f, peers * slots), BF16)
     sample_flops = 2 * peers * f * 256 * members * slots
@@ -527,12 +553,12 @@
     u, packed, z_first, z_last, x_first, x_last = call(
         first_kernel,
         (shaped((zn * f, total_y), F32), blocks, edge, edge, x_edge, x_edge),
-        (v, w, xlo, xhi, zlo, zhi, inverse),
+        (place, v, w, xlo, xhi, zlo, zhi, inverse),
         scratch=[pltpu.VMEM((zn * f, total_y), BF16)],
         flops=solve_flops,
     )
-    zlo, zhi = shift((z_last, z_first), ("px", "tr"))
-    xlo, xhi = shift((x_last, x_first), "pz")
+    zlo, zhi = swap_pairs(z_first, z_last, ("px", "tr"))
+    xlo, xhi = swap_pairs(x_first, x_last, "pz")
     sent = call(
         sample_kernel,
         both,
@@ -544,17 +570,26 @@
     packed, sent = call(
         second_kernel,
         (blocks, both),
-        (u, w, ids, zlo, zhi, xlo, xhi, inverse, sent),
+        (place, u, w, ids, zlo, zhi, xlo, xhi, inverse, sent),
         scratch=[pltpu.VMEM((zn * f, total_y), BF16), pltpu.VMEM((zn * f, total_y), F32)]
         + sampling
         + [pltpu.SemaphoreType.DMA((7,))],
         flops=solve_flops + sample_flops,
-        far_in=(8,),
+        far_in=(9,),
         far_out=(0, 1),
-        aliases={8: 1},
-    )
-    sent, place = lax.optimization_barrier((sent, place))
+        aliases={9: 1},
+    )
     rows_all = exchange(sent, ("pz", "tr"))
+    packed = call(
+        copy_kernel,
+        shaped((peers, 2 * f, lanes), BF16),
+        (packed.reshape(peers, 2 * f, lanes),),
+        scratch=[pltpu.SemaphoreType.DMA((1,))],
+        flops=6e9,
+        far_in=(0,),
+        far_out=(0,),
+    )
+    packed, rows_all = lax.optimization_barrier((packed, rows_all))
 
     member_in = weight_in[0]
     member_out = weight_out[0]
@@ -577,7 +612,13 @@
             shaped((hid // 2, width), BF16),
         ),
         (place, rows_all, member_in, member_out),
+        scratch=[
+            pltpu.VMEM((width, hid), BF16),
+            pltpu.VMEM((hid, width), BF16),
+            pltpu.SemaphoreType.DMA((3,)),
+        ],
         flops=matmul_flops * 5 // 2,
+        far_in=(2, 3),
     )
     got_out = swap_cores(away_out)
     din, away_in = call(
@@ -605,10 +646,10 @@
         flops=matmul_flops // 2,
     )
     packed, top = lax.optimization_barrier((packed, top))
-    arrived = shift_chips(top, bottom)
-    planes = exchange(packed.reshape(peers, 2 * f, lanes), "pz")
-    plus, minus = call(relay_kernel, (block, block), (plus, minus, *arrived))
-    arrived = shift_chips(plus, minus)
+    arrived = swap_pairs(top, bottom, "px", 2)
+    planes = exchange(packed, "pz")
+    sent = call(relay_kernel, (block, block), (place, plus, minus, *arrived))
+    arrived = swap_pairs(*sent, "px", 2)
     share_out, share_in = call(
         finish_kernel,
         (shaped((rows_out, width), F32), shaped((rows_in, hid), F32)),

time: 159 us -> 162 us (1.019)
  blocking collectives: 91.7 us -> 0 us
  waiting for transfers between devices: 16.4 us -> 83.6 us
  Pallas kernels: 21.8 us -> 40.1 us
  starting transfers between devices: 25.2 us -> 34.3 us
    all_to_all x2 -> x0, blocking collectives: 91.7 us -> none  [exchange(): return lax.all_to_all(array, axis, split_axis=0, concat_axis=0, tiled=True)]
    all_to_all x1 -> x3, waiting for transfers between devices: 0.01 us -> 60.3 us  [exchange(): return lax.all_to_all(array, axis, split_axis=0, concat_axis=0, tiled=True)]
    pallas_call x12 -> x13, Pallas kernels: 21.8 us -> 40.1 us  [call(): pl.pallas_call(kernel, out_shape=pinned if isinstance(out_shape, tuple) e...]
    all_to_all x1 -> x3, starting transfers between devices: 5.1 us -> 22.6 us  [exchange(): return lax.all_to_all(array, axis, split_axis=0, concat_axis=0, tiled=True)]
    ppermute x10, starting transfers between devices: 19.5 us -> 11 us  [the longest x5 7.21 us: swap_pairs(): lax.ppermute(second, axis, both(below))]
    ppermute x10, waiting for transfers between devices: 15.8 us -> 22.7 us  [the longest x5 13.9 us: swap_pairs(): lax.ppermute(first, axis, both(above))]
  transfers between devices with their start and end apart: 13 -> 15, of which waited for: 7 -> 11; matrix products, arithmetic and copies ran while one was open for 2% -> 2% of each run, Pallas kernels for 5% -> 13%
where the time goes in v8:
time: 162 us; the launch traced here: 161 us
  waiting for transfers between devices  83.6 us (52%)
  Pallas kernels  40.1 us (25%)
  starting transfers between devices  34.3 us (21%)
  other arithmetic  2.59 us (2%)
    all_to_all x3, waiting for transfers between devices, exchange(): return lax.all_to_all(array, axis, split_axis=0, concat_axis=0, tiled=True)  60.3 us
    pallas_call x13, Pallas kernels, call(): pl.pallas_call(kernel, out_shape=pinned if isinstance(out_shape, tuple) e...  40.1 us
    all_to_all x3, starting transfers between devices, exchange(): return lax.all_to_all(array, axis, split_axis=0, concat_axis=0, tiled=True)  22.6 us
    ppermute x5, waiting for transfers between devices, swap_pairs(): lax.ppermute(first, axis, both(above))  13.9 us
    ppermute x5, waiting for transfers between devices, swap_pairs(): lax.ppermute(second, axis, both(below))  8.8 us
    ppermute x5, starting transfers between devices, swap_pairs(): lax.ppermute(second, axis, both(below))  7.21 us
    ppermute x5, starting transfers between devices, swap_pairs(): lax.ppermute(first, axis, both(above))  3.84 us
  transfers between devices with their start and end apart: 15, of which 11 were waited for; matrix products, arithmetic and copies ran while one was open for 2% of the time, Pallas kernels for 13%

profile of v8, /device:TPU:2, one launch (start us, length us, event | category | flops | bytes accessed | tf_op | source)
XLA Modules:
  0.0 161.3 jit_solution(3354237028684193391)
XLA Ops:
  0.6 2.6 %shard_map.94 = bf16[16,152,128]{2,1,0:T(8,128)(2,1)} custom-call(f32[64,3,4,256]{3,2,1,0:T(4,128)} %bitcast.17, f32[64,4,256]{2,1,0:T(4,128)} %w_far.1, s32[24,32]{1,0:T(8,128)} %bitcast.19, s32[1,32]{1,0:T(1,128)} %bitcast.20), custom_call_target="tpu_custom_call" | custom-call | flops 1000000 | bytes 1674368 | tf_op jit(solution)/shard_map/pallas_call | solution.py:35
  3.2 10.0 %all-to-all-start = ((bf16[16,152,128]{2,1,0:T(8,128)(2,1)}), bf16[16,152,128]{2,1,0:T(8,128)(2,1)S(1)}, u32[]{:S(2)}, u32[]{:S(2)}) async-start(bf16[16,152,128]{2,1,0:T(8,128)(2,1)} %shard_map.94), calls=%async_computation | async-start | bytes 1245184 | tf_op jit(solution)/shard_map/all_to_all | solution.py:491
  13.2 0.1 pad_add_fusion.place.refs_0_
  13.2 18.0 %all-to-all-done.got = bf16[16,152,128]{2,1,0:T(8,128)(2,1)S(1)} async-done(((bf16[16,152,128]{2,1,0:T(8,128)(2,1)}), bf16[16,152,128]{2,1,0:T(8,128)(2,1)S(1)}, u32[]{:S(2)}, u32[]{:S(2)}) %all-to-all-start) | async-done | bytes 622624 | tf_op jit(solution)/shard_map/all_to_all | solution.py:491
  31.3 0.9 shard_map.95
  32.2 2.2 %collective-permute-start = (bf16[48,1024]{1,0:T(8,128)(2,1)S(1)}, bf16[48,1024]{1,0:T(8,128)(2,1)S(1)}, u32[]{:S(2)}, u32[]{:S(2)}) collective-permute-start(bf16[48,1024]{1,0:T(8,128)(2,1)S(1)} %get-tuple-element.46), channel_id=1, source_target_pairs={{0,1},{32,33},{64,65},{96,97},{128,129},{160,161},{192,193},{224,2... | collective-permute-start | bytes 294920 | tf_op jit(solution)/shard_map/ppermute | solution.py:82
  34.4 0.6 collective-permute-start.1
  35.0 2.5 %convert_element_type.3.a = bf16[1024,1024]{1,0:T(8,128)(2,1)S(1)} convert(f32[1024,1024]{1,0:T(8,128)} %param.9) | non-fusion elementwise | flops 1048576 | bytes 6291456 | tf_op jit(solution)/shard_map/convert_element_type | solution.py:529
  37.5 0.9 collective-permute-done.z_in
  38.4 4.6 %collective-permute-done.1.z_in_other = bf16[48,1024]{1,0:T(8,128)(2,1)S(1)} collective-permute-done((bf16[48,1024]{1,0:T(8,128)(2,1)S(1)}, bf16[48,1024]{1,0:T(8,128)(2,1)S(1)}, u32[]{:S(2)}, u32[]{:S(2)}) %collective-permute-start.1) | collective-permute-done | bytes 98336 | tf_op jit(solution)/shard_map/ppermute | solution.py:82
  42.9 1.9 %shard_map.96 = (f32[192,1024]{1,0:T(8,128)S(1)}, bf16[8,2,96,128]{3,2,1,0:T(8,128)(2,1)S(1)}, bf16[48,1024]{1,0:T(8,128)(2,1)S(1)}, bf16[48,1024]{1,0:T(8,128)(...) custom-call(s32[4]{0:T(128)S(1)} %pad_add_fusion.place.refs_0_, bf16[192,1024]{1,0:T(8,128)(2,1)S(1)} %get-tuple-element.42.v, ...), custom_call_target="tpu_custom_call" | custom-call | flops 402653184 | bytes 4390928 | tf_op jit(solution)/shard_map/pallas_call | solution.py:35
  44.9 0.1 collective-permute-start.2
  45.0 2.8 %collective-permute-start.3 = (bf16[48,1024]{1,0:T(8,128)(2,1)S(1)}, bf16[48,1024]{1,0:T(8,128)(2,1)S(1)}, u32[]{:S(2)}, u32[]{:S(2)}) collective-permute-start(bf16[48,1024]{1,0:T(8,128)(2,1)S(1)} %get-tuple-element.51), channel_id=1, source_target_pairs={{1,32},{33,64},{65,96},{97,128},{129,160},{161,192},{193,224},{225... | collective-permute-start | bytes 294920 | tf_op jit(solution)/shard_map/ppermute | solution.py:82
  47.7 0.6 collective-permute-start.4
  48.4 0.0 collective-permute-start.5
  48.4 2.8 %shard_map.97.sent_in = bf16[32,96,384]{2,1,0:T(8,128)(2,1)} custom-call(bf16[8,2,96,128]{3,2,1,0:T(8,128)(2,1)S(1)} %get-tuple-element.54.packed, s32[16,8,128]{2,1,0:T(8,128)S(1)} %get-tuple-element.49.ids), custom_call_target="tpu_custom_call" | custom-call | flops 301989888 | bytes 2818048 | tf_op jit(solution)/shard_map/pallas_call | solution.py:35
  51.2 1.5 collective-permute-done.4.x_in
  52.7 1.2 collective-permute-done.5.x_in_other
  53.9 0.0 collective-permute-done.2.z_in
  53.9 0.0 collective-permute-done.3.z_in_other
  53.9 4.4 %shard_map.98 = (bf16[8,2,96,128]{3,2,1,0:T(8,128)(2,1)}, bf16[32,96,384]{2,1,0:T(8,128)(2,1)}) custom-call(s32[4]{0:T(128)S(1)} %pad_add_fusion.place.refs_0_, f32[192,1024]{1,0:T(8,128)S(1)} %get-tuple-element.48.u, bf16[64,1024]{1,0:T(8,128)(2,1)S(1)} %get-tuple-element.43.w, ...), custom_call_target="tpu_custom_call", output_to_operand_aliasing={{1}: (9, {})} | custom-call | flops 704643072 | bytes 8486928 | tf_op jit(solution)/shard_map/pallas_call | solution.py:35
  58.3 7.0 %all-to-all-start.1 = ((bf16[32,96,384]{2,1,0:T(8,128)(2,1)}), bf16[32,96,384]{2,1,0:T(8,128)(2,1)S(1)}, u32[]{:S(2)}, u32[]{:S(2)}) async-start(bf16[32,96,384]{2,1,0:T(8,128)(2,1)} %get-tuple-element.56), calls=%async_computation.1 | async-start | bytes 4718592 | tf_op jit(solution)/shard_map/all_to_all | solution.py:491
  65.3 13.0 %shard_map.99 = bf16[16,96,128]{2,1,0:T(8,128)(2,1)} custom-call(bf16[16,96,128]{2,1,0:T(8,128)(2,1)} %bitcast.24), custom_call_target="tpu_custom_call" | custom-call | flops 6000000000 | bytes 786432 | tf_op jit(solution)/shard_map/pallas_call | solution.py:35
  78.4 42.2 %all-to-all-done.1.refs_1_ = bf16[32,96,384]{2,1,0:T(8,128)(2,1)S(1)} async-done(((bf16[32,96,384]{2,1,0:T(8,128)(2,1)}), bf16[32,96,384]{2,1,0:T(8,128)(2,1)S(1)}, u32[]{:S(2)}, u32[]{:S(2)}) %all-to-all-start.1) | async-done | bytes 2359328 | tf_op jit(solution)/shard_map/all_to_all | solution.py:491
  120.6 0.0 copy-start
  120.6 6.3 %shard_map.100 = (bf16[768,768]{1,0:T(8,128)(2,1)S(1)}, bf16[1024,768]{1,0:T(8,128)(2,1)S(1)}, bf16[1024,768]{1,0:T(8,128)(2,1)S(1)}, bf16[768,768]{1,0:T(8,128)(2,1)S(1)}, bf16[512,768]{1,0:T(8,128)(2,1)S(1)}) custom-call(s32[4]{0:T(128)S(1)} %pad_add_fusion.place.refs_0_, bf16[32,96,384]{2,1,0:T(8,128)(2,1)S(1)} %all-to-all-done.1.refs_1_, ...), custom_call_target="tpu_custom_call" | custom-call | flops 3019898880 | bytes 11796496 | tf_op jit(solution)/shard_map/pallas_call | solution.py:35
  126.9 0.1 collective-permute-start.7
  127.0 0.0 copy-done
  127.0 2.5 %shard_map.101 = (bf16[1024,768]{1,0:T(8,128)(2,1)S(1)}, bf16[384,1024]{1,0:T(8,128)(2,1)S(1)}) custom-call(s32[4]{0:T(128)S(1)} %pad_add_fusion.place.refs_0_, bf16[768,768]{1,0:T(8,128)(2,1)S(1)} %get-tuple-element.60.d, bf16[1024,768]{1,0:T(8,128)(2,1)S(1)} %get-tuple-element.61.slope, bf16[1024,768]{1,0:T(8,128)(2,1)S(1)} %bitcast.16, ...), custom_call_target="tpu_custom_call" | custom-call | flops 1811939328 | bytes 7864336 | tf_op jit(solution)/shard_map/pallas_call | solution.py:35
  129.5 0.6 collective-permute-start.6
  130.1 0.0 collective-permute-done.7.got
  130.1 1.4 shard_map.102
  131.5 0.5 collective-permute-done.6.got
  132.0 1.4 shard_map.103
  133.4 5.6 %all-to-all-start.2 = ((bf16[16,96,128]{2,1,0:T(8,128)(2,1)}), bf16[16,96,128]{2,1,0:T(8,128)(2,1)S(1)}, u32[]{:S(2)}, u32[]{:S(2)}) async-start(bf16[16,96,128]{2,1,0:T(8,128)(2,1)} %shard_map.99), calls=%async_computation.2 | async-start | bytes 786432 | tf_op jit(solution)/shard_map/all_to_all | solution.py:491
  139.1 0.8 collective-permute-start.8
  139.8 1.9 %collective-permute-start.9 = (bf16[2,64,768]{2,1,0:T(8,128)(2,1)S(1)}, bf16[2,64,768]{2,1,0:T(8,128)(2,1)S(1)}, u32[]{:S(2)}, u32[]{:S(2)}) collective-permute-start(bf16[2,64,768]{2,1,0:T(8,128)(2,1)S(1)} %get-tuple-element.76), channel_id=1, source_target_pairs={{64,128},{96,160},{192,0},{224,32},{128,64},{160,96},{0,192},{32,2... | collective-permute-start | bytes 589832 | tf_op jit(solution)/shard_map/ppermute | solution.py:82
  141.7 3.9 %collective-permute-done.8.got_first = bf16[2,64,768]{2,1,0:T(8,128)(2,1)S(1)} collective-permute-done((bf16[2,64,768]{2,1,0:T(8,128)(2,1)S(1)}, bf16[2,64,768]{2,1,0:T(8,128)(2,1)S(1)}, u32[]{:S(2)}, u32[]{:S(2)}) %collective-permute-start.8) | collective-permute-done | bytes 196640 | tf_op jit(solution)/shard_map/ppermute | solution.py:82
  145.7 1.7 %collective-permute-done.9.got_second = bf16[2,64,768]{2,1,0:T(8,128)(2,1)S(1)} collective-permute-done((bf16[2,64,768]{2,1,0:T(8,128)(2,1)S(1)}, bf16[2,64,768]{2,1,0:T(8,128)(2,1)S(1)}, u32[]{:S(2)}, u32[]{:S(2)}) %collective-permute-start.9) | collective-permute-done | bytes 196640 | tf_op jit(solution)/shard_map/ppermute | solution.py:82
  147.4 0.8 shard_map.105
  148.2 0.1 collective-permute-start.10
  148.3 1.9 %collective-permute-start.11 = (bf16[2,128,768]{2,1,0:T(8,128)(2,1)S(1)}, bf16[2,128,768]{2,1,0:T(8,128)(2,1)S(1)}, u32[]{:S(2)}, u32[]{:S(2)}) collective-permute-start(bf16[2,128,768]{2,1,0:T(8,128)(2,1)S(1)} %get-tuple-element.78), channel_id=1, source_target_pairs={{64,128},{96,160},{192,0},{224,32},{128,64},{160,96},{0,192},{32,2... | collective-permute-start | bytes 1179656 | tf_op jit(solution)/shard_map/ppermute | solution.py:82
  150.3 7.6 %collective-permute-done.10.from_before = bf16[2,128,768]{2,1,0:T(8,128)(2,1)S(1)} collective-permute-done((bf16[2,128,768]{2,1,0:T(8,128)(2,1)S(1)}, bf16[2,128,768]{2,1,0:T(8,128)(2,1)S(1)}, u32[]{:S(2)}, u32[]{:S(2)}) %collective-permute-start.10) | collective-permute-done | bytes 393248 | tf_op jit(solution)/shard_map/ppermute | solution.py:82
  157.9 1.3 collective-permute-done.11.from_after
  159.2 0.9 shard_map.106
  160.2 0.0 all-to-all-done.2.got
  160.2 1.2 shard_map.104
Async XLA Ops:
  3.2 28.1 %all-to-all-start = ((bf16[16,152,128]{2,1,0:T(8,128)(2,1)}), bf16[16,152,128]{2,1,0:T(8,128)(2,1)S(1)}, u32[]{:S(2)}, u32[]{:S(2)}) async-start(bf16[16,152,128]{2,1,0:T(8,128)(2,1)} %shard_map.94), calls=%async_computation | async-start | bytes 1245184 | tf_op jit(solution)/shard_map/all_to_all | solution.py:491
  32.2 6.2 %collective-permute-start = (bf16[48,1024]{1,0:T(8,128)(2,1)S(1)}, bf16[48,1024]{1,0:T(8,128)(2,1)S(1)}, u32[]{:S(2)}, u32[]{:S(2)}) collective-permute-start(bf16[48,1024]{1,0:T(8,128)(2,1)S(1)} %get-tuple-element.46), channel_id=1, source_target_pairs={{0,1},{32,33},{64,65},{96,97},{128,129},{160,161},{192,193},{224,2... | collective-permute-start | bytes 294920 | tf_op jit(solution)/shard_map/ppermute | solution.py:82
  34.4 8.6 %collective-permute-start.1 = (bf16[48,1024]{1,0:T(8,128)(2,1)S(1)}, bf16[48,1024]{1,0:T(8,128)(2,1)S(1)}, u32[]{:S(2)}, u32[]{:S(2)}) collective-permute-start(bf16[48,1024]{1,0:T(8,128)(2,1)S(1)} %get-tuple-element.47), channel_id=1, source_target_pairs={{1,32},{33,64},{65,96},{97,128},{129,160},{161,192},{193,224},{225... | collective-permute-start | bytes 294920 | tf_op jit(solution)/shard_map/ppermute | solution.py:82
  44.9 9.1 %collective-permute-start.2 = (bf16[48,1024]{1,0:T(8,128)(2,1)S(1)}, bf16[48,1024]{1,0:T(8,128)(2,1)S(1)}, u32[]{:S(2)}, u32[]{:S(2)}) collective-permute-start(bf16[48,1024]{1,0:T(8,128)(2,1)S(1)} %get-tuple-element.50), channel_id=1, source_target_pairs={{0,1},{32,33},{64,65},{96,97},{128,129},{160,161},{192,193},{224,2... | collective-permute-start | bytes 294920 | tf_op jit(solution)/shard_map/ppermute | solution.py:82
  45.0 9.0 %collective-permute-start.3 = (bf16[48,1024]{1,0:T(8,128)(2,1)S(1)}, bf16[48,1024]{1,0:T(8,128)(2,1)S(1)}, u32[]{:S(2)}, u32[]{:S(2)}) collective-permute-start(bf16[48,1024]{1,0:T(8,128)(2,1)S(1)} %get-tuple-element.51), channel_id=1, source_target_pairs={{1,32},{33,64},{65,96},{97,128},{129,160},{161,192},{193,224},{225... | collective-permute-start | bytes 294920 | tf_op jit(solution)/shard_map/ppermute | solution.py:82
  47.7 5.0 %collective-permute-start.4 = (f32[12,1024]{1,0:T(8,128)S(1)}, f32[12,1024]{1,0:T(8,128)S(1)}, u32[]{:S(2)}, u32[]{:S(2)}) collective-permute-start(f32[12,1024]{1,0:T(8,128)S(1)} %get-tuple-element.52), channel_id=1, source_target_pairs={{0,2},{4,6},{8,10},{12,14},{16,18},{20,22},{24,26},{28,30},{2,0},{... | collective-permute-start | bytes 147464 | tf_op jit(solution)/shard_map/ppermute | solution.py:82
  48.4 5.6 %collective-permute-start.5 = (f32[12,1024]{1,0:T(8,128)S(1)}, f32[12,1024]{1,0:T(8,128)S(1)}, u32[]{:S(2)}, u32[]{:S(2)}) collective-permute-start(f32[12,1024]{1,0:T(8,128)S(1)} %get-tuple-element.53), channel_id=1, source_target_pairs={{2,4},{6,8},{10,12},{14,16},{18,20},{22,24},{26,28},{30,0},{4,2},{... | collective-permute-start | bytes 147464 | tf_op jit(solution)/shard_map/ppermute | solution.py:82
  58.3 62.3 %all-to-all-start.1 = ((bf16[32,96,384]{2,1,0:T(8,128)(2,1)}), bf16[32,96,384]{2,1,0:T(8,128)(2,1)S(1)}, u32[]{:S(2)}, u32[]{:S(2)}) async-start(bf16[32,96,384]{2,1,0:T(8,128)(2,1)} %get-tuple-element.56), calls=%async_computation.1 | async-start | bytes 4718592 | tf_op jit(solution)/shard_map/all_to_all | solution.py:491
  120.6 6.4 %copy-start = (bf16[1,1024,768]{2,1,0:T(8,128)(2,1)S(1)}, bf16[1,1024,768]{2,1,0:T(8,128)(2,1)}, u32[]{:S(2)}) copy-start(bf16[1,1024,768]{2,1,0:T(8,128)(2,1)} %param.13) | copy-start | bytes 4718596
  126.9 3.2 %collective-permute-start.7 = (bf16[512,768]{1,0:T(8,128)(2,1)S(1)}, bf16[512,768]{1,0:T(8,128)(2,1)S(1)}, u32[]{:S(2)}, u32[]{:S(2)}) collective-permute-start(bf16[512,768]{1,0:T(8,128)(2,1)S(1)} %get-tuple-element.65), channel_id=1, source_target_pairs={{0,32},{32,0},{64,96},{96,64},{128,160},{160,128},{192,224},{224,1... | collective-permute-start | bytes 2359304 | tf_op jit(solution)/shard_map/ppermute | solution.py:496
  129.5 2.5 %collective-permute-start.6 = (bf16[384,1024]{1,0:T(8,128)(2,1)S(1)}, bf16[384,1024]{1,0:T(8,128)(2,1)S(1)}, u32[]{:S(2)}, u32[]{:S(2)}) collective-permute-start(bf16[384,1024]{1,0:T(8,128)(2,1)S(1)} %get-tuple-element.63), channel_id=1, source_target_pairs={{0,32},{32,0},{64,96},{96,64},{128,160},{160,128},{192,224},{224,1... | collective-permute-start | bytes 2359304 | tf_op jit(solution)/shard_map/ppermute | solution.py:496
  133.4 26.7 %all-to-all-start.2 = ((bf16[16,96,128]{2,1,0:T(8,128)(2,1)}), bf16[16,96,128]{2,1,0:T(8,128)(2,1)S(1)}, u32[]{:S(2)}, u32[]{:S(2)}) async-start(bf16[16,96,128]{2,1,0:T(8,128)(2,1)} %shard_map.99), calls=%async_computation.2 | async-start | bytes 786432 | tf_op jit(solution)/shard_map/all_to_all | solution.py:491
  139.1 6.6 %collective-permute-start.8 = (bf16[2,64,768]{2,1,0:T(8,128)(2,1)S(1)}, bf16[2,64,768]{2,1,0:T(8,128)(2,1)S(1)}, u32[]{:S(2)}, u32[]{:S(2)}) collective-permute-start(bf16[2,64,768]{2,1,0:T(8,128)(2,1)S(1)} %get-tuple-element.75), channel_id=1, source_target_pairs={{0,64},{32,96},{128,192},{160,224},{64,0},{96,32},{192,128},{224,1... | collective-permute-start | bytes 589832 | tf_op jit(solution)/shard_map/ppermute | solution.py:82
  139.8 7.5 %collective-permute-start.9 = (bf16[2,64,768]{2,1,0:T(8,128)(2,1)S(1)}, bf16[2,64,768]{2,1,0:T(8,128)(2,1)S(1)}, u32[]{:S(2)}, u32[]{:S(2)}) collective-permute-start(bf16[2,64,768]{2,1,0:T(8,128)(2,1)S(1)} %get-tuple-element.76), channel_id=1, source_target_pairs={{64,128},{96,160},{192,0},{224,32},{128,64},{160,96},{0,192},{32,2... | collective-permute-start | bytes 589832 | tf_op jit(solution)/shard_map/ppermute | solution.py:82
  148.2 9.7 %collective-permute-start.10 = (bf16[2,128,768]{2,1,0:T(8,128)(2,1)S(1)}, bf16[2,128,768]{2,1,0:T(8,128)(2,1)S(1)}, u32[]{:S(2)}, u32[]{:S(2)}) collective-permute-start(bf16[2,128,768]{2,1,0:T(8,128)(2,1)S(1)} %get-tuple-element.77), channel_id=1, source_target_pairs={{0,64},{32,96},{128,192},{160,224},{64,0},{96,32},{192,128},{224,1... | collective-permute-start | bytes 1179656 | tf_op jit(solution)/shard_map/ppermute | solution.py:82
  148.3 10.9 %collective-permute-start.11 = (bf16[2,128,768]{2,1,0:T(8,128)(2,1)S(1)}, bf16[2,128,768]{2,1,0:T(8,128)(2,1)S(1)}, u32[]{:S(2)}, u32[]{:S(2)}) collective-permute-start(bf16[2,128,768]{2,1,0:T(8,128)(2,1)S(1)} %get-tuple-element.78), channel_id=1, source_target_pairs={{64,128},{96,160},{192,0},{224,32},{128,64},{160,96},{0,192},{32,2... | collective-permute-start | bytes 1179656 | tf_op jit(solution)/shard_map/ppermute | solution.py:82

commit v9 on v7

--- a/solution.py
+++ b/solution.py
@@ -332,17 +332,29 @@
     return lax.dot_general(left, right, (((0,), (0,)), ((), ())), preferred_element_type=F32)
 
 
-def forward_kernel(scale, place, got, w_in, w_out, x, hidden, slope, d, away):
+def forward_kernel(
+    scale, place, got, w_in_far, w_out_far, x, hidden, slope, d, away, w_in, w_out, sems
+):
+    copies = Copies(sems)
     f = got.shape[1] // 2
+    wide = 512
+    count = hidden.shape[0] // wide
+    parts = [(slice(None), pl.ds(i * wide, wide)) for i in range(count)]
+    arriving = copies.start(w_in_far.at[parts[0]], w_in.at[parts[0]])
     gather_rows(got, 0, x)
-    wide = 512
-    for i in range(hidden.shape[0] // wide):
+    for i in range(count):
         at = slice(i * wide, (i + 1) * wide)
+        copies.wait(arriving)
+        if i + 1 < count:
+            arriving = copies.start(w_in_far.at[parts[i + 1]], w_in.at[parts[i + 1]])
+        else:
+            copies.start(w_out_far, w_out)
         pre = over_first(w_in[:, at], x[...])
         logistic = jax.nn.sigmoid(pre)
         hidden[at, :] = (pre * logistic).astype(BF16)
         slope[at, :] = (logistic * (1.0 + pre * (1.0 - logistic))).astype(slope.dtype)
     gather_rows(got, f, d)
+    copies.finish()
     predicted = over_first(w_out[...], hidden[...])
     d[...] = ((predicted - d[...].astype(F32)) * scale).astype(BF16)
     away_blocks(hidden, d, place[0], away, away.shape[0] // 4)
@@ -553,7 +565,6 @@
         far_out=(0, 1),
         aliases={8: 1},
     )
-    sent, place = lax.optimization_barrier((sent, place))
     rows_all = exchange(sent, ("pz", "tr"))
 
     member_in = weight_in[0]
@@ -577,7 +588,13 @@
             shaped((hid // 2, width), BF16),
         ),
         (place, rows_all, member_in, member_out),
+        scratch=[
+            pltpu.VMEM((width, hid), BF16),
+            pltpu.VMEM((hid, width), BF16),
+            pltpu.SemaphoreType.DMA((3,)),
+        ],
         flops=matmul_flops * 5 // 2,
+        far_in=(2, 3),
     )
     got_out = swap_cores(away_out)
     din, away_in = call(
@@ -607,12 +624,13 @@
     packed, top = lax.optimization_barrier((packed, top))
     arrived = shift_chips(top, bottom)
     planes = exchange(packed.reshape(peers, 2 * f, lanes), "pz")
-    plus, minus = call(relay_kernel, (block, block), (plus, minus, *arrived))
+    plus, minus = call(relay_kernel, (block, block), (plus, minus, *arrived), flops=6e9)
     arrived = shift_chips(plus, minus)
     share_out, share_in = call(
         finish_kernel,
         (shaped((rows_out, width), F32), shaped((rows_in, hid), F32)),
         (own_out, own_in, *arrived),
+        flops=1e6,
     )
     result = call(planes_kernel, shaped((yn, comps, zn, xn), F32), (planes,))
     return (result.transpose(0, 2, 1, 3), share_in[None], share_out[None])

time: 159 us -> 155 us (0.975)
  blocking collectives: 91.7 us -> 28.6 us
  waiting for transfers between devices: 16.4 us -> 65.5 us
  starting transfers between devices: 25.2 us -> 32.9 us
  Pallas kernels: 21.8 us -> 23.9 us
    all_to_all x2 -> x1, blocking collectives: 91.7 us -> 28.6 us  [exchange(): return lax.all_to_all(array, axis, split_axis=0, concat_axis=0, tiled=True)]
    all_to_all x1 -> x2, waiting for transfers between devices: 0.01 us -> 53.6 us  [exchange(): return lax.all_to_all(array, axis, split_axis=0, concat_axis=0, tiled=True)]
    all_to_all x1 -> x2, starting transfers between devices: 5.1 us -> 12.4 us  [exchange(): return lax.all_to_all(array, axis, split_axis=0, concat_axis=0, tiled=True)]
    ppermute x4, waiting for transfers between devices: 13.3 us -> 8.66 us  [shift_chips(): return (lax.ppermute(forward, 'px', up), lax.ppermute(backward, 'px', down))]
    pallas_call x12, Pallas kernels: 21.8 us -> 23.9 us  [call(): pl.pallas_call(kernel, out_shape=pinned if isinstance(out_shape, tuple) e...]
  transfers between devices with their start and end apart: 13 -> 14, of which waited for: 7 -> 7; matrix products, arithmetic and copies ran while one was open for 2% -> 2% of each run, Pallas kernels for 5% -> 5%
where the time goes in v9:
time: 155 us; the launch traced here: 154 us
  waiting for transfers between devices  65.5 us (42%)
  starting transfers between devices  32.9 us (21%)
  blocking collectives  28.6 us (18%)
  Pallas kernels  23.9 us (15%)
  other arithmetic  2.58 us (2%)
    all_to_all x2, waiting for transfers between devices, exchange(): return lax.all_to_all(array, axis, split_axis=0, concat_axis=0, tiled=True)  53.6 us
    all_to_all x1, blocking collectives, exchange(): return lax.all_to_all(array, axis, split_axis=0, concat_axis=0, tiled=True)  28.6 us
    pallas_call x12, Pallas kernels, call(): pl.pallas_call(kernel, out_shape=pinned if isinstance(out_shape, tuple) e...  23.9 us
    ppermute x6, starting transfers between devices, shift(): return (lax.ppermute(last, axis, up), lax.ppermute(first, axis, down))  12.9 us
    all_to_all x2, starting transfers between devices, exchange(): return lax.all_to_all(array, axis, split_axis=0, concat_axis=0, tiled=True)  12.4 us
    ppermute x4, waiting for transfers between devices, shift_chips(): return (lax.ppermute(forward, 'px', up), lax.ppermute(backward, 'px', down))  8.66 us
    ppermute x4, starting transfers between devices, shift_chips(): return (lax.ppermute(forward, 'px', up), lax.ppermute(backward, 'px', down))  6.74 us
  transfers between devices with their start and end apart: 14, of which 7 were waited for; matrix products, arithmetic and copies ran while one was open for 2% of the time, Pallas kernels for 5%

profile of v9, /device:TPU:2, one launch (start us, length us, event | category | flops | bytes accessed | tf_op | source)
XLA Modules:
  0.0 154.2 jit_solution(9653448076786364048)
XLA Ops:
  0.6 1.8 %shard_map.94 = bf16[16,152,128]{2,1,0:T(8,128)(2,1)S(1)} custom-call(f32[64,3,4,256]{3,2,1,0:T(4,128)} %bitcast.15, f32[64,4,256]{2,1,0:T(4,128)} %w_far.1, s32[24,32]{1,0:T(8,128)} %bitcast.17, s32[1,32]{1,0:T(1,128)} %bitcast.18), custom_call_target="tpu_custom_call" | custom-call | flops 1000000 | bytes 1674368 | tf_op jit(solution)/shard_map/pallas_call | solution.py:35
  2.4 28.6 %all_to_all.15.got = bf16[16,152,128]{2,1,0:T(8,128)(2,1)S(1)} all-to-all(bf16[16,152,128]{2,1,0:T(8,128)(2,1)S(1)} %shard_map.94), channel_id=1, replica_groups=mesh['px'=8,'pz'=16,'tr'=2] {'pz'}, dimensions={0} | all-to-all | bytes 1245184 | tf_op jit(solution)/shard_map/all_to_all | solution.py:470
  31.0 0.3 shard_map.95
  31.3 2.2 %collective-permute-start = (bf16[48,1024]{1,0:T(8,128)(2,1)S(1)}, bf16[48,1024]{1,0:T(8,128)(2,1)S(1)}, u32[]{:S(2)}, u32[]{:S(2)}) collective-permute-start(bf16[48,1024]{1,0:T(8,128)(2,1)S(1)} %get-tuple-element.44), channel_id=1, source_target_pairs={{0,1},{1,32},{32,33},{33,64},{64,65},{65,96},{96,97},{97,128},{128... | collective-permute-start | bytes 294920 | tf_op jit(solution)/shard_map/ppermute | solution.py:81
  33.5 3.2 %collective-permute-start.1 = (bf16[48,1024]{1,0:T(8,128)(2,1)S(1)}, bf16[48,1024]{1,0:T(8,128)(2,1)S(1)}, u32[]{:S(2)}, u32[]{:S(2)}) collective-permute-start(bf16[48,1024]{1,0:T(8,128)(2,1)S(1)} %get-tuple-element.45), channel_id=1, source_target_pairs={{1,0},{32,1},{33,32},{64,33},{65,64},{96,65},{97,96},{128,97},{129... | collective-permute-start | bytes 294920 | tf_op jit(solution)/shard_map/ppermute | solution.py:81
  36.8 2.5 %convert_element_type.3.a = bf16[1024,1024]{1,0:T(8,128)(2,1)S(1)} convert(f32[1024,1024]{1,0:T(8,128)} %param.9) | non-fusion elementwise | flops 1048576 | bytes 6291456 | tf_op jit(solution)/shard_map/convert_element_type | solution.py:515
  39.3 0.3 collective-permute-done.zlo
  39.6 0.4 collective-permute-done.1.zhi
  40.1 1.3 shard_map.96
  41.3 0.2 collective-permute-start.2
  41.6 5.2 %collective-permute-start.3 = (bf16[48,1024]{1,0:T(8,128)(2,1)S(1)}, bf16[48,1024]{1,0:T(8,128)(2,1)S(1)}, u32[]{:S(2)}, u32[]{:S(2)}) collective-permute-start(bf16[48,1024]{1,0:T(8,128)(2,1)S(1)} %get-tuple-element.49), channel_id=1, source_target_pairs={{1,0},{32,1},{33,32},{64,33},{65,64},{96,65},{97,96},{128,97},{129... | collective-permute-start | bytes 294920 | tf_op jit(solution)/shard_map/ppermute | solution.py:81
  46.8 1.5 collective-permute-start.4
  48.3 0.5 collective-permute-start.5
  48.8 2.8 %shard_map.97.sent_in = bf16[32,96,384]{2,1,0:T(8,128)(2,1)} custom-call(bf16[8,2,96,128]{3,2,1,0:T(8,128)(2,1)S(1)} %get-tuple-element.52.packed, s32[16,8,128]{2,1,0:T(8,128)S(1)} %get-tuple-element.47.ids), custom_call_target="tpu_custom_call" | custom-call | flops 301989888 | bytes 2818048 | tf_op jit(solution)/shard_map/pallas_call | solution.py:35
  51.6 0.1 collective-permute-done.4.xlo
  51.7 1.7 %collective-permute-done.5.xhi = f32[12,1024]{1,0:T(8,128)S(1)} collective-permute-done((f32[12,1024]{1,0:T(8,128)S(1)}, f32[12,1024]{1,0:T(8,128)S(1)}, u32[]{:S(2)}, u32[]{:S(2)}) %collective-permute-start.5) | collective-permute-done | bytes 49184 | tf_op jit(solution)/shard_map/ppermute | solution.py:81
  53.5 0.0 collective-permute-done.2.zlo
  53.5 0.0 collective-permute-done.3.zhi
  53.5 3.7 %shard_map.98 = (bf16[8,2,96,128]{3,2,1,0:T(8,128)(2,1)}, bf16[32,96,384]{2,1,0:T(8,128)(2,1)}) custom-call(f32[192,1024]{1,0:T(8,128)S(1)} %get-tuple-element.46.u, bf16[64,1024]{1,0:T(8,128)(2,1)S(1)} %get-tuple-element.41.w, s32[16,8,128]{2,1,0:T(8,128)S(1)} %get-tuple-element.47.ids, ...), custom_call_target="tpu_custom_call", output_to_operand_aliasing={{1}: (8, {})} | custom-call | flops 704643072 | bytes 8486912 | tf_op jit(solution)/shard_map/pallas_call | solution.py:35
  57.2 6.9 %all-to-all-start.1 = ((bf16[32,96,384]{2,1,0:T(8,128)(2,1)}), bf16[32,96,384]{2,1,0:T(8,128)(2,1)S(1)}, u32[]{:S(2)}, u32[]{:S(2)}) async-start(bf16[32,96,384]{2,1,0:T(8,128)(2,1)} %get-tuple-element.54), calls=%async_computation.1 | async-start | bytes 4718592 | tf_op jit(solution)/shard_map/all_to_all | solution.py:470
  64.1 0.1 pad_add_fusion.refs_0_.place
  64.2 53.5 %all-to-all-done.1.refs_1_ = bf16[32,96,384]{2,1,0:T(8,128)(2,1)S(1)} async-done(((bf16[32,96,384]{2,1,0:T(8,128)(2,1)}), bf16[32,96,384]{2,1,0:T(8,128)(2,1)S(1)}, u32[]{:S(2)}, u32[]{:S(2)}) %all-to-all-start.1) | async-done | bytes 2359328 | tf_op jit(solution)/shard_map/all_to_all | solution.py:470
  117.8 0.0 copy-start
  117.8 6.6 %shard_map.99 = (bf16[768,768]{1,0:T(8,128)(2,1)S(1)}, bf16[1024,768]{1,0:T(8,128)(2,1)S(1)}, bf16[1024,768]{1,0:T(8,128)(2,1)S(1)}, bf16[768,768]{1,0:T(8,128)(2,1)S(1)}, bf16[512,768]{1,0:T(8,128)(2,1)S(1)}) custom-call(s32[2]{0:T(128)S(1)} %pad_add_fusion.refs_0_.place, bf16[32,96,384]{2,1,0:T(8,128)(2,1)S(1)} %all-to-all-done.1.refs_1_, ...), custom_call_target="tpu_custom_call" | custom-call | flops 3019898880 | bytes 11796488 | tf_op jit(solution)/shard_map/pallas_call | solution.py:35
  124.3 0.1 collective-permute-start.7
  124.4 0.0 copy-done
  124.4 2.5 %shard_map.100 = (bf16[1024,768]{1,0:T(8,128)(2,1)S(1)}, bf16[384,1024]{1,0:T(8,128)(2,1)S(1)}) custom-call(s32[2]{0:T(128)S(1)} %pad_add_fusion.refs_0_.place, bf16[768,768]{1,0:T(8,128)(2,1)S(1)} %get-tuple-element.56.d, bf16[1024,768]{1,0:T(8,128)(2,1)S(1)} %get-tuple-element.57.slope, bf16[1024,768]{1,0:T(8,128)(2,1)S(1)} %bitcast.14, ...), custom_call_target="tpu_custom_call" | custom-call | flops 1811939328 | bytes 7864328 | tf_op jit(solution)/shard_map/pallas_call | solution.py:35
  127.0 0.8 collective-permute-start.6
  127.8 0.0 collective-permute-done.7.got
  127.8 1.3 shard_map.101
  129.1 0.6 collective-permute-done.6.got
  129.7 1.4 shard_map.102
  131.1 1.6 %collective-permute-start.8 = (bf16[2,64,768]{2,1,0:T(8,128)(2,1)S(1)}, bf16[2,64,768]{2,1,0:T(8,128)(2,1)S(1)}, u32[]{:S(2)}, u32[]{:S(2)}) collective-permute-start(bf16[2,64,768]{2,1,0:T(8,128)(2,1)S(1)} %get-tuple-element.71), channel_id=1, source_target_pairs={{0,64},{32,96},{64,128},{96,160},{128,192},{160,224},{192,0},{224,... | collective-permute-start | bytes 589832 | tf_op jit(solution)/shard_map/ppermute | solution.py:482
  132.7 1.8 %collective-permute-start.9 = (bf16[2,64,768]{2,1,0:T(8,128)(2,1)S(1)}, bf16[2,64,768]{2,1,0:T(8,128)(2,1)S(1)}, u32[]{:S(2)}, u32[]{:S(2)}) collective-permute-start(bf16[2,64,768]{2,1,0:T(8,128)(2,1)S(1)} %get-tuple-element.72), channel_id=1, source_target_pairs={{64,0},{96,32},{128,64},{160,96},{192,128},{224,160},{0,192},{32,2... | collective-permute-start | bytes 589832 | tf_op jit(solution)/shard_map/ppermute | solution.py:482
  134.5 5.5 %all-to-all-start.2 = ((bf16[16,96,128]{2,1,0:T(8,128)(2,1)}), bf16[16,96,128]{2,1,0:T(8,128)(2,1)S(1)}, u32[]{:S(2)}, u32[]{:S(2)}) async-start(bf16[16,96,128]{2,1,0:T(8,128)(2,1)} %bitcast.8), calls=%async_computation.2 | async-start | bytes 786432 | tf_op jit(solution)/shard_map/all_to_all | solution.py:470
  140.0 0.0 collective-permute-done.8.from_before
  140.0 0.0 collective-permute-done.9.from_after
  140.0 0.1 shard_map.104
  140.1 1.7 %collective-permute-start.10 = (bf16[2,128,768]{2,1,0:T(8,128)(2,1)S(1)}, bf16[2,128,768]{2,1,0:T(8,128)(2,1)S(1)}, u32[]{:S(2)}, u32[]{:S(2)}) collective-permute-start(bf16[2,128,768]{2,1,0:T(8,128)(2,1)S(1)} %get-tuple-element.73), channel_id=1, source_target_pairs={{0,64},{32,96},{64,128},{96,160},{128,192},{160,224},{192,0},{224,... | collective-permute-start | bytes 1179656 | tf_op jit(solution)/shard_map/ppermute | solution.py:482
  141.8 1.6 %collective-permute-start.11 = (bf16[2,128,768]{2,1,0:T(8,128)(2,1)S(1)}, bf16[2,128,768]{2,1,0:T(8,128)(2,1)S(1)}, u32[]{:S(2)}, u32[]{:S(2)}) collective-permute-start(bf16[2,128,768]{2,1,0:T(8,128)(2,1)S(1)} %get-tuple-element.74), channel_id=1, source_target_pairs={{64,0},{96,32},{128,64},{160,96},{192,128},{224,160},{0,192},{32,2... | collective-permute-start | bytes 1179656 | tf_op jit(solution)/shard_map/ppermute | solution.py:482
  143.4 8.7 %collective-permute-done.10.from_before = bf16[2,128,768]{2,1,0:T(8,128)(2,1)S(1)} collective-permute-done((bf16[2,128,768]{2,1,0:T(8,128)(2,1)S(1)}, bf16[2,128,768]{2,1,0:T(8,128)(2,1)S(1)}, u32[]{:S(2)}, u32[]{:S(2)}) %collective-permute-start.10) | collective-permute-done | bytes 393248 | tf_op jit(solution)/shard_map/ppermute | solution.py:482
  152.1 0.0 collective-permute-done.11.from_after
  152.1 0.9 shard_map.105
  153.0 0.0 all-to-all-done.2.got
  153.1 1.2 shard_map.103
Async XLA Ops:
  31.3 8.3 %collective-permute-start = (bf16[48,1024]{1,0:T(8,128)(2,1)S(1)}, bf16[48,1024]{1,0:T(8,128)(2,1)S(1)}, u32[]{:S(2)}, u32[]{:S(2)}) collective-permute-start(bf16[48,1024]{1,0:T(8,128)(2,1)S(1)} %get-tuple-element.44), channel_id=1, source_target_pairs={{0,1},{1,32},{32,33},{33,64},{64,65},{65,96},{96,97},{97,128},{128... | collective-permute-start | bytes 294920 | tf_op jit(solution)/shard_map/ppermute | solution.py:81
  33.5 6.5 %collective-permute-start.1 = (bf16[48,1024]{1,0:T(8,128)(2,1)S(1)}, bf16[48,1024]{1,0:T(8,128)(2,1)S(1)}, u32[]{:S(2)}, u32[]{:S(2)}) collective-permute-start(bf16[48,1024]{1,0:T(8,128)(2,1)S(1)} %get-tuple-element.45), channel_id=1, source_target_pairs={{1,0},{32,1},{33,32},{64,33},{65,64},{96,65},{97,96},{128,97},{129... | collective-permute-start | bytes 294920 | tf_op jit(solution)/shard_map/ppermute | solution.py:81
  41.3 12.1 %collective-permute-start.2 = (bf16[48,1024]{1,0:T(8,128)(2,1)S(1)}, bf16[48,1024]{1,0:T(8,128)(2,1)S(1)}, u32[]{:S(2)}, u32[]{:S(2)}) collective-permute-start(bf16[48,1024]{1,0:T(8,128)(2,1)S(1)} %get-tuple-element.48), channel_id=1, source_target_pairs={{0,1},{1,32},{32,33},{33,64},{64,65},{65,96},{96,97},{97,128},{128... | collective-permute-start | bytes 294920 | tf_op jit(solution)/shard_map/ppermute | solution.py:81
  41.6 11.9 %collective-permute-start.3 = (bf16[48,1024]{1,0:T(8,128)(2,1)S(1)}, bf16[48,1024]{1,0:T(8,128)(2,1)S(1)}, u32[]{:S(2)}, u32[]{:S(2)}) collective-permute-start(bf16[48,1024]{1,0:T(8,128)(2,1)S(1)} %get-tuple-element.49), channel_id=1, source_target_pairs={{1,0},{32,1},{33,32},{64,33},{65,64},{96,65},{97,96},{128,97},{129... | collective-permute-start | bytes 294920 | tf_op jit(solution)/shard_map/ppermute | solution.py:81
  46.8 4.9 %collective-permute-start.4 = (f32[12,1024]{1,0:T(8,128)S(1)}, f32[12,1024]{1,0:T(8,128)S(1)}, u32[]{:S(2)}, u32[]{:S(2)}) collective-permute-start(f32[12,1024]{1,0:T(8,128)S(1)} %get-tuple-element.50), channel_id=1, source_target_pairs={{0,2},{2,4},{4,6},{6,8},{8,10},{10,12},{12,14},{14,16},{16,18},{18... | collective-permute-start | bytes 147464 | tf_op jit(solution)/shard_map/ppermute | solution.py:81
  48.3 5.2 %collective-permute-start.5 = (f32[12,1024]{1,0:T(8,128)S(1)}, f32[12,1024]{1,0:T(8,128)S(1)}, u32[]{:S(2)}, u32[]{:S(2)}) collective-permute-start(f32[12,1024]{1,0:T(8,128)S(1)} %get-tuple-element.51), channel_id=1, source_target_pairs={{2,0},{4,2},{6,4},{8,6},{10,8},{12,10},{14,12},{16,14},{18,16},{20... | collective-permute-start | bytes 147464 | tf_op jit(solution)/shard_map/ppermute | solution.py:81
  57.2 60.6 %all-to-all-start.1 = ((bf16[32,96,384]{2,1,0:T(8,128)(2,1)}), bf16[32,96,384]{2,1,0:T(8,128)(2,1)S(1)}, u32[]{:S(2)}, u32[]{:S(2)}) async-start(bf16[32,96,384]{2,1,0:T(8,128)(2,1)} %get-tuple-element.54), calls=%async_computation.1 | async-start | bytes 4718592 | tf_op jit(solution)/shard_map/all_to_all | solution.py:470
  117.8 6.7 %copy-start = (bf16[1,1024,768]{2,1,0:T(8,128)(2,1)S(1)}, bf16[1,1024,768]{2,1,0:T(8,128)(2,1)}, u32[]{:S(2)}) copy-start(bf16[1,1024,768]{2,1,0:T(8,128)(2,1)} %param.13) | copy-start | bytes 4718596
  124.3 3.5 %collective-permute-start.7 = (bf16[512,768]{1,0:T(8,128)(2,1)S(1)}, bf16[512,768]{1,0:T(8,128)(2,1)S(1)}, u32[]{:S(2)}, u32[]{:S(2)}) collective-permute-start(bf16[512,768]{1,0:T(8,128)(2,1)S(1)} %get-tuple-element.61), channel_id=1, source_target_pairs={{0,32},{32,0},{64,96},{96,64},{128,160},{160,128},{192,224},{224,1... | collective-permute-start | bytes 2359304 | tf_op jit(solution)/shard_map/ppermute | solution.py:475
  127.0 2.7 %collective-permute-start.6 = (bf16[384,1024]{1,0:T(8,128)(2,1)S(1)}, bf16[384,1024]{1,0:T(8,128)(2,1)S(1)}, u32[]{:S(2)}, u32[]{:S(2)}) collective-permute-start(bf16[384,1024]{1,0:T(8,128)(2,1)S(1)} %get-tuple-element.59), channel_id=1, source_target_pairs={{0,32},{32,0},{64,96},{96,64},{128,160},{160,128},{192,224},{224,1... | collective-permute-start | bytes 2359304 | tf_op jit(solution)/shard_map/ppermute | solution.py:475
  131.1 8.9 %collective-permute-start.8 = (bf16[2,64,768]{2,1,0:T(8,128)(2,1)S(1)}, bf16[2,64,768]{2,1,0:T(8,128)(2,1)S(1)}, u32[]{:S(2)}, u32[]{:S(2)}) collective-permute-start(bf16[2,64,768]{2,1,0:T(8,128)(2,1)S(1)} %get-tuple-element.71), channel_id=1, source_target_pairs={{0,64},{32,96},{64,128},{96,160},{128,192},{160,224},{192,0},{224,... | collective-permute-start | bytes 589832 | tf_op jit(solution)/shard_map/ppermute | solution.py:482
  132.7 7.3 %collective-permute-start.9 = (bf16[2,64,768]{2,1,0:T(8,128)(2,1)S(1)}, bf16[2,64,768]{2,1,0:T(8,128)(2,1)S(1)}, u32[]{:S(2)}, u32[]{:S(2)}) collective-permute-start(bf16[2,64,768]{2,1,0:T(8,128)(2,1)S(1)} %get-tuple-element.72), channel_id=1, source_target_pairs={{64,0},{96,32},{128,64},{160,96},{192,128},{224,160},{0,192},{32,2... | collective-permute-start | bytes 589832 | tf_op jit(solution)/shard_map/ppermute | solution.py:482
  134.5 18.5 %all-to-all-start.2 = ((bf16[16,96,128]{2,1,0:T(8,128)(2,1)}), bf16[16,96,128]{2,1,0:T(8,128)(2,1)S(1)}, u32[]{:S(2)}, u32[]{:S(2)}) async-start(bf16[16,96,128]{2,1,0:T(8,128)(2,1)} %bitcast.8), calls=%async_computation.2 | async-start | bytes 786432 | tf_op jit(solution)/shard_map/all_to_all | solution.py:470
  140.1 12.0 %collective-permute-start.10 = (bf16[2,128,768]{2,1,0:T(8,128)(2,1)S(1)}, bf16[2,128,768]{2,1,0:T(8,128)(2,1)S(1)}, u32[]{:S(2)}, u32[]{:S(2)}) collective-permute-start(bf16[2,128,768]{2,1,0:T(8,128)(2,1)S(1)} %get-tuple-element.73), channel_id=1, source_target_pairs={{0,64},{32,96},{64,128},{96,160},{128,192},{160,224},{192,0},{224,... | collective-permute-start | bytes 1179656 | tf_op jit(solution)/shard_map/ppermute | solution.py:482
  141.8 10.3 %collective-permute-start.11 = (bf16[2,128,768]{2,1,0:T(8,128)(2,1)S(1)}, bf16[2,128,768]{2,1,0:T(8,128)(2,1)S(1)}, u32[]{:S(2)}, u32[]{:S(2)}) collective-permute-start(bf16[2,128,768]{2,1,0:T(8,128)(2,1)S(1)} %get-tuple-element.74), channel_id=1, source_target_pairs={{64,0},{96,32},{128,64},{160,96},{192,128},{224,160},{0,192},{32,2... | collective-permute-start | bytes 1179656 | tf_op jit(solution)/shard_map/ppermute | solution.py:482

commit v10 on v9

--- a/solution.py
+++ b/solution.py
@@ -414,38 +414,49 @@
 
 
 def keep_in_kernel(
-    place, x, din, got, plus_out, minus_out, far_out, own, plus, minus, top, bottom
+    place, x, din, got, plus_out, minus_out, far_out, own, up, down, plus, minus
 ):
     rows, width = plus_out.shape
     half = rows // 2
-    plus[0] = plus_out[...]
-    minus[0] = minus_out[...]
-    top[0] = far_out[:half]
-    bottom[0] = far_out[half:]
+
+    def put(which, far_block, plus_block, minus_block):
+        up[which, :half] = far_block[:half]
+        up[which, half:] = plus_block[half:]
+        down[which, :half] = minus_block[:half]
+        down[which, half:] = far_block[half:]
+        plus[which] = plus_block[:half]
+        minus[which] = minus_block[half:]
+
+    put(0, far_out[...], plus_out[...], minus_out[...])
     value = over_rows(own_blocks(place, x, own.shape[0]), din[...])
-    far = fold(add_other_core(place, value, got, 0, 2), rows, width).astype(BF16)
-    top[1] = far[:half]
-    bottom[1] = far[half:]
-    plus[1] = fold(add_other_core(place, value, got, 1, 1), rows, width).astype(BF16)
-    minus[1] = fold(add_other_core(place, value, got, 2, 3), rows, width).astype(BF16)
+    put(
+        1,
+        *(
+            fold(add_other_core(place, value, got, n, k), rows, width).astype(BF16)
+            for n, k in ((0, 2), (1, 1), (2, 3))
+        ),
+    )
     own[...] = add_other_core(place, value, got, 3, 0)
 
 
-def relay_kernel(plus, minus, from_before, from_after, plus_out, minus_out):
-    half = from_before.shape[1]
+def relay_kernel(plus, minus, from_before, from_after, up, down):
+    half = plus.shape[1]
     for which in range(plus.shape[0]):
-        plus_out[which, :half] = (
-            plus[which, :half].astype(F32) + from_before[which].astype(F32)
-        ).astype(BF16)
-        plus_out[which, half:] = plus[which, half:]
-        minus_out[which, :half] = minus[which, :half]
-        minus_out[which, half:] = (
-            minus[which, half:].astype(F32) + from_after[which].astype(F32)
-        ).astype(BF16)
-
-
-def finish_kernel(own_out, own_in, from_before, from_after, share_out, share_in):
-    total = [from_before[k].astype(F32) + from_after[k].astype(F32) for k in range(2)]
+        before = from_before[which, :half].astype(F32)
+        after = from_after[which, half:].astype(F32)
+        up[which] = (plus[which].astype(F32) + before).astype(BF16)
+        down[which] = (minus[which].astype(F32) + after).astype(BF16)
+
+
+def finish_kernel(
+    own_out, own_in, first_before, first_after, last_before, last_after, share_out, share_in
+):
+    half = last_before.shape[1]
+    total = []
+    for k in range(2):
+        upper = first_after[k, :half].astype(F32) + last_before[k].astype(F32)
+        lower = first_before[k, half:].astype(F32) + last_after[k].astype(F32)
+        total.append(jnp.concatenate([upper, lower], axis=0))
     share_out[...] = own_out[...] + total[0]
     share_in[...] = own_in[...] + unfold(total[1], share_in.shape[0])
 
@@ -615,21 +626,21 @@
     )
     block = shaped((2, rows_out, width), BF16)
     part = shaped((2, rows_out // 2, width), BF16)
-    own_in, plus, minus, top, bottom = call(
+    own_in, up, down, plus, minus = call(
         keep_in_kernel,
         (shaped((rows_in, hid), F32), block, block, part, part),
         (place, x, din, got_in, plus, minus, far),
         flops=matmul_flops // 2,
     )
-    packed, top = lax.optimization_barrier((packed, top))
-    arrived = shift_chips(top, bottom)
+    packed, up = lax.optimization_barrier((packed, up))
+    arrived = shift_chips(up, down)
     planes = exchange(packed.reshape(peers, 2 * f, lanes), "pz")
-    plus, minus = call(relay_kernel, (block, block), (plus, minus, *arrived), flops=6e9)
-    arrived = shift_chips(plus, minus)
+    up, down = call(relay_kernel, (part, part), (plus, minus, *arrived), flops=6e9)
+    last = shift_chips(up, down)
     share_out, share_in = call(
         finish_kernel,
         (shaped((rows_out, width), F32), shaped((rows_in, hid), F32)),
-        (own_out, own_in, *arrived),
+        (own_out, own_in, *arrived, *last),
         flops=1e6,
     )
     result = call(planes_kernel, shaped((yn, comps, zn, xn), F32), (planes,))

time: 155 us -> 155 us (level)
  transfers between devices with their start and end apart: 14 -> 14, of which waited for: 7 -> 8; matrix products, arithmetic and copies ran while one was open for 2% -> 2% of each run, Pallas kernels for 5% -> 5%
where the time goes in v10:
time: 155 us; the launch traced here: 154 us
  waiting for transfers between devices  65.5 us (42%)
  starting transfers between devices  32.9 us (21%)
  blocking collectives  28.6 us (18%)
  Pallas kernels  23.9 us (15%)
  other arithmetic  2.58 us (2%)
    all_to_all x2, waiting for transfers between devices, exchange(): return lax.all_to_all(array, axis, split_axis=0, concat_axis=0, tiled=True)  53.6 us
    all_to_all x1, blocking collectives, exchange(): return lax.all_to_all(array, axis, split_axis=0, concat_axis=0, tiled=True)  28.6 us
    pallas_call x12, Pallas kernels, call(): pl.pallas_call(kernel, out_shape=pinned if isinstance(out_shape, tuple) e...  23.9 us
    ppermute x6, starting transfers between devices, shift(): return (lax.ppermute(last, axis, up), lax.ppermute(first, axis, down))  12.9 us
    all_to_all x2, starting transfers between devices, exchange(): return lax.all_to_all(array, axis, split_axis=0, concat_axis=0, tiled=True)  12.4 us
    ppermute x4, waiting for transfers between devices, shift_chips(): return (lax.ppermute(forward, 'px', up), lax.ppermute(backward, 'px', down))  8.68 us
    ppermute x4, starting transfers between devices, shift_chips(): return (lax.ppermute(forward, 'px', up), lax.ppermute(backward, 'px', down))  6.74 us
  transfers between devices with their start and end apart: 14, of which 8 were waited for; matrix products, arithmetic and copies ran while one was open for 2% of the time, Pallas kernels for 5%

profile of v10, /device:TPU:2, one launch (start us, length us, event | category | flops | bytes accessed | tf_op | source)
XLA Modules:
  0.0 154.2 jit_solution(6019443425159249078)
XLA Ops:
  0.6 1.8 %shard_map.94 = bf16[16,152,128]{2,1,0:T(8,128)(2,1)S(1)} custom-call(f32[64,3,4,256]{3,2,1,0:T(4,128)} %bitcast.15, f32[64,4,256]{2,1,0:T(4,128)} %w_far.1, s32[24,32]{1,0:T(8,128)} %bitcast.17, s32[1,32]{1,0:T(1,128)} %bitcast.18), custom_call_target="tpu_custom_call" | custom-call | flops 1000000 | bytes 1674368 | tf_op jit(solution)/shard_map/pallas_call | solution.py:35
  2.4 28.6 %all_to_all.15.got = bf16[16,152,128]{2,1,0:T(8,128)(2,1)S(1)} all-to-all(bf16[16,152,128]{2,1,0:T(8,128)(2,1)S(1)} %shard_map.94), channel_id=1, replica_groups=mesh['px'=8,'pz'=16,'tr'=2] {'pz'}, dimensions={0} | all-to-all | bytes 1245184 | tf_op jit(solution)/shard_map/all_to_all | solution.py:481
  31.0 0.3 shard_map.95
  31.3 2.2 %collective-permute-start = (bf16[48,1024]{1,0:T(8,128)(2,1)S(1)}, bf16[48,1024]{1,0:T(8,128)(2,1)S(1)}, u32[]{:S(2)}, u32[]{:S(2)}) collective-permute-start(bf16[48,1024]{1,0:T(8,128)(2,1)S(1)} %get-tuple-element.44), channel_id=1, source_target_pairs={{0,1},{1,32},{32,33},{33,64},{64,65},{65,96},{96,97},{97,128},{128... | collective-permute-start | bytes 294920 | tf_op jit(solution)/shard_map/ppermute | solution.py:81
  33.5 3.2 %collective-permute-start.1 = (bf16[48,1024]{1,0:T(8,128)(2,1)S(1)}, bf16[48,1024]{1,0:T(8,128)(2,1)S(1)}, u32[]{:S(2)}, u32[]{:S(2)}) collective-permute-start(bf16[48,1024]{1,0:T(8,128)(2,1)S(1)} %get-tuple-element.45), channel_id=1, source_target_pairs={{1,0},{32,1},{33,32},{64,33},{65,64},{96,65},{97,96},{128,97},{129... | collective-permute-start | bytes 294920 | tf_op jit(solution)/shard_map/ppermute | solution.py:81
  36.8 2.5 %convert_element_type.3.a = bf16[1024,1024]{1,0:T(8,128)(2,1)S(1)} convert(f32[1024,1024]{1,0:T(8,128)} %param.9) | non-fusion elementwise | flops 1048576 | bytes 6291456 | tf_op jit(solution)/shard_map/convert_element_type | solution.py:526
  39.3 0.3 collective-permute-done.zlo
  39.6 0.4 collective-permute-done.1.zhi
  40.1 1.3 shard_map.96
  41.3 0.2 collective-permute-start.2
  41.6 5.2 %collective-permute-start.3 = (bf16[48,1024]{1,0:T(8,128)(2,1)S(1)}, bf16[48,1024]{1,0:T(8,128)(2,1)S(1)}, u32[]{:S(2)}, u32[]{:S(2)}) collective-permute-start(bf16[48,1024]{1,0:T(8,128)(2,1)S(1)} %get-tuple-element.49), channel_id=1, source_target_pairs={{1,0},{32,1},{33,32},{64,33},{65,64},{96,65},{97,96},{128,97},{129... | collective-permute-start | bytes 294920 | tf_op jit(solution)/shard_map/ppermute | solution.py:81
  46.8 1.5 collective-permute-start.4
  48.3 0.5 collective-permute-start.5
  48.8 2.8 %shard_map.97.sent_in = bf16[32,96,384]{2,1,0:T(8,128)(2,1)} custom-call(bf16[8,2,96,128]{3,2,1,0:T(8,128)(2,1)S(1)} %get-tuple-element.52.packed, s32[16,8,128]{2,1,0:T(8,128)S(1)} %get-tuple-element.47.ids), custom_call_target="tpu_custom_call" | custom-call | flops 301989888 | bytes 2818048 | tf_op jit(solution)/shard_map/pallas_call | solution.py:35
  51.6 0.1 collective-permute-done.4.xlo
  51.7 1.7 %collective-permute-done.5.xhi = f32[12,1024]{1,0:T(8,128)S(1)} collective-permute-done((f32[12,1024]{1,0:T(8,128)S(1)}, f32[12,1024]{1,0:T(8,128)S(1)}, u32[]{:S(2)}, u32[]{:S(2)}) %collective-permute-start.5) | collective-permute-done | bytes 49184 | tf_op jit(solution)/shard_map/ppermute | solution.py:81
  53.5 0.0 collective-permute-done.2.zlo
  53.5 0.0 collective-permute-done.3.zhi
  53.5 3.7 %shard_map.98 = (bf16[8,2,96,128]{3,2,1,0:T(8,128)(2,1)}, bf16[32,96,384]{2,1,0:T(8,128)(2,1)}) custom-call(f32[192,1024]{1,0:T(8,128)S(1)} %get-tuple-element.46.u, bf16[64,1024]{1,0:T(8,128)(2,1)S(1)} %get-tuple-element.41.w, s32[16,8,128]{2,1,0:T(8,128)S(1)} %get-tuple-element.47.ids, ...), custom_call_target="tpu_custom_call", output_to_operand_aliasing={{1}: (8, {})} | custom-call | flops 704643072 | bytes 8486912 | tf_op jit(solution)/shard_map/pallas_call | solution.py:35
  57.2 6.9 %all-to-all-start.1 = ((bf16[32,96,384]{2,1,0:T(8,128)(2,1)}), bf16[32,96,384]{2,1,0:T(8,128)(2,1)S(1)}, u32[]{:S(2)}, u32[]{:S(2)}) async-start(bf16[32,96,384]{2,1,0:T(8,128)(2,1)} %get-tuple-element.54), calls=%async_computation.1 | async-start | bytes 4718592 | tf_op jit(solution)/shard_map/all_to_all | solution.py:481
  64.1 0.1 pad_add_fusion.refs_0_.place
  64.2 53.5 %all-to-all-done.1.refs_1_ = bf16[32,96,384]{2,1,0:T(8,128)(2,1)S(1)} async-done(((bf16[32,96,384]{2,1,0:T(8,128)(2,1)}), bf16[32,96,384]{2,1,0:T(8,128)(2,1)S(1)}, u32[]{:S(2)}, u32[]{:S(2)}) %all-to-all-start.1) | async-done | bytes 2359328 | tf_op jit(solution)/shard_map/all_to_all | solution.py:481
  117.8 0.0 copy-start
  117.8 6.6 %shard_map.99 = (bf16[768,768]{1,0:T(8,128)(2,1)S(1)}, bf16[1024,768]{1,0:T(8,128)(2,1)S(1)}, bf16[1024,768]{1,0:T(8,128)(2,1)S(1)}, bf16[768,768]{1,0:T(8,128)(2,1)S(1)}, bf16[512,768]{1,0:T(8,128)(2,1)S(1)}) custom-call(s32[2]{0:T(128)S(1)} %pad_add_fusion.refs_0_.place, bf16[32,96,384]{2,1,0:T(8,128)(2,1)S(1)} %all-to-all-done.1.refs_1_, ...), custom_call_target="tpu_custom_call" | custom-call | flops 3019898880 | bytes 11796488 | tf_op jit(solution)/shard_map/pallas_call | solution.py:35
  124.3 0.1 collective-permute-start.7
  124.4 0.0 copy-done
  124.4 2.5 %shard_map.100 = (bf16[1024,768]{1,0:T(8,128)(2,1)S(1)}, bf16[384,1024]{1,0:T(8,128)(2,1)S(1)}) custom-call(s32[2]{0:T(128)S(1)} %pad_add_fusion.refs_0_.place, bf16[768,768]{1,0:T(8,128)(2,1)S(1)} %get-tuple-element.56.d, bf16[1024,768]{1,0:T(8,128)(2,1)S(1)} %get-tuple-element.57.slope, bf16[1024,768]{1,0:T(8,128)(2,1)S(1)} %bitcast.14, ...), custom_call_target="tpu_custom_call" | custom-call | flops 1811939328 | bytes 7864328 | tf_op jit(solution)/shard_map/pallas_call | solution.py:35
  127.0 0.8 collective-permute-start.6
  127.8 0.0 collective-permute-done.7.got
  127.8 1.3 shard_map.101
  129.1 0.6 collective-permute-done.6.got
  129.7 1.4 shard_map.102
  131.1 1.6 %collective-permute-start.8 = (bf16[2,128,768]{2,1,0:T(8,128)(2,1)S(1)}, bf16[2,128,768]{2,1,0:T(8,128)(2,1)S(1)}, u32[]{:S(2)}, u32[]{:S(2)}) collective-permute-start(bf16[2,128,768]{2,1,0:T(8,128)(2,1)S(1)} %get-tuple-element.69), channel_id=1, source_target_pairs={{0,64},{32,96},{64,128},{96,160},{128,192},{160,224},{192,0},{224,... | collective-permute-start | bytes 1179656 | tf_op jit(solution)/shard_map/ppermute | solution.py:493
  132.7 1.8 %collective-permute-start.9 = (bf16[2,128,768]{2,1,0:T(8,128)(2,1)S(1)}, bf16[2,128,768]{2,1,0:T(8,128)(2,1)S(1)}, u32[]{:S(2)}, u32[]{:S(2)}) collective-permute-start(bf16[2,128,768]{2,1,0:T(8,128)(2,1)S(1)} %get-tuple-element.70), channel_id=1, source_target_pairs={{64,0},{96,32},{128,64},{160,96},{192,128},{224,160},{0,192},{32,2... | collective-permute-start | bytes 1179656 | tf_op jit(solution)/shard_map/ppermute | solution.py:493
  134.5 5.5 %all-to-all-start.2 = ((bf16[16,96,128]{2,1,0:T(8,128)(2,1)}), bf16[16,96,128]{2,1,0:T(8,128)(2,1)S(1)}, u32[]{:S(2)}, u32[]{:S(2)}) async-start(bf16[16,96,128]{2,1,0:T(8,128)(2,1)} %bitcast.8), calls=%async_computation.2 | async-start | bytes 786432 | tf_op jit(solution)/shard_map/all_to_all | solution.py:481
  140.0 4.1 %collective-permute-done.8.from_before.first_before = bf16[2,128,768]{2,1,0:T(8,128)(2,1)S(1)} collective-permute-done((bf16[2,128,768]{2,1,0:T(8,128)(2,1)S(1)}, bf16[2,128,768]{2,1,0:T(8,128)(2,1)S(1)}, u32[]{:S(2)}, u32[]{:S(2)}) %collective-permute-start.8) | collective-permute-done | bytes 393248 | tf_op jit(solution)/shard_map/ppermute | solution.py:493
  144.1 0.0 collective-permute-done.9.from_after.first_after
  144.1 0.1 shard_map.104
  144.2 1.8 %collective-permute-start.10 = (bf16[2,64,768]{2,1,0:T(8,128)(2,1)S(1)}, bf16[2,64,768]{2,1,0:T(8,128)(2,1)S(1)}, u32[]{:S(2)}, u32[]{:S(2)}) collective-permute-start(bf16[2,64,768]{2,1,0:T(8,128)(2,1)S(1)} %get-tuple-element.73), channel_id=1, source_target_pairs={{0,64},{32,96},{64,128},{96,160},{128,192},{160,224},{192,0},{224,... | collective-permute-start | bytes 589832 | tf_op jit(solution)/shard_map/ppermute | solution.py:493
  146.0 1.5 collective-permute-start.11
  147.5 4.6 %collective-permute-done.10.last_before = bf16[2,64,768]{2,1,0:T(8,128)(2,1)S(1)} collective-permute-done((bf16[2,64,768]{2,1,0:T(8,128)(2,1)S(1)}, bf16[2,64,768]{2,1,0:T(8,128)(2,1)S(1)}, u32[]{:S(2)}, u32[]{:S(2)}) %collective-permute-start.10) | collective-permute-done | bytes 196640 | tf_op jit(solution)/shard_map/ppermute | solution.py:493
  152.1 0.0 collective-permute-done.11.last_after
  152.1 0.9 shard_map.105
  153.0 0.0 all-to-all-done.2.got
  153.1 1.2 shard_map.103
Async XLA Ops:
  31.3 8.3 %collective-permute-start = (bf16[48,1024]{1,0:T(8,128)(2,1)S(1)}, bf16[48,1024]{1,0:T(8,128)(2,1)S(1)}, u32[]{:S(2)}, u32[]{:S(2)}) collective-permute-start(bf16[48,1024]{1,0:T(8,128)(2,1)S(1)} %get-tuple-element.44), channel_id=1, source_target_pairs={{0,1},{1,32},{32,33},{33,64},{64,65},{65,96},{96,97},{97,128},{128... | collective-permute-start | bytes 294920 | tf_op jit(solution)/shard_map/ppermute | solution.py:81
  33.5 6.5 %collective-permute-start.1 = (bf16[48,1024]{1,0:T(8,128)(2,1)S(1)}, bf16[48,1024]{1,0:T(8,128)(2,1)S(1)}, u32[]{:S(2)}, u32[]{:S(2)}) collective-permute-start(bf16[48,1024]{1,0:T(8,128)(2,1)S(1)} %get-tuple-element.45), channel_id=1, source_target_pairs={{1,0},{32,1},{33,32},{64,33},{65,64},{96,65},{97,96},{128,97},{129... | collective-permute-start | bytes 294920 | tf_op jit(solution)/shard_map/ppermute | solution.py:81
  41.3 12.1 %collective-permute-start.2 = (bf16[48,1024]{1,0:T(8,128)(2,1)S(1)}, bf16[48,1024]{1,0:T(8,128)(2,1)S(1)}, u32[]{:S(2)}, u32[]{:S(2)}) collective-permute-start(bf16[48,1024]{1,0:T(8,128)(2,1)S(1)} %get-tuple-element.48), channel_id=1, source_target_pairs={{0,1},{1,32},{32,33},{33,64},{64,65},{65,96},{96,97},{97,128},{128... | collective-permute-start | bytes 294920 | tf_op jit(solution)/shard_map/ppermute | solution.py:81
  41.6 11.9 %collective-permute-start.3 = (bf16[48,1024]{1,0:T(8,128)(2,1)S(1)}, bf16[48,1024]{1,0:T(8,128)(2,1)S(1)}, u32[]{:S(2)}, u32[]{:S(2)}) collective-permute-start(bf16[48,1024]{1,0:T(8,128)(2,1)S(1)} %get-tuple-element.49), channel_id=1, source_target_pairs={{1,0},{32,1},{33,32},{64,33},{65,64},{96,65},{97,96},{128,97},{129... | collective-permute-start | bytes 294920 | tf_op jit(solution)/shard_map/ppermute | solution.py:81
  46.8 4.9 %collective-permute-start.4 = (f32[12,1024]{1,0:T(8,128)S(1)}, f32[12,1024]{1,0:T(8,128)S(1)}, u32[]{:S(2)}, u32[]{:S(2)}) collective-permute-start(f32[12,1024]{1,0:T(8,128)S(1)} %get-tuple-element.50), channel_id=1, source_target_pairs={{0,2},{2,4},{4,6},{6,8},{8,10},{10,12},{12,14},{14,16},{16,18},{18... | collective-permute-start | bytes 147464 | tf_op jit(solution)/shard_map/ppermute | solution.py:81
  48.3 5.2 %collective-permute-start.5 = (f32[12,1024]{1,0:T(8,128)S(1)}, f32[12,1024]{1,0:T(8,128)S(1)}, u32[]{:S(2)}, u32[]{:S(2)}) collective-permute-start(f32[12,1024]{1,0:T(8,128)S(1)} %get-tuple-element.51), channel_id=1, source_target_pairs={{2,0},{4,2},{6,4},{8,6},{10,8},{12,10},{14,12},{16,14},{18,16},{20... | collective-permute-start | bytes 147464 | tf_op jit(solution)/shard_map/ppermute | solution.py:81
  57.2 60.6 %all-to-all-start.1 = ((bf16[32,96,384]{2,1,0:T(8,128)(2,1)}), bf16[32,96,384]{2,1,0:T(8,128)(2,1)S(1)}, u32[]{:S(2)}, u32[]{:S(2)}) async-start(bf16[32,96,384]{2,1,0:T(8,128)(2,1)} %get-tuple-element.54), calls=%async_computation.1 | async-start | bytes 4718592 | tf_op jit(solution)/shard_map/all_to_all | solution.py:481
  117.8 6.7 %copy-start = (bf16[1,1024,768]{2,1,0:T(8,128)(2,1)S(1)}, bf16[1,1024,768]{2,1,0:T(8,128)(2,1)}, u32[]{:S(2)}) copy-start(bf16[1,1024,768]{2,1,0:T(8,128)(2,1)} %param.13) | copy-start | bytes 4718596
  124.3 3.5 %collective-permute-start.7 = (bf16[512,768]{1,0:T(8,128)(2,1)S(1)}, bf16[512,768]{1,0:T(8,128)(2,1)S(1)}, u32[]{:S(2)}, u32[]{:S(2)}) collective-permute-start(bf16[512,768]{1,0:T(8,128)(2,1)S(1)} %get-tuple-element.61), channel_id=1, source_target_pairs={{0,32},{32,0},{64,96},{96,64},{128,160},{160,128},{192,224},{224,1... | collective-permute-start | bytes 2359304 | tf_op jit(solution)/shard_map/ppermute | solution.py:486
  127.0 2.7 %collective-permute-start.6 = (bf16[384,1024]{1,0:T(8,128)(2,1)S(1)}, bf16[384,1024]{1,0:T(8,128)(2,1)S(1)}, u32[]{:S(2)}, u32[]{:S(2)}) collective-permute-start(bf16[384,1024]{1,0:T(8,128)(2,1)S(1)} %get-tuple-element.59), channel_id=1, source_target_pairs={{0,32},{32,0},{64,96},{96,64},{128,160},{160,128},{192,224},{224,1... | collective-permute-start | bytes 2359304 | tf_op jit(solution)/shard_map/ppermute | solution.py:486
  131.1 13.0 %collective-permute-start.8 = (bf16[2,128,768]{2,1,0:T(8,128)(2,1)S(1)}, bf16[2,128,768]{2,1,0:T(8,128)(2,1)S(1)}, u32[]{:S(2)}, u32[]{:S(2)}) collective-permute-start(bf16[2,128,768]{2,1,0:T(8,128)(2,1)S(1)} %get-tuple-element.69), channel_id=1, source_target_pairs={{0,64},{32,96},{64,128},{96,160},{128,192},{160,224},{192,0},{224,... | collective-permute-start | bytes 1179656 | tf_op jit(solution)/shard_map/ppermute | solution.py:493
  132.7 11.4 %collective-permute-start.9 = (bf16[2,128,768]{2,1,0:T(8,128)(2,1)S(1)}, bf16[2,128,768]{2,1,0:T(8,128)(2,1)S(1)}, u32[]{:S(2)}, u32[]{:S(2)}) collective-permute-start(bf16[2,128,768]{2,1,0:T(8,128)(2,1)S(1)} %get-tuple-element.70), channel_id=1, source_target_pairs={{64,0},{96,32},{128,64},{160,96},{192,128},{224,160},{0,192},{32,2... | collective-permute-start | bytes 1179656 | tf_op jit(solution)/shard_map/ppermute | solution.py:493
  134.5 18.5 %all-to-all-start.2 = ((bf16[16,96,128]{2,1,0:T(8,128)(2,1)}), bf16[16,96,128]{2,1,0:T(8,128)(2,1)S(1)}, u32[]{:S(2)}, u32[]{:S(2)}) async-start(bf16[16,96,128]{2,1,0:T(8,128)(2,1)} %bitcast.8), calls=%async_computation.2 | async-start | bytes 786432 | tf_op jit(solution)/shard_map/all_to_all | solution.py:481
  144.2 7.9 %collective-permute-start.10 = (bf16[2,64,768]{2,1,0:T(8,128)(2,1)S(1)}, bf16[2,64,768]{2,1,0:T(8,128)(2,1)S(1)}, u32[]{:S(2)}, u32[]{:S(2)}) collective-permute-start(bf16[2,64,768]{2,1,0:T(8,128)(2,1)S(1)} %get-tuple-element.73), channel_id=1, source_target_pairs={{0,64},{32,96},{64,128},{96,160},{128,192},{160,224},{192,0},{224,... | collective-permute-start | bytes 589832 | tf_op jit(solution)/shard_map/ppermute | solution.py:493
  146.0 6.1 %collective-permute-start.11 = (bf16[2,64,768]{2,1,0:T(8,128)(2,1)S(1)}, bf16[2,64,768]{2,1,0:T(8,128)(2,1)S(1)}, u32[]{:S(2)}, u32[]{:S(2)}) collective-permute-start(bf16[2,64,768]{2,1,0:T(8,128)(2,1)S(1)} %get-tuple-element.74), channel_id=1, source_target_pairs={{64,0},{96,32},{128,64},{160,96},{192,128},{224,160},{0,192},{32,2... | collective-permute-start | bytes 589832 | tf_op jit(solution)/shard_map/ppermute | solution.py:493

commit v11 on v10

--- a/solution.py
+++ b/solution.py
@@ -81,7 +81,7 @@
     return lax.ppermute(last, axis, up), lax.ppermute(first, axis, down)
 
 
-HALO_ROWS = 24
+HALO_ROWS = 40
 GROUP = 8
 
 
@@ -102,14 +102,15 @@
             base = zh * half + c * xl
             for q in range(peers):
                 out[q, base : base + xl, :] = turned[q * xl : (q + 1) * xl].astype(BF16)
-            if c == comps:
-                continue
+            group = zn // 2 * comps
             for q in range(peers):
-                before = (q * xl - 1) % xn
-                after = (q + 1) * xl % xn
-                r = q * HALO_ROWS + zh * comps + c
-                edge[r : r + 1] = turned[before : before + 1]
-                edge[r + zn // 2 * comps : r + zn // 2 * comps + 1] = turned[after : after + 1]
+                columns = [(q * xl + k) % xn for k in (-2, -1, xl, xl + 1)]
+                r, step = q * HALO_ROWS + zh * comps + c, group
+                if c == comps:
+                    r, step = q * HALO_ROWS + 4 * group + zh, zn // 2
+                    columns = columns[1:3]
+                for k, x in enumerate(columns):
+                    edge[r + k * step : r + k * step + 1] = turned[x : x + 1]
     start = zn // 2 * half
     slots, members = index.shape
     slot = lax.broadcasted_iota(jnp.int32, (slots, members), 0)
@@ -119,6 +120,7 @@
     numbers = jnp.concatenate([live[k * rows : (k + 1) * rows] for k in range(sides)], axis=1)
     numbers = jnp.concatenate([numbers, jnp.zeros((8 - rows, lanes_of), F32)], axis=0)
     for q in range(peers):
+        edge[(q + 1) * HALO_ROWS - 12 : (q + 1) * HALO_ROWS - 8] = jnp.zeros((4, lanes_of), F32)
         edge[(q + 1) * HALO_ROWS - 8 : (q + 1) * HALO_ROWS] = numbers
         out[q, start : start + HALO_ROWS, :] = edge[
             q * HALO_ROWS : (q + 1) * HALO_ROWS
@@ -146,7 +148,7 @@
             packed[j, 1, zh * f : (zh + 1) * f, :] = odd.astype(BF16)
 
 
-def spread_kernel(got, v, w, xlo, xhi, zlo, zhi, ids):
+def spread_kernel(got, v, w, x_halo, w_halo, zlo, zhi, ids):
     peers, rows, lanes = got.shape
     table = got[:, rows - 8 :, :].astype(F32).reshape(peers * 8, lanes).astype(BF16)
     members = 32
@@ -187,12 +189,19 @@
                 whole = sides[side]
                 v[z * f : (z + 1) * f, at] = whole[zh * half : zh * half + f].astype(BF16)
                 w[z * xl : (z + 1) * xl, at] = whole[zh * half + f : (zh + 1) * half].astype(BF16)
-                r = zn // 2 * half + zh * comps
-                xlo[z * comps : (z + 1) * comps, at] = whole[r : r + comps]
-                r = r + zn // 2 * comps
-                xhi[z * comps : (z + 1) * comps, at] = whole[r : r + comps]
-    zlo[...] = v[0:f]
-    zhi[...] = v[(zn - 1) * f : zn * f]
+                group = zn // 2 * comps
+                for k in range(4):
+                    r = zn // 2 * half + k * group + zh * comps
+                    to = k * zn * comps + z * comps
+                    x_halo[to : to + comps, at] = whole[r : r + comps]
+                for k in range(2):
+                    r = zn // 2 * half + 4 * group + k * (zn // 2) + zh
+                    w_halo[k * zn + z : k * zn + z + 1, at] = whole[r : r + 1]
+    for edge, z in ((zlo, 0), (zhi, zn - 1)):
+        sides = [x_halo[(k * zn + z) * comps : (k * zn + z + 1) * comps] for k in (1, 2)]
+        fill = jnp.zeros((8 - 2 * comps, v.shape[1]), F32)
+        plane = v[z * f : (z + 1) * f].astype(F32)
+        edge[...] = jnp.concatenate([plane, *sides, fill], axis=0).astype(BF16)
 
 
 def explicit_plane(z, u, w, zlo, zhi, x_before, x_after, e):
@@ -222,22 +231,55 @@
         e[at] = (cur + factor * (total - 6.0 * cur)).astype(BF16)
 
 
+def explicit_sides(v, x_halo, w_halo, zlo, zhi):
+    zn = 4
+    rows = x_halo.shape[0] // 4
+    comps = rows // zn
+    xl = v.shape[0] // rows
+    cols = v.shape[1]
+    lane = lax.broadcasted_iota(jnp.int32, (rows, cols), 1)
+    blocks = [v[r * xl : (r + 1) * xl].astype(F32) for r in range(rows)]
+    inner = [
+        jnp.concatenate([block[k : k + 1] for block in blocks], axis=0) for k in (0, xl - 1)
+    ]
+    z_before, z_after = zlo[rows * xl // zn :].astype(F32), zhi[rows * xl // zn :].astype(F32)
+    values = []
+    for k in range(2):
+        cur = x_halo[(k + 1) * rows : (k + 2) * rows]
+        total = inner[k] + x_halo[3 * k * rows : (3 * k + 1) * rows]
+        part = slice(k * comps, (k + 1) * comps)
+        total = total + jnp.concatenate([z_before[part], cur[: rows - comps]], axis=0)
+        total = total + jnp.concatenate([cur[comps:], z_after[part]], axis=0)
+        total = total + jnp.where(lane == 0, 0.0, pltpu.roll(cur, 1, 1))
+        total = total + jnp.where(lane == cols - 1, 0.0, pltpu.roll(cur, cols - 1, 1))
+        factor = jnp.concatenate(
+            [jnp.broadcast_to(w_halo[r : r + 1], (comps, cols)) for r in range(k * zn, (k + 1) * zn)],
+            axis=0,
+        )
+        values.append(cur + diffusion_factor * factor * (total - 6.0 * cur))
+    return values
+
+
 def first_kernel(
-    v, w, xlo, xhi, zlo, zhi, a, u, packed, z_first, z_last, x_first, x_last, e
+    v, w, x_halo, w_halo, zlo, zhi, a, u, packed, z_first, z_last, x_before_out, x_after_out, e
 ):
-    x_before, x_after = xlo[...], xhi[...]
     zn = 4
+    rows = x_halo.shape[0] // 4
+    count = v.shape[0]
+    f = count // zn
+    x_before, x_after = x_halo[rows : 2 * rows], x_halo[2 * rows : 3 * rows]
     for z in range(zn):
-        explicit_plane(z, v, w, zlo, zhi, x_before, x_after, e)
-    u[...] = solve(e, a)
-    f = zlo.shape[0]
+        explicit_plane(z, v, w, zlo.at[pl.ds(0, f)], zhi.at[pl.ds(0, f)], x_before, x_after, e)
+    fill = jnp.zeros((e.shape[0] - count - 2 * rows, v.shape[1]), F32)
+    e[count:] = jnp.concatenate(
+        [*explicit_sides(v, x_halo, w_halo, zlo, zhi), fill], axis=0
+    ).astype(BF16)
+    solved = solve(e, a)
+    u[...] = solved[:count]
+    x_before_out[...] = solved[count : count + rows]
+    x_after_out[...] = solved[count + rows : count + 2 * rows]
     z_first[...] = u[0:f].astype(BF16)
     z_last[...] = u[(zn - 1) * f : zn * f].astype(BF16)
-    xl = w.shape[0] // zn
-    groups = u.shape[0] // xl
-    for r in range(groups):
-        x_first[r : r + 1] = u[r * xl : r * xl + 1]
-        x_last[r : r + 1] = u[(r + 1) * xl - 1 : (r + 1) * xl]
     pack_columns(u, packed, zn)
 
 
@@ -529,10 +571,12 @@
     edge = shaped((f, total_y), BF16)
     x_edge = shaped((zn * comps, total_y), F32)
     ids_all = shaped((peers, 8, lanes), jnp.int32)
-    v, w, xlo, xhi, zlo, zhi, ids = call(
+    wide_edge = shaped((f + 8, total_y), BF16)
+    v, w, x_halo, w_halo, zlo, zhi, ids = call(
         spread_kernel,
         (shaped((zn * f, total_y), BF16), shaped((zn * xl, total_y), BF16))
-        + (x_edge, x_edge, edge, edge, ids_all),
+        + (shaped((4 * zn * comps, total_y), F32), shaped((2 * zn, total_y), F32))
+        + (wide_edge, wide_edge, ids_all),
         (got,),
     )
     zlo, zhi = shift((zhi, zlo), ("px", "tr"))
@@ -547,15 +591,14 @@
     blocks = shaped((peers // 2, 2, 2 * f, lanes), BF16)
     half_blocks = shaped((peers // 2, 2 * f, lanes), BF16)
     sampling[0] = pltpu.VMEM(blocks.shape, BF16)
-    u, packed, z_first, z_last, x_first, x_last = call(
+    u, packed, z_first, z_last, xlo, xhi = call(
         first_kernel,
         (shaped((zn * f, total_y), F32), blocks, edge, edge, x_edge, x_edge),
-        (v, w, xlo, xhi, zlo, zhi, inverse),
-        scratch=[pltpu.VMEM((zn * f, total_y), BF16)],
+        (v, w, x_halo, w_halo, zlo, zhi, inverse),
+        scratch=[pltpu.VMEM((zn * f + 32, total_y), BF16)],
         flops=solve_flops,
     )
     zlo, zhi = shift((z_last, z_first), ("px", "tr"))
-    xlo, xhi = shift((x_last, x_first), "pz")
     sent = call(
         sample_kernel,
         both,

time: 155 us -> 155 us (level)
  starting transfers between devices: 32.9 us -> 30 us
    all_to_all x2, waiting for transfers between devices: 53.6 us -> 57.8 us  [exchange(): return lax.all_to_all(array, axis, split_axis=0, concat_axis=0, tiled=True)]
    ppermute x6 -> x4, starting transfers between devices: 12.9 us -> 10.9 us  [shift(): return (lax.ppermute(last, axis, up), lax.ppermute(first, axis, down))]
    ppermute x4, waiting for transfers between devices: 8.68 us -> 7.09 us  [shift_chips(): return (lax.ppermute(forward, 'px', up), lax.ppermute(backward, 'px', down))]
  transfers between devices with their start and end apart: 14 -> 12, of which waited for: 8 -> 7; matrix products, arithmetic and copies ran while one was open for 2% -> 2% of each run, Pallas kernels for 5% -> 5%
where the time goes in v11:
time: 155 us; the launch traced here: 154 us
  waiting for transfers between devices  66.8 us (43%)
  starting transfers between devices  30 us (19%)
  blocking collectives  29.8 us (19%)
  Pallas kernels  24.1 us (16%)
  other arithmetic  2.58 us (2%)
    all_to_all x2, waiting for transfers between devices, exchange(): return lax.all_to_all(array, axis, split_axis=0, concat_axis=0, tiled=True)  57.8 us
    all_to_all x1, blocking collectives, exchange(): return lax.all_to_all(array, axis, split_axis=0, concat_axis=0, tiled=True)  29.8 us
    pallas_call x12, Pallas kernels, call(): pl.pallas_call(kernel, out_shape=pinned if isinstance(out_shape, tuple) e...  24.1 us
    all_to_all x2, starting transfers between devices, exchange(): return lax.all_to_all(array, axis, split_axis=0, concat_axis=0, tiled=True)  11.8 us
    ppermute x4, starting transfers between devices, shift(): return (lax.ppermute(last, axis, up), lax.ppermute(first, axis, down))  10.9 us
    ppermute x4, waiting for transfers between devices, shift_chips(): return (lax.ppermute(forward, 'px', up), lax.ppermute(backward, 'px', down))  7.09 us
    ppermute x4, starting transfers between devices, shift_chips(): return (lax.ppermute(forward, 'px', up), lax.ppermute(backward, 'px', down))  6.64 us
  transfers between devices with their start and end apart: 12, of which 7 were waited for; matrix products, arithmetic and copies ran while one was open for 2% of the time, Pallas kernels for 5%

profile of v11, /device:TPU:2, one launch (start us, length us, event | category | flops | bytes accessed | tf_op | source)
XLA Modules:
  0.0 154.1 jit_solution(9215735803818025607)
XLA Ops:
  0.6 1.8 %shard_map.94 = bf16[16,168,128]{2,1,0:T(8,128)(2,1)S(1)} custom-call(f32[64,3,4,256]{3,2,1,0:T(4,128)} %bitcast.15, f32[64,4,256]{2,1,0:T(4,128)} %w_far.1, s32[24,32]{1,0:T(8,128)} %bitcast.17, s32[1,32]{1,0:T(1,128)} %bitcast.18), custom_call_target="tpu_custom_call" | custom-call | flops 1000000 | bytes 1739904 | tf_op jit(solution)/shard_map/pallas_call | solution.py:35
  2.4 29.8 %all_to_all.15.got = bf16[16,168,128]{2,1,0:T(8,128)(2,1)S(1)} all-to-all(bf16[16,168,128]{2,1,0:T(8,128)(2,1)S(1)} %shard_map.94), channel_id=1, replica_groups=mesh['px'=8,'pz'=16,'tr'=2] {'pz'}, dimensions={0} | all-to-all | bytes 1376256 | tf_op jit(solution)/shard_map/all_to_all | solution.py:523
  32.3 0.4 shard_map.95
  32.7 2.2 %collective-permute-start = (bf16[56,1024]{1,0:T(8,128)(2,1)S(1)}, bf16[56,1024]{1,0:T(8,128)(2,1)S(1)}, u32[]{:S(2)}, u32[]{:S(2)}) collective-permute-start(bf16[56,1024]{1,0:T(8,128)(2,1)S(1)} %get-tuple-element.44), channel_id=1, source_target_pairs={{0,1},{1,32},{32,33},{33,64},{64,65},{65,96},{96,97},{97,128},{128... | collective-permute-start | bytes 344072 | tf_op jit(solution)/shard_map/ppermute | solution.py:81
  34.9 3.2 %collective-permute-start.1 = (bf16[56,1024]{1,0:T(8,128)(2,1)S(1)}, bf16[56,1024]{1,0:T(8,128)(2,1)S(1)}, u32[]{:S(2)}, u32[]{:S(2)}) collective-permute-start(bf16[56,1024]{1,0:T(8,128)(2,1)S(1)} %get-tuple-element.45), channel_id=1, source_target_pairs={{1,0},{32,1},{33,32},{64,33},{65,64},{96,65},{97,96},{128,97},{129... | collective-permute-start | bytes 344072 | tf_op jit(solution)/shard_map/ppermute | solution.py:81
  38.1 2.5 %convert_element_type.3.a = bf16[1024,1024]{1,0:T(8,128)(2,1)S(1)} convert(f32[1024,1024]{1,0:T(8,128)} %param.9) | non-fusion elementwise | flops 1048576 | bytes 6291456 | tf_op jit(solution)/shard_map/convert_element_type | solution.py:568
  40.7 0.7 collective-permute-done.zlo
  41.4 0.6 collective-permute-done.1.zhi
  42.0 1.4 shard_map.96
  43.4 0.1 collective-permute-start.2
  43.5 5.3 %collective-permute-start.3 = (bf16[48,1024]{1,0:T(8,128)(2,1)S(1)}, bf16[48,1024]{1,0:T(8,128)(2,1)S(1)}, u32[]{:S(2)}, u32[]{:S(2)}) collective-permute-start(bf16[48,1024]{1,0:T(8,128)(2,1)S(1)} %get-tuple-element.49), channel_id=1, source_target_pairs={{1,0},{32,1},{33,32},{64,33},{65,64},{96,65},{97,96},{128,97},{129... | collective-permute-start | bytes 294920 | tf_op jit(solution)/shard_map/ppermute | solution.py:81
  48.8 2.7 %shard_map.97.sent_in = bf16[32,96,384]{2,1,0:T(8,128)(2,1)} custom-call(bf16[8,2,96,128]{3,2,1,0:T(8,128)(2,1)S(1)} %get-tuple-element.52.packed, s32[16,8,128]{2,1,0:T(8,128)S(1)} %get-tuple-element.47.ids), custom_call_target="tpu_custom_call" | custom-call | flops 301989888 | bytes 2818048 | tf_op jit(solution)/shard_map/pallas_call | solution.py:35
  51.6 0.0 collective-permute-done.2.zlo
  51.6 0.0 collective-permute-done.3.zhi
  51.6 3.7 %shard_map.98 = (bf16[8,2,96,128]{3,2,1,0:T(8,128)(2,1)}, bf16[32,96,384]{2,1,0:T(8,128)(2,1)}) custom-call(f32[192,1024]{1,0:T(8,128)S(1)} %get-tuple-element.46.u, bf16[64,1024]{1,0:T(8,128)(2,1)S(1)} %get-tuple-element.41.w, s32[16,8,128]{2,1,0:T(8,128)S(1)} %get-tuple-element.47.ids, ...), custom_call_target="tpu_custom_call", output_to_operand_aliasing={{1}: (8, {})} | custom-call | flops 704643072 | bytes 8486912 | tf_op jit(solution)/shard_map/pallas_call | solution.py:35
  55.3 5.2 %all-to-all-start.1 = ((bf16[32,96,384]{2,1,0:T(8,128)(2,1)}), bf16[32,96,384]{2,1,0:T(8,128)(2,1)S(1)}, u32[]{:S(2)}, u32[]{:S(2)}) async-start(bf16[32,96,384]{2,1,0:T(8,128)(2,1)} %get-tuple-element.54), calls=%async_computation.1 | async-start | bytes 4718592 | tf_op jit(solution)/shard_map/all_to_all | solution.py:523
  60.5 0.1 pad_add_fusion.refs_0_.place
  60.6 56.2 %all-to-all-done.1.refs_1_ = bf16[32,96,384]{2,1,0:T(8,128)(2,1)S(1)} async-done(((bf16[32,96,384]{2,1,0:T(8,128)(2,1)}), bf16[32,96,384]{2,1,0:T(8,128)(2,1)S(1)}, u32[]{:S(2)}, u32[]{:S(2)}) %all-to-all-start.1) | async-done | bytes 2359328 | tf_op jit(solution)/shard_map/all_to_all | solution.py:523
  116.8 0.0 copy-start
  116.8 6.6 %shard_map.99 = (bf16[768,768]{1,0:T(8,128)(2,1)S(1)}, bf16[1024,768]{1,0:T(8,128)(2,1)S(1)}, bf16[1024,768]{1,0:T(8,128)(2,1)S(1)}, bf16[768,768]{1,0:T(8,128)(2,1)S(1)}, bf16[512,768]{1,0:T(8,128)(2,1)S(1)}) custom-call(s32[2]{0:T(128)S(1)} %pad_add_fusion.refs_0_.place, bf16[32,96,384]{2,1,0:T(8,128)(2,1)S(1)} %all-to-all-done.1.refs_1_, ...), custom_call_target="tpu_custom_call" | custom-call | flops 3019898880 | bytes 11796488 | tf_op jit(solution)/shard_map/pallas_call | solution.py:35
  123.4 0.2 collective-permute-start.5
  123.6 0.0 copy-done
  123.6 2.5 %shard_map.100 = (bf16[1024,768]{1,0:T(8,128)(2,1)S(1)}, bf16[384,1024]{1,0:T(8,128)(2,1)S(1)}) custom-call(s32[2]{0:T(128)S(1)} %pad_add_fusion.refs_0_.place, bf16[768,768]{1,0:T(8,128)(2,1)S(1)} %get-tuple-element.56.d, bf16[1024,768]{1,0:T(8,128)(2,1)S(1)} %get-tuple-element.57.slope, bf16[1024,768]{1,0:T(8,128)(2,1)S(1)} %bitcast.14, ...), custom_call_target="tpu_custom_call" | custom-call | flops 1811939328 | bytes 7864328 | tf_op jit(solution)/shard_map/pallas_call | solution.py:35
  126.1 0.5 collective-permute-start.4
  126.6 0.0 collective-permute-done.5.got
  126.6 1.3 shard_map.101
  127.9 0.6 collective-permute-done.4.got
  128.5 1.4 shard_map.102
  129.9 1.1 collective-permute-start.6
  131.0 2.2 %collective-permute-start.7 = (bf16[2,128,768]{2,1,0:T(8,128)(2,1)S(1)}, bf16[2,128,768]{2,1,0:T(8,128)(2,1)S(1)}, u32[]{:S(2)}, u32[]{:S(2)}) collective-permute-start(bf16[2,128,768]{2,1,0:T(8,128)(2,1)S(1)} %get-tuple-element.70), channel_id=1, source_target_pairs={{64,0},{96,32},{128,64},{160,96},{192,128},{224,160},{0,192},{32,2... | collective-permute-start | bytes 1179656 | tf_op jit(solution)/shard_map/ppermute | solution.py:535
  133.2 6.6 %all-to-all-start.2 = ((bf16[16,96,128]{2,1,0:T(8,128)(2,1)}), bf16[16,96,128]{2,1,0:T(8,128)(2,1)S(1)}, u32[]{:S(2)}, u32[]{:S(2)}) async-start(bf16[16,96,128]{2,1,0:T(8,128)(2,1)} %bitcast.8), calls=%async_computation.2 | async-start | bytes 786432 | tf_op jit(solution)/shard_map/all_to_all | solution.py:523
  139.8 2.7 %collective-permute-done.6.from_before.first_before = bf16[2,128,768]{2,1,0:T(8,128)(2,1)S(1)} collective-permute-done((bf16[2,128,768]{2,1,0:T(8,128)(2,1)S(1)}, bf16[2,128,768]{2,1,0:T(8,128)(2,1)S(1)}, u32[]{:S(2)}, u32[]{:S(2)}) %collective-permute-start.6) | collective-permute-done | bytes 393248 | tf_op jit(solution)/shard_map/ppermute | solution.py:535
  142.6 0.0 collective-permute-done.7.from_after.first_after
  142.6 0.1 shard_map.104
  142.7 1.0 collective-permute-start.8
  143.6 2.3 %collective-permute-start.9 = (bf16[2,64,768]{2,1,0:T(8,128)(2,1)S(1)}, bf16[2,64,768]{2,1,0:T(8,128)(2,1)S(1)}, u32[]{:S(2)}, u32[]{:S(2)}) collective-permute-start(bf16[2,64,768]{2,1,0:T(8,128)(2,1)S(1)} %get-tuple-element.74), channel_id=1, source_target_pairs={{64,0},{96,32},{128,64},{160,96},{192,128},{224,160},{0,192},{32,2... | collective-permute-start | bytes 589832 | tf_op jit(solution)/shard_map/ppermute | solution.py:535
  146.0 4.3 %collective-permute-done.8.last_before = bf16[2,64,768]{2,1,0:T(8,128)(2,1)S(1)} collective-permute-done((bf16[2,64,768]{2,1,0:T(8,128)(2,1)S(1)}, bf16[2,64,768]{2,1,0:T(8,128)(2,1)S(1)}, u32[]{:S(2)}, u32[]{:S(2)}) %collective-permute-start.8) | collective-permute-done | bytes 196640 | tf_op jit(solution)/shard_map/ppermute | solution.py:535
  150.3 0.0 collective-permute-done.9.last_after
  150.3 0.9 shard_map.105
  151.3 1.6 %all-to-all-done.2.got = bf16[16,96,128]{2,1,0:T(8,128)(2,1)S(1)} async-done(((bf16[16,96,128]{2,1,0:T(8,128)(2,1)}), bf16[16,96,128]{2,1,0:T(8,128)(2,1)S(1)}, u32[]{:S(2)}, u32[]{:S(2)}) %all-to-all-start.2) | async-done | bytes 393248 | tf_op jit(solution)/shard_map/all_to_all | solution.py:523
  152.9 1.2 shard_map.103
Async XLA Ops:
  32.7 8.7 %collective-permute-start = (bf16[56,1024]{1,0:T(8,128)(2,1)S(1)}, bf16[56,1024]{1,0:T(8,128)(2,1)S(1)}, u32[]{:S(2)}, u32[]{:S(2)}) collective-permute-start(bf16[56,1024]{1,0:T(8,128)(2,1)S(1)} %get-tuple-element.44), channel_id=1, source_target_pairs={{0,1},{1,32},{32,33},{33,64},{64,65},{65,96},{96,97},{97,128},{128... | collective-permute-start | bytes 344072 | tf_op jit(solution)/shard_map/ppermute | solution.py:81
  34.9 7.1 %collective-permute-start.1 = (bf16[56,1024]{1,0:T(8,128)(2,1)S(1)}, bf16[56,1024]{1,0:T(8,128)(2,1)S(1)}, u32[]{:S(2)}, u32[]{:S(2)}) collective-permute-start(bf16[56,1024]{1,0:T(8,128)(2,1)S(1)} %get-tuple-element.45), channel_id=1, source_target_pairs={{1,0},{32,1},{33,32},{64,33},{65,64},{96,65},{97,96},{128,97},{129... | collective-permute-start | bytes 344072 | tf_op jit(solution)/shard_map/ppermute | solution.py:81
  43.4 8.2 %collective-permute-start.2 = (bf16[48,1024]{1,0:T(8,128)(2,1)S(1)}, bf16[48,1024]{1,0:T(8,128)(2,1)S(1)}, u32[]{:S(2)}, u32[]{:S(2)}) collective-permute-start(bf16[48,1024]{1,0:T(8,128)(2,1)S(1)} %get-tuple-element.48), channel_id=1, source_target_pairs={{0,1},{1,32},{32,33},{33,64},{64,65},{65,96},{96,97},{97,128},{128... | collective-permute-start | bytes 294920 | tf_op jit(solution)/shard_map/ppermute | solution.py:81
  43.5 8.1 %collective-permute-start.3 = (bf16[48,1024]{1,0:T(8,128)(2,1)S(1)}, bf16[48,1024]{1,0:T(8,128)(2,1)S(1)}, u32[]{:S(2)}, u32[]{:S(2)}) collective-permute-start(bf16[48,1024]{1,0:T(8,128)(2,1)S(1)} %get-tuple-element.49), channel_id=1, source_target_pairs={{1,0},{32,1},{33,32},{64,33},{65,64},{96,65},{97,96},{128,97},{129... | collective-permute-start | bytes 294920 | tf_op jit(solution)/shard_map/ppermute | solution.py:81
  55.3 61.5 %all-to-all-start.1 = ((bf16[32,96,384]{2,1,0:T(8,128)(2,1)}), bf16[32,96,384]{2,1,0:T(8,128)(2,1)S(1)}, u32[]{:S(2)}, u32[]{:S(2)}) async-start(bf16[32,96,384]{2,1,0:T(8,128)(2,1)} %get-tuple-element.54), calls=%async_computation.1 | async-start | bytes 4718592 | tf_op jit(solution)/shard_map/all_to_all | solution.py:523
  116.8 6.8 %copy-start = (bf16[1,1024,768]{2,1,0:T(8,128)(2,1)S(1)}, bf16[1,1024,768]{2,1,0:T(8,128)(2,1)}, u32[]{:S(2)}) copy-start(bf16[1,1024,768]{2,1,0:T(8,128)(2,1)} %param.13) | copy-start | bytes 4718596
  123.4 3.2 %collective-permute-start.5 = (bf16[512,768]{1,0:T(8,128)(2,1)S(1)}, bf16[512,768]{1,0:T(8,128)(2,1)S(1)}, u32[]{:S(2)}, u32[]{:S(2)}) collective-permute-start(bf16[512,768]{1,0:T(8,128)(2,1)S(1)} %get-tuple-element.61), channel_id=1, source_target_pairs={{0,32},{32,0},{64,96},{96,64},{128,160},{160,128},{192,224},{224,1... | collective-permute-start | bytes 2359304 | tf_op jit(solution)/shard_map/ppermute | solution.py:528
  126.1 2.4 %collective-permute-start.4 = (bf16[384,1024]{1,0:T(8,128)(2,1)S(1)}, bf16[384,1024]{1,0:T(8,128)(2,1)S(1)}, u32[]{:S(2)}, u32[]{:S(2)}) collective-permute-start(bf16[384,1024]{1,0:T(8,128)(2,1)S(1)} %get-tuple-element.59), channel_id=1, source_target_pairs={{0,32},{32,0},{64,96},{96,64},{128,160},{160,128},{192,224},{224,1... | collective-permute-start | bytes 2359304 | tf_op jit(solution)/shard_map/ppermute | solution.py:528
  129.9 12.7 %collective-permute-start.6 = (bf16[2,128,768]{2,1,0:T(8,128)(2,1)S(1)}, bf16[2,128,768]{2,1,0:T(8,128)(2,1)S(1)}, u32[]{:S(2)}, u32[]{:S(2)}) collective-permute-start(bf16[2,128,768]{2,1,0:T(8,128)(2,1)S(1)} %get-tuple-element.69), channel_id=1, source_target_pairs={{0,64},{32,96},{64,128},{96,160},{128,192},{160,224},{192,0},{224,... | collective-permute-start | bytes 1179656 | tf_op jit(solution)/shard_map/ppermute | solution.py:535
  131.0 11.6 %collective-permute-start.7 = (bf16[2,128,768]{2,1,0:T(8,128)(2,1)S(1)}, bf16[2,128,768]{2,1,0:T(8,128)(2,1)S(1)}, u32[]{:S(2)}, u32[]{:S(2)}) collective-permute-start(bf16[2,128,768]{2,1,0:T(8,128)(2,1)S(1)} %get-tuple-element.70), channel_id=1, source_target_pairs={{64,0},{96,32},{128,64},{160,96},{192,128},{224,160},{0,192},{32,2... | collective-permute-start | bytes 1179656 | tf_op jit(solution)/shard_map/ppermute | solution.py:535
  133.2 19.7 %all-to-all-start.2 = ((bf16[16,96,128]{2,1,0:T(8,128)(2,1)}), bf16[16,96,128]{2,1,0:T(8,128)(2,1)S(1)}, u32[]{:S(2)}, u32[]{:S(2)}) async-start(bf16[16,96,128]{2,1,0:T(8,128)(2,1)} %bitcast.8), calls=%async_computation.2 | async-start | bytes 786432 | tf_op jit(solution)/shard_map/all_to_all | solution.py:523
  142.7 7.7 %collective-permute-start.8 = (bf16[2,64,768]{2,1,0:T(8,128)(2,1)S(1)}, bf16[2,64,768]{2,1,0:T(8,128)(2,1)S(1)}, u32[]{:S(2)}, u32[]{:S(2)}) collective-permute-start(bf16[2,64,768]{2,1,0:T(8,128)(2,1)S(1)} %get-tuple-element.73), channel_id=1, source_target_pairs={{0,64},{32,96},{64,128},{96,160},{128,192},{160,224},{192,0},{224,... | collective-permute-start | bytes 589832 | tf_op jit(solution)/shard_map/ppermute | solution.py:535
  143.6 6.7 %collective-permute-start.9 = (bf16[2,64,768]{2,1,0:T(8,128)(2,1)S(1)}, bf16[2,64,768]{2,1,0:T(8,128)(2,1)S(1)}, u32[]{:S(2)}, u32[]{:S(2)}) collective-permute-start(bf16[2,64,768]{2,1,0:T(8,128)(2,1)S(1)} %get-tuple-element.74), channel_id=1, source_target_pairs={{64,0},{96,32},{128,64},{160,96},{192,128},{224,160},{0,192},{32,2... | collective-permute-start | bytes 589832 | tf_op jit(solution)/shard_map/ppermute | solution.py:535

commit v12 on v11

--- a/solution.py
+++ b/solution.py
@@ -261,7 +261,7 @@
 
 
 def first_kernel(
-    v, w, x_halo, w_halo, zlo, zhi, a, u, packed, z_first, z_last, x_before_out, x_after_out, e
+    v, w, x_halo, w_halo, zlo, zhi, a, u, z_first, z_last, x_before_out, x_after_out, e
 ):
     zn = 4
     rows = x_halo.shape[0] // 4
@@ -280,11 +280,11 @@
     x_after_out[...] = solved[count + rows : count + 2 * rows]
     z_first[...] = u[0:f].astype(BF16)
     z_last[...] = u[(zn - 1) * f : zn * f].astype(BF16)
-    pack_columns(u, packed, zn)
-
-
-def sample_kernel(packed, ids, sent_far, picked, sent, sems):
+
+
+def sample_kernel(u, ids, sent_far, packed, picked, sent, sems):
     copies = Copies(sems)
+    pack_columns(u, packed, 4)
     sample(packed, ids, picked, sent, message_part(copies, sent, sent_far, 0))
     copies.finish()
 
@@ -379,13 +379,13 @@
 ):
     copies = Copies(sems)
     f = got.shape[1] // 2
-    wide = 512
-    count = hidden.shape[0] // wide
-    parts = [(slice(None), pl.ds(i * wide, wide)) for i in range(count)]
+    count = 2
+    bounds = [0, hidden.shape[0] // 4, hidden.shape[0]]
+    parts = [(slice(None), pl.ds(i, j - i)) for i, j in zip(bounds, bounds[1:])]
     arriving = copies.start(w_in_far.at[parts[0]], w_in.at[parts[0]])
     gather_rows(got, 0, x)
     for i in range(count):
-        at = slice(i * wide, (i + 1) * wide)
+        at = slice(bounds[i], bounds[i + 1])
         copies.wait(arriving)
         if i + 1 < count:
             arriving = copies.start(w_in_far.at[parts[i + 1]], w_in.at[parts[i + 1]])
@@ -591,9 +591,9 @@
     blocks = shaped((peers // 2, 2, 2 * f, lanes), BF16)
     half_blocks = shaped((peers // 2, 2 * f, lanes), BF16)
     sampling[0] = pltpu.VMEM(blocks.shape, BF16)
-    u, packed, z_first, z_last, xlo, xhi = call(
+    u, z_first, z_last, xlo, xhi = call(
         first_kernel,
-        (shaped((zn * f, total_y), F32), blocks, edge, edge, x_edge, x_edge),
+        (shaped((zn * f, total_y), F32), edge, edge, x_edge, x_edge),
         (v, w, x_halo, w_halo, zlo, zhi, inverse),
         scratch=[pltpu.VMEM((zn * f + 32, total_y), BF16)],
         flops=solve_flops,
@@ -602,8 +602,8 @@
     sent = call(
         sample_kernel,
         both,
-        (packed, ids),
-        scratch=sampling[1:] + [pltpu.SemaphoreType.DMA((6,))],
+        (u, ids),
+        scratch=sampling + [pltpu.SemaphoreType.DMA((6,))],
         flops=sample_flops,
         far_out=(0,),
     )

time: 155 us -> 156 us (level)
  no operation moved by 1% of the time
where the time goes in v12:
time: 156 us; the launch traced here: 155 us
  waiting for transfers between devices  66.7 us (43%)
  starting transfers between devices  30.3 us (19%)
  blocking collectives  29.8 us (19%)
  Pallas kernels  24.5 us (16%)
  other arithmetic  2.58 us (2%)
    all_to_all x2, waiting for transfers between devices, exchange(): return lax.all_to_all(array, axis, split_axis=0, concat_axis=0, tiled=True)  58 us
    all_to_all x1, blocking collectives, exchange(): return lax.all_to_all(array, axis, split_axis=0, concat_axis=0, tiled=True)  29.8 us
    pallas_call x12, Pallas kernels, call(): pl.pallas_call(kernel, out_shape=pinned if isinstance(out_shape, tuple) e...  24.5 us
    all_to_all x2, starting transfers between devices, exchange(): return lax.all_to_all(array, axis, split_axis=0, concat_axis=0, tiled=True)  12 us
    ppermute x4, starting transfers between devices, shift(): return (lax.ppermute(last, axis, up), lax.ppermute(first, axis, down))  10.9 us
    ppermute x4, waiting for transfers between devices, shift_chips(): return (lax.ppermute(forward, 'px', up), lax.ppermute(backward, 'px', down))  6.84 us
    ppermute x4, starting transfers between devices, shift_chips(): return (lax.ppermute(forward, 'px', up), lax.ppermute(backward, 'px', down))  6.64 us
  transfers between devices with their start and end apart: 12, of which 7 were waited for; matrix products, arithmetic and copies ran while one was open for 2% of the time, Pallas kernels for 5%

profile of v12, /device:TPU:2, one launch (start us, length us, event | category | flops | bytes accessed | tf_op | source)
XLA Modules:
  0.0 154.7 jit_solution(3370051803520807494)
XLA Ops:
  0.6 1.8 %shard_map.94 = bf16[16,168,128]{2,1,0:T(8,128)(2,1)S(1)} custom-call(f32[64,3,4,256]{3,2,1,0:T(4,128)} %bitcast.15, f32[64,4,256]{2,1,0:T(4,128)} %w_far.1, s32[24,32]{1,0:T(8,128)} %bitcast.17, s32[1,32]{1,0:T(1,128)} %bitcast.18), custom_call_target="tpu_custom_call" | custom-call | flops 1000000 | bytes 1739904 | tf_op jit(solution)/shard_map/pallas_call | solution.py:35
  2.4 29.8 %all_to_all.15.got = bf16[16,168,128]{2,1,0:T(8,128)(2,1)S(1)} all-to-all(bf16[16,168,128]{2,1,0:T(8,128)(2,1)S(1)} %shard_map.94), channel_id=1, replica_groups=mesh['px'=8,'pz'=16,'tr'=2] {'pz'}, dimensions={0} | all-to-all | bytes 1376256 | tf_op jit(solution)/shard_map/all_to_all | solution.py:523
  32.3 0.4 shard_map.95
  32.7 2.2 %collective-permute-start = (bf16[56,1024]{1,0:T(8,128)(2,1)S(1)}, bf16[56,1024]{1,0:T(8,128)(2,1)S(1)}, u32[]{:S(2)}, u32[]{:S(2)}) collective-permute-start(bf16[56,1024]{1,0:T(8,128)(2,1)S(1)} %get-tuple-element.43), channel_id=1, source_target_pairs={{0,1},{1,32},{32,33},{33,64},{64,65},{65,96},{96,97},{97,128},{128... | collective-permute-start | bytes 344072 | tf_op jit(solution)/shard_map/ppermute | solution.py:81
  34.9 3.2 %collective-permute-start.1 = (bf16[56,1024]{1,0:T(8,128)(2,1)S(1)}, bf16[56,1024]{1,0:T(8,128)(2,1)S(1)}, u32[]{:S(2)}, u32[]{:S(2)}) collective-permute-start(bf16[56,1024]{1,0:T(8,128)(2,1)S(1)} %get-tuple-element.44), channel_id=1, source_target_pairs={{1,0},{32,1},{33,32},{64,33},{65,64},{96,65},{97,96},{128,97},{129... | collective-permute-start | bytes 344072 | tf_op jit(solution)/shard_map/ppermute | solution.py:81
  38.1 2.5 %convert_element_type.3.a = bf16[1024,1024]{1,0:T(8,128)(2,1)S(1)} convert(f32[1024,1024]{1,0:T(8,128)} %param.9) | non-fusion elementwise | flops 1048576 | bytes 6291456 | tf_op jit(solution)/shard_map/convert_element_type | solution.py:568
  40.7 0.7 collective-permute-done.zlo
  41.4 0.6 collective-permute-done.1.zhi
  42.0 1.3 shard_map.96
  43.3 0.1 collective-permute-start.2
  43.4 5.3 %collective-permute-start.3 = (bf16[48,1024]{1,0:T(8,128)(2,1)S(1)}, bf16[48,1024]{1,0:T(8,128)(2,1)S(1)}, u32[]{:S(2)}, u32[]{:S(2)}) collective-permute-start(bf16[48,1024]{1,0:T(8,128)(2,1)S(1)} %get-tuple-element.48), channel_id=1, source_target_pairs={{1,0},{32,1},{33,32},{64,33},{65,64},{96,65},{97,96},{128,97},{129... | collective-permute-start | bytes 294920 | tf_op jit(solution)/shard_map/ppermute | solution.py:81
  48.7 2.9 %shard_map.97.sent_in = bf16[32,96,384]{2,1,0:T(8,128)(2,1)} custom-call(f32[192,1024]{1,0:T(8,128)S(1)} %get-tuple-element.45.u, s32[16,8,128]{2,1,0:T(8,128)S(1)} %get-tuple-element.46.ids), custom_call_target="tpu_custom_call" | custom-call | flops 301989888 | bytes 3211264 | tf_op jit(solution)/shard_map/pallas_call | solution.py:35
  51.6 0.0 collective-permute-done.2.zlo
  51.6 0.0 collective-permute-done.3.zhi
  51.7 3.7 %shard_map.98 = (bf16[8,2,96,128]{3,2,1,0:T(8,128)(2,1)}, bf16[32,96,384]{2,1,0:T(8,128)(2,1)}) custom-call(f32[192,1024]{1,0:T(8,128)S(1)} %get-tuple-element.45.u, bf16[64,1024]{1,0:T(8,128)(2,1)S(1)} %get-tuple-element.40.w, s32[16,8,128]{2,1,0:T(8,128)S(1)} %get-tuple-element.46.ids, ...), custom_call_target="tpu_custom_call", output_to_operand_aliasing={{1}: (8, {})} | custom-call | flops 704643072 | bytes 8486912 | tf_op jit(solution)/shard_map/pallas_call | solution.py:35
  55.4 5.2 %all-to-all-start.1 = ((bf16[32,96,384]{2,1,0:T(8,128)(2,1)}), bf16[32,96,384]{2,1,0:T(8,128)(2,1)S(1)}, u32[]{:S(2)}, u32[]{:S(2)}) async-start(bf16[32,96,384]{2,1,0:T(8,128)(2,1)} %get-tuple-element.52), calls=%async_computation.1 | async-start | bytes 4718592 | tf_op jit(solution)/shard_map/all_to_all | solution.py:523
  60.6 0.1 pad_add_fusion.refs_0_.place
  60.7 56.1 %all-to-all-done.1.refs_1_ = bf16[32,96,384]{2,1,0:T(8,128)(2,1)S(1)} async-done(((bf16[32,96,384]{2,1,0:T(8,128)(2,1)}), bf16[32,96,384]{2,1,0:T(8,128)(2,1)S(1)}, u32[]{:S(2)}, u32[]{:S(2)}) %all-to-all-start.1) | async-done | bytes 2359328 | tf_op jit(solution)/shard_map/all_to_all | solution.py:523
  116.7 0.0 copy-start
  116.7 6.9 %shard_map.99 = (bf16[768,768]{1,0:T(8,128)(2,1)S(1)}, bf16[1024,768]{1,0:T(8,128)(2,1)S(1)}, bf16[1024,768]{1,0:T(8,128)(2,1)S(1)}, bf16[768,768]{1,0:T(8,128)(2,1)S(1)}, bf16[512,768]{1,0:T(8,128)(2,1)S(1)}) custom-call(s32[2]{0:T(128)S(1)} %pad_add_fusion.refs_0_.place, bf16[32,96,384]{2,1,0:T(8,128)(2,1)S(1)} %all-to-all-done.1.refs_1_, ...), custom_call_target="tpu_custom_call" | custom-call | flops 3019898880 | bytes 11796488 | tf_op jit(solution)/shard_map/pallas_call | solution.py:35
  123.7 0.2 collective-permute-start.5
  123.9 0.0 copy-done
  123.9 2.5 %shard_map.100 = (bf16[1024,768]{1,0:T(8,128)(2,1)S(1)}, bf16[384,1024]{1,0:T(8,128)(2,1)S(1)}) custom-call(s32[2]{0:T(128)S(1)} %pad_add_fusion.refs_0_.place, bf16[768,768]{1,0:T(8,128)(2,1)S(1)} %get-tuple-element.54.d, bf16[1024,768]{1,0:T(8,128)(2,1)S(1)} %get-tuple-element.55.slope, bf16[1024,768]{1,0:T(8,128)(2,1)S(1)} %bitcast.14, ...), custom_call_target="tpu_custom_call" | custom-call | flops 1811939328 | bytes 7864328 | tf_op jit(solution)/shard_map/pallas_call | solution.py:35
  126.4 0.5 collective-permute-start.4
  126.9 0.0 collective-permute-done.5.got
  126.9 1.4 shard_map.101
  128.3 0.5 collective-permute-done.4.got
  128.8 1.4 shard_map.102
  130.2 1.1 collective-permute-start.6
  131.3 2.3 %collective-permute-start.7 = (bf16[2,128,768]{2,1,0:T(8,128)(2,1)S(1)}, bf16[2,128,768]{2,1,0:T(8,128)(2,1)S(1)}, u32[]{:S(2)}, u32[]{:S(2)}) collective-permute-start(bf16[2,128,768]{2,1,0:T(8,128)(2,1)S(1)} %get-tuple-element.68), channel_id=1, source_target_pairs={{64,0},{96,32},{128,64},{160,96},{192,128},{224,160},{0,192},{32,2... | collective-permute-start | bytes 1179656 | tf_op jit(solution)/shard_map/ppermute | solution.py:535
  133.5 6.8 %all-to-all-start.2 = ((bf16[16,96,128]{2,1,0:T(8,128)(2,1)}), bf16[16,96,128]{2,1,0:T(8,128)(2,1)S(1)}, u32[]{:S(2)}, u32[]{:S(2)}) async-start(bf16[16,96,128]{2,1,0:T(8,128)(2,1)} %bitcast.8), calls=%async_computation.2 | async-start | bytes 786432 | tf_op jit(solution)/shard_map/all_to_all | solution.py:523
  140.4 2.5 %collective-permute-done.6.from_before.first_before = bf16[2,128,768]{2,1,0:T(8,128)(2,1)S(1)} collective-permute-done((bf16[2,128,768]{2,1,0:T(8,128)(2,1)S(1)}, bf16[2,128,768]{2,1,0:T(8,128)(2,1)S(1)}, u32[]{:S(2)}, u32[]{:S(2)}) %collective-permute-start.6) | collective-permute-done | bytes 393248 | tf_op jit(solution)/shard_map/ppermute | solution.py:535
  142.9 0.0 collective-permute-done.7.from_after.first_after
  142.9 0.1 shard_map.104
  143.0 1.0 collective-permute-start.8
  144.0 2.3 %collective-permute-start.9 = (bf16[2,64,768]{2,1,0:T(8,128)(2,1)S(1)}, bf16[2,64,768]{2,1,0:T(8,128)(2,1)S(1)}, u32[]{:S(2)}, u32[]{:S(2)}) collective-permute-start(bf16[2,64,768]{2,1,0:T(8,128)(2,1)S(1)} %get-tuple-element.72), channel_id=1, source_target_pairs={{64,0},{96,32},{128,64},{160,96},{192,128},{224,160},{0,192},{32,2... | collective-permute-start | bytes 589832 | tf_op jit(solution)/shard_map/ppermute | solution.py:535
  146.3 4.3 %collective-permute-done.8.last_before = bf16[2,64,768]{2,1,0:T(8,128)(2,1)S(1)} collective-permute-done((bf16[2,64,768]{2,1,0:T(8,128)(2,1)S(1)}, bf16[2,64,768]{2,1,0:T(8,128)(2,1)S(1)}, u32[]{:S(2)}, u32[]{:S(2)}) %collective-permute-start.8) | collective-permute-done | bytes 196640 | tf_op jit(solution)/shard_map/ppermute | solution.py:535
  150.6 0.0 collective-permute-done.9.last_after
  150.6 0.9 shard_map.105
  151.6 1.9 %all-to-all-done.2.got = bf16[16,96,128]{2,1,0:T(8,128)(2,1)S(1)} async-done(((bf16[16,96,128]{2,1,0:T(8,128)(2,1)}), bf16[16,96,128]{2,1,0:T(8,128)(2,1)S(1)}, u32[]{:S(2)}, u32[]{:S(2)}) %all-to-all-start.2) | async-done | bytes 393248 | tf_op jit(solution)/shard_map/all_to_all | solution.py:523
  153.5 1.2 shard_map.103
Async XLA Ops:
  32.7 8.7 %collective-permute-start = (bf16[56,1024]{1,0:T(8,128)(2,1)S(1)}, bf16[56,1024]{1,0:T(8,128)(2,1)S(1)}, u32[]{:S(2)}, u32[]{:S(2)}) collective-permute-start(bf16[56,1024]{1,0:T(8,128)(2,1)S(1)} %get-tuple-element.43), channel_id=1, source_target_pairs={{0,1},{1,32},{32,33},{33,64},{64,65},{65,96},{96,97},{97,128},{128... | collective-permute-start | bytes 344072 | tf_op jit(solution)/shard_map/ppermute | solution.py:81
  34.9 7.1 %collective-permute-start.1 = (bf16[56,1024]{1,0:T(8,128)(2,1)S(1)}, bf16[56,1024]{1,0:T(8,128)(2,1)S(1)}, u32[]{:S(2)}, u32[]{:S(2)}) collective-permute-start(bf16[56,1024]{1,0:T(8,128)(2,1)S(1)} %get-tuple-element.44), channel_id=1, source_target_pairs={{1,0},{32,1},{33,32},{64,33},{65,64},{96,65},{97,96},{128,97},{129... | collective-permute-start | bytes 344072 | tf_op jit(solution)/shard_map/ppermute | solution.py:81
  43.3 8.3 %collective-permute-start.2 = (bf16[48,1024]{1,0:T(8,128)(2,1)S(1)}, bf16[48,1024]{1,0:T(8,128)(2,1)S(1)}, u32[]{:S(2)}, u32[]{:S(2)}) collective-permute-start(bf16[48,1024]{1,0:T(8,128)(2,1)S(1)} %get-tuple-element.47), channel_id=1, source_target_pairs={{0,1},{1,32},{32,33},{33,64},{64,65},{65,96},{96,97},{97,128},{128... | collective-permute-start | bytes 294920 | tf_op jit(solution)/shard_map/ppermute | solution.py:81
  43.4 8.2 %collective-permute-start.3 = (bf16[48,1024]{1,0:T(8,128)(2,1)S(1)}, bf16[48,1024]{1,0:T(8,128)(2,1)S(1)}, u32[]{:S(2)}, u32[]{:S(2)}) collective-permute-start(bf16[48,1024]{1,0:T(8,128)(2,1)S(1)} %get-tuple-element.48), channel_id=1, source_target_pairs={{1,0},{32,1},{33,32},{64,33},{65,64},{96,65},{97,96},{128,97},{129... | collective-permute-start | bytes 294920 | tf_op jit(solution)/shard_map/ppermute | solution.py:81
  55.4 61.4 %all-to-all-start.1 = ((bf16[32,96,384]{2,1,0:T(8,128)(2,1)}), bf16[32,96,384]{2,1,0:T(8,128)(2,1)S(1)}, u32[]{:S(2)}, u32[]{:S(2)}) async-start(bf16[32,96,384]{2,1,0:T(8,128)(2,1)} %get-tuple-element.52), calls=%async_computation.1 | async-start | bytes 4718592 | tf_op jit(solution)/shard_map/all_to_all | solution.py:523
  116.7 7.1 %copy-start = (bf16[1,1024,768]{2,1,0:T(8,128)(2,1)S(1)}, bf16[1,1024,768]{2,1,0:T(8,128)(2,1)}, u32[]{:S(2)}) copy-start(bf16[1,1024,768]{2,1,0:T(8,128)(2,1)} %param.13) | copy-start | bytes 4718596
  123.7 3.2 %collective-permute-start.5 = (bf16[512,768]{1,0:T(8,128)(2,1)S(1)}, bf16[512,768]{1,0:T(8,128)(2,1)S(1)}, u32[]{:S(2)}, u32[]{:S(2)}) collective-permute-start(bf16[512,768]{1,0:T(8,128)(2,1)S(1)} %get-tuple-element.59), channel_id=1, source_target_pairs={{0,32},{32,0},{64,96},{96,64},{128,160},{160,128},{192,224},{224,1... | collective-permute-start | bytes 2359304 | tf_op jit(solution)/shard_map/ppermute | solution.py:528
  126.4 2.4 %collective-permute-start.4 = (bf16[384,1024]{1,0:T(8,128)(2,1)S(1)}, bf16[384,1024]{1,0:T(8,128)(2,1)S(1)}, u32[]{:S(2)}, u32[]{:S(2)}) collective-permute-start(bf16[384,1024]{1,0:T(8,128)(2,1)S(1)} %get-tuple-element.57), channel_id=1, source_target_pairs={{0,32},{32,0},{64,96},{96,64},{128,160},{160,128},{192,224},{224,1... | collective-permute-start | bytes 2359304 | tf_op jit(solution)/shard_map/ppermute | solution.py:528
  130.2 12.7 %collective-permute-start.6 = (bf16[2,128,768]{2,1,0:T(8,128)(2,1)S(1)}, bf16[2,128,768]{2,1,0:T(8,128)(2,1)S(1)}, u32[]{:S(2)}, u32[]{:S(2)}) collective-permute-start(bf16[2,128,768]{2,1,0:T(8,128)(2,1)S(1)} %get-tuple-element.67), channel_id=1, source_target_pairs={{0,64},{32,96},{64,128},{96,160},{128,192},{160,224},{192,0},{224,... | collective-permute-start | bytes 1179656 | tf_op jit(solution)/shard_map/ppermute | solution.py:535
  131.3 11.6 %collective-permute-start.7 = (bf16[2,128,768]{2,1,0:T(8,128)(2,1)S(1)}, bf16[2,128,768]{2,1,0:T(8,128)(2,1)S(1)}, u32[]{:S(2)}, u32[]{:S(2)}) collective-permute-start(bf16[2,128,768]{2,1,0:T(8,128)(2,1)S(1)} %get-tuple-element.68), channel_id=1, source_target_pairs={{64,0},{96,32},{128,64},{160,96},{192,128},{224,160},{0,192},{32,2... | collective-permute-start | bytes 1179656 | tf_op jit(solution)/shard_map/ppermute | solution.py:535
  133.5 19.9 %all-to-all-start.2 = ((bf16[16,96,128]{2,1,0:T(8,128)(2,1)}), bf16[16,96,128]{2,1,0:T(8,128)(2,1)S(1)}, u32[]{:S(2)}, u32[]{:S(2)}) async-start(bf16[16,96,128]{2,1,0:T(8,128)(2,1)} %bitcast.8), calls=%async_computation.2 | async-start | bytes 786432 | tf_op jit(solution)/shard_map/all_to_all | solution.py:523
  143.0 7.6 %collective-permute-start.8 = (bf16[2,64,768]{2,1,0:T(8,128)(2,1)S(1)}, bf16[2,64,768]{2,1,0:T(8,128)(2,1)S(1)}, u32[]{:S(2)}, u32[]{:S(2)}) collective-permute-start(bf16[2,64,768]{2,1,0:T(8,128)(2,1)S(1)} %get-tuple-element.71), channel_id=1, source_target_pairs={{0,64},{32,96},{64,128},{96,160},{128,192},{160,224},{192,0},{224,... | collective-permute-start | bytes 589832 | tf_op jit(solution)/shard_map/ppermute | solution.py:535
  144.0 6.6 %collective-permute-start.9 = (bf16[2,64,768]{2,1,0:T(8,128)(2,1)S(1)}, bf16[2,64,768]{2,1,0:T(8,128)(2,1)S(1)}, u32[]{:S(2)}, u32[]{:S(2)}) collective-permute-start(bf16[2,64,768]{2,1,0:T(8,128)(2,1)S(1)} %get-tuple-element.72), channel_id=1, source_target_pairs={{64,0},{96,32},{128,64},{160,96},{192,128},{224,160},{0,192},{32,2... | collective-permute-start | bytes 589832 | tf_op jit(solution)/shard_map/ppermute | solution.py:535
